TPU v7x, 256 devices: a whole 4x4x8 slice. The times are simulated.
256 devices in a mesh: ia: 32 (over z, x_lo, core), ja: 4 (over y), ka: 2 (over x_hi).
Axes of the slice: x: 4 (x_hi: 2, x_lo: 2; x = x_hi * 2 + x_lo), y: 4, z: 8, core: 2. Of those that a mesh axis runs over, the one named last changes fastest.
Arguments:
- tensor: float32 [8192, 8, 8192], P('ja', 'ka', 'ia'), may hold values from -6 to 6
- factor_a: float32 [8192, 128], P('ia'), may hold values from -1 to 1
- factor_c: float32 [8, 128], P('ka'), may hold values from -2 to 2
- gram_c: float32 [128, 128], replicated, may hold values from -12 to 24, as said below
Outputs:
- factor_b: float32 [8192, 128], P('ja')
- factor_c_new: float32 [8, 128], P('ka')
Inputs may be any that keep to these rules, and one draw needn't show every extreme that they name: `gram_c`: symmetric positive definite.
All inputs are finite; a program needn't handle non-finite values.
Results may differ from a plain program's by a relative error of at most 0.000071.
Values sent between devices are 32-bit elements; how exact they have to be, the bound alone decides.
No kernel may reach another device: no remote copies, remote signals or barrier semaphores. Data moves between devices by JAX's collectives and lax.ppermute only.
A program may use at most 64 MiB of HBM per device.

v0:
```python
import jax
import jax.numpy as jnp
from jax import lax
from jax.sharding import PartitionSpec as P


def right_solve(rhs, system):
    lower = jnp.linalg.cholesky(system)
    middle = lax.linalg.triangular_solve(lower, rhs, left_side=False, lower=True, transpose_a=True)
    return lax.linalg.triangular_solve(
        lower, middle, left_side=False, lower=True, transpose_a=False
    )


def body(tensor, factor_a, factor_c, gram_c):
    high = lax.Precision.HIGHEST
    mode_two, mode_three, mode_one = tensor.shape
    rank = factor_a.shape[1]
    gram_a = lax.psum(
        jnp.dot(factor_a.T, factor_a, precision=high, preferred_element_type=jnp.float32), "ia"
    )
    system_b = gram_a * gram_c
    count = mode_two // lax.axis_size("ia") * lax.axis_size("ia")
    flat = jnp.dot(
        tensor.reshape(count * mode_three, mode_one),
        factor_a,
        precision=high,
        preferred_element_type=jnp.float32,
    )
    shares = lax.psum_scatter(
        flat.reshape(count, mode_three, rank), "ia", scatter_dimension=0, tiled=True
    )
    local_b = lax.psum(jnp.sum(shares * factor_c[None, :, :], axis=1), "ka")
    rows_b = right_solve(local_b, system_b)
    local_c = jnp.sum(shares * rows_b[:, None, :], axis=0)
    local_gram = jnp.dot(rows_b.T, rows_b, precision=high, preferred_element_type=jnp.float32)
    mttkrp_c, gram_b = lax.psum((local_c, local_gram), ("ia", "ja"))
    factor_b = lax.all_gather(rows_b, "ia", axis=0, tiled=True)
    factor_c_new = right_solve(mttkrp_c, gram_a * gram_b)
    return (factor_b, factor_c_new)


def solution(mesh):
    placed = (P("ja", "ka", "ia"), P("ia", None), P("ka", None), P())
    return jax.shard_map(
        body, mesh=mesh, in_specs=placed, out_specs=(P("ja", None), P("ka", None)), check_vma=False
    )
```

profile of v0, /device:TPU:2, one launch (start us, length us, event | category | flops | bytes accessed | tf_op | source)
XLA Modules:
  0.0 1340.3 jit_solution(12914689093623090301)
XLA Ops:
  7.2 0.0 copy-start
  7.2 0.0 all-reduce.3.cloned.1.call-start
  7.2 0.8 copy-done
  8.1 1.0 fusion.15
  9.1 0.0 all-reduce.3.cloned.1.call-update
  9.1 0.0 copy-start.2
  9.1 0.0 copy-start.3
  9.1 0.0 reduce-scatter.2.cloned.1.call-start
  9.2 11.6 fusion
  20.7 0.0 reduce-scatter.2.cloned.1.call-update
  20.8 0.0 all-reduce.5.cloned.1.call-start
  20.8 0.0 copy-done.2
  20.8 0.1 copy.8
  20.9 185.0 %all-reduce.3.cloned.1.call-done = f32[128,128]{0,1:T(8,128)} async-done(((f32[128,128]{0,1:T(8,128)}), f32[128,128]{0,1:T(8,128)}) %all-reduce.3.cloned.1.call-update) | async-done | bytes 65552 | tf_op jit(solution)/shard_map/psum | solution.py:19
  206.0 0.8 mul.24
  206.8 0.1 copy.9
  206.9 11.7 cholesky.44
  218.7 0.6 compare_reduce_fusion.1
  219.3 0.7 fusion.3
  220.0 9.8 custom-call.12
  229.8 97.7 %reduce-scatter.2.cloned.1.call-done = f32[64,4,128]{2,0,1:T(8,128)} async-done(((f32[2048,4,128]{2,0,1:T(8,128)}), f32[64,4,128]{2,0,1:T(8,128)}) %reduce-scatter.2.cloned.1.call-update) | async-done | bytes 131088 | tf_op jit(solution)/shard_map/reduce_scatter | solution.py:30
  327.5 0.0 copy-done.3
  327.5 0.9 multiply_reduce_fusion.1
  328.4 11.0 psum.28
  339.5 0.2 fusion.12
  339.7 0.2 fusion.10
  339.9 0.0 copy-start.1
  339.9 0.9 fusion.16
  340.9 0.0 all-reduce.5.cloned.1.call-update
  340.9 0.0 all-gather.2.cloned.1.call-start
  340.9 0.0 copy-done.1
  340.9 0.5 all-gather.2.cloned.1.call-update
  341.5 0.9 multiply_reduce_fusion
  342.4 266.7 %psum.30 = f32[4,128]{1,0:T(4,128)S(1)} all-reduce(f32[4,128]{1,0:T(4,128)S(1)} %multiply_reduce_fusion), channel_id=1, replica_groups=mesh['ia'=32,'ja'=4,'ka'=2] {'ia','ja'}, use_global_device_ids=true, to_apply=%region_7.9 | all-reduce | flops 512 | bytes 4096 | tf_op jit(solution)/shard_map/psum | solution.py:37
  609.1 653.8 %all-reduce.5.cloned.1.call-done = f32[128,128]{0,1:T(8,128)} async-done(((f32[128,128]{0,1:T(8,128)}), f32[128,128]{0,1:T(8,128)}) %all-reduce.5.cloned.1.call-update) | async-done | bytes 65552 | tf_op jit(solution)/shard_map/psum | solution.py:37
  1262.8 0.9 mul.27
  1263.7 0.1 copy.11
  1263.8 11.7 cholesky.55
  1275.6 0.6 compare_reduce_fusion
  1276.2 0.7 fusion.4
  1276.9 9.8 custom-call.13
  1286.7 0.2 fusion.7
  1286.9 0.8 fusion.5
  1287.7 43.8 %all-gather.2.cloned.1.call-done = f32[2048,128]{1,0:T(8,128)} async-done(((f32[64,128]{1,0:T(8,128)}), f32[2048,128]{1,0:T(8,128)}) %all-gather.2.cloned.1.call-update) | async-done | bytes 1048592 | tf_op jit(solution)/shard_map/all_gather | solution.py:38
  1331.5 2.3 copy.19
  (4 shorter events, 0.1 us)
Async XLA Ops:
  7.2 0.9 copy-start
  7.2 198.8 %all-reduce.3.cloned.1.call-start = ((), (), s32[]{:S(2)}) async-start(), calls=%async_computation.2 | async-start | bytes 131072 | tf_op jit(solution)/shard_map/psum | solution.py:19
  9.1 11.7 copy-start.2
  9.1 318.4 %copy-start.3 = (f32[4,128]{1,0:T(4,128)S(1)}, f32[4,128]{1,0:T(4,128)}, u32[]{:S(2)}) copy-start(f32[4,128]{1,0:T(4,128)} %param.7) | copy-start | bytes 6148
  9.1 318.4 %reduce-scatter.2.cloned.1.call-start = ((), (), s32[]{:S(2)}) async-start(), calls=%async_computation.1 | async-start | bytes 4325376 | tf_op jit(solution)/shard_map/reduce_scatter | solution.py:30
  20.8 1242.1 %all-reduce.5.cloned.1.call-start = ((), (), s32[]{:S(2)}) async-start(), calls=%async_computation.4 | async-start | bytes 131072 | tf_op jit(solution)/shard_map/psum | solution.py:37
  339.9 1.0 copy-start.1
  340.9 990.6 %all-gather.2.cloned.1.call-start = ((), (), s32[]{:S(2)}) async-start(), calls=%async_computation.3 | async-start | bytes 1081344 | tf_op jit(solution)/shard_map/all_gather | solution.py:38
Sparse Core Ops, SparseCore 0:
  11.2 194.7 all-reduce.2
  208.7 118.8 reduce-scatter.1
  341.0 921.7 all-reduce.4
  1264.6 66.8 all-gather.1
where the time goes:
time: 1340 us
  waiting for transfers between devices  981 us (73%)
  blocking collectives  278 us (21%)
  other arithmetic  49.3 us (4%)
  matrix products  14.9 us (1%)
  between operations  13.9 us (1%)
    psum x1, waiting for transfers between devices, body(): mttkrp_c, gram_b = lax.psum((local_c, local_gram), ('ia', 'ja'))  654 us
    psum x1, blocking collectives, body(): mttkrp_c, gram_b = lax.psum((local_c, local_gram), ('ia', 'ja'))  267 us
    psum x1, waiting for transfers between devices, body(): lax.psum(jnp.dot(factor_a.T, factor_a, precision=high, preferred_element_...  185 us
    reduce_scatter x1, waiting for transfers between devices, body(): lax.psum_scatter(flat.reshape(count, mode_three, rank), 'ia', scatter_dim...  97.7 us
    all_gather x1, waiting for transfers between devices, body(): factor_b = lax.all_gather(rows_b, 'ia', axis=0, tiled=True)  43.8 us
  transfers between devices with their start and end apart: 4, of which 4 were waited for; matrix products, arithmetic and copies ran while one was open for 5% of the time, Pallas kernels for 0%

commit v1 on v0

v1 whole, which is shorter than its diff:
```python
import jax
import jax.numpy as jnp
from jax import lax
from jax.sharding import Mesh, PartitionSpec as P

HIGH = lax.Precision.HIGHEST
PLANE = ("xl", "xh", "z")


def right_solve(rhs, system):
    lower = jnp.linalg.cholesky(system)
    middle = lax.linalg.triangular_solve(lower, rhs, left_side=False, lower=True, transpose_a=True)
    return lax.linalg.triangular_solve(
        lower, middle, left_side=False, lower=True, transpose_a=False
    )


def swap(x, axis):
    return lax.ppermute(x, axis, [(0, 1), (1, 0)])


def gather(x, axes):
    n = lax.axis_size(axes)
    return lax.all_to_all(jnp.broadcast_to(x[None], (n,) + x.shape), axes, 0, 0)


def body(tensor, factor_a, factor_c, gram_c):
    f32 = jnp.float32
    mode_two, mode_three, mode_one = tensor.shape
    rank = factor_a.shape[1]
    core = lax.axis_index("c")
    plane = lax.axis_size(PLANE)
    pieces = 2 * plane
    rows, extra = mode_two // pieces, rank // pieces

    gram_part = jnp.dot(factor_a.T, factor_a, precision=HIGH, preferred_element_type=f32)
    partial = jnp.dot(
        tensor.reshape(mode_two * mode_three, mode_one),
        factor_a,
        precision=HIGH,
        preferred_element_type=f32,
    ).reshape(mode_two, mode_three, rank)
    part_b = jnp.sum(partial * factor_c[None], axis=1)

    both = jnp.concatenate(
        [
            part_b.reshape(2, plane, rows, rank),
            (0.5 * gram_part).reshape(2, plane, extra, rank),
        ],
        axis=2,
    )
    mine = lax.dynamic_index_in_dim(both, core, 0, keepdims=False)
    other = lax.dynamic_index_in_dim(both, 1 - core, 0, keepdims=False)
    half = mine + swap(other, "c")
    piece = jnp.sum(lax.all_to_all(half, PLANE, 0, 0), axis=0)

    column = gather(piece, "z")
    square = gather(column, ("xl", "xh")).reshape(plane, rows + extra, rank)
    theirs = swap(square, "c")
    first = jnp.where(core == 0, square, theirs)
    second = jnp.where(core == 0, theirs, square)
    whole = jnp.stack([first, second]).reshape(pieces, rows + extra, rank)
    mttkrp_b = whole[:, :rows].reshape(mode_two, rank)
    gram_a = whole[:, rows:].reshape(rank, rank)

    factor_b = right_solve(mttkrp_b, gram_a * gram_c)

    local_c = jnp.sum(partial * factor_b[:, None, :], axis=0)
    local_c = local_c + swap(local_c, "c")
    mttkrp_c = jnp.sum(gather(local_c, ("z", "xl", "y")), axis=0)
    gram_b = jnp.dot(factor_b.T, factor_b, precision=HIGH, preferred_element_type=f32)
    n = lax.axis_size("y")
    away = [lax.ppermute(gram_b, "y", [(i, i ^ k) for i in range(n)]) for k in range(1, n)]
    gram_b = (gram_b + away[0]) + (away[1] + away[2])
    factor_c_new = right_solve(mttkrp_c, gram_a * gram_b)
    return (factor_b, factor_c_new)


def solution(mesh):
    axes = (mesh.shape["ia"] // 4, 2, 2, mesh.shape["ja"], mesh.shape["ka"])
    fine = Mesh(mesh.devices.reshape(axes), ("z", "xl", "c", "y", "xh"))
    split = ("z", "xl", "c")
    placed = (P("y", "xh", split), P(split, None), P("xh", None), P())
    return jax.shard_map(
        body, mesh=fine, in_specs=placed, out_specs=(P("y", None), P("xh", None)), check_vma=False
    )
```

time: 1340 us -> 141 us (0.11)
  waiting for transfers between devices: 981 us -> 4.93 us
  blocking collectives: 278 us -> 54.6 us
    psum x2 -> x0, waiting for transfers between devices: 839 us -> none  [the longest x1 654 us: body(): mttkrp_c, gram_b = lax.psum((local_c, local_gram), ('ia', 'ja'))]
    psum x2 -> x0, blocking collectives: 278 us -> none  [the longest x1 267 us: body(): mttkrp_c, gram_b = lax.psum((local_c, local_gram), ('ia', 'ja'))]
    reduce_scatter x1 -> x0, waiting for transfers between devices: 97.7 us -> none  [body(): lax.psum_scatter(flat.reshape(count, mode_three, rank), 'ia', scatter_dim...]
    all_to_all x0 -> x3, blocking collectives: none -> 54.6 us  [the longest x1 30 us: body(): piece = jnp.sum(lax.all_to_all(half, PLANE, 0, 0), axis=0)]
    all_gather x1 -> x0, waiting for transfers between devices: 43.8 us -> none  [body(): factor_b = lax.all_gather(rows_b, 'ia', axis=0, tiled=True)]
  transfers between devices with their start and end apart: 4 -> 7, of which waited for: 4 -> 3; matrix products, arithmetic and copies ran while one was open for 5% -> 17% of each run, Pallas kernels for 0% -> 0%
where the time goes in v1:
time: 141 us; the launch traced here: 139 us
  blocking collectives  54.6 us (39%)
  other arithmetic  46.8 us (33%)
  matrix products  16.8 us (12%)
  starting transfers between devices  12.1 us (9%)
  waiting for transfers between devices  4.93 us (3%)
  local copies, waits for them, and re-layouts  3.34 us (2%)
    all_to_all x1, blocking collectives, body(): piece = jnp.sum(lax.all_to_all(half, PLANE, 0, 0), axis=0)  30 us
    another operation x6, other arithmetic, right_solve(): lower = jnp.linalg.cholesky(system)  24.8 us
    all_to_all x2, blocking collectives, gather(): return lax.all_to_all(jnp.broadcast_to(x[None], (n,) + x.shape), axes, 0, 0)  24.6 us
    another operation x4, other arithmetic, right_solve(): lax.linalg.triangular_solve(lower, rhs, left_side=False, lower=True, tran...  20.9 us
    dot_general x1, matrix products, body(): jnp.dot(tensor.reshape(mode_two * mode_three, mode_one), factor_a, precis...  11.6 us
    all_to_all x1, starting transfers between devices, gather(): return lax.all_to_all(jnp.broadcast_to(x[None], (n,) + x.shape), axes, 0, 0)  6.85 us
    ppermute x3, waiting for transfers between devices, swap(): return lax.ppermute(x, axis, [(0, 1), (1, 0)])  4.92 us
    ppermute x3, starting transfers between devices, body(): lax.ppermute(gram_b, 'y', [(i, i ^ k) for i in range(n)])  4.79 us
  transfers between devices with their start and end apart: 7, of which 3 were waited for; matrix products, arithmetic and copies ran while one was open for 17% of the time, Pallas kernels for 0%

profile of v1, /device:TPU:2, one launch (start us, length us, event | category | flops | bytes accessed | tf_op | source)
XLA Modules:
  0.0 139.4 jit_solution(255645103496786653)
XLA Ops:
  0.6 0.0 copy-start
  0.6 0.9 copy-done
  1.5 0.4 convolution_multiply_fusion
  1.9 11.6 %multiply_reduce_fusion.1 = (f32[2048,128]{1,0:T(8,128)S(1)}, f32[2048,4,128]{2,0,1:T(8,128)}) fusion(f32[4,128]{1,0:T(4,128)} %param.7, f32[256,128]{1,0:T(8,128)S(1)} %copy-done, f32[2048,4,256]{2,1,0:T(4,128)} %param.5), kind=kOutput, calls=%fused_computation.3 | convolution fusion | flops 3223060480 | bytes 13764608 | tf_op jit(solution)/shard_map/dot_general | solution.py:37
  13.6 0.1 fusion.3
  13.7 0.1 copy.133
  13.8 0.1 collective-permute-start
  13.9 1.9 %collective-permute-done = f32[32,34,128]{2,0,1:T(8,128)S(1)} collective-permute-done((f32[32,34,128]{2,0,1:T(8,128)S(1)}, f32[32,34,128]{2,0,1:T(8,128)S(1)}, u32[]{:S(2)}, u32[]{:S(2)}) %collective-permute-start) | collective-permute-done | bytes 557088 | tf_op jit(solution)/shard_map/ppermute | solution.py:19
  15.8 0.0 copy-start.3
  15.8 0.1 bitcast_add_fusion
  16.0 0.3 copy.103
  16.3 30.0 %all_to_all.20 = f32[32,34,128]{2,1,0:T(8,128)S(1)} all-to-all(f32[32,34,128]{2,1,0:T(8,128)S(1)} %copy.103), channel_id=1, replica_groups=mesh['z'=8,'xl'=2,'c'=2,'y'=4,'xh'=2] {'xl','xh','z'}, dimensions={0} | all-to-all | bytes 1114112 | tf_op jit(solution)/shard_map/all_to_all | solution.py:55
  46.3 0.1 reduce_sum.37
  46.4 14.1 %all_to_all.21 = f32[8,34,128]{2,1,0:T(8,128)S(1)} all-to-all(f32[8,34,128]{2,1,0:T(8,128)S(1)} %broadcast_in_dim.6), channel_id=1, replica_groups=mesh['z'=8,'xl'=2,'c'=2,'y'=4,'xh'=2] {'z'}, dimensions={0} | all-to-all | bytes 278528 | tf_op jit(solution)/shard_map/all_to_all | solution.py:24
  60.5 10.5 %all_to_all.22 = f32[4,8,34,128]{3,1,2,0:T(8,128)S(1)} all-to-all(f32[4,8,34,128]{3,1,2,0:T(8,128)S(1)} %broadcast_in_dim.7), channel_id=1, replica_groups=mesh['z'=8,'xl'=2,'c'=2,'y'=4,'xh'=2] {'xl','xh'}, dimensions={0} | all-to-all | bytes 1114112 | tf_op jit(solution)/shard_map/all_to_all | solution.py:24
  71.0 0.1 copy.132
  71.1 0.3 collective-permute-start.1
  71.4 0.0 copy-done.3
  71.4 0.1 copy.110
  71.5 1.8 %collective-permute-done.1 = f32[32,34,128]{2,0,1:T(8,128)S(1)} collective-permute-done((f32[32,34,128]{2,0,1:T(8,128)S(1)}, f32[32,34,128]{2,0,1:T(8,128)S(1)}, u32[]{:S(2)}, u32[]{:S(2)}) %collective-permute-start.1) | collective-permute-done | bytes 557088 | tf_op jit(solution)/shard_map/ppermute | solution.py:19
  73.3 0.1 select_bitcast_fusion.1
  73.5 0.1 pad_maximum_fusion
  73.6 0.1 copy.106
  73.7 0.1 slice.28
  73.8 0.1 copy.108
  73.8 0.1 copy.109
  73.9 0.1 copy.111
  74.0 11.7 %cholesky.44 = f32[128,128]{1,0:T(8,128)S(1)} custom-call(f32[128,128]{1,0:T(8,128)S(1)} %fusion.16), custom_call_target="Cholesky" | custom-call | tf_op jit(solution)/shard_map/jit(cholesky)/cholesky | solution.py:11
  85.8 0.6 compare_reduce_fusion.1
  86.4 0.7 fusion.5
  87.1 9.8 %custom-call.12 = f32[1,128,128]{1,2,0:T(8,128)S(1)} custom-call(f32[1,128,128]{2,1,0:T(8,128)S(1)} %fusion.5), custom_call_target="InvertDiagBlocksLowerTriangular" | custom-call | tf_op jit(solution)/shard_map/triangular_solve | solution.py:12
  96.9 0.0 copy-start.1
  96.9 0.6 copy.107
  97.5 1.0 fusion.14
  98.5 1.0 fusion.12
  99.5 0.0 copy-start.2
  99.5 1.8 %fusion.17 = f32[128,128]{0,1:T(8,128)S(1)} fusion(f32[2048,128]{1,0:T(8,128)S(1)} %fusion.12), kind=kOutput, calls=%fused_computation.41 | convolution fusion | flops 402653184 | bytes 1114112 | tf_op jit(solution)/shard_map/dot_general | solution.py:71
  101.3 1.7 %collective-permute-start.3 = (f32[128,128]{0,1:T(8,128)S(1)}, f32[128,128]{0,1:T(8,128)S(1)}, u32[]{:S(2)}, u32[]{:S(2)}) collective-permute-start(f32[128,128]{0,1:T(8,128)S(1)} %fusion.17), channel_id=1, source_target_pairs={{0,2},{2,0},{4,6},{6,4},{1,3},{3,1},{5,7},{7,5},{8,10},{10,8},{12,... | collective-permute-start | bytes 196616 | tf_op jit(solution)/shard_map/ppermute | solution.py:73
  103.0 2.9 %collective-permute-start.4 = (f32[128,128]{0,1:T(8,128)S(1)}, f32[128,128]{0,1:T(8,128)S(1)}, u32[]{:S(2)}, u32[]{:S(2)}) collective-permute-start(f32[128,128]{0,1:T(8,128)S(1)} %fusion.17), channel_id=1, source_target_pairs={{0,4},{2,6},{4,0},{6,2},{1,5},{3,7},{5,1},{7,3},{8,12},{10,14},{12... | collective-permute-start | bytes 196616 | tf_op jit(solution)/shard_map/ppermute | solution.py:73
  105.9 0.2 collective-permute-start.5
  106.1 0.0 copy-done.1
  106.1 0.4 multiply_reduce_fusion
  106.5 0.1 collective-permute-start.2
  106.6 1.1 collective-permute-done.2
  107.8 0.7 broadcast_in_dim.8
  108.4 6.8 %all-to-all-start.3 = ((f32[64,4,128]{2,1,0:T(4,128)}), f32[64,4,128]{2,1,0:T(4,128)S(1)}, u32[]{:S(2)}, u32[]{:S(2)}) async-start(f32[64,4,128]{2,1,0:T(4,128)} %broadcast_in_dim.8), calls=%async_computation.3 | async-start | bytes 262144 | tf_op jit(solution)/shard_map/all_to_all | solution.py:24
  115.3 0.0 collective-permute-done.3
  115.3 0.0 collective-permute-done.4
  115.3 0.0 collective-permute-done.5
  115.4 0.1 copy.118
  115.5 0.0 copy-done.2
  115.5 11.7 %cholesky.55 = f32[128,128]{1,0:T(8,128)S(1)} custom-call(f32[128,128]{1,0:T(8,128)S(1)} %fusion.11), custom_call_target="Cholesky" | custom-call | tf_op jit(solution)/shard_map/jit(cholesky)/cholesky | solution.py:11
  127.2 0.6 compare_reduce_fusion
  127.9 0.7 fusion.6
  128.5 9.8 %custom-call.13 = f32[1,128,128]{1,2,0:T(8,128)S(1)} custom-call(f32[1,128,128]{2,1,0:T(8,128)S(1)} %fusion.6), custom_call_target="InvertDiagBlocksLowerTriangular" | custom-call | tf_op jit(solution)/shard_map/triangular_solve | solution.py:12
  138.4 0.0 all-to-all-done.3
  138.4 0.1 reduce_sum.39
  138.4 0.2 fusion.9
  138.6 0.8 fusion.7
  (11 shorter events, 0.2 us)
Async XLA Ops:
  0.6 0.9 copy-start
  13.8 2.0 %collective-permute-start = (f32[32,34,128]{2,0,1:T(8,128)S(1)}, f32[32,34,128]{2,0,1:T(8,128)S(1)}, u32[]{:S(2)}, u32[]{:S(2)}) collective-permute-start(f32[32,34,128]{2,0,1:T(8,128)S(1)} %bitcast.61), channel_id=1, source_target_pairs={{0,8},{8,0},{1,9},{9,1},{2,10},{10,2},{3,11},{11,3},{4,12},{12,4},... | collective-permute-start | bytes 1671176 | tf_op jit(solution)/shard_map/ppermute | solution.py:19
  15.8 55.5 %copy-start.3 = (f32[128,128]{1,0:T(8,128)S(1)}, f32[128,128]{1,0:T(8,128)}, u32[]{:S(2)}) copy-start(f32[128,128]{1,0:T(8,128)} %param.8) | copy-start | bytes 196612
  71.1 2.2 %collective-permute-start.1 = (f32[32,34,128]{2,0,1:T(8,128)S(1)}, f32[32,34,128]{2,0,1:T(8,128)S(1)}, u32[]{:S(2)}, u32[]{:S(2)}) collective-permute-start(f32[32,34,128]{2,0,1:T(8,128)S(1)} %bitcast.60), channel_id=1, source_target_pairs={{0,8},{8,0},{1,9},{9,1},{2,10},{10,2},{3,11},{11,3},{4,12},{12,4},... | collective-permute-start | bytes 1671176 | tf_op jit(solution)/shard_map/ppermute | solution.py:19
  96.9 9.2 %copy-start.1 = (f32[2048,4,128]{2,0,1:T(8,128)S(1)}, f32[2048,4,128]{2,0,1:T(8,128)}, u32[]{:S(2)}) copy-start(f32[2048,4,128]{2,0,1:T(8,128)} %get-tuple-element.8) | copy-start | bytes 12582916
  99.5 16.0 %copy-start.2 = (f32[2048,128]{1,0:T(8,128)}, f32[2048,128]{1,0:T(8,128)S(1)}, u32[]{:S(2)}) copy-start(f32[2048,128]{1,0:T(8,128)S(1)} %fusion.12) | copy-start | bytes 3145732
  101.3 14.0 %collective-permute-start.3 = (f32[128,128]{0,1:T(8,128)S(1)}, f32[128,128]{0,1:T(8,128)S(1)}, u32[]{:S(2)}, u32[]{:S(2)}) collective-permute-start(f32[128,128]{0,1:T(8,128)S(1)} %fusion.17), channel_id=1, source_target_pairs={{0,2},{2,0},{4,6},{6,4},{1,3},{3,1},{5,7},{7,5},{8,10},{10,8},{12,... | collective-permute-start | bytes 196616 | tf_op jit(solution)/shard_map/ppermute | solution.py:73
  103.0 12.3 %collective-permute-start.4 = (f32[128,128]{0,1:T(8,128)S(1)}, f32[128,128]{0,1:T(8,128)S(1)}, u32[]{:S(2)}, u32[]{:S(2)}) collective-permute-start(f32[128,128]{0,1:T(8,128)S(1)} %fusion.17), channel_id=1, source_target_pairs={{0,4},{2,6},{4,0},{6,2},{1,5},{3,7},{5,1},{7,3},{8,12},{10,14},{12... | collective-permute-start | bytes 196616 | tf_op jit(solution)/shard_map/ppermute | solution.py:73
  105.9 9.4 %collective-permute-start.5 = (f32[128,128]{0,1:T(8,128)S(1)}, f32[128,128]{0,1:T(8,128)S(1)}, u32[]{:S(2)}, u32[]{:S(2)}) collective-permute-start(f32[128,128]{0,1:T(8,128)S(1)} %fusion.17), channel_id=1, source_target_pairs={{0,6},{2,4},{4,2},{6,0},{1,7},{3,5},{5,3},{7,1},{8,14},{10,12},{12... | collective-permute-start | bytes 196616 | tf_op jit(solution)/shard_map/ppermute | solution.py:73
  106.5 1.2 collective-permute-start.2
  108.4 29.9 %all-to-all-start.3 = ((f32[64,4,128]{2,1,0:T(4,128)}), f32[64,4,128]{2,1,0:T(4,128)S(1)}, u32[]{:S(2)}, u32[]{:S(2)}) async-start(f32[64,4,128]{2,1,0:T(4,128)} %broadcast_in_dim.8), calls=%async_computation.3 | async-start | bytes 262144 | tf_op jit(solution)/shard_map/all_to_all | solution.py:24

commit v2 on v1

v2 whole, which is shorter than its diff:
```python
import functools

import jax
import jax.numpy as jnp
from jax import lax
from jax.experimental import pallas as pl
from jax.experimental.pallas import tpu as pltpu
from jax.sharding import Mesh, PartitionSpec as P

HIGH = lax.Precision.HIGHEST
F32 = jnp.float32
PLANE = ("z", "xl", "xh")
VMEM = pl.BlockSpec(memory_space=pltpu.VMEM)


def dot(a, b):
    return jnp.dot(a, b, precision=HIGH, preferred_element_type=F32)


def spd_inverse(a, step):
    n = a.shape[0]
    lane = lax.broadcasted_iota(jnp.int32, (step, n), 1)
    row_of = lax.broadcasted_iota(jnp.int32, (step, n), 0)
    lane_all = lax.broadcasted_iota(jnp.int32, (n, n), 1)
    zero = jnp.zeros((step, n), F32)
    for p in range(0, n, step):
        panel = a[p : p + step]
        columns = [jnp.broadcast_to(panel[:, p + c : p + c + 1], (step, n)) for c in range(step)]
        for c in range(step):
            column = columns[c]
            inverse = 1.0 / jnp.broadcast_to(column[c : c + 1], (step, n))
            pivot = row_of == c

            def eliminate(x):
                row = jnp.broadcast_to(x[c : c + 1], (step, n)) * inverse
                return jnp.where(pivot, row, x - column * row)

            panel = eliminate(jnp.where(lane == p + c, jnp.where(pivot, 1.0, 0.0), panel))
            for q in range(c + 1, step):
                columns[q] = eliminate(columns[q])
        spread = [zero] * (p // step) + [panel] + [zero] * ((n - p) // step - 1)
        rest = jnp.where((lane_all >= p) & (lane_all < p + step), 0.0, a)
        rest = rest - dot(a, jnp.concatenate(spread, axis=0))
        pieces = [rest[:p], panel, rest[p + step :]]
        a = jnp.concatenate([x for x in pieces if x.shape[0]], axis=0)
    return a


def inverse_kernel(first_ref, second_ref, out_ref):
    out_ref[...] = spd_inverse(first_ref[...] * second_ref[...], 16)


def inverse_of_product(first, second):
    return pl.pallas_call(
        inverse_kernel,
        out_shape=jax.ShapeDtypeStruct(first.shape, F32),
        in_specs=[VMEM, VMEM],
        out_specs=VMEM,
        name="inverse_of_product",
    )(first, second)


def swap(x, axis):
    return lax.ppermute(x, axis, [(0, 1), (1, 0)])


def gather(x, axes):
    n = lax.axis_size(axes)
    return lax.all_to_all(jnp.broadcast_to(x[None], (n,) + x.shape), axes, 0, 0)


def body(tensor, factor_a, factor_c, gram_c):
    mode_two, mode_three, mode_one = tensor.shape
    rank = factor_a.shape[1]
    core = lax.axis_index("c")
    plane = lax.axis_size(PLANE)
    pieces = 2 * plane
    rows, extra = mode_two // pieces, rank // pieces

    gram_part = dot(factor_a.T, factor_a)
    partial = dot(tensor.reshape(mode_two * mode_three, mode_one), factor_a)
    partial = partial.reshape(mode_two, mode_three, rank)
    part_b = jnp.sum(partial * factor_c[None], axis=1)

    both = jnp.concatenate(
        [
            part_b.reshape(2, plane, rows, rank),
            (0.5 * gram_part).reshape(2, plane, extra, rank),
        ],
        axis=2,
    )
    mine = lax.dynamic_index_in_dim(both, core, 0, keepdims=False)
    other = lax.dynamic_index_in_dim(both, 1 - core, 0, keepdims=False)
    half = mine + swap(other, "c")
    piece = jnp.sum(lax.all_to_all(half, PLANE, 0, 0), axis=0)

    square = gather(piece, PLANE)
    theirs = swap(square, "c")
    first = jnp.where(core == 0, square, theirs)
    second = jnp.where(core == 0, theirs, square)
    whole = jnp.stack([first, second]).reshape(pieces, rows + extra, rank)
    mttkrp_b = whole[:, :rows].reshape(mode_two, rank)
    gram_a = whole[:, rows:].reshape(rank, rank)

    factor_b = dot(mttkrp_b, inverse_of_product(gram_a, gram_c))

    local_c = jnp.sum(partial * factor_b[:, None, :], axis=0)
    local_c = local_c + swap(local_c, "c")
    mttkrp_c = jnp.sum(gather(local_c, ("z", "xl", "y")), axis=0)
    gram_b = dot(factor_b.T, factor_b)
    n = lax.axis_size("y")
    away = [lax.ppermute(gram_b, "y", [(i, i ^ k) for i in range(n)]) for k in range(1, n)]
    gram_b = (gram_b + away[0]) + (away[1] + away[2])
    factor_c_new = dot(mttkrp_c, inverse_of_product(gram_a, gram_b))
    return (factor_b, factor_c_new)


def solution(mesh):
    axes = (mesh.shape["ia"] // 4, 2, 2, mesh.shape["ja"], mesh.shape["ka"])
    fine = Mesh(mesh.devices.reshape(axes), ("z", "xl", "c", "y", "xh"))
    split = ("z", "xl", "c")
    placed = (P("y", "xh", split), P(split, None), P("xh", None), P())
    return jax.shard_map(
        body, mesh=fine, in_specs=placed, out_specs=(P("y", None), P("xh", None)), check_vma=False
    )
```

time: 141 us -> 113 us (0.80)
  other arithmetic: 46.8 us -> 1.69 us
  Pallas kernels: 0 us -> 10.8 us
  waiting for transfers between devices: 4.93 us -> 9.62 us
    another operation x10 -> x0, other arithmetic: 45.7 us -> none  [the longest x6 24.8 us: right_solve(): lower = jnp.linalg.cholesky(system)]
    pallas_call x0 -> x2, Pallas kernels: none -> 10.8 us  [inverse_of_product(): pl.pallas_call(inverse_kernel, out_shape=jax.ShapeDtypeStruct(first.shape...]
    all_to_all x1, waiting for transfers between devices: 0.01 us -> 4.59 us  [gather(): return lax.all_to_all(jnp.broadcast_to(x[None], (n,) + x.shape), axes, 0, 0)]
    dot_general x3 -> x5, matrix products: 13.8 us -> 17.4 us  [dot(): return jnp.dot(a, b, precision=HIGH, preferred_element_type=F32)]
    another operation x4 -> x0, matrix products: 2.92 us -> none  [the longest x2 1.81 us: right_solve(): lax.linalg.triangular_solve(lower, middle, left_side=False, lower=True, t...]
    all_to_all x2 -> x1, blocking collectives: 24.6 us -> 24.2 us  [gather(): return lax.all_to_all(jnp.broadcast_to(x[None], (n,) + x.shape), axes, 0, 0)]
  transfers between devices with their start and end apart: 7 -> 7, of which waited for: 3 -> 4; matrix products, arithmetic and copies ran while one was open for 17% -> 2% of each run, Pallas kernels for 0% -> 5%
where the time goes in v2:
time: 113 us; the launch traced here: 112 us
  blocking collectives  55.6 us (49%)
  matrix products  17.4 us (15%)
  starting transfers between devices  12.6 us (11%)
  Pallas kernels  10.8 us (10%)
  waiting for transfers between devices  9.62 us (9%)
  local copies, waits for them, and re-layouts  3.56 us (3%)
  other arithmetic  1.69 us (1%)
    all_to_all x1, blocking collectives, body(): piece = jnp.sum(lax.all_to_all(half, PLANE, 0, 0), axis=0)  31.4 us
    all_to_all x1, blocking collectives, gather(): return lax.all_to_all(jnp.broadcast_to(x[None], (n,) + x.shape), axes, 0, 0)  24.2 us
    dot_general x5, matrix products, dot(): return jnp.dot(a, b, precision=HIGH, preferred_element_type=F32)  17.4 us
    pallas_call x2, Pallas kernels, inverse_of_product(): pl.pallas_call(inverse_kernel, out_shape=jax.ShapeDtypeStruct(first.shape...  10.8 us
    all_to_all x1, starting transfers between devices, gather(): return lax.all_to_all(jnp.broadcast_to(x[None], (n,) + x.shape), axes, 0, 0)  8.01 us
    ppermute x3, waiting for transfers between devices, swap(): return lax.ppermute(x, axis, [(0, 1), (1, 0)])  5.03 us
    all_to_all x1, waiting for transfers between devices, gather(): return lax.all_to_all(jnp.broadcast_to(x[None], (n,) + x.shape), axes, 0, 0)  4.59 us
    ppermute x3, starting transfers between devices, body(): lax.ppermute(gram_b, 'y', [(i, i ^ k) for i in range(n)])  4.18 us
  transfers between devices with their start and end apart: 7, of which 4 were waited for; matrix products, arithmetic and copies ran while one was open for 2% of the time, Pallas kernels for 5%

profile of v2, /device:TPU:2, one launch (start us, length us, event | category | flops | bytes accessed | tf_op | source)
XLA Modules:
  0.0 112.1 jit_solution(17361387085992756930)
XLA Ops:
  0.6 0.0 copy-start
  0.6 0.9 copy-done
  1.5 0.4 convolution_multiply_fusion
  1.9 11.6 %multiply_reduce_fusion.1 = (f32[2048,128]{1,0:T(8,128)S(1)}, f32[2048,4,128]{2,0,1:T(8,128)}) fusion(f32[4,128]{1,0:T(4,128)} %param.6, f32[256,128]{1,0:T(8,128)S(1)} %copy-done, f32[2048,4,256]{2,1,0:T(4,128)} %param.4), kind=kOutput, calls=%fused_computation.3 | convolution fusion | flops 3223060480 | bytes 13764608 | tf_op jit(solution)/shard_map/dot_general | solution.py:17
  13.5 0.1 fusion.3
  13.6 0.1 copy.57
  13.8 0.1 collective-permute-start
  13.9 1.9 %collective-permute-done = f32[32,34,128]{2,0,1:T(8,128)S(1)} collective-permute-done((f32[32,34,128]{2,0,1:T(8,128)S(1)}, f32[32,34,128]{2,0,1:T(8,128)S(1)}, u32[]{:S(2)}, u32[]{:S(2)}) %collective-permute-start) | collective-permute-done | bytes 557088 | tf_op jit(solution)/shard_map/ppermute | solution.py:64
  15.8 0.1 bitcast_add_fusion
  15.9 0.3 copy.41
  16.3 31.4 %all_to_all.15 = f32[32,34,128]{2,1,0:T(8,128)S(1)} all-to-all(f32[32,34,128]{2,1,0:T(8,128)S(1)} %copy.41), channel_id=1, replica_groups=mesh['z'=8,'xl'=2,'c'=2,'y'=4,'xh'=2] {'z','xl','xh'}, dimensions={0} | all-to-all | bytes 1114112 | tf_op jit(solution)/shard_map/all_to_all | solution.py:95
  47.6 0.1 reduce_sum.37
  47.7 24.2 %all_to_all.16 = f32[32,34,128]{2,1,0:T(8,128)S(1)} all-to-all(f32[32,34,128]{2,1,0:T(8,128)S(1)} %broadcast_in_dim.4), channel_id=1, replica_groups=mesh['z'=8,'xl'=2,'c'=2,'y'=4,'xh'=2] {'z','xl','xh'}, dimensions={0} | all-to-all | bytes 1114112 | tf_op jit(solution)/shard_map/all_to_all | solution.py:69
  72.0 0.1 copy.43
  72.1 0.3 collective-permute-start.1
  72.4 1.9 %collective-permute-done.1 = f32[32,34,128]{2,0,1:T(8,128)S(1)} collective-permute-done((f32[32,34,128]{2,0,1:T(8,128)S(1)}, f32[32,34,128]{2,0,1:T(8,128)S(1)}, u32[]{:S(2)}, u32[]{:S(2)}) %collective-permute-start.1) | collective-permute-done | bytes 557088 | tf_op jit(solution)/shard_map/ppermute | solution.py:64
  74.3 0.2 select_bitcast_fusion.1
  74.5 0.1 pad_maximum_fusion
  74.6 0.1 slice.8
  74.7 0.6 copy.46
  75.4 0.7 copy.47
  76.0 5.4 %inverse_of_product.2 = f32[128,128]{1,0:T(8,128)} custom-call(f32[128,128]{1,0:T(8,128)} %bitcast.33, f32[128,128]{1,0:T(8,128)} %second_ref.1), custom_call_target="tpu_custom_call" | custom-call | tf_op jit(solution)/shard_map/inverse_of_product/pallas_call | solution.py:54
  81.5 0.0 copy-start.1
  81.5 2.0 %fusion.5 = f32[2048,128]{1,0:T(8,128)S(1)} fusion(f32[2048,128]{1,0:T(8,128)S(1)} %bitcast.32, f32[128,128]{1,0:T(8,128)} %inverse_of_product.2), kind=kOutput, calls=%fused_computation.18 | convolution fusion | flops 402653184 | bytes 2162688 | tf_op jit(solution)/shard_map/dot_general | solution.py:17
  83.4 0.0 copy-start.2
  83.4 1.8 %fusion.6 = f32[128,128]{1,0:T(8,128)S(1)} fusion(f32[2048,128]{1,0:T(8,128)S(1)} %fusion.5), kind=kOutput, calls=%fused_computation.19 | convolution fusion | flops 402653184 | bytes 1114112 | tf_op jit(solution)/shard_map/dot_general | solution.py:17
  85.3 3.1 %collective-permute-start.5 = (f32[128,128]{1,0:T(8,128)S(1)}, f32[128,128]{1,0:T(8,128)S(1)}, u32[]{:S(2)}, u32[]{:S(2)}) collective-permute-start(f32[128,128]{1,0:T(8,128)S(1)} %fusion.6), channel_id=1, source_target_pairs={{0,6},{2,4},{4,2},{6,0},{1,7},{3,5},{5,3},{7,1},{8,14},{10,12},{12... | collective-permute-start | bytes 196616 | tf_op jit(solution)/shard_map/ppermute | solution.py:112
  88.4 0.6 collective-permute-start.4
  89.0 0.4 collective-permute-start.3
  89.4 0.0 copy-done.1
  89.4 0.4 multiply_reduce_fusion
  89.9 0.1 collective-permute-start.2
  90.0 1.1 %collective-permute-done.2 = f32[4,128]{1,0:T(4,128)S(1)} collective-permute-done((f32[4,128]{1,0:T(4,128)S(1)}, f32[4,128]{1,0:T(4,128)S(1)}, u32[]{:S(2)}, u32[]{:S(2)}) %collective-permute-start.2) | collective-permute-done | bytes 2080 | tf_op jit(solution)/shard_map/ppermute | solution.py:64
  91.1 0.7 broadcast_in_dim.5
  91.8 8.0 %all-to-all-start.2 = ((f32[64,4,128]{2,1,0:T(4,128)}), f32[64,4,128]{2,1,0:T(4,128)S(1)}, u32[]{:S(2)}, u32[]{:S(2)}) async-start(f32[64,4,128]{2,1,0:T(4,128)} %broadcast_in_dim.5), calls=%async_computation.2 | async-start | bytes 262144 | tf_op jit(solution)/shard_map/all_to_all | solution.py:69
  99.8 0.0 collective-permute-done.5
  99.8 0.0 collective-permute-done.4
  99.8 0.0 collective-permute-done.3
  99.8 0.6 add_add_fusion.second_ref
  100.5 5.4 %inverse_of_product.3 = f32[128,128]{1,0:T(8,128)} custom-call(f32[128,128]{1,0:T(8,128)} %bitcast.34, f32[128,128]{1,0:T(8,128)} %add_add_fusion.second_ref), custom_call_target="tpu_custom_call" | custom-call | tf_op jit(solution)/shard_map/inverse_of_product/pallas_call | solution.py:54
  105.9 4.6 %all-to-all-done.2 = f32[64,4,128]{2,1,0:T(4,128)S(1)} async-done(((f32[64,4,128]{2,1,0:T(4,128)}), f32[64,4,128]{2,1,0:T(4,128)S(1)}, u32[]{:S(2)}, u32[]{:S(2)}) %all-to-all-start.2) | async-done | bytes 131104 | tf_op jit(solution)/shard_map/all_to_all | solution.py:69
  110.5 0.1 reduce_sum.39
  110.5 0.0 copy-done.2
  110.5 1.6 %fusion.7 = f32[4,128]{1,0:T(4,128)} fusion(f32[4,128]{1,0:T(4,128)S(1)} %reduce_sum.39, f32[128,128]{1,0:T(8,128)} %inverse_of_product.3), kind=kOutput, calls=%fused_computation.20 | convolution fusion | flops 786432 | bytes 69632 | tf_op jit(solution)/shard_map/dot_general | solution.py:17
  (3 shorter events, 0.1 us)
Async XLA Ops:
  0.6 0.9 copy-start
  13.8 2.0 %collective-permute-start = (f32[32,34,128]{2,0,1:T(8,128)S(1)}, f32[32,34,128]{2,0,1:T(8,128)S(1)}, u32[]{:S(2)}, u32[]{:S(2)}) collective-permute-start(f32[32,34,128]{2,0,1:T(8,128)S(1)} %bitcast.35), channel_id=1, source_target_pairs={{0,8},{8,0},{1,9},{9,1},{2,10},{10,2},{3,11},{11,3},{4,12},{12,4},... | collective-permute-start | bytes 1671176 | tf_op jit(solution)/shard_map/ppermute | solution.py:64
  72.1 2.2 %collective-permute-start.1 = (f32[32,34,128]{2,0,1:T(8,128)S(1)}, f32[32,34,128]{2,0,1:T(8,128)S(1)}, u32[]{:S(2)}, u32[]{:S(2)}) collective-permute-start(f32[32,34,128]{2,0,1:T(8,128)S(1)} %copy.43), channel_id=1, source_target_pairs={{0,8},{8,0},{1,9},{9,1},{2,10},{10,2},{3,11},{11,3},{4,12},{12,4},... | collective-permute-start | bytes 1671176 | tf_op jit(solution)/shard_map/ppermute | solution.py:64
  81.5 8.0 %copy-start.1 = (f32[2048,4,128]{2,0,1:T(8,128)S(1)}, f32[2048,4,128]{2,0,1:T(8,128)}, u32[]{:S(2)}) copy-start(f32[2048,4,128]{2,0,1:T(8,128)} %get-tuple-element.7) | copy-start | bytes 12582916
  83.4 27.1 %copy-start.2 = (f32[2048,128]{1,0:T(8,128)}, f32[2048,128]{1,0:T(8,128)S(1)}, u32[]{:S(2)}) copy-start(f32[2048,128]{1,0:T(8,128)S(1)} %fusion.5) | copy-start | bytes 3145732
  85.3 14.5 %collective-permute-start.5 = (f32[128,128]{1,0:T(8,128)S(1)}, f32[128,128]{1,0:T(8,128)S(1)}, u32[]{:S(2)}, u32[]{:S(2)}) collective-permute-start(f32[128,128]{1,0:T(8,128)S(1)} %fusion.6), channel_id=1, source_target_pairs={{0,6},{2,4},{4,2},{6,0},{1,7},{3,5},{5,3},{7,1},{8,14},{10,12},{12... | collective-permute-start | bytes 196616 | tf_op jit(solution)/shard_map/ppermute | solution.py:112
  88.4 11.4 %collective-permute-start.4 = (f32[128,128]{1,0:T(8,128)S(1)}, f32[128,128]{1,0:T(8,128)S(1)}, u32[]{:S(2)}, u32[]{:S(2)}) collective-permute-start(f32[128,128]{1,0:T(8,128)S(1)} %fusion.6), channel_id=1, source_target_pairs={{0,4},{2,6},{4,0},{6,2},{1,5},{3,7},{5,1},{7,3},{8,12},{10,14},{12... | collective-permute-start | bytes 196616 | tf_op jit(solution)/shard_map/ppermute | solution.py:112
  89.0 10.8 %collective-permute-start.3 = (f32[128,128]{1,0:T(8,128)S(1)}, f32[128,128]{1,0:T(8,128)S(1)}, u32[]{:S(2)}, u32[]{:S(2)}) collective-permute-start(f32[128,128]{1,0:T(8,128)S(1)} %fusion.6), channel_id=1, source_target_pairs={{0,2},{2,0},{4,6},{6,4},{1,3},{3,1},{5,7},{7,5},{8,10},{10,8},{12,... | collective-permute-start | bytes 196616 | tf_op jit(solution)/shard_map/ppermute | solution.py:112
  89.9 1.2 %collective-permute-start.2 = (f32[4,128]{1,0:T(4,128)S(1)}, f32[4,128]{1,0:T(4,128)S(1)}, u32[]{:S(2)}, u32[]{:S(2)}) collective-permute-start(f32[4,128]{1,0:T(4,128)S(1)} %multiply_reduce_fusion), channel_id=1, source_target_pairs={{0,8},{8,0},{1,9},{9,1},{2,10},{10,2},{3,11},{11,3},{4,12},{12,4},... | collective-permute-start | bytes 6152 | tf_op jit(solution)/shard_map/ppermute | solution.py:64
  91.8 18.7 %all-to-all-start.2 = ((f32[64,4,128]{2,1,0:T(4,128)}), f32[64,4,128]{2,1,0:T(4,128)S(1)}, u32[]{:S(2)}, u32[]{:S(2)}) async-start(f32[64,4,128]{2,1,0:T(4,128)} %broadcast_in_dim.5), calls=%async_computation.2 | async-start | bytes 262144 | tf_op jit(solution)/shard_map/all_to_all | solution.py:69

commit v3 on v2

--- a/solution.py
+++ b/solution.py
@@ -1,3 +1,5 @@
+import functools
+
 import functools
 
 import jax
@@ -9,12 +11,17 @@
 
 HIGH = lax.Precision.HIGHEST
 F32 = jnp.float32
+BF16 = jnp.bfloat16
 PLANE = ("z", "xl", "xh")
 VMEM = pl.BlockSpec(memory_space=pltpu.VMEM)
 
 
 def dot(a, b):
     return jnp.dot(a, b, precision=HIGH, preferred_element_type=F32)
+
+
+def mxu(a, b):
+    return jnp.dot(a, b, preferred_element_type=F32)
 
 
 def spd_inverse(a, step):
@@ -60,8 +67,103 @@
     )(first, second)
 
 
-def swap(x, axis):
-    return lax.ppermute(x, axis, [(0, 1), (1, 0)])
+def split3(x):
+    high = x.astype(BF16)
+    rest = x - high.astype(F32)
+    middle = rest.astype(BF16)
+    return high, middle, (rest - middle.astype(F32)).astype(BF16)
+
+
+def contract_kernel(chunk, half_ref, x_hbm, a_ref, c_ref, p_ref, b_ref, x_ref, w_ref, sems):
+    count, rows, rank = p_ref.shape
+    span = 2 * count
+    base = half_ref[0] * (rows * span)
+    copies = []
+    for n, at in enumerate(range(0, rows, chunk)):
+        size = chunk * span
+        copy = pltpu.make_async_copy(
+            x_hbm.at[pl.ds(base + at * span, size)], x_ref.at[pl.ds(at * span, size)], sems.at[n]
+        )
+        copy.start()
+        copies.append(copy)
+    for n, part in enumerate(split3(a_ref[...])):
+        w_ref[:, n * rank : (n + 1) * rank] = part
+    for n, at in enumerate(range(0, rows, chunk)):
+        copies[n].wait()
+        for row in range(at, at + chunk, 128):
+            total = None
+            for k in range(count):
+                x = jnp.concatenate(
+                    [
+                        x_ref[pl.ds(row * span + k, 128, stride=span), :],
+                        x_ref[pl.ds(row * span + count + k, 128, stride=span), :],
+                    ],
+                    axis=1,
+                )
+                high, middle, low = split3(x)
+                wide = w_ref[:, : 2 * rank]
+                y = mxu(high, wide) + mxu(middle, wide)
+                small = mxu(low, w_ref[:, :rank]) + mxu(high, w_ref[:, 2 * rank :])
+                value = y[:, :rank] + y[:, rank:] + small
+                p_ref[k, row : row + 128] = value
+                term = value * c_ref[k : k + 1, :]
+                total = term if total is None else total + term
+            b_ref[row : row + 128] = total
+
+
+def contract(half, x, factor_a, factor_c, rows):
+    count, (depth, rank) = factor_c.shape[0], factor_a.shape
+    chunk = 256
+    return pl.pallas_call(
+        functools.partial(contract_kernel, chunk),
+        out_shape=[
+            jax.ShapeDtypeStruct((count, rows, rank), F32),
+            jax.ShapeDtypeStruct((rows, rank), F32),
+        ],
+        in_specs=[
+            pl.BlockSpec(memory_space=pltpu.SMEM),
+            pl.BlockSpec(memory_space=pltpu.HBM),
+            VMEM,
+            VMEM,
+        ],
+        out_specs=[VMEM, VMEM],
+        scratch_shapes=[
+            pltpu.VMEM((rows * 2 * count, depth // 2), F32),
+            pltpu.VMEM((depth, 3 * rank), BF16),
+            pltpu.SemaphoreType.DMA((rows // chunk,)),
+        ],
+        compiler_params=pltpu.CompilerParams(vmem_limit_bytes=24 << 20),
+        name="contract",
+    )(half, x, factor_a, factor_c)
+
+
+def moments_kernel(f_ref, p_ref, c_ref, g_ref):
+    f = f_ref[...]
+    g_ref[...] = lax.dot_general(
+        f, f, (((0,), (0,)), ((), ())), precision=HIGH, preferred_element_type=F32
+    )
+    for k in range(p_ref.shape[0]):
+        c_ref[k : k + 1] = jnp.sum(p_ref[k] * f, axis=0, keepdims=True)
+
+
+def moments(f, p):
+    count, _, rank = p.shape
+    return pl.pallas_call(
+        moments_kernel,
+        out_shape=[
+            jax.ShapeDtypeStruct((count, rank), F32),
+            jax.ShapeDtypeStruct((rank, rank), F32),
+        ],
+        in_specs=[VMEM, VMEM],
+        out_specs=[VMEM, VMEM],
+        compiler_params=pltpu.CompilerParams(vmem_limit_bytes=24 << 20),
+        name="moments",
+    )(f, p)
+
+
+def swap(x, axis, bit=1):
+    n = lax.axis_size(axis)
+    return lax.ppermute(x, axis, [(i, i ^ bit) for i in range(n)])
 
 
 def gather(x, axes):
@@ -74,42 +176,38 @@
     rank = factor_a.shape[1]
     core = lax.axis_index("c")
     plane = lax.axis_size(PLANE)
-    pieces = 2 * plane
-    rows, extra = mode_two // pieces, rank // pieces
-
-    gram_part = dot(factor_a.T, factor_a)
-    partial = dot(tensor.reshape(mode_two * mode_three, mode_one), factor_a)
-    partial = partial.reshape(mode_two, mode_three, rank)
-    part_b = jnp.sum(partial * factor_c[None], axis=1)
-
-    both = jnp.concatenate(
-        [
-            part_b.reshape(2, plane, rows, rank),
-            (0.5 * gram_part).reshape(2, plane, extra, rank),
-        ],
-        axis=2,
-    )
-    mine = lax.dynamic_index_in_dim(both, core, 0, keepdims=False)
-    other = lax.dynamic_index_in_dim(both, 1 - core, 0, keepdims=False)
-    half = mine + swap(other, "c")
-    piece = jnp.sum(lax.all_to_all(half, PLANE, 0, 0), axis=0)
-
-    square = gather(piece, PLANE)
-    theirs = swap(square, "c")
-    first = jnp.where(core == 0, square, theirs)
-    second = jnp.where(core == 0, theirs, square)
-    whole = jnp.stack([first, second]).reshape(pieces, rows + extra, rank)
-    mttkrp_b = whole[:, :rows].reshape(mode_two, rank)
-    gram_a = whole[:, rows:].reshape(rank, rank)
-
-    factor_b = dot(mttkrp_b, inverse_of_product(gram_a, gram_c))
-
-    local_c = jnp.sum(partial * factor_b[:, None, :], axis=0)
+    half = mode_two // 2
+    rows = half // plane
+
+    gram_a = dot(factor_a.T, factor_a)
+    for axis, bit in (("c", 1), ("xl", 1), ("z", 1), ("z", 2), ("z", 4)):
+        gram_a = gram_a + swap(gram_a, axis, bit)
+    inverse = inverse_of_product(gram_a, gram_c)
+
+    lanes = mode_one // 2
+    flat = tensor.reshape(mode_two, mode_three, 2, lanes).transpose(0, 2, 1, 3)
+    flat = flat.reshape(mode_two * mode_three * 2, lanes)
+    index = core.astype(jnp.int32).reshape(1)
+    p_other, b_other = contract(1 - index, flat, factor_a, factor_c, half)
+    p_mine, b_mine = contract(index, flat, factor_a, factor_c, half)
+    b_half = b_mine + swap(b_other, "c")
+    shares = lax.all_to_all(b_half.reshape(plane, rows, rank), PLANE, 0, 0)
+    piece = dot(jnp.sum(shares, axis=0), inverse)
+
+    f_mine = gather(piece, PLANE).reshape(half, rank)
+    f_other = swap(f_mine, "c")
+    c_mine, g_mine = moments(f_mine, p_mine)
+    c_other, g_other = moments(f_other, p_other)
+    first = jnp.where(core == 0, f_mine, f_other)
+    second = jnp.where(core == 0, f_other, f_mine)
+    factor_b = jnp.concatenate([first, second], axis=0)
+
+    local_c = c_mine + c_other
     local_c = local_c + swap(local_c, "c")
     mttkrp_c = jnp.sum(gather(local_c, ("z", "xl", "y")), axis=0)
-    gram_b = dot(factor_b.T, factor_b)
-    n = lax.axis_size("y")
-    away = [lax.ppermute(gram_b, "y", [(i, i ^ k) for i in range(n)]) for k in range(1, n)]
+    lower = jnp.where(core == 0, g_mine, g_other)
+    gram_b = lower + jnp.where(core == 0, g_other, g_mine)
+    away = [swap(gram_b, "y", bit) for bit in (1, 2, 3)]
     gram_b = (gram_b + away[0]) + (away[1] + away[2])
     factor_c_new = dot(mttkrp_c, inverse_of_product(gram_a, gram_b))
     return (factor_b, factor_c_new)

time: 113 us -> 115 us (1.018)
  blocking collectives: 55.6 us -> 22.8 us
  starting transfers between devices: 12.6 us -> 32.8 us
  waiting for transfers between devices: 9.62 us -> 24.5 us
  matrix products: 17.4 us -> 2.97 us
  Pallas kernels: 10.8 us -> 18.8 us
  local copies, waits for them, and re-layouts: 3.56 us -> 8.63 us
  other arithmetic: 1.69 us -> 3.4 us
    all_to_all x1 -> x0, blocking collectives: 31.4 us -> none  [body(): piece = jnp.sum(lax.all_to_all(half, PLANE, 0, 0), axis=0)]
    ppermute x6 -> x11, waiting for transfers between devices: 5.03 us -> 20.9 us  [swap(): return lax.ppermute(x, axis, [(i, i ^ bit) for i in range(n)])]
    dot_general x5 -> x3, matrix products: 17.4 us -> 2.97 us  [dot(): return jnp.dot(a, b, precision=HIGH, preferred_element_type=F32)]
    all_to_all x0 -> x1, starting transfers between devices: none -> 11.6 us  [body(): shares = lax.all_to_all(b_half.reshape(plane, rows, rank), PLANE, 0, 0)]
    ppermute x6 -> x11, starting transfers between devices: 4.64 us -> 13.2 us  [swap(): return lax.ppermute(x, axis, [(i, i ^ bit) for i in range(n)])]
    pallas_call x0 -> x4, Pallas kernels: none -> 7.94 us  [the longest x2 6.53 us: contract(): pl.pallas_call(functools.partial(contract_kernel, chunk), out_shape=[jax....]
    unnamed x6 -> x14, local copies, waits for them, and re-layouts: 0.91 us -> 7.9 us
    all_to_all x1, blocking collectives: 24.2 us -> 22.8 us  [gather(): return lax.all_to_all(jnp.broadcast_to(x[None], (n,) + x.shape), axes, 0, 0)]
  transfers between devices with their start and end apart: 7 -> 13, of which waited for: 4 -> 7; matrix products, arithmetic and copies ran while one was open for 2% -> 3% of each run, Pallas kernels for 5% -> 13%
where the time goes in v3:
time: 115 us
  starting transfers between devices  32.8 us (29%)
  waiting for transfers between devices  24.5 us (21%)
  blocking collectives  22.8 us (20%)
  Pallas kernels  18.8 us (16%)
  local copies, waits for them, and re-layouts  8.63 us (8%)
  other arithmetic  3.4 us (3%)
  matrix products  2.97 us (3%)
    all_to_all x1, blocking collectives, gather(): return lax.all_to_all(jnp.broadcast_to(x[None], (n,) + x.shape), axes, 0, 0)  22.8 us
    ppermute x11, waiting for transfers between devices, swap(): return lax.ppermute(x, axis, [(i, i ^ bit) for i in range(n)])  20.9 us
    ppermute x11, starting transfers between devices, swap(): return lax.ppermute(x, axis, [(i, i ^ bit) for i in range(n)])  13.2 us
    all_to_all x1, starting transfers between devices, body(): shares = lax.all_to_all(b_half.reshape(plane, rows, rank), PLANE, 0, 0)  11.6 us
    pallas_call x2, Pallas kernels, inverse_of_product(): pl.pallas_call(inverse_kernel, out_shape=jax.ShapeDtypeStruct(first.shape...  10.8 us
    all_to_all x1, starting transfers between devices, gather(): return lax.all_to_all(jnp.broadcast_to(x[None], (n,) + x.shape), axes, 0, 0)  7.97 us
    unnamed x14, local copies, waits for them, and re-layouts  7.9 us
    pallas_call x2, Pallas kernels, contract(): pl.pallas_call(functools.partial(contract_kernel, chunk), out_shape=[jax....  6.53 us
  transfers between devices with their start and end apart: 13, of which 7 were waited for; matrix products, arithmetic and copies ran while one was open for 3% of the time, Pallas kernels for 13%

profile of v3, /device:TPU:2, one launch (start us, length us, event | category | flops | bytes accessed | tf_op | source)
XLA Modules:
  0.0 114.7 jit_solution(884207418138420784)
XLA Ops:
  0.6 0.0 copy-start
  0.6 3.4 %copy-done = f32[2048,4,256]{2,1,0:T(4,128)S(1)} copy-done((f32[2048,4,256]{2,1,0:T(4,128)S(1)}, f32[2048,4,256]{2,1,0:T(4,128)}, u32[]{:S(2)}) %copy-start) | copy-done | bytes 8388632
  4.0 0.0 copy-start.2
  4.0 0.9 copy-done.2
  4.9 0.0 copy-start.6
  4.9 0.7 copy-done.6
  5.6 0.0 copy-start.1
  5.6 3.3 %contract.3 = (f32[4,1024,128]{2,1,0:T(8,128)S(1)}, f32[1024,128]{1,0:T(8,128)S(1)}) custom-call(s32[1]{0:T(128)S(6)} %sub.3.half_ref, f32[16384,128]{1,0:T(8,128)S(1)} %bitcast.16, f32[256,128]{1,0:T(8,128)S(1)} %copy-done.2, f32[4,128]{1,0:T(4,128)S(1)} %copy-done.6), custom_call_target="tpu_custom_call" | custom-call | tf_op jit(solution)/shard_map/contract/pallas_call | solution.py:117
  8.9 0.1 collective-permute-start
  9.0 0.0 copy-done.1
  9.0 3.3 %contract.2 = (f32[4,1024,128]{2,1,0:T(8,128)S(1)}, f32[1024,128]{1,0:T(8,128)S(1)}) custom-call(s32[1]{0:T(128)} %bitcast.half_ref, f32[16384,128]{1,0:T(8,128)S(1)} %bitcast.17, f32[256,128]{1,0:T(8,128)S(1)} %copy-done.2, f32[4,128]{1,0:T(4,128)S(1)} %copy-done.6), custom_call_target="tpu_custom_call" | custom-call | tf_op jit(solution)/shard_map/contract/pallas_call | solution.py:117
  12.3 0.0 copy-start.4
  12.3 1.3 %copy-done.4 = f32[4,1024,128]{2,1,0:T(8,128)} copy-done((f32[4,1024,128]{2,1,0:T(8,128)}, f32[4,1024,128]{2,1,0:T(8,128)S(1)}, u32[]{:S(2)}) %copy-start.4) | copy-done | bytes 2097176
  13.6 0.0 copy-start.3
  13.6 0.0 collective-permute-done
  13.6 0.8 add.36
  14.5 11.6 %all-to-all-start = ((f32[32,32,128]{2,1,0:T(8,128)}), f32[32,32,128]{2,1,0:T(8,128)S(1)}, u32[]{:S(2)}, u32[]{:S(2)}) async-start(f32[32,32,128]{2,1,0:T(8,128)} %bitcast.6), calls=%async_computation | async-start | bytes 1048576 | tf_op jit(solution)/shard_map/all_to_all | solution.py:194
  26.1 0.0 copy-done.3
  26.1 0.4 fusion
  26.5 0.1 collective-permute-start.1
  26.6 1.2 %collective-permute-done.1 = f32[128,128]{1,0:T(8,128)S(1)} collective-permute-done((f32[128,128]{1,0:T(8,128)S(1)}, f32[128,128]{1,0:T(8,128)S(1)}, u32[]{:S(2)}, u32[]{:S(2)}) %collective-permute-start.1) | collective-permute-done | bytes 65568 | tf_op jit(solution)/shard_map/ppermute | solution.py:166
  27.8 0.3 collective-permute-start.2
  28.2 5.0 %collective-permute-done.2 = f32[128,128]{1,0:T(8,128)S(1)} collective-permute-done((f32[128,128]{1,0:T(8,128)S(1)}, f32[128,128]{1,0:T(8,128)S(1)}, u32[]{:S(2)}, u32[]{:S(2)}) %collective-permute-start.2) | collective-permute-done | bytes 65568 | tf_op jit(solution)/shard_map/ppermute | solution.py:166
  33.1 1.2 %collective-permute-start.3 = (f32[128,128]{1,0:T(8,128)S(1)}, f32[128,128]{1,0:T(8,128)S(1)}, u32[]{:S(2)}, u32[]{:S(2)}) collective-permute-start(f32[128,128]{1,0:T(8,128)S(1)} %add.38), channel_id=1, source_target_pairs={{0,32},{32,0},{64,96},{96,64},{128,160},{160,128},{192,224},{224,1... | collective-permute-start | bytes 196616 | tf_op jit(solution)/shard_map/ppermute | solution.py:166
  34.3 6.7 %collective-permute-done.3 = f32[128,128]{1,0:T(8,128)S(1)} collective-permute-done((f32[128,128]{1,0:T(8,128)S(1)}, f32[128,128]{1,0:T(8,128)S(1)}, u32[]{:S(2)}, u32[]{:S(2)}) %collective-permute-start.3) | collective-permute-done | bytes 65568 | tf_op jit(solution)/shard_map/ppermute | solution.py:166
  41.1 1.9 %collective-permute-start.4 = (f32[128,128]{1,0:T(8,128)S(1)}, f32[128,128]{1,0:T(8,128)S(1)}, u32[]{:S(2)}, u32[]{:S(2)}) collective-permute-start(f32[128,128]{1,0:T(8,128)S(1)} %add.39), channel_id=1, source_target_pairs={{0,64},{32,96},{64,0},{96,32},{128,192},{160,224},{192,128},{224,1... | collective-permute-start | bytes 196616 | tf_op jit(solution)/shard_map/ppermute | solution.py:166
  43.0 3.8 %collective-permute-done.4 = f32[128,128]{1,0:T(8,128)S(1)} collective-permute-done((f32[128,128]{1,0:T(8,128)S(1)}, f32[128,128]{1,0:T(8,128)S(1)}, u32[]{:S(2)}, u32[]{:S(2)}) %collective-permute-start.4) | collective-permute-done | bytes 65568 | tf_op jit(solution)/shard_map/ppermute | solution.py:166
  46.8 5.3 %collective-permute-start.5 = (f32[128,128]{1,0:T(8,128)S(1)}, f32[128,128]{1,0:T(8,128)S(1)}, u32[]{:S(2)}, u32[]{:S(2)}) collective-permute-start(f32[128,128]{1,0:T(8,128)S(1)} %add.40), channel_id=1, source_target_pairs={{0,128},{32,160},{64,192},{96,224},{128,0},{160,32},{192,64},{224,... | collective-permute-start | bytes 196616 | tf_op jit(solution)/shard_map/ppermute | solution.py:166
  52.1 3.1 %collective-permute-done.5 = f32[128,128]{1,0:T(8,128)S(1)} collective-permute-done((f32[128,128]{1,0:T(8,128)S(1)}, f32[128,128]{1,0:T(8,128)S(1)}, u32[]{:S(2)}, u32[]{:S(2)}) %collective-permute-start.5) | collective-permute-done | bytes 65568 | tf_op jit(solution)/shard_map/ppermute | solution.py:166
  55.2 0.6 add.41.first_ref
  55.9 5.4 %inverse_of_product.2 = f32[128,128]{1,0:T(8,128)} custom-call(f32[128,128]{1,0:T(8,128)} %add.41.first_ref, f32[128,128]{1,0:T(8,128)} %second_ref.1), custom_call_target="tpu_custom_call" | custom-call | tf_op jit(solution)/shard_map/inverse_of_product/pallas_call | solution.py:61
  61.3 0.0 all-to-all-done
  61.3 1.0 fusion.1
  62.3 0.1 broadcast_in_dim.4
  62.4 22.8 %all_to_all.15 = f32[32,32,128]{2,1,0:T(8,128)S(1)} all-to-all(f32[32,32,128]{2,1,0:T(8,128)S(1)} %broadcast_in_dim.4), channel_id=1, replica_groups=mesh['z'=8,'xl'=2,'c'=2,'y'=4,'xh'=2] {'z','xl','xh'}, dimensions={0} | all-to-all | bytes 1048576 | tf_op jit(solution)/shard_map/all_to_all | solution.py:171
  85.3 0.0 collective-permute-start.6
  85.3 0.0 copy-start.5
  85.3 1.6 %copy-done.5 = f32[4,1024,128]{2,1,0:T(8,128)S(1)} copy-done((f32[4,1024,128]{2,1,0:T(8,128)S(1)}, f32[4,1024,128]{2,1,0:T(8,128)}, u32[]{:S(2)}) %copy-start.5) | copy-done | bytes 2097176
  86.9 0.7 moments.2
  87.6 0.0 collective-permute-done.6.f_ref
  87.6 0.7 moments.3
  88.3 3.1 %collective-permute-start.10 = (f32[128,128]{1,0:T(8,128)S(1)}, f32[128,128]{1,0:T(8,128)S(1)}, u32[]{:S(2)}, u32[]{:S(2)}) collective-permute-start(f32[128,128]{1,0:T(8,128)S(1)} %select_add_fusion), channel_id=1, source_target_pairs={{0,6},{2,4},{4,2},{6,0},{1,7},{3,5},{5,3},{7,1},{8,14},{10,12},{12... | collective-permute-start | bytes 196616 | tf_op jit(solution)/shard_map/ppermute | solution.py:166
  91.4 0.6 collective-permute-start.9
  92.0 0.5 collective-permute-start.8
  92.5 0.0 collective-permute-start.7
  92.5 0.1 broadcast_select_fusion.1
  92.6 1.1 collective-permute-done.7
  93.7 0.7 broadcast_in_dim.5
  94.3 8.0 %all-to-all-start.2 = ((f32[64,4,128]{2,1,0:T(4,128)}), f32[64,4,128]{2,1,0:T(4,128)S(1)}, u32[]{:S(2)}, u32[]{:S(2)}) async-start(f32[64,4,128]{2,1,0:T(4,128)} %broadcast_in_dim.5), calls=%async_computation.2 | async-start | bytes 262144 | tf_op jit(solution)/shard_map/all_to_all | solution.py:171
  102.3 1.0 pad_maximum_fusion
  103.4 0.0 collective-permute-done.10
  103.4 0.0 collective-permute-done.9
  103.4 0.0 collective-permute-done.8
  103.4 0.6 add_add_fusion.second_ref
  104.0 5.4 %inverse_of_product.3 = f32[128,128]{1,0:T(8,128)} custom-call(f32[128,128]{1,0:T(8,128)} %add.41.first_ref, f32[128,128]{1,0:T(8,128)} %add_add_fusion.second_ref), custom_call_target="tpu_custom_call" | custom-call | tf_op jit(solution)/shard_map/inverse_of_product/pallas_call | solution.py:61
  109.4 3.6 %all-to-all-done.2 = f32[64,4,128]{2,1,0:T(4,128)S(1)} async-done(((f32[64,4,128]{2,1,0:T(4,128)}), f32[64,4,128]{2,1,0:T(4,128)S(1)}, u32[]{:S(2)}, u32[]{:S(2)}) %all-to-all-start.2) | async-done | bytes 131104 | tf_op jit(solution)/shard_map/all_to_all | solution.py:171
  113.0 0.1 reduce_sum.19
  113.1 1.6 %fusion.2 = f32[4,128]{1,0:T(4,128)} fusion(f32[4,128]{1,0:T(4,128)S(1)} %reduce_sum.19, f32[128,128]{1,0:T(8,128)} %inverse_of_product.3), kind=kOutput, calls=%fused_computation.7 | convolution fusion | flops 786432 | bytes 69632 | tf_op jit(solution)/shard_map/dot_general | solution.py:20
  (8 shorter events, 0.1 us)
Async XLA Ops:
  0.6 3.4 %copy-start = (f32[2048,4,256]{2,1,0:T(4,128)S(1)}, f32[2048,4,256]{2,1,0:T(4,128)}, u32[]{:S(2)}) copy-start(f32[2048,4,256]{2,1,0:T(4,128)} %param.4) | copy-start | bytes 25165828
  4.0 0.9 copy-start.2
  4.9 0.7 copy-start.6
  5.6 3.4 %copy-start.1 = (f32[2048,4,256]{2,1,0:T(4,128)S(1)}, f32[2048,4,256]{2,1,0:T(4,128)}, u32[]{:S(2)}) copy-start(f32[2048,4,256]{2,1,0:T(4,128)} %param.4) | copy-start | bytes 25165828
  8.9 4.7 %collective-permute-start = (f32[1024,128]{1,0:T(8,128)S(1)}, f32[1024,128]{1,0:T(8,128)S(1)}, u32[]{:S(2)}, u32[]{:S(2)}) collective-permute-start(f32[1024,128]{1,0:T(8,128)S(1)} %get-tuple-element.11), channel_id=1, source_target_pairs={{0,8},{8,0},{1,9},{9,1},{2,10},{10,2},{3,11},{11,3},{4,12},{12,4},... | collective-permute-start | bytes 1572872 | tf_op jit(solution)/shard_map/ppermute | solution.py:166
  12.3 1.3 %copy-start.4 = (f32[4,1024,128]{2,1,0:T(8,128)}, f32[4,1024,128]{2,1,0:T(8,128)S(1)}, u32[]{:S(2)}) copy-start(f32[4,1024,128]{2,1,0:T(8,128)S(1)} %get-tuple-element.12.p_ref) | copy-start | bytes 6291460
  13.6 12.5 %copy-start.3 = (f32[256,128]{1,0:T(8,128)S(1)}, f32[256,128]{1,0:T(8,128)}, u32[]{:S(2)}) copy-start(f32[256,128]{1,0:T(8,128)} %a_ref.3) | copy-start | bytes 393220
  14.5 46.8 %all-to-all-start = ((f32[32,32,128]{2,1,0:T(8,128)}), f32[32,32,128]{2,1,0:T(8,128)S(1)}, u32[]{:S(2)}, u32[]{:S(2)}) async-start(f32[32,32,128]{2,1,0:T(8,128)} %bitcast.6), calls=%async_computation | async-start | bytes 1048576 | tf_op jit(solution)/shard_map/all_to_all | solution.py:194
  26.5 1.3 %collective-permute-start.1 = (f32[128,128]{1,0:T(8,128)S(1)}, f32[128,128]{1,0:T(8,128)S(1)}, u32[]{:S(2)}, u32[]{:S(2)}) collective-permute-start(f32[128,128]{1,0:T(8,128)S(1)} %fusion), channel_id=1, source_target_pairs={{0,8},{8,0},{1,9},{9,1},{2,10},{10,2},{3,11},{11,3},{4,12},{12,4},... | collective-permute-start | bytes 196616 | tf_op jit(solution)/shard_map/ppermute | solution.py:166
  27.8 5.3 %collective-permute-start.2 = (f32[128,128]{1,0:T(8,128)S(1)}, f32[128,128]{1,0:T(8,128)S(1)}, u32[]{:S(2)}, u32[]{:S(2)}) collective-permute-start(f32[128,128]{1,0:T(8,128)S(1)} %add.37), channel_id=1, source_target_pairs={{0,16},{16,0},{1,17},{17,1},{2,18},{18,2},{3,19},{19,3},{4,20},{20... | collective-permute-start | bytes 196616 | tf_op jit(solution)/shard_map/ppermute | solution.py:166
  33.1 7.9 %collective-permute-start.3 = (f32[128,128]{1,0:T(8,128)S(1)}, f32[128,128]{1,0:T(8,128)S(1)}, u32[]{:S(2)}, u32[]{:S(2)}) collective-permute-start(f32[128,128]{1,0:T(8,128)S(1)} %add.38), channel_id=1, source_target_pairs={{0,32},{32,0},{64,96},{96,64},{128,160},{160,128},{192,224},{224,1... | collective-permute-start | bytes 196616 | tf_op jit(solution)/shard_map/ppermute | solution.py:166
  41.1 5.7 %collective-permute-start.4 = (f32[128,128]{1,0:T(8,128)S(1)}, f32[128,128]{1,0:T(8,128)S(1)}, u32[]{:S(2)}, u32[]{:S(2)}) collective-permute-start(f32[128,128]{1,0:T(8,128)S(1)} %add.39), channel_id=1, source_target_pairs={{0,64},{32,96},{64,0},{96,32},{128,192},{160,224},{192,128},{224,1... | collective-permute-start | bytes 196616 | tf_op jit(solution)/shard_map/ppermute | solution.py:166
  46.8 8.5 %collective-permute-start.5 = (f32[128,128]{1,0:T(8,128)S(1)}, f32[128,128]{1,0:T(8,128)S(1)}, u32[]{:S(2)}, u32[]{:S(2)}) collective-permute-start(f32[128,128]{1,0:T(8,128)S(1)} %add.40), channel_id=1, source_target_pairs={{0,128},{32,160},{64,192},{96,224},{128,0},{160,32},{192,64},{224,... | collective-permute-start | bytes 196616 | tf_op jit(solution)/shard_map/ppermute | solution.py:166
  85.3 2.3 %collective-permute-start.6 = (f32[1024,128]{1,0:T(8,128)S(1)}, f32[1024,128]{1,0:T(8,128)S(1)}, u32[]{:S(2)}, u32[]{:S(2)}) collective-permute-start(f32[1024,128]{1,0:T(8,128)S(1)} %bitcast.18), channel_id=1, source_target_pairs={{0,8},{8,0},{1,9},{9,1},{2,10},{10,2},{3,11},{11,3},{4,12},{12,4},... | collective-permute-start | bytes 1572872 | tf_op jit(solution)/shard_map/ppermute | solution.py:166
  85.3 1.6 %copy-start.5 = (f32[4,1024,128]{2,1,0:T(8,128)S(1)}, f32[4,1024,128]{2,1,0:T(8,128)}, u32[]{:S(2)}) copy-start(f32[4,1024,128]{2,1,0:T(8,128)} %copy-done.4) | copy-start | bytes 6291460
  88.3 15.1 %collective-permute-start.10 = (f32[128,128]{1,0:T(8,128)S(1)}, f32[128,128]{1,0:T(8,128)S(1)}, u32[]{:S(2)}, u32[]{:S(2)}) collective-permute-start(f32[128,128]{1,0:T(8,128)S(1)} %select_add_fusion), channel_id=1, source_target_pairs={{0,6},{2,4},{4,2},{6,0},{1,7},{3,5},{5,3},{7,1},{8,14},{10,12},{12... | collective-permute-start | bytes 196616 | tf_op jit(solution)/shard_map/ppermute | solution.py:166
  91.4 12.0 %collective-permute-start.9 = (f32[128,128]{1,0:T(8,128)S(1)}, f32[128,128]{1,0:T(8,128)S(1)}, u32[]{:S(2)}, u32[]{:S(2)}) collective-permute-start(f32[128,128]{1,0:T(8,128)S(1)} %select_add_fusion), channel_id=1, source_target_pairs={{0,4},{2,6},{4,0},{6,2},{1,5},{3,7},{5,1},{7,3},{8,12},{10,14},{12... | collective-permute-start | bytes 196616 | tf_op jit(solution)/shard_map/ppermute | solution.py:166
  92.0 11.3 %collective-permute-start.8 = (f32[128,128]{1,0:T(8,128)S(1)}, f32[128,128]{1,0:T(8,128)S(1)}, u32[]{:S(2)}, u32[]{:S(2)}) collective-permute-start(f32[128,128]{1,0:T(8,128)S(1)} %select_add_fusion), channel_id=1, source_target_pairs={{0,2},{2,0},{4,6},{6,4},{1,3},{3,1},{5,7},{7,5},{8,10},{10,8},{12,... | collective-permute-start | bytes 196616 | tf_op jit(solution)/shard_map/ppermute | solution.py:166
  92.5 1.2 %collective-permute-start.7 = (f32[4,128]{1,0:T(4,128)S(1)}, f32[4,128]{1,0:T(4,128)S(1)}, u32[]{:S(2)}, u32[]{:S(2)}) collective-permute-start(f32[4,128]{1,0:T(4,128)S(1)} %add.42), channel_id=1, source_target_pairs={{0,8},{8,0},{1,9},{9,1},{2,10},{10,2},{3,11},{11,3},{4,12},{12,4},... | collective-permute-start | bytes 6152 | tf_op jit(solution)/shard_map/ppermute | solution.py:166
  94.3 18.7 %all-to-all-start.2 = ((f32[64,4,128]{2,1,0:T(4,128)}), f32[64,4,128]{2,1,0:T(4,128)S(1)}, u32[]{:S(2)}, u32[]{:S(2)}) async-start(f32[64,4,128]{2,1,0:T(4,128)} %broadcast_in_dim.5), calls=%async_computation.2 | async-start | bytes 262144 | tf_op jit(solution)/shard_map/all_to_all | solution.py:171

commit v4 on v3

--- a/solution.py
+++ b/solution.py
@@ -63,8 +63,36 @@
         out_shape=jax.ShapeDtypeStruct(first.shape, F32),
         in_specs=[VMEM, VMEM],
         out_specs=VMEM,
+        cost_estimate=pl.CostEstimate(flops=5 * 10**9, transcendentals=128, bytes_accessed=3 * 2**16),
         name="inverse_of_product",
     )(first, second)
+
+
+def finish_kernel(first_ref, second_ref, half_ref, mine_hbm, other_hbm, inv_ref, out_hbm, sems):
+    half = half_ref[0]
+    mine = pltpu.make_async_copy(mine_hbm, out_hbm.at[half], sems.at[0])
+    other = pltpu.make_async_copy(other_hbm, out_hbm.at[1 - half], sems.at[1])
+    mine.start()
+    other.start()
+    inv_ref[...] = spd_inverse(first_ref[...] * second_ref[...], 16)
+    mine.wait()
+    other.wait()
+
+
+def finish(first, second, half, mine, other):
+    anywhere = pl.BlockSpec(memory_space=pl.ANY)
+    return pl.pallas_call(
+        finish_kernel,
+        out_shape=[
+            jax.ShapeDtypeStruct(first.shape, F32),
+            jax.ShapeDtypeStruct((2,) + mine.shape, F32),
+        ],
+        in_specs=[VMEM, VMEM, pl.BlockSpec(memory_space=pltpu.SMEM), anywhere, anywhere],
+        out_specs=[VMEM, anywhere],
+        scratch_shapes=[pltpu.SemaphoreType.DMA((2,))],
+        cost_estimate=pl.CostEstimate(flops=5 * 10**9, transcendentals=128, bytes_accessed=2**22),
+        name="finish",
+    )(first, second, half, mine, other)
 
 
 def split3(x):
@@ -133,6 +161,11 @@
             pltpu.SemaphoreType.DMA((rows // chunk,)),
         ],
         compiler_params=pltpu.CompilerParams(vmem_limit_bytes=24 << 20),
+        cost_estimate=pl.CostEstimate(
+            flops=16 * count * rows * depth * rank,
+            transcendentals=0,
+            bytes_accessed=4 * count * rows * (depth + rank),
+        ),
         name="contract",
     )(half, x, factor_a, factor_c)
 
@@ -178,38 +211,41 @@
     plane = lax.axis_size(PLANE)
     half = mode_two // 2
     rows = half // plane
-
-    gram_a = dot(factor_a.T, factor_a)
-    for axis, bit in (("c", 1), ("xl", 1), ("z", 1), ("z", 2), ("z", 4)):
-        gram_a = gram_a + swap(gram_a, axis, bit)
-    inverse = inverse_of_product(gram_a, gram_c)
-
     lanes = mode_one // 2
     flat = tensor.reshape(mode_two, mode_three, 2, lanes).transpose(0, 2, 1, 3)
     flat = flat.reshape(mode_two * mode_three * 2, lanes)
+    flat = pltpu.with_memory_space_constraint(flat, pltpu.HBM)
     index = core.astype(jnp.int32).reshape(1)
-    p_other, b_other = contract(1 - index, flat, factor_a, factor_c, half)
+
+    gram_a = dot(factor_a.T, factor_a)
+    gram_a = gram_a + swap(gram_a, "c")
+    other, gram_a = lax.optimization_barrier((1 - index, gram_a))
+    p_other, b_other = contract(other, flat, factor_a, factor_c, half)
+    gram_a = gram_a + swap(gram_a, "xl")
+    index, gram_a = lax.optimization_barrier((index, gram_a))
     p_mine, b_mine = contract(index, flat, factor_a, factor_c, half)
     b_half = b_mine + swap(b_other, "c")
+    gram_a = gram_a + swap(gram_a, "z", 1)
+    b_half, gram_a = lax.optimization_barrier((b_half, gram_a))
     shares = lax.all_to_all(b_half.reshape(plane, rows, rank), PLANE, 0, 0)
+    gram_a = gram_a + swap(gram_a, "z", 2)
+    p_other, gram_a = lax.optimization_barrier((p_other, gram_a))
+    gram_a = gram_a + swap(gram_a, "z", 4)
+    inverse = inverse_of_product(gram_a, gram_c)
+    partial = p_mine + swap(p_other, "c")
+    shares, partial = lax.optimization_barrier((shares, partial))
     piece = dot(jnp.sum(shares, axis=0), inverse)
 
     f_mine = gather(piece, PLANE).reshape(half, rank)
-    f_other = swap(f_mine, "c")
-    c_mine, g_mine = moments(f_mine, p_mine)
-    c_other, g_other = moments(f_other, p_other)
-    first = jnp.where(core == 0, f_mine, f_other)
-    second = jnp.where(core == 0, f_other, f_mine)
-    factor_b = jnp.concatenate([first, second], axis=0)
-
-    local_c = c_mine + c_other
+    local_c, gram_b = moments(f_mine, partial)
     local_c = local_c + swap(local_c, "c")
+    gram_b = gram_b + swap(gram_b, "c")
+    away = [swap(gram_b, "y", bit) for bit in (1, 2, 3)]
     mttkrp_c = jnp.sum(gather(local_c, ("z", "xl", "y")), axis=0)
-    lower = jnp.where(core == 0, g_mine, g_other)
-    gram_b = lower + jnp.where(core == 0, g_other, g_mine)
-    away = [swap(gram_b, "y", bit) for bit in (1, 2, 3)]
     gram_b = (gram_b + away[0]) + (away[1] + away[2])
-    factor_c_new = dot(mttkrp_c, inverse_of_product(gram_a, gram_b))
+    last, factor_b = finish(gram_a, gram_b, index, f_mine, swap(f_mine, "c"))
+    factor_b = factor_b.reshape(mode_two, rank)
+    factor_c_new = dot(mttkrp_c, last)
     return (factor_b, factor_c_new)
 
 

time: 115 us -> 155 us (1.35)
  Pallas kernels: 18.8 us -> 48.9 us
  waiting for transfers between devices: 24.5 us -> 33.2 us
  starting transfers between devices: 32.8 us -> 37.1 us
  local copies, waits for them, and re-layouts: 8.63 us -> 4.44 us
    pallas_call x0 -> x1, Pallas kernels: none -> 34.4 us  [finish(): pl.pallas_call(finish_kernel, out_shape=[jax.ShapeDtypeStruct(first.shape...]
    all_to_all x1, waiting for transfers between devices: 3.59 us -> 10 us  [gather(): return lax.all_to_all(jnp.broadcast_to(x[None], (n,) + x.shape), axes, 0, 0)]
    pallas_call x2 -> x1, Pallas kernels: 10.8 us -> 5.43 us  [inverse_of_product(): pl.pallas_call(inverse_kernel, out_shape=jax.ShapeDtypeStruct(first.shape...]
    ppermute x11 -> x13, starting transfers between devices: 13.2 us -> 18 us  [swap(): return lax.ppermute(x, axis, [(i, i ^ bit) for i in range(n)])]
    unnamed x14, local copies, waits for them, and re-layouts: 7.9 us -> 3.7 us
    add x7, other arithmetic: 0.68 us -> 3.15 us  [the longest x1 2.46 us: body(): partial = p_mine + swap(p_other, 'c')]
    ppermute x11 -> x13, waiting for transfers between devices: 20.9 us -> 23.2 us  [swap(): return lax.ppermute(x, axis, [(i, i ^ bit) for i in range(n)])]
    pallas_call x2, Pallas kernels: 6.53 us -> 8.36 us  [contract(): pl.pallas_call(functools.partial(contract_kernel, chunk), out_shape=[jax....]
  transfers between devices with their start and end apart: 13 -> 15, of which waited for: 7 -> 7; matrix products, arithmetic and copies ran while one was open for 3% -> 3% of each run, Pallas kernels for 13% -> 7%
where the time goes in v4:
time: 155 us; the launch traced here: 154 us
  Pallas kernels  48.9 us (32%)
  starting transfers between devices  37.1 us (24%)
  waiting for transfers between devices  33.2 us (21%)
  blocking collectives  21.6 us (14%)
  other arithmetic  4.78 us (3%)
  local copies, waits for them, and re-layouts  4.44 us (3%)
  matrix products  3.11 us (2%)
    pallas_call x1, Pallas kernels, finish(): pl.pallas_call(finish_kernel, out_shape=[jax.ShapeDtypeStruct(first.shape...  34.4 us
    ppermute x13, waiting for transfers between devices, swap(): return lax.ppermute(x, axis, [(i, i ^ bit) for i in range(n)])  23.2 us
    all_to_all x1, blocking collectives, gather(): return lax.all_to_all(jnp.broadcast_to(x[None], (n,) + x.shape), axes, 0, 0)  21.6 us
    ppermute x13, starting transfers between devices, swap(): return lax.ppermute(x, axis, [(i, i ^ bit) for i in range(n)])  18 us
    all_to_all x1, starting transfers between devices, body(): shares = lax.all_to_all(b_half.reshape(plane, rows, rank), PLANE, 0, 0)  10.7 us
    all_to_all x1, waiting for transfers between devices, gather(): return lax.all_to_all(jnp.broadcast_to(x[None], (n,) + x.shape), axes, 0, 0)  10 us
    all_to_all x1, starting transfers between devices, gather(): return lax.all_to_all(jnp.broadcast_to(x[None], (n,) + x.shape), axes, 0, 0)  8.43 us
    pallas_call x2, Pallas kernels, contract(): pl.pallas_call(functools.partial(contract_kernel, chunk), out_shape=[jax....  8.36 us
  transfers between devices with their start and end apart: 15, of which 7 were waited for; matrix products, arithmetic and copies ran while one was open for 3% of the time, Pallas kernels for 7%

profile of v4, /device:TPU:2, one launch (start us, length us, event | category | flops | bytes accessed | tf_op | source)
XLA Modules:
  0.0 154.0 jit_solution(11631696891781501902)
XLA Ops:
  0.6 1.4 fusion
  2.0 0.1 collective-permute-start
  2.1 1.2 collective-permute-done
  3.4 0.0 copy-start
  3.4 0.9 copy-done
  4.3 0.0 copy-start.4
  4.3 0.7 copy-done.4
  4.9 0.0 copy-start.1
  4.9 4.2 %contract.2 = (f32[4,1024,128]{2,1,0:T(8,128)S(1)}, f32[1024,128]{1,0:T(8,128)S(1)}) custom-call(s32[1]{0:T(128)S(6)} %sub.3.half_ref, f32[16384,128]{1,0:T(8,128)} %bitcast.18, f32[256,128]{1,0:T(8,128)S(1)} %copy-done, f32[4,128]{1,0:T(4,128)S(1)} %copy-done.4), custom_call_target="tpu_custom_call" | custom-call | flops 2147483648 | bytes 6291456 | tf_op jit(solution)/shard_map/contract/pallas_call | solution.py:145
  9.1 0.3 collective-permute-start.2
  9.4 2.3 %collective-permute-start.1 = (f32[128,128]{1,0:T(8,128)S(1)}, f32[128,128]{1,0:T(8,128)S(1)}, u32[]{:S(2)}, u32[]{:S(2)}) collective-permute-start(f32[128,128]{1,0:T(8,128)S(1)} %add.36), channel_id=1, source_target_pairs={{0,16},{16,0},{1,17},{17,1},{2,18},{18,2},{3,19},{19,3},{4,20},{20... | collective-permute-start | bytes 196616 | tf_op jit(solution)/shard_map/ppermute | solution.py:199
  11.7 2.6 %collective-permute-done.1 = f32[128,128]{1,0:T(8,128)S(1)} collective-permute-done((f32[128,128]{1,0:T(8,128)S(1)}, f32[128,128]{1,0:T(8,128)S(1)}, u32[]{:S(2)}, u32[]{:S(2)}) %collective-permute-start.1) | collective-permute-done | bytes 65568 | tf_op jit(solution)/shard_map/ppermute | solution.py:199
  14.3 1.5 collective-permute-start.3
  15.8 0.0 copy-done.1
  15.8 4.2 %contract.3 = (f32[4,1024,128]{2,1,0:T(8,128)S(1)}, f32[1024,128]{1,0:T(8,128)S(1)}) custom-call(s32[1]{0:T(128)} %bitcast.half_ref, f32[16384,128]{1,0:T(8,128)} %bitcast.19, f32[256,128]{1,0:T(8,128)S(1)} %copy-done.1, f32[4,128]{1,0:T(4,128)S(1)} %copy-done.4), custom_call_target="tpu_custom_call" | custom-call | flops 2147483648 | bytes 6291456 | tf_op jit(solution)/shard_map/contract/pallas_call | solution.py:145
  19.9 0.0 copy-start.2
  19.9 1.3 copy-done.2
  21.3 0.0 collective-permute-done.3
  21.3 0.0 collective-permute-done.2
  21.3 0.9 add.38
  22.2 3.3 %collective-permute-start.4 = (f32[128,128]{1,0:T(8,128)S(1)}, f32[128,128]{1,0:T(8,128)S(1)}, u32[]{:S(2)}, u32[]{:S(2)}) collective-permute-start(f32[128,128]{1,0:T(8,128)S(1)} %add.39), channel_id=1, source_target_pairs={{0,64},{32,96},{64,0},{96,32},{128,192},{160,224},{192,128},{224,1... | collective-permute-start | bytes 196616 | tf_op jit(solution)/shard_map/ppermute | solution.py:199
  25.4 2.7 %collective-permute-done.4 = f32[128,128]{1,0:T(8,128)S(1)} collective-permute-done((f32[128,128]{1,0:T(8,128)S(1)}, f32[128,128]{1,0:T(8,128)S(1)}, u32[]{:S(2)}, u32[]{:S(2)}) %collective-permute-start.4) | collective-permute-done | bytes 65568 | tf_op jit(solution)/shard_map/ppermute | solution.py:199
  28.1 0.1 collective-permute-start.6
  28.2 10.7 %all-to-all-start = ((f32[32,32,128]{2,1,0:T(8,128)}), f32[32,32,128]{2,1,0:T(8,128)S(1)}, u32[]{:S(2)}, u32[]{:S(2)}) async-start(f32[32,32,128]{2,1,0:T(8,128)} %bitcast.6), calls=%async_computation | async-start | bytes 1048576 | tf_op jit(solution)/shard_map/all_to_all | solution.py:230
  38.9 5.6 %collective-permute-start.5 = (f32[128,128]{1,0:T(8,128)S(1)}, f32[128,128]{1,0:T(8,128)S(1)}, u32[]{:S(2)}, u32[]{:S(2)}) collective-permute-start(f32[128,128]{1,0:T(8,128)S(1)} %add.40), channel_id=1, source_target_pairs={{0,128},{32,160},{64,192},{96,224},{128,0},{160,32},{192,64},{224,... | collective-permute-start | bytes 196616 | tf_op jit(solution)/shard_map/ppermute | solution.py:199
  44.5 14.6 %collective-permute-done.5 = f32[128,128]{1,0:T(8,128)S(1)} collective-permute-done((f32[128,128]{1,0:T(8,128)S(1)}, f32[128,128]{1,0:T(8,128)S(1)}, u32[]{:S(2)}, u32[]{:S(2)}) %collective-permute-start.5) | collective-permute-done | bytes 65568 | tf_op jit(solution)/shard_map/ppermute | solution.py:199
  59.2 0.6 add.41.first_ref
  59.8 5.4 %inverse_of_product.1 = f32[128,128]{1,0:T(8,128)} custom-call(f32[128,128]{1,0:T(8,128)} %add.41.first_ref, f32[128,128]{1,0:T(8,128)} %second_ref.1), custom_call_target="tpu_custom_call" | custom-call | flops 5000000000 | bytes 196608 | tf_op jit(solution)/shard_map/inverse_of_product/pallas_call | solution.py:61
  65.2 0.0 collective-permute-done.6
  65.2 0.0 copy-start.5
  65.2 2.5 %add.42.p_ref = f32[4,1024,128]{2,1,0:T(8,128)S(1)} add(f32[4,1024,128]{2,1,0:T(8,128)} %copy-done.2, f32[4,1024,128]{2,1,0:T(8,128)} %collective-permute-done.6) | non-fusion elementwise | flops 524288 | bytes 6291456 | tf_op jit(solution)/shard_map/add | solution.py:235
  67.7 0.0 all-to-all-done
  67.8 0.0 copy-done.5
  67.8 0.2 fusion.1
  67.9 0.1 broadcast_in_dim.4
  68.0 21.6 %all_to_all.15 = f32[32,32,128]{2,1,0:T(8,128)S(1)} all-to-all(f32[32,32,128]{2,1,0:T(8,128)S(1)} %broadcast_in_dim.4), channel_id=1, replica_groups=mesh['z'=8,'xl'=2,'c'=2,'y'=4,'xh'=2] {'z','xl','xh'}, dimensions={0} | all-to-all | bytes 1048576 | tf_op jit(solution)/shard_map/all_to_all | solution.py:204
  89.6 0.0 copy-start.3
  89.6 0.0 collective-permute-start.11
  89.6 0.7 moments.1
  90.4 0.6 collective-permute-start.7
  90.9 0.9 collective-permute-done.7
  91.9 3.3 %collective-permute-start.9 = (f32[128,128]{1,0:T(8,128)S(1)}, f32[128,128]{1,0:T(8,128)S(1)}, u32[]{:S(2)}, u32[]{:S(2)}) collective-permute-start(f32[128,128]{1,0:T(8,128)S(1)} %add.43), channel_id=1, source_target_pairs={{0,4},{2,6},{4,0},{6,2},{1,5},{3,7},{5,1},{7,3},{8,12},{10,14},{12... | collective-permute-start | bytes 196616 | tf_op jit(solution)/shard_map/ppermute | solution.py:199
  95.1 1.1 collective-permute-start.10
  96.2 0.0 collective-permute-start.8
  96.2 0.0 collective-permute-start.12
  96.2 1.2 collective-permute-done.12
  97.4 0.7 broadcast_in_dim.5
  98.0 8.4 %all-to-all-start.2 = ((f32[64,4,128]{2,1,0:T(4,128)}), f32[64,4,128]{2,1,0:T(4,128)S(1)}, u32[]{:S(2)}, u32[]{:S(2)}) async-start(f32[64,4,128]{2,1,0:T(4,128)} %broadcast_in_dim.5), calls=%async_computation.2 | async-start | bytes 262144 | tf_op jit(solution)/shard_map/all_to_all | solution.py:204
  106.5 0.0 collective-permute-done.9
  106.5 0.0 collective-permute-done.10
  106.5 0.0 collective-permute-done.8
  106.5 0.6 add_add_fusion.second_ref
  107.2 10.0 %all-to-all-done.2 = f32[64,4,128]{2,1,0:T(4,128)S(1)} async-done(((f32[64,4,128]{2,1,0:T(4,128)}), f32[64,4,128]{2,1,0:T(4,128)S(1)}, u32[]{:S(2)}, u32[]{:S(2)}) %all-to-all-start.2) | async-done | bytes 131104 | tf_op jit(solution)/shard_map/all_to_all | solution.py:204
  117.2 0.1 reduce_sum.19
  117.2 0.0 collective-permute-done.11.other_hbm
  117.2 0.0 copy-done.3
  117.3 0.0 copy-start.6
  117.3 0.8 copy-done.6
  118.1 34.4 %finish.1 = (f32[128,128]{1,0:T(8,128)}, f32[2,1024,128]{2,1,0:T(8,128)}) custom-call(f32[128,128]{1,0:T(8,128)} %add.41.first_ref, f32[128,128]{1,0:T(8,128)} %add_add_fusion.second_ref, s32[1]{0:T(128)} %bitcast.half_ref, f32[1024,128]{1,0:T(8,128)} %bitcast.17, f32[1024,128]{1,0:T(8,128)} %copy-done.6), custom_call_target="tpu_custom_call" | custom-call | flops 5000000000 | bytes 4194304 | tf_op jit(solution)/shard_map/finish/pallas_call | solution.py:84
  152.4 1.6 %fusion.2 = f32[4,128]{1,0:T(4,128)} fusion(f32[4,128]{1,0:T(4,128)S(1)} %reduce_sum.19, f32[128,128]{1,0:T(8,128)} %get-tuple-element.37), kind=kOutput, calls=%fused_computation.3 | convolution fusion | flops 786432 | bytes 69632 | tf_op jit(solution)/shard_map/dot_general | solution.py:20
  (7 shorter events, 0.1 us)
Async XLA Ops:
  2.0 1.3 collective-permute-start
  3.4 0.9 copy-start
  4.3 0.7 copy-start.4
  4.9 10.8 %copy-start.1 = (f32[256,128]{1,0:T(8,128)S(1)}, f32[256,128]{1,0:T(8,128)}, u32[]{:S(2)}) copy-start(f32[256,128]{1,0:T(8,128)} %a_ref.3) | copy-start | bytes 393220
  9.1 12.1 %collective-permute-start.2 = (f32[1024,128]{1,0:T(8,128)S(1)}, f32[1024,128]{1,0:T(8,128)S(1)}, u32[]{:S(2)}, u32[]{:S(2)}) collective-permute-start(f32[1024,128]{1,0:T(8,128)S(1)} %get-tuple-element.25), channel_id=1, source_target_pairs={{0,8},{8,0},{1,9},{9,1},{2,10},{10,2},{3,11},{11,3},{4,12},{12,4},... | collective-permute-start | bytes 1572872 | tf_op jit(solution)/shard_map/ppermute | solution.py:199
  9.4 4.9 %collective-permute-start.1 = (f32[128,128]{1,0:T(8,128)S(1)}, f32[128,128]{1,0:T(8,128)S(1)}, u32[]{:S(2)}, u32[]{:S(2)}) collective-permute-start(f32[128,128]{1,0:T(8,128)S(1)} %add.36), channel_id=1, source_target_pairs={{0,16},{16,0},{1,17},{17,1},{2,18},{18,2},{3,19},{19,3},{4,20},{20... | collective-permute-start | bytes 196616 | tf_op jit(solution)/shard_map/ppermute | solution.py:199
  14.3 7.0 %collective-permute-start.3 = (f32[128,128]{1,0:T(8,128)S(1)}, f32[128,128]{1,0:T(8,128)S(1)}, u32[]{:S(2)}, u32[]{:S(2)}) collective-permute-start(f32[128,128]{1,0:T(8,128)S(1)} %add.37), channel_id=1, source_target_pairs={{0,32},{32,0},{64,96},{96,64},{128,160},{160,128},{192,224},{224,1... | collective-permute-start | bytes 196616 | tf_op jit(solution)/shard_map/ppermute | solution.py:199
  19.9 1.3 copy-start.2
  22.2 5.9 %collective-permute-start.4 = (f32[128,128]{1,0:T(8,128)S(1)}, f32[128,128]{1,0:T(8,128)S(1)}, u32[]{:S(2)}, u32[]{:S(2)}) collective-permute-start(f32[128,128]{1,0:T(8,128)S(1)} %add.39), channel_id=1, source_target_pairs={{0,64},{32,96},{64,0},{96,32},{128,192},{160,224},{192,128},{224,1... | collective-permute-start | bytes 196616 | tf_op jit(solution)/shard_map/ppermute | solution.py:199
  28.1 37.1 %collective-permute-start.6 = (f32[4,1024,128]{2,1,0:T(8,128)S(1)}, f32[4,1024,128]{2,1,0:T(8,128)}, u32[]{:S(2)}, u32[]{:S(2)}) collective-permute-start(f32[4,1024,128]{2,1,0:T(8,128)S(1)} %get-tuple-element.31), channel_id=1, source_target_pairs={{0,8},{8,0},{1,9},{9,1},{2,10},{10,2},{3,11},{11,3},{4,12},{12,4},... | collective-permute-start | bytes 6291464 | tf_op jit(solution)/shard_map/ppermute | solution.py:199
  28.2 39.5 %all-to-all-start = ((f32[32,32,128]{2,1,0:T(8,128)}), f32[32,32,128]{2,1,0:T(8,128)S(1)}, u32[]{:S(2)}, u32[]{:S(2)}) async-start(f32[32,32,128]{2,1,0:T(8,128)} %bitcast.6), calls=%async_computation | async-start | bytes 1048576 | tf_op jit(solution)/shard_map/all_to_all | solution.py:230
  38.9 20.3 %collective-permute-start.5 = (f32[128,128]{1,0:T(8,128)S(1)}, f32[128,128]{1,0:T(8,128)S(1)}, u32[]{:S(2)}, u32[]{:S(2)}) collective-permute-start(f32[128,128]{1,0:T(8,128)S(1)} %add.40), channel_id=1, source_target_pairs={{0,128},{32,160},{64,192},{96,224},{128,0},{160,32},{192,64},{224,... | collective-permute-start | bytes 196616 | tf_op jit(solution)/shard_map/ppermute | solution.py:199
  65.2 2.5 %copy-start.5 = (f32[128,128]{1,0:T(8,128)S(1)}, f32[128,128]{1,0:T(8,128)}, u32[]{:S(2)}) copy-start(f32[128,128]{1,0:T(8,128)} %inverse_of_product.1) | copy-start | bytes 196612
  89.6 27.6 %copy-start.3 = (f32[32,32,128]{2,1,0:T(8,128)}, f32[32,32,128]{2,1,0:T(8,128)S(1)}, u32[]{:S(2)}) copy-start(f32[32,32,128]{2,1,0:T(8,128)S(1)} %all_to_all.15) | copy-start | bytes 1572868
  89.6 27.6 %collective-permute-start.11 = (f32[1024,128]{1,0:T(8,128)S(1)}, f32[1024,128]{1,0:T(8,128)S(1)}, u32[]{:S(2)}, u32[]{:S(2)}) collective-permute-start(f32[1024,128]{1,0:T(8,128)S(1)} %bitcast.15), channel_id=1, source_target_pairs={{0,8},{8,0},{1,9},{9,1},{2,10},{10,2},{3,11},{11,3},{4,12},{12,4},... | collective-permute-start | bytes 1572872 | tf_op jit(solution)/shard_map/ppermute | solution.py:199
  90.4 1.5 collective-permute-start.7
  91.9 14.6 %collective-permute-start.9 = (f32[128,128]{1,0:T(8,128)S(1)}, f32[128,128]{1,0:T(8,128)S(1)}, u32[]{:S(2)}, u32[]{:S(2)}) collective-permute-start(f32[128,128]{1,0:T(8,128)S(1)} %add.43), channel_id=1, source_target_pairs={{0,4},{2,6},{4,0},{6,2},{1,5},{3,7},{5,1},{7,3},{8,12},{10,14},{12... | collective-permute-start | bytes 196616 | tf_op jit(solution)/shard_map/ppermute | solution.py:199
  95.1 11.4 %collective-permute-start.10 = (f32[128,128]{1,0:T(8,128)S(1)}, f32[128,128]{1,0:T(8,128)S(1)}, u32[]{:S(2)}, u32[]{:S(2)}) collective-permute-start(f32[128,128]{1,0:T(8,128)S(1)} %add.43), channel_id=1, source_target_pairs={{0,6},{2,4},{4,2},{6,0},{1,7},{3,5},{5,3},{7,1},{8,14},{10,12},{12... | collective-permute-start | bytes 196616 | tf_op jit(solution)/shard_map/ppermute | solution.py:199
  96.2 10.3 %collective-permute-start.8 = (f32[128,128]{1,0:T(8,128)S(1)}, f32[128,128]{1,0:T(8,128)S(1)}, u32[]{:S(2)}, u32[]{:S(2)}) collective-permute-start(f32[128,128]{1,0:T(8,128)S(1)} %add.43), channel_id=1, source_target_pairs={{0,2},{2,0},{4,6},{6,4},{1,3},{3,1},{5,7},{7,5},{8,10},{10,8},{12,... | collective-permute-start | bytes 196616 | tf_op jit(solution)/shard_map/ppermute | solution.py:199
  96.2 1.2 collective-permute-start.12
  98.0 19.1 %all-to-all-start.2 = ((f32[64,4,128]{2,1,0:T(4,128)}), f32[64,4,128]{2,1,0:T(4,128)S(1)}, u32[]{:S(2)}, u32[]{:S(2)}) async-start(f32[64,4,128]{2,1,0:T(4,128)} %broadcast_in_dim.5), calls=%async_computation.2 | async-start | bytes 262144 | tf_op jit(solution)/shard_map/all_to_all | solution.py:204
  117.3 0.8 copy-start.6

commit v5 on v3

--- a/solution.py
+++ b/solution.py
@@ -12,8 +12,10 @@
 HIGH = lax.Precision.HIGHEST
 F32 = jnp.float32
 BF16 = jnp.bfloat16
-PLANE = ("z", "xl", "xh")
+RING = ("xl", "xh")
 VMEM = pl.BlockSpec(memory_space=pltpu.VMEM)
+HBM = pl.BlockSpec(memory_space=pltpu.HBM)
+SMEM = pl.BlockSpec(memory_space=pltpu.SMEM)
 
 
 def dot(a, b):
@@ -63,8 +65,26 @@
         out_shape=jax.ShapeDtypeStruct(first.shape, F32),
         in_specs=[VMEM, VMEM],
         out_specs=VMEM,
+        cost_estimate=pl.CostEstimate(flops=5 * 10**9, transcendentals=128, bytes_accessed=3 * 2**16),
         name="inverse_of_product",
     )(first, second)
+
+
+def assemble_kernel(at_ref, mine_ref, other_ref, out_ref):
+    count = mine_ref.shape[0]
+    for n in range(count):
+        out_ref[at_ref[0] * count + (at_ref[1] ^ n)] = mine_ref[n]
+        out_ref[(1 - at_ref[0]) * count + (at_ref[1] ^ n)] = other_ref[n]
+
+
+def assemble(at, mine, other):
+    return pl.pallas_call(
+        assemble_kernel,
+        out_shape=jax.ShapeDtypeStruct((2 * mine.shape[0],) + mine.shape[1:], F32),
+        in_specs=[SMEM, VMEM, VMEM],
+        out_specs=VMEM,
+        name="assemble",
+    )(at, mine, other)
 
 
 def split3(x):
@@ -74,15 +94,15 @@
     return high, middle, (rest - middle.astype(F32)).astype(BF16)
 
 
-def contract_kernel(chunk, half_ref, x_hbm, a_ref, c_ref, p_ref, b_ref, x_ref, w_ref, sems):
+def contract_kernel(chunk, at_ref, x_hbm, a_ref, c_ref, p_hbm, b_ref, x_ref, w_ref, p_ref, sems):
     count, rows, rank = p_ref.shape
     span = 2 * count
-    base = half_ref[0] * (rows * span)
     copies = []
     for n, at in enumerate(range(0, rows, chunk)):
         size = chunk * span
+        block = at_ref[0] * (rows // chunk) + (at_ref[1] ^ n)
         copy = pltpu.make_async_copy(
-            x_hbm.at[pl.ds(base + at * span, size)], x_ref.at[pl.ds(at * span, size)], sems.at[n]
+            x_hbm.at[pl.ds(block * size, size)], x_ref.at[pl.ds(at * span, size)], sems.at[n]
         )
         copy.start()
         copies.append(copy)
@@ -109,56 +129,144 @@
                 term = value * c_ref[k : k + 1, :]
                 total = term if total is None else total + term
             b_ref[row : row + 128] = total
-
-
-def contract(half, x, factor_a, factor_c, rows):
+        copy = pltpu.make_async_copy(
+            p_ref.at[:, pl.ds(at, chunk)],
+            p_hbm.at[:, pl.ds(at, chunk)],
+            sems.at[len(copies)],
+        )
+        copy.start()
+        copies.append(copy)
+    for copy in copies[rows // chunk :]:
+        copy.wait()
+
+
+def contract(at, x, factor_a, factor_c, rows):
     count, (depth, rank) = factor_c.shape[0], factor_a.shape
-    chunk = 256
+    chunk = rows // 4
     return pl.pallas_call(
         functools.partial(contract_kernel, chunk),
         out_shape=[
-            jax.ShapeDtypeStruct((count, rows, rank), F32),
+            pltpu.HBM((count, rows, rank), F32),
             jax.ShapeDtypeStruct((rows, rank), F32),
         ],
-        in_specs=[
-            pl.BlockSpec(memory_space=pltpu.SMEM),
-            pl.BlockSpec(memory_space=pltpu.HBM),
-            VMEM,
-            VMEM,
-        ],
-        out_specs=[VMEM, VMEM],
+        in_specs=[SMEM, HBM, VMEM, VMEM],
+        out_specs=[HBM, VMEM],
         scratch_shapes=[
             pltpu.VMEM((rows * 2 * count, depth // 2), F32),
             pltpu.VMEM((depth, 3 * rank), BF16),
-            pltpu.SemaphoreType.DMA((rows // chunk,)),
+            pltpu.VMEM((count, rows, rank), F32),
+            pltpu.SemaphoreType.DMA((2 * rows // chunk,)),
         ],
         compiler_params=pltpu.CompilerParams(vmem_limit_bytes=24 << 20),
+        cost_estimate=pl.CostEstimate(
+            flops=16 * count * rows * depth * rank,
+            transcendentals=0,
+            bytes_accessed=4 * count * rows * (depth + rank),
+        ),
         name="contract",
-    )(half, x, factor_a, factor_c)
-
-
-def moments_kernel(f_ref, p_ref, c_ref, g_ref):
+    )(at, x, factor_a, factor_c)
+
+
+def parcels_kernel(x_ref, b_ref, b_far_ref, g_ref, g_far_ref, *outs):
+    depth, rows, _ = outs[0].shape
+    block, slab = b_ref.shape[0] // 4, g_ref.shape[0] // 4
+    some, few = block // depth, slab // depth
+    for n, out in enumerate(outs):
+        for z in range(depth):
+            at = n * block + z * some
+            out[z, :some] = b_ref[at : at + some] + b_far_ref[at : at + some]
+        for a in range(4):
+
+            @pl.when((x_ref[0] ^ n) == a)
+            def _():
+                for z in range(depth):
+                    at = a * slab + z * few
+                    out[z, some:] = 0.5 * (g_ref[at : at + few] + g_far_ref[at : at + few])
+
+
+def parcels(x, b, b_far, g, g_far, depth):
+    rank = b.shape[1]
+    shape = jax.ShapeDtypeStruct((depth, (b.shape[0] + g.shape[0]) // (4 * depth), rank), F32)
+    return pl.pallas_call(
+        parcels_kernel,
+        out_shape=[shape] * 4,
+        in_specs=[SMEM] + [VMEM] * 4,
+        out_specs=[VMEM] * 4,
+        name="parcels",
+    )(x, b, b_far, g, g_far)
+
+
+def spread_kernel(x_ref, out_ref):
+    out_ref[...] = jnp.broadcast_to(jnp.sum(x_ref[...], axis=0)[None], out_ref.shape)
+
+
+def spread(x):
+    return pl.pallas_call(
+        spread_kernel,
+        out_shape=jax.ShapeDtypeStruct(x.shape, F32),
+        in_specs=[VMEM],
+        out_specs=VMEM,
+        name="spread",
+    )(x)
+
+
+def solve_kernel(x_ref, *refs):
+    columns, (h_ref, p_hbm, q_hbm, g_ref, f_ref, out_ref, p_ref, q_ref, sems) = refs[:4], refs[4:]
+    depth, every, rank = columns[0].shape
+    few = rank // (4 * depth)
+    some = every - few
+    copies = [
+        pltpu.make_async_copy(p_hbm, p_ref, sems.at[0]),
+        pltpu.make_async_copy(q_hbm, q_ref, sems.at[1]),
+    ]
+    for copy in copies:
+        copy.start()
+    for n in range(4):
+        for a in range(4):
+
+            @pl.when((x_ref[0] ^ n) == a)
+            def _():
+                for z in range(depth):
+                    at = (a * depth + z) * few
+                    g_ref[at : at + few] = columns[n][z, some:]
+
+    inverse = spd_inverse(g_ref[...] * h_ref[...], 16)
+    block = depth * some
+    for n in range(4):
+        f = dot(columns[n][:, :some].reshape(block, rank), inverse)
+        f_ref[n * block : (n + 1) * block] = f
     f = f_ref[...]
-    g_ref[...] = lax.dot_general(
+    out_ref[:rank] = lax.dot_general(
         f, f, (((0,), (0,)), ((), ())), precision=HIGH, preferred_element_type=F32
     )
+    out_ref[rank:] = jnp.zeros((out_ref.shape[0] - rank, rank), F32)
+    for copy in copies:
+        copy.wait()
     for k in range(p_ref.shape[0]):
-        c_ref[k : k + 1] = jnp.sum(p_ref[k] * f, axis=0, keepdims=True)
-
-
-def moments(f, p):
-    count, _, rank = p.shape
-    return pl.pallas_call(
-        moments_kernel,
+        both = (p_ref[k] + q_ref[k]) * f_ref[...]
+        out_ref[rank + k : rank + k + 1] = jnp.sum(both, axis=0, keepdims=True)
+
+
+def solve(x, columns, gram_c, first, second):
+    count, rows, rank = first.shape
+    square = jax.ShapeDtypeStruct((rank, rank), F32)
+    return pl.pallas_call(
+        solve_kernel,
         out_shape=[
-            jax.ShapeDtypeStruct((count, rank), F32),
-            jax.ShapeDtypeStruct((rank, rank), F32),
+            square,
+            jax.ShapeDtypeStruct((rows, rank), F32),
+            jax.ShapeDtypeStruct((rank + 8 * pl.cdiv(count, 8), rank), F32),
         ],
-        in_specs=[VMEM, VMEM],
-        out_specs=[VMEM, VMEM],
+        in_specs=[SMEM] + [VMEM] * 5 + [HBM] * 2,
+        out_specs=[VMEM] * 3,
+        scratch_shapes=[
+            pltpu.VMEM((count, rows, rank), F32),
+            pltpu.VMEM((count, rows, rank), F32),
+            pltpu.SemaphoreType.DMA((2,)),
+        ],
         compiler_params=pltpu.CompilerParams(vmem_limit_bytes=24 << 20),
-        name="moments",
-    )(f, p)
+        name="solve",
+    )(x, *columns, gram_c, first, second)
 
 
 def swap(x, axis, bit=1):
@@ -174,43 +282,39 @@
 def body(tensor, factor_a, factor_c, gram_c):
     mode_two, mode_three, mode_one = tensor.shape
     rank = factor_a.shape[1]
-    core = lax.axis_index("c")
-    plane = lax.axis_size(PLANE)
+    core = lax.axis_index("c").astype(jnp.int32)
+    x = lax.axis_index(RING).astype(jnp.int32)
+    depth = lax.axis_size("z")
     half = mode_two // 2
-    rows = half // plane
-
-    gram_a = dot(factor_a.T, factor_a)
-    for axis, bit in (("c", 1), ("xl", 1), ("z", 1), ("z", 2), ("z", 4)):
-        gram_a = gram_a + swap(gram_a, axis, bit)
-    inverse = inverse_of_product(gram_a, gram_c)
-
     lanes = mode_one // 2
     flat = tensor.reshape(mode_two, mode_three, 2, lanes).transpose(0, 2, 1, 3)
     flat = flat.reshape(mode_two * mode_three * 2, lanes)
-    index = core.astype(jnp.int32).reshape(1)
-    p_other, b_other = contract(1 - index, flat, factor_a, factor_c, half)
-    p_mine, b_mine = contract(index, flat, factor_a, factor_c, half)
-    b_half = b_mine + swap(b_other, "c")
-    shares = lax.all_to_all(b_half.reshape(plane, rows, rank), PLANE, 0, 0)
-    piece = dot(jnp.sum(shares, axis=0), inverse)
-
-    f_mine = gather(piece, PLANE).reshape(half, rank)
-    f_other = swap(f_mine, "c")
-    c_mine, g_mine = moments(f_mine, p_mine)
-    c_other, g_other = moments(f_other, p_other)
-    first = jnp.where(core == 0, f_mine, f_other)
-    second = jnp.where(core == 0, f_other, f_mine)
-    factor_b = jnp.concatenate([first, second], axis=0)
-
-    local_c = c_mine + c_other
-    local_c = local_c + swap(local_c, "c")
-    mttkrp_c = jnp.sum(gather(local_c, ("z", "xl", "y")), axis=0)
-    lower = jnp.where(core == 0, g_mine, g_other)
-    gram_b = lower + jnp.where(core == 0, g_other, g_mine)
-    away = [swap(gram_b, "y", bit) for bit in (1, 2, 3)]
-    gram_b = (gram_b + away[0]) + (away[1] + away[2])
-    factor_c_new = dot(mttkrp_c, inverse_of_product(gram_a, gram_b))
-    return (factor_b, factor_c_new)
+    flat = pltpu.with_memory_space_constraint(flat, pltpu.HBM)
+
+    p_other, b_other = contract(jnp.stack([1 - core, x]), flat, factor_a, factor_c, half)
+    p_mine, b_mine = contract(jnp.stack([core, x]), flat, factor_a, factor_c, half)
+    gram_part = dot(factor_a.T, factor_a)
+    at = x.reshape(1)
+    sent = parcels(at, b_mine, swap(b_other, "c"), gram_part, swap(gram_part, "c"), depth)
+    got = [sent[0]] + [swap(sent[n], RING, n) for n in (1, 2, 3)]
+    column = (got[0] + got[1]) + (got[2] + got[3])
+    column = spread(lax.all_to_all(column, "z", 0, 0))
+    column = lax.all_to_all(column, "z", 0, 0)
+    columns = [column] + [swap(column, RING, n) for n in (1, 2, 3)]
+    gram_a, f_mine, sums = solve(at, columns, gram_c, p_mine, swap(p_other, "c"))
+
+    sums = sums + swap(sums, "c")
+    away = [swap(sums, "y", bit) for bit in (1, 2, 3)]
+    sums = (sums + away[0]) + (away[1] + away[2])
+    gram_b, local_c = sums[:rank], sums[rank : rank + mode_three]
+    mttkrp_c = jnp.sum(gather(local_c, ("z", "xl")), axis=0)
+    last, f_other = lax.optimization_barrier(
+        (inverse_of_product(gram_a, gram_b), swap(f_mine, "c"))
+    )
+    shape = (4, half // 4, rank)
+    factor_b = assemble(jnp.stack([core, x]), f_mine.reshape(shape), f_other.reshape(shape))
+    factor_c_new = dot(mttkrp_c, last)
+    return (factor_b.reshape(mode_two, rank), factor_c_new)
 
 
 def solution(mesh):

time: 115 us -> 109 us (0.948)
  starting transfers between devices: 32.8 us -> 16 us
  Pallas kernels: 18.8 us -> 28.5 us
  blocking collectives: 22.8 us -> 30.9 us
  other arithmetic: 3.4 us -> 1.09 us
  matrix products: 2.97 us -> 1.13 us
  waiting for transfers between devices: 24.5 us -> 22.8 us
    pallas_call x4 -> x6, Pallas kernels: 7.94 us -> 23.1 us  [the longest x2 11.1 us: contract(): pl.pallas_call(functools.partial(contract_kernel, chunk), out_shape=[pltp...]
    all_to_all x1 -> x0, starting transfers between devices: 11.6 us -> none  [body(): shares = lax.all_to_all(b_half.reshape(plane, rows, rank), PLANE, 0, 0)]
    all_to_all x1 -> x2, blocking collectives: 22.8 us -> 30.9 us  [the longest x1 18.2 us: body(): column = spread(lax.all_to_all(column, 'z', 0, 0))]
    pallas_call x2 -> x1, Pallas kernels: 10.8 us -> 5.42 us  [inverse_of_product(): pl.pallas_call(inverse_kernel, out_shape=jax.ShapeDtypeStruct(first.shape...]
    all_to_all x1, starting transfers between devices: 7.97 us -> 3.49 us  [gather(): return lax.all_to_all(jnp.broadcast_to(x[None], (n,) + x.shape), axes, 0, 0)]
    dot_general x3 -> x2, matrix products: 2.97 us -> 1.13 us  [dot(): return jnp.dot(a, b, precision=HIGH, preferred_element_type=F32)]
    unnamed x14 -> x28, local copies, waits for them, and re-layouts: 7.9 us -> 6.26 us
    all_to_all x1, waiting for transfers between devices: 3.59 us -> 2.06 us  [gather(): return lax.all_to_all(jnp.broadcast_to(x[None], (n,) + x.shape), axes, 0, 0)]
  transfers between devices with their start and end apart: 13 -> 15, of which waited for: 7 -> 8; matrix products, arithmetic and copies ran while one was open for 3% -> 2% of each run, Pallas kernels for 13% -> 14%
where the time goes in v5:
time: 109 us
  blocking collectives  30.9 us (28%)
  Pallas kernels  28.5 us (26%)
  waiting for transfers between devices  22.8 us (21%)
  starting transfers between devices  16 us (15%)
  local copies, waits for them, and re-layouts  7.51 us (7%)
  matrix products  1.13 us (1%)
  other arithmetic  1.09 us (1%)
    ppermute x14, waiting for transfers between devices, swap(): return lax.ppermute(x, axis, [(i, i ^ bit) for i in range(n)])  20.8 us
    all_to_all x1, blocking collectives, body(): column = spread(lax.all_to_all(column, 'z', 0, 0))  18.2 us
    all_to_all x1, blocking collectives, body(): column = lax.all_to_all(column, 'z', 0, 0)  12.7 us
    ppermute x14, starting transfers between devices, swap(): return lax.ppermute(x, axis, [(i, i ^ bit) for i in range(n)])  12.5 us
    pallas_call x2, Pallas kernels, contract(): pl.pallas_call(functools.partial(contract_kernel, chunk), out_shape=[pltp...  11.1 us
    unnamed x28, local copies, waits for them, and re-layouts  6.26 us
    pallas_call x1, Pallas kernels, solve(): pl.pallas_call(solve_kernel, out_shape=[square, jax.ShapeDtypeStruct((row...  5.9 us
    pallas_call x1, Pallas kernels, inverse_of_product(): pl.pallas_call(inverse_kernel, out_shape=jax.ShapeDtypeStruct(first.shape...  5.42 us
  transfers between devices with their start and end apart: 15, of which 8 were waited for; matrix products, arithmetic and copies ran while one was open for 2% of the time, Pallas kernels for 14%

profile of v5, /device:TPU:2, one launch (start us, length us, event | category | flops | bytes accessed | tf_op | source)
XLA Modules:
  0.0 108.9 jit_solution(13939415875482149942)
XLA Ops:
  0.6 0.1 pad_add_fusion
  0.7 0.0 copy-start.7
  0.7 0.9 copy-done
  1.6 0.7 copy-done.6
  2.3 5.6 %contract.3 = (f32[4,1024,128]{2,1,0:T(8,128)}, f32[1024,128]{1,0:T(8,128)S(1)}) custom-call(s32[2]{0:T(128)S(1)} %get-tuple-element.29.at_ref, f32[16384,128]{1,0:T(8,128)} %bitcast.16, f32[256,128]{1,0:T(8,128)S(1)} %copy-done, f32[4,128]{1,0:T(4,128)S(1)} %copy-done.6), custom_call_target="tpu_custom_call" | custom-call | flops 2147483648 | bytes 6291456 | tf_op jit(solution)/shard_map/contract/pallas_call | solution.py:146
  7.9 0.1 collective-permute-start.8
  8.0 0.5 collective-permute-start
  8.5 0.4 fusion.g_ref
  8.9 0.0 copy-start.11
  8.9 0.2 collective-permute-start.1
  9.1 0.0 copy-done.7
  9.1 0.0 copy-done.1
  9.1 5.5 %contract.2 = (f32[4,1024,128]{2,1,0:T(8,128)}, f32[1024,128]{1,0:T(8,128)S(1)}) custom-call(s32[2]{0:T(128)S(1)} %get-tuple-element.28.at_ref, f32[16384,128]{1,0:T(8,128)} %bitcast.17, f32[256,128]{1,0:T(8,128)S(1)} %copy-done.1, f32[4,128]{1,0:T(4,128)S(1)} %copy-done.6), custom_call_target="tpu_custom_call" | custom-call | flops 2147483648 | bytes 6291456 | tf_op jit(solution)/shard_map/contract/pallas_call | solution.py:146
  14.6 0.0 copy-done.11
  14.7 0.0 copy-start.4
  14.7 0.8 copy-done.4
  15.4 0.0 collective-permute-done.1.g_far_ref
  15.5 0.0 collective-permute-done.b_far_ref
  15.5 0.0 copy-start.10
  15.5 0.6 copy-done.12
  16.1 0.2 copy-done.10
  16.3 2.2 %parcels.1 = (f32[8,36,128]{2,1,0:T(8,128)}, f32[8,36,128]{2,1,0:T(8,128)}, f32[8,36,128]{2,1,0:T(8,128)}, f32[8,36,128]{2,1,0:T(8,128)}) custom-call(s32[1]{0:T(128)} %bitcast.1.x_ref, f32[1024,128]{1,0:T(8,128)} %copy-done.4, f32[1024,128]{1,0:T(8,128)} %copy-done.10, f32[128,128]{1,0:T(8,128)} %copy-done.11, f32[128,128]{1,0:T(8,128)} %copy-done.12), custom_call_target="tpu_custom_call" | custom-call | tf_op jit(solution)/shard_map/parcels/pallas_call | solution.py:190
  18.5 2.1 %collective-permute-start.2 = (f32[8,36,128]{2,1,0:T(8,128)}, f32[8,36,128]{2,1,0:T(8,128)S(1)}, u32[]{:S(2)}, u32[]{:S(2)}) collective-permute-start(f32[8,36,128]{2,1,0:T(8,128)} %get-tuple-element.18), channel_id=1, source_target_pairs={{0,1},{1,0},{16,17},{17,16},{2,3},{3,2},{18,19},{19,18},{4,5},{5,4... | collective-permute-start | bytes 442376 | tf_op jit(solution)/shard_map/ppermute | solution.py:274
  20.7 1.4 %collective-permute-start.3 = (f32[8,36,128]{2,1,0:T(8,128)}, f32[8,36,128]{2,1,0:T(8,128)S(1)}, u32[]{:S(2)}, u32[]{:S(2)}) collective-permute-start(f32[8,36,128]{2,1,0:T(8,128)} %get-tuple-element.19), channel_id=1, source_target_pairs={{0,16},{1,17},{16,0},{17,1},{2,18},{3,19},{18,2},{19,3},{4,20},{5,... | collective-permute-start | bytes 442376 | tf_op jit(solution)/shard_map/ppermute | solution.py:274
  22.1 0.5 collective-permute-start.4
  22.6 4.6 %collective-permute-done.2 = f32[8,36,128]{2,1,0:T(8,128)S(1)} collective-permute-done((f32[8,36,128]{2,1,0:T(8,128)}, f32[8,36,128]{2,1,0:T(8,128)S(1)}, u32[]{:S(2)}, u32[]{:S(2)}) %collective-permute-start.2) | collective-permute-done | bytes 147488 | tf_op jit(solution)/shard_map/ppermute | solution.py:274
  27.3 3.1 %collective-permute-done.3 = f32[8,36,128]{2,1,0:T(8,128)S(1)} collective-permute-done((f32[8,36,128]{2,1,0:T(8,128)}, f32[8,36,128]{2,1,0:T(8,128)S(1)}, u32[]{:S(2)}, u32[]{:S(2)}) %collective-permute-start.3) | collective-permute-done | bytes 147488 | tf_op jit(solution)/shard_map/ppermute | solution.py:274
  30.4 0.0 collective-permute-done.4
  30.4 1.0 add_add_fusion
  31.3 18.2 %all_to_all.15.x_ref = f32[8,36,128]{2,1,0:T(8,128)} all-to-all(f32[8,36,128]{2,1,0:T(8,128)S(1)} %add_add_fusion), channel_id=1, replica_groups=mesh['z'=8,'xl'=2,'c'=2,'y'=4,'xh'=2] {'z'}, dimensions={0} | all-to-all | bytes 294912 | tf_op jit(solution)/shard_map/all_to_all | solution.py:301
  49.6 1.6 %spread.1 = f32[8,36,128]{2,1,0:T(8,128)} custom-call(f32[8,36,128]{2,1,0:T(8,128)} %all_to_all.15.x_ref), custom_call_target="tpu_custom_call" | custom-call | tf_op jit(solution)/shard_map/spread/pallas_call | solution.py:204
  51.2 12.7 %all_to_all.16.refs_0_ = f32[8,36,128]{2,1,0:T(8,128)S(1)} all-to-all(f32[8,36,128]{2,1,0:T(8,128)} %spread.1), channel_id=1, replica_groups=mesh['z'=8,'xl'=2,'c'=2,'y'=4,'xh'=2] {'z'}, dimensions={0} | all-to-all | bytes 294912 | tf_op jit(solution)/shard_map/all_to_all | solution.py:302
  63.9 1.5 %collective-permute-start.7 = (f32[8,36,128]{2,1,0:T(8,128)S(1)}, f32[8,36,128]{2,1,0:T(8,128)S(1)}, u32[]{:S(2)}, u32[]{:S(2)}) collective-permute-start(f32[8,36,128]{2,1,0:T(8,128)S(1)} %all_to_all.16.refs_0_), channel_id=1, source_target_pairs={{0,17},{1,16},{16,1},{17,0},{2,19},{3,18},{18,3},{19,2},{4,21},{5,... | collective-permute-start | bytes 442376 | tf_op jit(solution)/shard_map/ppermute | solution.py:274
  65.4 1.8 %collective-permute-start.6 = (f32[8,36,128]{2,1,0:T(8,128)S(1)}, f32[8,36,128]{2,1,0:T(8,128)S(1)}, u32[]{:S(2)}, u32[]{:S(2)}) collective-permute-start(f32[8,36,128]{2,1,0:T(8,128)S(1)} %all_to_all.16.refs_0_), channel_id=1, source_target_pairs={{0,16},{1,17},{16,0},{17,1},{2,18},{3,19},{18,2},{19,3},{4,20},{5,... | collective-permute-start | bytes 442376 | tf_op jit(solution)/shard_map/ppermute | solution.py:274
  67.2 0.2 collective-permute-start.5
  67.4 3.6 %collective-permute-done.7.refs_3_ = f32[8,36,128]{2,1,0:T(8,128)S(1)} collective-permute-done((f32[8,36,128]{2,1,0:T(8,128)S(1)}, f32[8,36,128]{2,1,0:T(8,128)S(1)}, u32[]{:S(2)}, u32[]{:S(2)}) %collective-permute-start.7) | collective-permute-done | bytes 147488 | tf_op jit(solution)/shard_map/ppermute | solution.py:274
  71.0 0.0 collective-permute-done.6.refs_2_
  71.0 3.1 %collective-permute-done.5.refs_1_ = f32[8,36,128]{2,1,0:T(8,128)S(1)} collective-permute-done((f32[8,36,128]{2,1,0:T(8,128)S(1)}, f32[8,36,128]{2,1,0:T(8,128)S(1)}, u32[]{:S(2)}, u32[]{:S(2)}) %collective-permute-start.5) | collective-permute-done | bytes 147488 | tf_op jit(solution)/shard_map/ppermute | solution.py:274
  74.0 0.0 collective-permute-done.8.refs_6_
  74.0 0.0 copy-done.5
  74.0 1.6 %copy-done.2 = f32[4,1024,128]{2,1,0:T(8,128)S(1)} copy-done((f32[4,1024,128]{2,1,0:T(8,128)S(1)}, f32[4,1024,128]{2,1,0:T(8,128)}, u32[]{:S(2)}) %copy-start.2) | copy-done | bytes 2097176
  75.6 5.9 %solve.1 = (f32[128,128]{1,0:T(8,128)S(1)}, f32[1024,128]{1,0:T(8,128)S(1)}, f32[136,128]{1,0:T(8,128)S(1)}) custom-call(s32[1]{0:T(128)} %bitcast.1.x_ref, f32[8,36,128]{2,1,0:T(8,128)S(1)} %all_to_all.16.refs_0_, f32[8,36,128]{2,1,0:T(8,128)S(1)} %collective-permute-done.5.refs_1_, f32[8,36,128]{2,1,0:T(8,128)S(1)} %collective-permute-done.6.refs_2_, ...), custom_call_target="tpu_custom_call" | custom-call | tf_op jit(solution)/shard_map/solve/pallas_call | solution.py:253
  81.5 0.0 copy-start.8
  81.5 0.6 copy-done.8
  82.2 0.0 collective-permute-start.9
  82.2 1.3 %collective-permute-done.9 = f32[136,128]{1,0:T(8,128)S(1)} collective-permute-done((f32[136,128]{1,0:T(8,128)S(1)}, f32[136,128]{1,0:T(8,128)S(1)}, u32[]{:S(2)}, u32[]{:S(2)}) %collective-permute-start.9) | collective-permute-done | bytes 69664 | tf_op jit(solution)/shard_map/ppermute | solution.py:274
  83.4 3.1 %collective-permute-start.12 = (f32[136,128]{1,0:T(8,128)S(1)}, f32[136,128]{1,0:T(8,128)S(1)}, u32[]{:S(2)}, u32[]{:S(2)}) collective-permute-start(f32[136,128]{1,0:T(8,128)S(1)} %add.28), channel_id=1, source_target_pairs={{0,6},{2,4},{4,2},{6,0},{1,7},{3,5},{5,3},{7,1},{8,14},{10,12},{12... | collective-permute-start | bytes 208904 | tf_op jit(solution)/shard_map/ppermute | solution.py:274
  86.5 0.6 collective-permute-start.11
  87.2 0.5 collective-permute-start.10
  87.6 0.0 collective-permute-start.13
  87.6 2.2 %collective-permute-done.12 = f32[136,128]{1,0:T(8,128)S(1)} collective-permute-done((f32[136,128]{1,0:T(8,128)S(1)}, f32[136,128]{1,0:T(8,128)S(1)}, u32[]{:S(2)}, u32[]{:S(2)}) %collective-permute-start.12) | collective-permute-done | bytes 69664 | tf_op jit(solution)/shard_map/ppermute | solution.py:274
  89.8 2.9 %collective-permute-done.11 = f32[136,128]{1,0:T(8,128)S(1)} collective-permute-done((f32[136,128]{1,0:T(8,128)S(1)}, f32[136,128]{1,0:T(8,128)S(1)}, u32[]{:S(2)}, u32[]{:S(2)}) %collective-permute-start.11) | collective-permute-done | bytes 69664 | tf_op jit(solution)/shard_map/ppermute | solution.py:274
  92.8 0.0 collective-permute-done.10
  92.8 0.6 slice.8.second_ref
  93.4 0.6 broadcast_in_dim.2
  94.0 3.5 %all-to-all-start.2 = ((f32[16,4,128]{2,1,0:T(4,128)}), f32[16,4,128]{2,1,0:T(4,128)S(1)}, u32[]{:S(2)}, u32[]{:S(2)}) async-start(f32[16,4,128]{2,1,0:T(4,128)} %broadcast_in_dim.2), calls=%async_computation.2 | async-start | bytes 65536 | tf_op jit(solution)/shard_map/all_to_all | solution.py:279
  97.5 5.4 %inverse_of_product.1 = f32[128,128]{1,0:T(8,128)} custom-call(f32[128,128]{1,0:T(8,128)} %copy-done.8, f32[128,128]{1,0:T(8,128)} %slice.8.second_ref), custom_call_target="tpu_custom_call" | custom-call | flops 5000000000 | bytes 196608 | tf_op jit(solution)/shard_map/inverse_of_product/pallas_call | solution.py:63
  102.9 0.0 copy-done.3
  103.0 2.1 %all-to-all-done.2 = f32[16,4,128]{2,1,0:T(4,128)S(1)} async-done(((f32[16,4,128]{2,1,0:T(4,128)}), f32[16,4,128]{2,1,0:T(4,128)S(1)}, u32[]{:S(2)}, u32[]{:S(2)}) %all-to-all-start.2) | async-done | bytes 32800 | tf_op jit(solution)/shard_map/all_to_all | solution.py:279
  105.0 0.0 collective-permute-done.13
  105.1 0.8 copy-done.9
  105.9 2.2 %assemble.1 = f32[8,256,128]{2,1,0:T(8,128)} custom-call(s32[2]{0:T(128)} %copy-done.7, f32[4,256,128]{2,1,0:T(8,128)} %bitcast.15, f32[4,256,128]{2,1,0:T(8,128)} %bitcast.19), custom_call_target="tpu_custom_call" | custom-call | tf_op jit(solution)/shard_map/assemble/pallas_call | solution.py:81
  108.1 0.0 copy-done.13
  108.1 0.7 fusion.1
  (13 shorter events, 0.1 us)
Async XLA Ops:
  0.7 8.4 %copy-start.7 = (s32[2]{0:T(128)}, s32[2]{0:T(128)S(1)}, u32[]{:S(2)}) copy-start(s32[2]{0:T(128)S(1)} %get-tuple-element.28.at_ref) | copy-start | bytes 28
  0.7 0.9 copy-start
  1.6 0.7 copy-start.6
  2.3 6.8 %copy-start.1 = (f32[256,128]{1,0:T(8,128)S(1)}, f32[256,128]{1,0:T(8,128)}, u32[]{:S(2)}) copy-start(f32[256,128]{1,0:T(8,128)} %a_ref.3) | copy-start | bytes 393220
  7.9 66.1 %collective-permute-start.8 = (f32[4,1024,128]{2,1,0:T(8,128)}, f32[4,1024,128]{2,1,0:T(8,128)S(1)}, u32[]{:S(2)}, u32[]{:S(2)}) collective-permute-start(f32[4,1024,128]{2,1,0:T(8,128)} %get-tuple-element.22), channel_id=1, source_target_pairs={{0,8},{8,0},{1,9},{9,1},{2,10},{10,2},{3,11},{11,3},{4,12},{12,4},... | collective-permute-start | bytes 6291464 | tf_op jit(solution)/shard_map/ppermute | solution.py:274
  8.0 7.5 %collective-permute-start = (f32[1024,128]{1,0:T(8,128)S(1)}, f32[1024,128]{1,0:T(8,128)S(1)}, u32[]{:S(2)}, u32[]{:S(2)}) collective-permute-start(f32[1024,128]{1,0:T(8,128)S(1)} %get-tuple-element.16), channel_id=1, source_target_pairs={{0,8},{8,0},{1,9},{9,1},{2,10},{10,2},{3,11},{11,3},{4,12},{12,4},... | collective-permute-start | bytes 1572872 | tf_op jit(solution)/shard_map/ppermute | solution.py:274
  8.9 5.8 %copy-start.11 = (f32[128,128]{1,0:T(8,128)}, f32[128,128]{1,0:T(8,128)S(1)}, u32[]{:S(2)}) copy-start(f32[128,128]{1,0:T(8,128)S(1)} %fusion.g_ref) | copy-start | bytes 196612
  8.9 6.6 %collective-permute-start.1 = (f32[128,128]{1,0:T(8,128)S(1)}, f32[128,128]{1,0:T(8,128)S(1)}, u32[]{:S(2)}, u32[]{:S(2)}) collective-permute-start(f32[128,128]{1,0:T(8,128)S(1)} %fusion.g_ref), channel_id=1, source_target_pairs={{0,8},{8,0},{1,9},{9,1},{2,10},{10,2},{3,11},{11,3},{4,12},{12,4},... | collective-permute-start | bytes 196616 | tf_op jit(solution)/shard_map/ppermute | solution.py:274
  14.7 0.8 copy-start.4
  15.4 58.6 %copy-start.5 = (f32[128,128]{1,0:T(8,128)S(1)}, f32[128,128]{1,0:T(8,128)}, u32[]{:S(2)}) copy-start(f32[128,128]{1,0:T(8,128)} %refs_4_.1) | copy-start | bytes 196612
  15.5 0.6 copy-start.12
  15.5 0.8 copy-start.10
  18.5 8.7 %collective-permute-start.2 = (f32[8,36,128]{2,1,0:T(8,128)}, f32[8,36,128]{2,1,0:T(8,128)S(1)}, u32[]{:S(2)}, u32[]{:S(2)}) collective-permute-start(f32[8,36,128]{2,1,0:T(8,128)} %get-tuple-element.18), channel_id=1, source_target_pairs={{0,1},{1,0},{16,17},{17,16},{2,3},{3,2},{18,19},{19,18},{4,5},{5,4... | collective-permute-start | bytes 442376 | tf_op jit(solution)/shard_map/ppermute | solution.py:274
  20.7 9.7 %collective-permute-start.3 = (f32[8,36,128]{2,1,0:T(8,128)}, f32[8,36,128]{2,1,0:T(8,128)S(1)}, u32[]{:S(2)}, u32[]{:S(2)}) collective-permute-start(f32[8,36,128]{2,1,0:T(8,128)} %get-tuple-element.19), channel_id=1, source_target_pairs={{0,16},{1,17},{16,0},{17,1},{2,18},{3,19},{18,2},{19,3},{4,20},{5,... | collective-permute-start | bytes 442376 | tf_op jit(solution)/shard_map/ppermute | solution.py:274
  22.1 8.3 %collective-permute-start.4 = (f32[8,36,128]{2,1,0:T(8,128)}, f32[8,36,128]{2,1,0:T(8,128)S(1)}, u32[]{:S(2)}, u32[]{:S(2)}) collective-permute-start(f32[8,36,128]{2,1,0:T(8,128)} %get-tuple-element.20), channel_id=1, source_target_pairs={{0,17},{1,16},{16,1},{17,0},{2,19},{3,18},{18,3},{19,2},{4,21},{5,... | collective-permute-start | bytes 442376 | tf_op jit(solution)/shard_map/ppermute | solution.py:274
  63.9 7.1 %collective-permute-start.7 = (f32[8,36,128]{2,1,0:T(8,128)S(1)}, f32[8,36,128]{2,1,0:T(8,128)S(1)}, u32[]{:S(2)}, u32[]{:S(2)}) collective-permute-start(f32[8,36,128]{2,1,0:T(8,128)S(1)} %all_to_all.16.refs_0_), channel_id=1, source_target_pairs={{0,17},{1,16},{16,1},{17,0},{2,19},{3,18},{18,3},{19,2},{4,21},{5,... | collective-permute-start | bytes 442376 | tf_op jit(solution)/shard_map/ppermute | solution.py:274
  65.4 5.6 %collective-permute-start.6 = (f32[8,36,128]{2,1,0:T(8,128)S(1)}, f32[8,36,128]{2,1,0:T(8,128)S(1)}, u32[]{:S(2)}, u32[]{:S(2)}) collective-permute-start(f32[8,36,128]{2,1,0:T(8,128)S(1)} %all_to_all.16.refs_0_), channel_id=1, source_target_pairs={{0,16},{1,17},{16,0},{17,1},{2,18},{3,19},{18,2},{19,3},{4,20},{5,... | collective-permute-start | bytes 442376 | tf_op jit(solution)/shard_map/ppermute | solution.py:274
  67.2 6.8 %collective-permute-start.5 = (f32[8,36,128]{2,1,0:T(8,128)S(1)}, f32[8,36,128]{2,1,0:T(8,128)S(1)}, u32[]{:S(2)}, u32[]{:S(2)}) collective-permute-start(f32[8,36,128]{2,1,0:T(8,128)S(1)} %all_to_all.16.refs_0_), channel_id=1, source_target_pairs={{0,1},{1,0},{16,17},{17,16},{2,3},{3,2},{18,19},{19,18},{4,5},{5,4... | collective-permute-start | bytes 442376 | tf_op jit(solution)/shard_map/ppermute | solution.py:274
  74.0 1.6 %copy-start.2 = (f32[4,1024,128]{2,1,0:T(8,128)S(1)}, f32[4,1024,128]{2,1,0:T(8,128)}, u32[]{:S(2)}) copy-start(f32[4,1024,128]{2,1,0:T(8,128)} %get-tuple-element.21.refs_5_) | copy-start | bytes 6291460
  81.5 0.6 copy-start.8
  82.2 20.8 %copy-start.3 = (f32[1024,128]{1,0:T(8,128)}, f32[1024,128]{1,0:T(8,128)S(1)}, u32[]{:S(2)}) copy-start(f32[1024,128]{1,0:T(8,128)S(1)} %get-tuple-element.23) | copy-start | bytes 1572868
  82.2 1.3 %collective-permute-start.9 = (f32[136,128]{1,0:T(8,128)S(1)}, f32[136,128]{1,0:T(8,128)S(1)}, u32[]{:S(2)}, u32[]{:S(2)}) collective-permute-start(f32[136,128]{1,0:T(8,128)S(1)} %get-tuple-element.25), channel_id=1, source_target_pairs={{0,8},{8,0},{1,9},{9,1},{2,10},{10,2},{3,11},{11,3},{4,12},{12,4},... | collective-permute-start | bytes 208904 | tf_op jit(solution)/shard_map/ppermute | solution.py:274
  83.4 6.4 %collective-permute-start.12 = (f32[136,128]{1,0:T(8,128)S(1)}, f32[136,128]{1,0:T(8,128)S(1)}, u32[]{:S(2)}, u32[]{:S(2)}) collective-permute-start(f32[136,128]{1,0:T(8,128)S(1)} %add.28), channel_id=1, source_target_pairs={{0,6},{2,4},{4,2},{6,0},{1,7},{3,5},{5,3},{7,1},{8,14},{10,12},{12... | collective-permute-start | bytes 208904 | tf_op jit(solution)/shard_map/ppermute | solution.py:274
  86.5 6.2 %collective-permute-start.11 = (f32[136,128]{1,0:T(8,128)S(1)}, f32[136,128]{1,0:T(8,128)S(1)}, u32[]{:S(2)}, u32[]{:S(2)}) collective-permute-start(f32[136,128]{1,0:T(8,128)S(1)} %add.28), channel_id=1, source_target_pairs={{0,4},{2,6},{4,0},{6,2},{1,5},{3,7},{5,1},{7,3},{8,12},{10,14},{12... | collective-permute-start | bytes 208904 | tf_op jit(solution)/shard_map/ppermute | solution.py:274
  87.2 5.6 %collective-permute-start.10 = (f32[136,128]{1,0:T(8,128)S(1)}, f32[136,128]{1,0:T(8,128)S(1)}, u32[]{:S(2)}, u32[]{:S(2)}) collective-permute-start(f32[136,128]{1,0:T(8,128)S(1)} %add.28), channel_id=1, source_target_pairs={{0,2},{2,0},{4,6},{6,4},{1,3},{3,1},{5,7},{7,5},{8,10},{10,8},{12,... | collective-permute-start | bytes 208904 | tf_op jit(solution)/shard_map/ppermute | solution.py:274
  87.6 17.4 %collective-permute-start.13 = (f32[1024,128]{1,0:T(8,128)S(1)}, f32[1024,128]{1,0:T(8,128)S(1)}, u32[]{:S(2)}, u32[]{:S(2)}) collective-permute-start(f32[1024,128]{1,0:T(8,128)S(1)} %get-tuple-element.23), channel_id=1, source_target_pairs={{0,8},{8,0},{1,9},{9,1},{2,10},{10,2},{3,11},{11,3},{4,12},{12,4},... | collective-permute-start | bytes 1572872 | tf_op jit(solution)/shard_map/ppermute | solution.py:274
  94.0 11.0 %all-to-all-start.2 = ((f32[16,4,128]{2,1,0:T(4,128)}), f32[16,4,128]{2,1,0:T(4,128)S(1)}, u32[]{:S(2)}, u32[]{:S(2)}) async-start(f32[16,4,128]{2,1,0:T(4,128)} %broadcast_in_dim.2), calls=%async_computation.2 | async-start | bytes 65536 | tf_op jit(solution)/shard_map/all_to_all | solution.py:279
  103.0 5.2 %copy-start.13 = (f32[128,128]{1,0:T(8,128)S(1)}, f32[128,128]{1,0:T(8,128)}, u32[]{:S(2)}) copy-start(f32[128,128]{1,0:T(8,128)} %inverse_of_product.1) | copy-start | bytes 196612
  105.0 0.8 copy-start.9

commit v6 on v5

--- a/solution.py
+++ b/solution.py
@@ -55,19 +55,45 @@
     return a
 
 
-def inverse_kernel(first_ref, second_ref, out_ref):
-    out_ref[...] = spd_inverse(first_ref[...] * second_ref[...], 16)
-
-
-def inverse_of_product(first, second):
+def total(refs, rows):
+    first, second, third, fourth = (ref[rows] for ref in refs)
+    return (first + second) + (third + fourth)
+
+
+def collect_kernel(*refs):
+    out_ref = refs[-1]
+    count, rank = out_ref.shape[1:]
+    part = total(refs[:-1], pl.ds(rank, count))
+    out_ref[...] = jnp.broadcast_to(part[None], out_ref.shape)
+
+
+def collect(parts, copies, count):
+    rank = parts[0].shape[1]
+    return pl.pallas_call(
+        collect_kernel,
+        out_shape=jax.ShapeDtypeStruct((copies, count, rank), F32),
+        in_specs=[VMEM] * 4,
+        out_specs=VMEM,
+        compiler_params=pltpu.CompilerParams(vmem_limit_bytes=2 << 20),
+        name="collect",
+    )(*parts)
+
+
+def inverse_kernel(first_ref, *refs):
+    out_ref = refs[-1]
+    second = total(refs[:-1], pl.ds(0, first_ref.shape[0]))
+    out_ref[...] = spd_inverse(first_ref[...] * second, 16)
+
+
+def inverse_of_product(first, parts):
     return pl.pallas_call(
         inverse_kernel,
         out_shape=jax.ShapeDtypeStruct(first.shape, F32),
-        in_specs=[VMEM, VMEM],
+        in_specs=[VMEM] * 5,
         out_specs=VMEM,
-        cost_estimate=pl.CostEstimate(flops=5 * 10**9, transcendentals=128, bytes_accessed=3 * 2**16),
+        compiler_params=pltpu.CompilerParams(vmem_limit_bytes=4 << 20),
         name="inverse_of_product",
-    )(first, second)
+    )(first, *parts)
 
 
 def assemble_kernel(at_ref, mine_ref, other_ref, out_ref):
@@ -83,6 +109,7 @@
         out_shape=jax.ShapeDtypeStruct((2 * mine.shape[0],) + mine.shape[1:], F32),
         in_specs=[SMEM, VMEM, VMEM],
         out_specs=VMEM,
+        compiler_params=pltpu.CompilerParams(vmem_limit_bytes=8 << 20),
         name="assemble",
     )(at, mine, other)
 
@@ -94,9 +121,16 @@
     return high, middle, (rest - middle.astype(F32)).astype(BF16)
 
 
-def contract_kernel(chunk, at_ref, x_hbm, a_ref, c_ref, p_hbm, b_ref, x_ref, w_ref, p_ref, sems):
+def contract_kernel(chunk, at_ref, x_hbm, a_hbm, c_hbm, p_hbm, b_ref, *scratch):
+    x_ref, w_ref, p_ref, a_ref, c_ref, sems = scratch
     count, rows, rank = p_ref.shape
     span = 2 * count
+    factors = [
+        pltpu.make_async_copy(a_hbm, a_ref, sems.at[2 * rows // chunk]),
+        pltpu.make_async_copy(c_hbm, c_ref, sems.at[2 * rows // chunk + 1]),
+    ]
+    factors[0].start()
+    factors[1].start()
     copies = []
     for n, at in enumerate(range(0, rows, chunk)):
         size = chunk * span
@@ -106,6 +140,8 @@
         )
         copy.start()
         copies.append(copy)
+    factors[0].wait()
+    factors[1].wait()
     for n, part in enumerate(split3(a_ref[...])):
         w_ref[:, n * rank : (n + 1) * rank] = part
     for n, at in enumerate(range(0, rows, chunk)):
@@ -149,15 +185,17 @@
             pltpu.HBM((count, rows, rank), F32),
             jax.ShapeDtypeStruct((rows, rank), F32),
         ],
-        in_specs=[SMEM, HBM, VMEM, VMEM],
+        in_specs=[SMEM, HBM, HBM, HBM],
         out_specs=[HBM, VMEM],
         scratch_shapes=[
             pltpu.VMEM((rows * 2 * count, depth // 2), F32),
             pltpu.VMEM((depth, 3 * rank), BF16),
             pltpu.VMEM((count, rows, rank), F32),
-            pltpu.SemaphoreType.DMA((2 * rows // chunk,)),
+            pltpu.VMEM((depth, rank), F32),
+            pltpu.VMEM((count, rank), F32),
+            pltpu.SemaphoreType.DMA((2 * rows // chunk + 2,)),
         ],
-        compiler_params=pltpu.CompilerParams(vmem_limit_bytes=24 << 20),
+        compiler_params=pltpu.CompilerParams(vmem_limit_bytes=12 << 20),
         cost_estimate=pl.CostEstimate(
             flops=16 * count * rows * depth * rank,
             transcendentals=0,
@@ -192,6 +230,7 @@
         out_shape=[shape] * 4,
         in_specs=[SMEM] + [VMEM] * 4,
         out_specs=[VMEM] * 4,
+        compiler_params=pltpu.CompilerParams(vmem_limit_bytes=6 << 20),
         name="parcels",
     )(x, b, b_far, g, g_far)
 
@@ -206,6 +245,7 @@
         out_shape=jax.ShapeDtypeStruct(x.shape, F32),
         in_specs=[VMEM],
         out_specs=VMEM,
+        compiler_params=pltpu.CompilerParams(vmem_limit_bytes=2 << 20),
         name="spread",
     )(x)
 
@@ -264,7 +304,7 @@
             pltpu.VMEM((count, rows, rank), F32),
             pltpu.SemaphoreType.DMA((2,)),
         ],
-        compiler_params=pltpu.CompilerParams(vmem_limit_bytes=24 << 20),
+        compiler_params=pltpu.CompilerParams(vmem_limit_bytes=12 << 20),
         name="solve",
     )(x, *columns, gram_c, first, second)
 
@@ -272,11 +312,6 @@
 def swap(x, axis, bit=1):
     n = lax.axis_size(axis)
     return lax.ppermute(x, axis, [(i, i ^ bit) for i in range(n)])
-
-
-def gather(x, axes):
-    n = lax.axis_size(axes)
-    return lax.all_to_all(jnp.broadcast_to(x[None], (n,) + x.shape), axes, 0, 0)
 
 
 def body(tensor, factor_a, factor_c, gram_c):
@@ -289,10 +324,12 @@
     lanes = mode_one // 2
     flat = tensor.reshape(mode_two, mode_three, 2, lanes).transpose(0, 2, 1, 3)
     flat = flat.reshape(mode_two * mode_three * 2, lanes)
-    flat = pltpu.with_memory_space_constraint(flat, pltpu.HBM)
-
-    p_other, b_other = contract(jnp.stack([1 - core, x]), flat, factor_a, factor_c, half)
-    p_mine, b_mine = contract(jnp.stack([core, x]), flat, factor_a, factor_c, half)
+    flat, a_hbm, c_hbm = (
+        pltpu.with_memory_space_constraint(v, pltpu.HBM) for v in (flat, factor_a, factor_c)
+    )
+
+    p_other, b_other = contract(jnp.stack([1 - core, x]), flat, a_hbm, c_hbm, half)
+    p_mine, b_mine = contract(jnp.stack([core, x]), flat, a_hbm, c_hbm, half)
     gram_part = dot(factor_a.T, factor_a)
     at = x.reshape(1)
     sent = parcels(at, b_mine, swap(b_other, "c"), gram_part, swap(gram_part, "c"), depth)
@@ -304,16 +341,16 @@
     gram_a, f_mine, sums = solve(at, columns, gram_c, p_mine, swap(p_other, "c"))
 
     sums = sums + swap(sums, "c")
-    away = [swap(sums, "y", bit) for bit in (1, 2, 3)]
-    sums = (sums + away[0]) + (away[1] + away[2])
-    gram_b, local_c = sums[:rank], sums[rank : rank + mode_three]
-    mttkrp_c = jnp.sum(gather(local_c, ("z", "xl")), axis=0)
-    last, f_other = lax.optimization_barrier(
-        (inverse_of_product(gram_a, gram_b), swap(f_mine, "c"))
-    )
+    parts = [sums] + [swap(sums, "y", bit) for bit in (1, 2, 3)]
+    plane = ("z", "xl")
+    spread_c = collect(parts, lax.axis_size(plane), mode_three)
+    spread_c, f_mine = lax.optimization_barrier((spread_c, f_mine))
+    mttkrp_c = jnp.sum(lax.all_to_all(spread_c, plane, 0, 0), axis=0)
+    f_other = swap(f_mine, "c")
     shape = (4, half // 4, rank)
     factor_b = assemble(jnp.stack([core, x]), f_mine.reshape(shape), f_other.reshape(shape))
-    factor_c_new = dot(mttkrp_c, last)
+    gram_a, factor_b = lax.optimization_barrier((gram_a, factor_b))
+    factor_c_new = dot(mttkrp_c, inverse_of_product(gram_a, parts))
     return (factor_b.reshape(mode_two, rank), factor_c_new)
 
 

time: 109 us -> 100 us (0.917)
  blocking collectives: 30.9 us -> 40.5 us
  local copies, waits for them, and re-layouts: 7.51 us -> 0.01 us
  Pallas kernels: 28.5 us -> 23 us
  starting transfers between devices: 16 us -> 12.8 us
  waiting for transfers between devices: 22.8 us -> 20.6 us
    all_to_all x0 -> x1, blocking collectives: none -> 10.6 us  [body(): mttkrp_c = jnp.sum(lax.all_to_all(spread_c, plane, 0, 0), axis=0)]
    unnamed x28 -> x6, local copies, waits for them, and re-layouts: 6.26 us -> 0.01 us
    all_to_all x1 -> x0, starting transfers between devices: 3.49 us -> none  [gather(): return lax.all_to_all(jnp.broadcast_to(x[None], (n,) + x.shape), axes, 0, 0)]
    pallas_call x1, Pallas kernels: 2.24 us -> 0.18 us  [parcels(): pl.pallas_call(parcels_kernel, out_shape=[shape] * 4, in_specs=[SMEM] + [...]
    all_to_all x1 -> x0, waiting for transfers between devices: 2.06 us -> none  [gather(): return lax.all_to_all(jnp.broadcast_to(x[None], (n,) + x.shape), axes, 0, 0)]
    pallas_call x1, Pallas kernels: 1.6 us -> 0.02 us  [spread(): pl.pallas_call(spread_kernel, out_shape=jax.ShapeDtypeStruct(x.shape, F32...]
    pallas_call x1, Pallas kernels: 5.42 us -> 3.93 us  [inverse_of_product(): pl.pallas_call(inverse_kernel, out_shape=jax.ShapeDtypeStruct(first.shape...]
  transfers between devices with their start and end apart: 15 -> 14, of which waited for: 8 -> 7; matrix products, arithmetic and copies ran while one was open for 2% -> 1% of each run, Pallas kernels for 14% -> 6%
where the time goes in v6:
time: 100 us; the launch traced here: 99 us
  blocking collectives  40.5 us (40%)
  Pallas kernels  23 us (23%)
  waiting for transfers between devices  20.6 us (21%)
  starting transfers between devices  12.8 us (13%)
  matrix products  1.13 us (1%)
    ppermute x14, waiting for transfers between devices, swap(): return lax.ppermute(x, axis, [(i, i ^ bit) for i in range(n)])  20.6 us
    all_to_all x1, blocking collectives, body(): column = spread(lax.all_to_all(column, 'z', 0, 0))  18.1 us
    ppermute x14, starting transfers between devices, swap(): return lax.ppermute(x, axis, [(i, i ^ bit) for i in range(n)])  12.8 us
    all_to_all x1, blocking collectives, body(): column = lax.all_to_all(column, 'z', 0, 0)  11.8 us
    pallas_call x2, Pallas kernels, contract(): pl.pallas_call(functools.partial(contract_kernel, chunk), out_shape=[pltp...  11.3 us
    all_to_all x1, blocking collectives, body(): mttkrp_c = jnp.sum(lax.all_to_all(spread_c, plane, 0, 0), axis=0)  10.6 us
    pallas_call x1, Pallas kernels, solve(): pl.pallas_call(solve_kernel, out_shape=[square, jax.ShapeDtypeStruct((row...  6.01 us
    pallas_call x1, Pallas kernels, inverse_of_product(): pl.pallas_call(inverse_kernel, out_shape=jax.ShapeDtypeStruct(first.shape...  3.93 us
  transfers between devices with their start and end apart: 14, of which 7 were waited for; matrix products, arithmetic and copies ran while one was open for 1% of the time, Pallas kernels for 6%

profile of v6, /device:TPU:2, one launch (start us, length us, event | category | flops | bytes accessed | tf_op | source)
XLA Modules:
  0.0 99.0 jit_solution(9316499806441268126)
XLA Ops:
  0.6 0.1 pad_add_fusion.1.at_ref
  0.7 0.0 copy-start.2
  0.7 5.6 %contract.3 = (f32[4,1024,128]{2,1,0:T(8,128)}, f32[1024,128]{1,0:T(8,128)S(1)}) custom-call(s32[2]{0:T(128)S(1)} %pad_add_fusion.1.at_ref, f32[16384,128]{1,0:T(8,128)} %bitcast.17, f32[256,128]{1,0:T(8,128)} %a_hbm.3, f32[4,128]{1,0:T(4,128)} %c_hbm.3), custom_call_target="tpu_custom_call" | custom-call | flops 2147483648 | bytes 6291456 | tf_op jit(solution)/shard_map/contract/pallas_call | solution.py:182
  6.4 0.1 collective-permute-start.8
  6.5 0.5 collective-permute-start
  7.0 0.0 copy-done.2
  7.0 0.4 fusion.g_ref
  7.4 0.2 collective-permute-start.1
  7.5 0.1 pad_add_fusion.at_ref
  7.6 5.7 %contract.2 = (f32[4,1024,128]{2,1,0:T(8,128)}, f32[1024,128]{1,0:T(8,128)S(1)}) custom-call(s32[2]{0:T(128)S(1)} %pad_add_fusion.at_ref, f32[16384,128]{1,0:T(8,128)} %bitcast.18, f32[256,128]{1,0:T(8,128)} %a_hbm.3, f32[4,128]{1,0:T(4,128)} %c_hbm.3), custom_call_target="tpu_custom_call" | custom-call | flops 2147483648 | bytes 6291456 | tf_op jit(solution)/shard_map/contract/pallas_call | solution.py:182
  13.3 0.0 copy-start
  13.3 0.0 copy-start.1
  13.3 0.0 collective-permute-done.1.g_far_ref
  13.3 0.0 collective-permute-done.b_far_ref
  13.3 0.2 parcels.1
  13.5 2.2 %collective-permute-start.2 = (f32[8,36,128]{2,1,0:T(8,128)S(1)}, f32[8,36,128]{2,1,0:T(8,128)S(1)}, u32[]{:S(2)}, u32[]{:S(2)}) collective-permute-start(f32[8,36,128]{2,1,0:T(8,128)S(1)} %get-tuple-element.20), channel_id=1, source_target_pairs={{0,1},{1,0},{16,17},{17,16},{2,3},{3,2},{18,19},{19,18},{4,5},{5,4... | collective-permute-start | bytes 442376 | tf_op jit(solution)/shard_map/ppermute | solution.py:314
  15.7 1.4 %collective-permute-start.3 = (f32[8,36,128]{2,1,0:T(8,128)S(1)}, f32[8,36,128]{2,1,0:T(8,128)S(1)}, u32[]{:S(2)}, u32[]{:S(2)}) collective-permute-start(f32[8,36,128]{2,1,0:T(8,128)S(1)} %get-tuple-element.21), channel_id=1, source_target_pairs={{0,16},{1,17},{16,0},{17,1},{2,18},{3,19},{18,2},{19,3},{4,20},{5,... | collective-permute-start | bytes 442376 | tf_op jit(solution)/shard_map/ppermute | solution.py:314
  17.2 0.5 collective-permute-start.4
  17.7 4.4 %collective-permute-done.2 = f32[8,36,128]{2,1,0:T(8,128)S(1)} collective-permute-done((f32[8,36,128]{2,1,0:T(8,128)S(1)}, f32[8,36,128]{2,1,0:T(8,128)S(1)}, u32[]{:S(2)}, u32[]{:S(2)}) %collective-permute-start.2) | collective-permute-done | bytes 147488 | tf_op jit(solution)/shard_map/ppermute | solution.py:314
  22.1 3.1 %collective-permute-done.3 = f32[8,36,128]{2,1,0:T(8,128)S(1)} collective-permute-done((f32[8,36,128]{2,1,0:T(8,128)S(1)}, f32[8,36,128]{2,1,0:T(8,128)S(1)}, u32[]{:S(2)}, u32[]{:S(2)}) %collective-permute-start.3) | collective-permute-done | bytes 147488 | tf_op jit(solution)/shard_map/ppermute | solution.py:314
  25.2 0.0 collective-permute-done.4
  25.3 18.1 %all_to_all.15.x_ref = f32[8,36,128]{2,1,0:T(8,128)S(1)} all-to-all(f32[8,36,128]{2,1,0:T(8,128)S(1)} %add_add_fusion), channel_id=1, replica_groups=mesh['z'=8,'xl'=2,'c'=2,'y'=4,'xh'=2] {'z'}, dimensions={0} | all-to-all | bytes 294912 | tf_op jit(solution)/shard_map/all_to_all | solution.py:338
  43.4 11.8 %all_to_all.16.refs_0_ = f32[8,36,128]{2,1,0:T(8,128)S(1)} all-to-all(f32[8,36,128]{2,1,0:T(8,128)S(1)} %spread.1), channel_id=1, replica_groups=mesh['z'=8,'xl'=2,'c'=2,'y'=4,'xh'=2] {'z'}, dimensions={0} | all-to-all | bytes 294912 | tf_op jit(solution)/shard_map/all_to_all | solution.py:339
  55.2 1.5 %collective-permute-start.7 = (f32[8,36,128]{2,1,0:T(8,128)S(1)}, f32[8,36,128]{2,1,0:T(8,128)S(1)}, u32[]{:S(2)}, u32[]{:S(2)}) collective-permute-start(f32[8,36,128]{2,1,0:T(8,128)S(1)} %all_to_all.16.refs_0_), channel_id=1, source_target_pairs={{0,17},{1,16},{16,1},{17,0},{2,19},{3,18},{18,3},{19,2},{4,21},{5,... | collective-permute-start | bytes 442376 | tf_op jit(solution)/shard_map/ppermute | solution.py:314
  56.7 1.8 %collective-permute-start.6 = (f32[8,36,128]{2,1,0:T(8,128)S(1)}, f32[8,36,128]{2,1,0:T(8,128)S(1)}, u32[]{:S(2)}, u32[]{:S(2)}) collective-permute-start(f32[8,36,128]{2,1,0:T(8,128)S(1)} %all_to_all.16.refs_0_), channel_id=1, source_target_pairs={{0,16},{1,17},{16,0},{17,1},{2,18},{3,19},{18,2},{19,3},{4,20},{5,... | collective-permute-start | bytes 442376 | tf_op jit(solution)/shard_map/ppermute | solution.py:314
  58.6 0.2 collective-permute-start.5
  58.7 3.6 %collective-permute-done.7.refs_3_ = f32[8,36,128]{2,1,0:T(8,128)S(1)} collective-permute-done((f32[8,36,128]{2,1,0:T(8,128)S(1)}, f32[8,36,128]{2,1,0:T(8,128)S(1)}, u32[]{:S(2)}, u32[]{:S(2)}) %collective-permute-start.7) | collective-permute-done | bytes 147488 | tf_op jit(solution)/shard_map/ppermute | solution.py:314
  62.3 0.0 collective-permute-done.6.refs_2_
  62.3 3.1 %collective-permute-done.5.refs_1_ = f32[8,36,128]{2,1,0:T(8,128)S(1)} collective-permute-done((f32[8,36,128]{2,1,0:T(8,128)S(1)}, f32[8,36,128]{2,1,0:T(8,128)S(1)}, u32[]{:S(2)}, u32[]{:S(2)}) %collective-permute-start.5) | collective-permute-done | bytes 147488 | tf_op jit(solution)/shard_map/ppermute | solution.py:314
  65.4 0.0 collective-permute-done.8.refs_6_
  65.4 0.0 copy-done
  65.4 0.0 copy-done.1
  65.4 6.0 %solve.1 = (f32[128,128]{1,0:T(8,128)S(1)}, f32[1024,128]{1,0:T(8,128)S(1)}, f32[136,128]{1,0:T(8,128)S(1)}) custom-call(s32[1]{0:T(128)} %bitcast.x_ref, f32[8,36,128]{2,1,0:T(8,128)S(1)} %all_to_all.16.refs_0_, f32[8,36,128]{2,1,0:T(8,128)S(1)} %collective-permute-done.5.refs_1_, f32[8,36,128]{2,1,0:T(8,128)S(1)} %collective-permute-done.6.refs_2_, ...), custom_call_target="tpu_custom_call" | custom-call | tf_op jit(solution)/shard_map/solve/pallas_call | solution.py:293
  71.4 0.1 collective-permute-start.9
  71.5 1.2 %collective-permute-done.9 = f32[136,128]{1,0:T(8,128)S(1)} collective-permute-done((f32[136,128]{1,0:T(8,128)S(1)}, f32[136,128]{1,0:T(8,128)S(1)}, u32[]{:S(2)}, u32[]{:S(2)}) %collective-permute-start.9) | collective-permute-done | bytes 69664 | tf_op jit(solution)/shard_map/ppermute | solution.py:314
  72.8 3.1 %collective-permute-start.12 = (f32[136,128]{1,0:T(8,128)S(1)}, f32[136,128]{1,0:T(8,128)S(1)}, u32[]{:S(2)}, u32[]{:S(2)}) collective-permute-start(f32[136,128]{1,0:T(8,128)S(1)} %add.19.refs_0_), channel_id=1, source_target_pairs={{0,6},{2,4},{4,2},{6,0},{1,7},{3,5},{5,3},{7,1},{8,14},{10,12},{12... | collective-permute-start | bytes 208904 | tf_op jit(solution)/shard_map/ppermute | solution.py:314
  75.9 0.6 collective-permute-start.11
  76.5 0.5 collective-permute-start.10
  76.9 2.2 %collective-permute-done.12.refs_3_ = f32[136,128]{1,0:T(8,128)S(1)} collective-permute-done((f32[136,128]{1,0:T(8,128)S(1)}, f32[136,128]{1,0:T(8,128)S(1)}, u32[]{:S(2)}, u32[]{:S(2)}) %collective-permute-start.12) | collective-permute-done | bytes 69664 | tf_op jit(solution)/shard_map/ppermute | solution.py:314
  79.2 2.9 %collective-permute-done.11.refs_2_ = f32[136,128]{1,0:T(8,128)S(1)} collective-permute-done((f32[136,128]{1,0:T(8,128)S(1)}, f32[136,128]{1,0:T(8,128)S(1)}, u32[]{:S(2)}, u32[]{:S(2)}) %collective-permute-start.11) | collective-permute-done | bytes 69664 | tf_op jit(solution)/shard_map/ppermute | solution.py:314
  82.1 0.0 collective-permute-done.10.refs_1_
  82.1 0.1 collective-permute-start.13
  82.2 10.6 %all_to_all.17 = f32[16,4,128]{2,1,0:T(4,128)S(1)} all-to-all(f32[16,4,128]{2,1,0:T(4,128)S(1)} %collect.1), channel_id=1, replica_groups=mesh['z'=8,'xl'=2,'c'=2,'y'=4,'xh'=2] {'z','xl'}, dimensions={0} | all-to-all | bytes 65536 | tf_op jit(solution)/shard_map/all_to_all | solution.py:348
  92.8 0.0 collective-permute-done.13
  92.8 1.6 %assemble.1 = f32[8,256,128]{2,1,0:T(8,128)} custom-call(s32[2]{0:T(128)S(1)} %pad_add_fusion.at_ref, f32[4,256,128]{2,1,0:T(8,128)S(1)} %bitcast.15, f32[4,256,128]{2,1,0:T(8,128)S(1)} %bitcast.16), custom_call_target="tpu_custom_call" | custom-call | tf_op jit(solution)/shard_map/assemble/pallas_call | solution.py:107
  94.4 3.9 %inverse_of_product.1 = f32[128,128]{1,0:T(8,128)S(1)} custom-call(f32[128,128]{1,0:T(8,128)S(1)} %get-tuple-element.31.first_ref, f32[136,128]{1,0:T(8,128)S(1)} %add.19.refs_0_, f32[136,128]{1,0:T(8,128)S(1)} %collective-permute-done.10.refs_1_, f32[136,128]{1,0:T(8,128)S(1)} %collective-permute-done.11.refs_2_, f32[136,128]{1,0:T(8,128)S(1)} %collective-permute-done.12.refs_3_), custom_call_target="tpu_custom_call" | custom-call | tf_op jit(solution)/shard_map/inverse_of_product/pallas_call | solution.py:89
  98.3 0.7 fusion.1
  (5 shorter events, 0.1 us)
Async XLA Ops:
  0.7 6.3 %copy-start.2 = (f32[256,128]{1,0:T(8,128)S(1)}, f32[256,128]{1,0:T(8,128)}, u32[]{:S(2)}) copy-start(f32[256,128]{1,0:T(8,128)} %a_hbm.3) | copy-start | bytes 393220
  6.4 59.0 %collective-permute-start.8 = (f32[4,1024,128]{2,1,0:T(8,128)}, f32[4,1024,128]{2,1,0:T(8,128)S(1)}, u32[]{:S(2)}, u32[]{:S(2)}) collective-permute-start(f32[4,1024,128]{2,1,0:T(8,128)} %get-tuple-element.24), channel_id=1, source_target_pairs={{0,8},{8,0},{1,9},{9,1},{2,10},{10,2},{3,11},{11,3},{4,12},{12,4},... | collective-permute-start | bytes 6291464 | tf_op jit(solution)/shard_map/ppermute | solution.py:314
  6.5 6.8 %collective-permute-start = (f32[1024,128]{1,0:T(8,128)S(1)}, f32[1024,128]{1,0:T(8,128)S(1)}, u32[]{:S(2)}, u32[]{:S(2)}) collective-permute-start(f32[1024,128]{1,0:T(8,128)S(1)} %get-tuple-element.18), channel_id=1, source_target_pairs={{0,8},{8,0},{1,9},{9,1},{2,10},{10,2},{3,11},{11,3},{4,12},{12,4},... | collective-permute-start | bytes 1572872 | tf_op jit(solution)/shard_map/ppermute | solution.py:314
  7.4 6.0 %collective-permute-start.1 = (f32[128,128]{1,0:T(8,128)S(1)}, f32[128,128]{1,0:T(8,128)S(1)}, u32[]{:S(2)}, u32[]{:S(2)}) collective-permute-start(f32[128,128]{1,0:T(8,128)S(1)} %fusion.g_ref), channel_id=1, source_target_pairs={{0,8},{8,0},{1,9},{9,1},{2,10},{10,2},{3,11},{11,3},{4,12},{12,4},... | collective-permute-start | bytes 196616 | tf_op jit(solution)/shard_map/ppermute | solution.py:314
  13.3 52.1 %copy-start = (f32[4,1024,128]{2,1,0:T(8,128)S(1)}, f32[4,1024,128]{2,1,0:T(8,128)}, u32[]{:S(2)}) copy-start(f32[4,1024,128]{2,1,0:T(8,128)} %get-tuple-element.23.refs_5_) | copy-start | bytes 6291460
  13.3 52.1 %copy-start.1 = (f32[128,128]{1,0:T(8,128)S(1)}, f32[128,128]{1,0:T(8,128)}, u32[]{:S(2)}) copy-start(f32[128,128]{1,0:T(8,128)} %refs_4_.1) | copy-start | bytes 196612
  13.5 8.6 %collective-permute-start.2 = (f32[8,36,128]{2,1,0:T(8,128)S(1)}, f32[8,36,128]{2,1,0:T(8,128)S(1)}, u32[]{:S(2)}, u32[]{:S(2)}) collective-permute-start(f32[8,36,128]{2,1,0:T(8,128)S(1)} %get-tuple-element.20), channel_id=1, source_target_pairs={{0,1},{1,0},{16,17},{17,16},{2,3},{3,2},{18,19},{19,18},{4,5},{5,4... | collective-permute-start | bytes 442376 | tf_op jit(solution)/shard_map/ppermute | solution.py:314
  15.7 9.5 %collective-permute-start.3 = (f32[8,36,128]{2,1,0:T(8,128)S(1)}, f32[8,36,128]{2,1,0:T(8,128)S(1)}, u32[]{:S(2)}, u32[]{:S(2)}) collective-permute-start(f32[8,36,128]{2,1,0:T(8,128)S(1)} %get-tuple-element.21), channel_id=1, source_target_pairs={{0,16},{1,17},{16,0},{17,1},{2,18},{3,19},{18,2},{19,3},{4,20},{5,... | collective-permute-start | bytes 442376 | tf_op jit(solution)/shard_map/ppermute | solution.py:314
  17.2 8.1 %collective-permute-start.4 = (f32[8,36,128]{2,1,0:T(8,128)S(1)}, f32[8,36,128]{2,1,0:T(8,128)S(1)}, u32[]{:S(2)}, u32[]{:S(2)}) collective-permute-start(f32[8,36,128]{2,1,0:T(8,128)S(1)} %get-tuple-element.22), channel_id=1, source_target_pairs={{0,17},{1,16},{16,1},{17,0},{2,19},{3,18},{18,3},{19,2},{4,21},{5,... | collective-permute-start | bytes 442376 | tf_op jit(solution)/shard_map/ppermute | solution.py:314
  55.2 7.1 %collective-permute-start.7 = (f32[8,36,128]{2,1,0:T(8,128)S(1)}, f32[8,36,128]{2,1,0:T(8,128)S(1)}, u32[]{:S(2)}, u32[]{:S(2)}) collective-permute-start(f32[8,36,128]{2,1,0:T(8,128)S(1)} %all_to_all.16.refs_0_), channel_id=1, source_target_pairs={{0,17},{1,16},{16,1},{17,0},{2,19},{3,18},{18,3},{19,2},{4,21},{5,... | collective-permute-start | bytes 442376 | tf_op jit(solution)/shard_map/ppermute | solution.py:314
  56.7 5.6 %collective-permute-start.6 = (f32[8,36,128]{2,1,0:T(8,128)S(1)}, f32[8,36,128]{2,1,0:T(8,128)S(1)}, u32[]{:S(2)}, u32[]{:S(2)}) collective-permute-start(f32[8,36,128]{2,1,0:T(8,128)S(1)} %all_to_all.16.refs_0_), channel_id=1, source_target_pairs={{0,16},{1,17},{16,0},{17,1},{2,18},{3,19},{18,2},{19,3},{4,20},{5,... | collective-permute-start | bytes 442376 | tf_op jit(solution)/shard_map/ppermute | solution.py:314
  58.6 6.8 %collective-permute-start.5 = (f32[8,36,128]{2,1,0:T(8,128)S(1)}, f32[8,36,128]{2,1,0:T(8,128)S(1)}, u32[]{:S(2)}, u32[]{:S(2)}) collective-permute-start(f32[8,36,128]{2,1,0:T(8,128)S(1)} %all_to_all.16.refs_0_), channel_id=1, source_target_pairs={{0,1},{1,0},{16,17},{17,16},{2,3},{3,2},{18,19},{19,18},{4,5},{5,4... | collective-permute-start | bytes 442376 | tf_op jit(solution)/shard_map/ppermute | solution.py:314
  71.4 1.3 %collective-permute-start.9 = (f32[136,128]{1,0:T(8,128)S(1)}, f32[136,128]{1,0:T(8,128)S(1)}, u32[]{:S(2)}, u32[]{:S(2)}) collective-permute-start(f32[136,128]{1,0:T(8,128)S(1)} %get-tuple-element.26), channel_id=1, source_target_pairs={{0,8},{8,0},{1,9},{9,1},{2,10},{10,2},{3,11},{11,3},{4,12},{12,4},... | collective-permute-start | bytes 208904 | tf_op jit(solution)/shard_map/ppermute | solution.py:314
  72.8 6.4 %collective-permute-start.12 = (f32[136,128]{1,0:T(8,128)S(1)}, f32[136,128]{1,0:T(8,128)S(1)}, u32[]{:S(2)}, u32[]{:S(2)}) collective-permute-start(f32[136,128]{1,0:T(8,128)S(1)} %add.19.refs_0_), channel_id=1, source_target_pairs={{0,6},{2,4},{4,2},{6,0},{1,7},{3,5},{5,3},{7,1},{8,14},{10,12},{12... | collective-permute-start | bytes 208904 | tf_op jit(solution)/shard_map/ppermute | solution.py:314
  75.9 6.2 %collective-permute-start.11 = (f32[136,128]{1,0:T(8,128)S(1)}, f32[136,128]{1,0:T(8,128)S(1)}, u32[]{:S(2)}, u32[]{:S(2)}) collective-permute-start(f32[136,128]{1,0:T(8,128)S(1)} %add.19.refs_0_), channel_id=1, source_target_pairs={{0,4},{2,6},{4,0},{6,2},{1,5},{3,7},{5,1},{7,3},{8,12},{10,14},{12... | collective-permute-start | bytes 208904 | tf_op jit(solution)/shard_map/ppermute | solution.py:314
  76.5 5.6 %collective-permute-start.10 = (f32[136,128]{1,0:T(8,128)S(1)}, f32[136,128]{1,0:T(8,128)S(1)}, u32[]{:S(2)}, u32[]{:S(2)}) collective-permute-start(f32[136,128]{1,0:T(8,128)S(1)} %add.19.refs_0_), channel_id=1, source_target_pairs={{0,2},{2,0},{4,6},{6,4},{1,3},{3,1},{5,7},{7,5},{8,10},{10,8},{12,... | collective-permute-start | bytes 208904 | tf_op jit(solution)/shard_map/ppermute | solution.py:314
  82.1 10.7 %collective-permute-start.13 = (f32[1024,128]{1,0:T(8,128)S(1)}, f32[1024,128]{1,0:T(8,128)S(1)}, u32[]{:S(2)}, u32[]{:S(2)}) collective-permute-start(f32[1024,128]{1,0:T(8,128)S(1)} %get-tuple-element.28), channel_id=1, source_target_pairs={{0,8},{8,0},{1,9},{9,1},{2,10},{10,2},{3,11},{11,3},{4,12},{12,4},... | collective-permute-start | bytes 1572872 | tf_op jit(solution)/shard_map/ppermute | solution.py:314

commit v7 on v6

--- a/solution.py
+++ b/solution.py
@@ -92,6 +92,7 @@
         in_specs=[VMEM] * 5,
         out_specs=VMEM,
         compiler_params=pltpu.CompilerParams(vmem_limit_bytes=4 << 20),
+        cost_estimate=pl.CostEstimate(flops=3 * 10**9, transcendentals=128, bytes_accessed=2**19),
         name="inverse_of_product",
     )(first, *parts)
 
@@ -341,15 +342,15 @@
     gram_a, f_mine, sums = solve(at, columns, gram_c, p_mine, swap(p_other, "c"))
 
     sums = sums + swap(sums, "c")
+    sums, f_mine = lax.optimization_barrier((sums, f_mine))
     parts = [sums] + [swap(sums, "y", bit) for bit in (1, 2, 3)]
+    shape = (4, half // 4, rank)
+    f_other = swap(f_mine, "c").reshape(shape)
+    factor_b = assemble(jnp.stack([core, x]), f_mine.reshape(shape), f_other)
+    parts[0], factor_b = lax.optimization_barrier((parts[0], factor_b))
     plane = ("z", "xl")
     spread_c = collect(parts, lax.axis_size(plane), mode_three)
-    spread_c, f_mine = lax.optimization_barrier((spread_c, f_mine))
     mttkrp_c = jnp.sum(lax.all_to_all(spread_c, plane, 0, 0), axis=0)
-    f_other = swap(f_mine, "c")
-    shape = (4, half // 4, rank)
-    factor_b = assemble(jnp.stack([core, x]), f_mine.reshape(shape), f_other.reshape(shape))
-    gram_a, factor_b = lax.optimization_barrier((gram_a, factor_b))
     factor_c_new = dot(mttkrp_c, inverse_of_product(gram_a, parts))
     return (factor_b.reshape(mode_two, rank), factor_c_new)
 

time: 100 us -> 95 us (0.950)
  blocking collectives: 40.5 us -> 30 us
  starting transfers between devices: 12.8 us -> 16.3 us
  waiting for transfers between devices: 20.6 us -> 22.7 us
    all_to_all x1 -> x0, blocking collectives: 10.6 us -> none  [body(): mttkrp_c = jnp.sum(lax.all_to_all(spread_c, plane, 0, 0), axis=0)]
    all_to_all x0 -> x1, waiting for transfers between devices: none -> 3.55 us  [body(): mttkrp_c = jnp.sum(lax.all_to_all(spread_c, plane, 0, 0), axis=0)]
    all_to_all x0 -> x1, starting transfers between devices: none -> 3.46 us  [body(): mttkrp_c = jnp.sum(lax.all_to_all(spread_c, plane, 0, 0), axis=0)]
    ppermute x14, waiting for transfers between devices: 20.6 us -> 19.2 us  [swap(): return lax.ppermute(x, axis, [(i, i ^ bit) for i in range(n)])]
  transfers between devices with their start and end apart: 14 -> 15, of which waited for: 7 -> 8; matrix products, arithmetic and copies ran while one was open for 1% -> 0% of each run, Pallas kernels for 6% -> 12%
where the time goes in v7:
time: 95 us; the launch traced here: 94.7 us
  blocking collectives  30 us (32%)
  Pallas kernels  23.6 us (25%)
  waiting for transfers between devices  22.7 us (24%)
  starting transfers between devices  16.3 us (17%)
  matrix products  1.13 us (1%)
    ppermute x14, waiting for transfers between devices, swap(): return lax.ppermute(x, axis, [(i, i ^ bit) for i in range(n)])  19.2 us
    all_to_all x1, blocking collectives, body(): column = spread(lax.all_to_all(column, 'z', 0, 0))  18.1 us
    ppermute x14, starting transfers between devices, swap(): return lax.ppermute(x, axis, [(i, i ^ bit) for i in range(n)])  12.9 us
    all_to_all x1, blocking collectives, body(): column = lax.all_to_all(column, 'z', 0, 0)  11.8 us
    pallas_call x2, Pallas kernels, contract(): pl.pallas_call(functools.partial(contract_kernel, chunk), out_shape=[pltp...  11.3 us
    pallas_call x1, Pallas kernels, solve(): pl.pallas_call(solve_kernel, out_shape=[square, jax.ShapeDtypeStruct((row...  6 us
    pallas_call x1, Pallas kernels, inverse_of_product(): pl.pallas_call(inverse_kernel, out_shape=jax.ShapeDtypeStruct(first.shape...  3.93 us
    all_to_all x1, waiting for transfers between devices, body(): mttkrp_c = jnp.sum(lax.all_to_all(spread_c, plane, 0, 0), axis=0)  3.55 us
  transfers between devices with their start and end apart: 15, of which 8 were waited for; matrix products, arithmetic and copies ran while one was open for 0% of the time, Pallas kernels for 12%

profile of v7, /device:TPU:2, one launch (start us, length us, event | category | flops | bytes accessed | tf_op | source)
XLA Modules:
  0.0 94.7 jit_solution(10342174778454354524)
XLA Ops:
  0.6 0.1 pad_add_fusion
  0.7 0.0 copy-start.2
  0.7 5.7 %contract.3 = (f32[4,1024,128]{2,1,0:T(8,128)}, f32[1024,128]{1,0:T(8,128)S(1)}) custom-call(s32[2]{0:T(128)S(1)} %get-tuple-element.33.at_ref, f32[16384,128]{1,0:T(8,128)} %bitcast.17, f32[256,128]{1,0:T(8,128)} %a_hbm.3, f32[4,128]{1,0:T(4,128)} %c_hbm.3), custom_call_target="tpu_custom_call" | custom-call | flops 2147483648 | bytes 6291456 | tf_op jit(solution)/shard_map/contract/pallas_call | solution.py:183
  6.4 0.1 collective-permute-start.8
  6.5 0.5 collective-permute-start
  7.0 0.0 copy-done.2
  7.0 0.4 fusion.g_ref
  7.4 0.2 collective-permute-start.1
  7.6 5.6 %contract.2 = (f32[4,1024,128]{2,1,0:T(8,128)}, f32[1024,128]{1,0:T(8,128)S(1)}) custom-call(s32[2]{0:T(128)S(1)} %get-tuple-element.32.at_ref, f32[16384,128]{1,0:T(8,128)} %bitcast.18, f32[256,128]{1,0:T(8,128)} %a_hbm.3, f32[4,128]{1,0:T(4,128)} %c_hbm.3), custom_call_target="tpu_custom_call" | custom-call | flops 2147483648 | bytes 6291456 | tf_op jit(solution)/shard_map/contract/pallas_call | solution.py:183
  13.2 0.0 copy-start
  13.2 0.0 copy-start.1
  13.2 0.0 collective-permute-done.1.g_far_ref
  13.2 0.0 collective-permute-done.b_far_ref
  13.2 0.2 parcels.1
  13.4 2.2 %collective-permute-start.2 = (f32[8,36,128]{2,1,0:T(8,128)S(1)}, f32[8,36,128]{2,1,0:T(8,128)S(1)}, u32[]{:S(2)}, u32[]{:S(2)}) collective-permute-start(f32[8,36,128]{2,1,0:T(8,128)S(1)} %get-tuple-element.20), channel_id=1, source_target_pairs={{0,1},{1,0},{16,17},{17,16},{2,3},{3,2},{18,19},{19,18},{4,5},{5,4... | collective-permute-start | bytes 442376 | tf_op jit(solution)/shard_map/ppermute | solution.py:315
  15.6 1.4 %collective-permute-start.3 = (f32[8,36,128]{2,1,0:T(8,128)S(1)}, f32[8,36,128]{2,1,0:T(8,128)S(1)}, u32[]{:S(2)}, u32[]{:S(2)}) collective-permute-start(f32[8,36,128]{2,1,0:T(8,128)S(1)} %get-tuple-element.21), channel_id=1, source_target_pairs={{0,16},{1,17},{16,0},{17,1},{2,18},{3,19},{18,2},{19,3},{4,20},{5,... | collective-permute-start | bytes 442376 | tf_op jit(solution)/shard_map/ppermute | solution.py:315
  17.1 0.5 collective-permute-start.4
  17.6 4.4 %collective-permute-done.2 = f32[8,36,128]{2,1,0:T(8,128)S(1)} collective-permute-done((f32[8,36,128]{2,1,0:T(8,128)S(1)}, f32[8,36,128]{2,1,0:T(8,128)S(1)}, u32[]{:S(2)}, u32[]{:S(2)}) %collective-permute-start.2) | collective-permute-done | bytes 147488 | tf_op jit(solution)/shard_map/ppermute | solution.py:315
  22.0 3.1 %collective-permute-done.3 = f32[8,36,128]{2,1,0:T(8,128)S(1)} collective-permute-done((f32[8,36,128]{2,1,0:T(8,128)S(1)}, f32[8,36,128]{2,1,0:T(8,128)S(1)}, u32[]{:S(2)}, u32[]{:S(2)}) %collective-permute-start.3) | collective-permute-done | bytes 147488 | tf_op jit(solution)/shard_map/ppermute | solution.py:315
  25.1 0.0 collective-permute-done.4
  25.2 18.1 %all_to_all.15.x_ref = f32[8,36,128]{2,1,0:T(8,128)S(1)} all-to-all(f32[8,36,128]{2,1,0:T(8,128)S(1)} %add_add_fusion), channel_id=1, replica_groups=mesh['z'=8,'xl'=2,'c'=2,'y'=4,'xh'=2] {'z'}, dimensions={0} | all-to-all | bytes 294912 | tf_op jit(solution)/shard_map/all_to_all | solution.py:339
  43.3 11.8 %all_to_all.16.refs_0_ = f32[8,36,128]{2,1,0:T(8,128)S(1)} all-to-all(f32[8,36,128]{2,1,0:T(8,128)S(1)} %spread.1), channel_id=1, replica_groups=mesh['z'=8,'xl'=2,'c'=2,'y'=4,'xh'=2] {'z'}, dimensions={0} | all-to-all | bytes 294912 | tf_op jit(solution)/shard_map/all_to_all | solution.py:340
  55.2 1.5 %collective-permute-start.7 = (f32[8,36,128]{2,1,0:T(8,128)S(1)}, f32[8,36,128]{2,1,0:T(8,128)S(1)}, u32[]{:S(2)}, u32[]{:S(2)}) collective-permute-start(f32[8,36,128]{2,1,0:T(8,128)S(1)} %all_to_all.16.refs_0_), channel_id=1, source_target_pairs={{0,17},{1,16},{16,1},{17,0},{2,19},{3,18},{18,3},{19,2},{4,21},{5,... | collective-permute-start | bytes 442376 | tf_op jit(solution)/shard_map/ppermute | solution.py:315
  56.7 1.8 %collective-permute-start.6 = (f32[8,36,128]{2,1,0:T(8,128)S(1)}, f32[8,36,128]{2,1,0:T(8,128)S(1)}, u32[]{:S(2)}, u32[]{:S(2)}) collective-permute-start(f32[8,36,128]{2,1,0:T(8,128)S(1)} %all_to_all.16.refs_0_), channel_id=1, source_target_pairs={{0,16},{1,17},{16,0},{17,1},{2,18},{3,19},{18,2},{19,3},{4,20},{5,... | collective-permute-start | bytes 442376 | tf_op jit(solution)/shard_map/ppermute | solution.py:315
  58.5 0.2 collective-permute-start.5
  58.7 3.6 %collective-permute-done.7.refs_3_ = f32[8,36,128]{2,1,0:T(8,128)S(1)} collective-permute-done((f32[8,36,128]{2,1,0:T(8,128)S(1)}, f32[8,36,128]{2,1,0:T(8,128)S(1)}, u32[]{:S(2)}, u32[]{:S(2)}) %collective-permute-start.7) | collective-permute-done | bytes 147488 | tf_op jit(solution)/shard_map/ppermute | solution.py:315
  62.2 0.0 collective-permute-done.6.refs_2_
  62.2 3.1 %collective-permute-done.5.refs_1_ = f32[8,36,128]{2,1,0:T(8,128)S(1)} collective-permute-done((f32[8,36,128]{2,1,0:T(8,128)S(1)}, f32[8,36,128]{2,1,0:T(8,128)S(1)}, u32[]{:S(2)}, u32[]{:S(2)}) %collective-permute-start.5) | collective-permute-done | bytes 147488 | tf_op jit(solution)/shard_map/ppermute | solution.py:315
  65.3 0.0 collective-permute-done.8.refs_6_
  65.3 0.0 copy-done
  65.3 0.0 copy-done.1
  65.3 6.0 %solve.1 = (f32[128,128]{1,0:T(8,128)S(1)}, f32[1024,128]{1,0:T(8,128)S(1)}, f32[136,128]{1,0:T(8,128)S(1)}) custom-call(s32[1]{0:T(128)} %bitcast.x_ref, f32[8,36,128]{2,1,0:T(8,128)S(1)} %all_to_all.16.refs_0_, f32[8,36,128]{2,1,0:T(8,128)S(1)} %collective-permute-done.5.refs_1_, f32[8,36,128]{2,1,0:T(8,128)S(1)} %collective-permute-done.6.refs_2_, ...), custom_call_target="tpu_custom_call" | custom-call | tf_op jit(solution)/shard_map/solve/pallas_call | solution.py:294
  71.3 0.1 collective-permute-start.9
  71.4 1.2 %collective-permute-done.9 = f32[136,128]{1,0:T(8,128)S(1)} collective-permute-done((f32[136,128]{1,0:T(8,128)S(1)}, f32[136,128]{1,0:T(8,128)S(1)}, u32[]{:S(2)}, u32[]{:S(2)}) %collective-permute-start.9) | collective-permute-done | bytes 69664 | tf_op jit(solution)/shard_map/ppermute | solution.py:315
  72.7 0.2 collective-permute-start.10
  72.9 3.0 %collective-permute-start.13 = (f32[136,128]{1,0:T(8,128)S(1)}, f32[136,128]{1,0:T(8,128)S(1)}, u32[]{:S(2)}, u32[]{:S(2)}) collective-permute-start(f32[136,128]{1,0:T(8,128)S(1)} %add.19.refs_0_), channel_id=1, source_target_pairs={{0,6},{2,4},{4,2},{6,0},{1,7},{3,5},{5,3},{7,1},{8,14},{10,12},{12... | collective-permute-start | bytes 208904 | tf_op jit(solution)/shard_map/ppermute | solution.py:315
  76.0 0.6 collective-permute-start.12
  76.6 0.4 collective-permute-start.11
  77.0 0.0 collective-permute-done.10
  77.0 1.6 %assemble.1 = f32[8,256,128]{2,1,0:T(8,128)} custom-call(s32[2]{0:T(128)S(1)} %get-tuple-element.32.at_ref, f32[4,256,128]{2,1,0:T(8,128)S(1)} %bitcast.15, f32[4,256,128]{2,1,0:T(8,128)S(1)} %bitcast.16), custom_call_target="tpu_custom_call" | custom-call | tf_op jit(solution)/shard_map/assemble/pallas_call | solution.py:108
  78.6 0.8 collective-permute-done.13.refs_3_
  79.4 2.9 %collective-permute-done.12.refs_2_ = f32[136,128]{1,0:T(8,128)S(1)} collective-permute-done((f32[136,128]{1,0:T(8,128)S(1)}, f32[136,128]{1,0:T(8,128)S(1)}, u32[]{:S(2)}, u32[]{:S(2)}) %collective-permute-start.12) | collective-permute-done | bytes 69664 | tf_op jit(solution)/shard_map/ppermute | solution.py:315
  82.4 0.0 collective-permute-done.11.refs_1_
  82.4 0.6 collect.1
  83.0 3.5 %all-to-all-start.2 = ((f32[16,4,128]{2,1,0:T(4,128)}), f32[16,4,128]{2,1,0:T(4,128)S(1)}, u32[]{:S(2)}, u32[]{:S(2)}) async-start(f32[16,4,128]{2,1,0:T(4,128)} %collect.1), calls=%async_computation.2 | async-start | bytes 65536 | tf_op jit(solution)/shard_map/all_to_all | solution.py:353
  86.4 3.9 %inverse_of_product.1 = f32[128,128]{1,0:T(8,128)S(1)} custom-call(f32[128,128]{1,0:T(8,128)S(1)} %get-tuple-element.31.first_ref, f32[136,128]{1,0:T(8,128)S(1)} %add.19.refs_0_, f32[136,128]{1,0:T(8,128)S(1)} %collective-permute-done.11.refs_1_, f32[136,128]{1,0:T(8,128)S(1)} %collective-permute-done.12.refs_2_, f32[136,128]{1,0:T(8,128)S(1)} %collective-permute-done.13.refs_3_), custom_call_target="tpu_custom_call" | custom-call | flops 3000000000 | bytes 524288 | tf_op jit(solution)/shard_map/inverse_of_product/pallas_call | solution.py:89
  90.4 3.6 %all-to-all-done.2 = f32[16,4,128]{2,1,0:T(4,128)S(1)} async-done(((f32[16,4,128]{2,1,0:T(4,128)}), f32[16,4,128]{2,1,0:T(4,128)S(1)}, u32[]{:S(2)}, u32[]{:S(2)}) %all-to-all-start.2) | async-done | bytes 32800 | tf_op jit(solution)/shard_map/all_to_all | solution.py:353
  94.0 0.7 fusion.1
  (4 shorter events, 0.1 us)
Async XLA Ops:
  0.7 6.3 %copy-start.2 = (f32[256,128]{1,0:T(8,128)S(1)}, f32[256,128]{1,0:T(8,128)}, u32[]{:S(2)}) copy-start(f32[256,128]{1,0:T(8,128)} %a_hbm.3) | copy-start | bytes 393220
  6.4 58.9 %collective-permute-start.8 = (f32[4,1024,128]{2,1,0:T(8,128)}, f32[4,1024,128]{2,1,0:T(8,128)S(1)}, u32[]{:S(2)}, u32[]{:S(2)}) collective-permute-start(f32[4,1024,128]{2,1,0:T(8,128)} %get-tuple-element.24), channel_id=1, source_target_pairs={{0,8},{8,0},{1,9},{9,1},{2,10},{10,2},{3,11},{11,3},{4,12},{12,4},... | collective-permute-start | bytes 6291464 | tf_op jit(solution)/shard_map/ppermute | solution.py:315
  6.5 6.8 %collective-permute-start = (f32[1024,128]{1,0:T(8,128)S(1)}, f32[1024,128]{1,0:T(8,128)S(1)}, u32[]{:S(2)}, u32[]{:S(2)}) collective-permute-start(f32[1024,128]{1,0:T(8,128)S(1)} %get-tuple-element.18), channel_id=1, source_target_pairs={{0,8},{8,0},{1,9},{9,1},{2,10},{10,2},{3,11},{11,3},{4,12},{12,4},... | collective-permute-start | bytes 1572872 | tf_op jit(solution)/shard_map/ppermute | solution.py:315
  7.4 5.9 %collective-permute-start.1 = (f32[128,128]{1,0:T(8,128)S(1)}, f32[128,128]{1,0:T(8,128)S(1)}, u32[]{:S(2)}, u32[]{:S(2)}) collective-permute-start(f32[128,128]{1,0:T(8,128)S(1)} %fusion.g_ref), channel_id=1, source_target_pairs={{0,8},{8,0},{1,9},{9,1},{2,10},{10,2},{3,11},{11,3},{4,12},{12,4},... | collective-permute-start | bytes 196616 | tf_op jit(solution)/shard_map/ppermute | solution.py:315
  13.2 52.1 %copy-start = (f32[4,1024,128]{2,1,0:T(8,128)S(1)}, f32[4,1024,128]{2,1,0:T(8,128)}, u32[]{:S(2)}) copy-start(f32[4,1024,128]{2,1,0:T(8,128)} %get-tuple-element.23.refs_5_) | copy-start | bytes 6291460
  13.2 52.1 %copy-start.1 = (f32[128,128]{1,0:T(8,128)S(1)}, f32[128,128]{1,0:T(8,128)}, u32[]{:S(2)}) copy-start(f32[128,128]{1,0:T(8,128)} %refs_4_.1) | copy-start | bytes 196612
  13.4 8.6 %collective-permute-start.2 = (f32[8,36,128]{2,1,0:T(8,128)S(1)}, f32[8,36,128]{2,1,0:T(8,128)S(1)}, u32[]{:S(2)}, u32[]{:S(2)}) collective-permute-start(f32[8,36,128]{2,1,0:T(8,128)S(1)} %get-tuple-element.20), channel_id=1, source_target_pairs={{0,1},{1,0},{16,17},{17,16},{2,3},{3,2},{18,19},{19,18},{4,5},{5,4... | collective-permute-start | bytes 442376 | tf_op jit(solution)/shard_map/ppermute | solution.py:315
  15.6 9.5 %collective-permute-start.3 = (f32[8,36,128]{2,1,0:T(8,128)S(1)}, f32[8,36,128]{2,1,0:T(8,128)S(1)}, u32[]{:S(2)}, u32[]{:S(2)}) collective-permute-start(f32[8,36,128]{2,1,0:T(8,128)S(1)} %get-tuple-element.21), channel_id=1, source_target_pairs={{0,16},{1,17},{16,0},{17,1},{2,18},{3,19},{18,2},{19,3},{4,20},{5,... | collective-permute-start | bytes 442376 | tf_op jit(solution)/shard_map/ppermute | solution.py:315
  17.1 8.1 %collective-permute-start.4 = (f32[8,36,128]{2,1,0:T(8,128)S(1)}, f32[8,36,128]{2,1,0:T(8,128)S(1)}, u32[]{:S(2)}, u32[]{:S(2)}) collective-permute-start(f32[8,36,128]{2,1,0:T(8,128)S(1)} %get-tuple-element.22), channel_id=1, source_target_pairs={{0,17},{1,16},{16,1},{17,0},{2,19},{3,18},{18,3},{19,2},{4,21},{5,... | collective-permute-start | bytes 442376 | tf_op jit(solution)/shard_map/ppermute | solution.py:315
  55.2 7.1 %collective-permute-start.7 = (f32[8,36,128]{2,1,0:T(8,128)S(1)}, f32[8,36,128]{2,1,0:T(8,128)S(1)}, u32[]{:S(2)}, u32[]{:S(2)}) collective-permute-start(f32[8,36,128]{2,1,0:T(8,128)S(1)} %all_to_all.16.refs_0_), channel_id=1, source_target_pairs={{0,17},{1,16},{16,1},{17,0},{2,19},{3,18},{18,3},{19,2},{4,21},{5,... | collective-permute-start | bytes 442376 | tf_op jit(solution)/shard_map/ppermute | solution.py:315
  56.7 5.6 %collective-permute-start.6 = (f32[8,36,128]{2,1,0:T(8,128)S(1)}, f32[8,36,128]{2,1,0:T(8,128)S(1)}, u32[]{:S(2)}, u32[]{:S(2)}) collective-permute-start(f32[8,36,128]{2,1,0:T(8,128)S(1)} %all_to_all.16.refs_0_), channel_id=1, source_target_pairs={{0,16},{1,17},{16,0},{17,1},{2,18},{3,19},{18,2},{19,3},{4,20},{5,... | collective-permute-start | bytes 442376 | tf_op jit(solution)/shard_map/ppermute | solution.py:315
  58.5 6.8 %collective-permute-start.5 = (f32[8,36,128]{2,1,0:T(8,128)S(1)}, f32[8,36,128]{2,1,0:T(8,128)S(1)}, u32[]{:S(2)}, u32[]{:S(2)}) collective-permute-start(f32[8,36,128]{2,1,0:T(8,128)S(1)} %all_to_all.16.refs_0_), channel_id=1, source_target_pairs={{0,1},{1,0},{16,17},{17,16},{2,3},{3,2},{18,19},{19,18},{4,5},{5,4... | collective-permute-start | bytes 442376 | tf_op jit(solution)/shard_map/ppermute | solution.py:315
  71.3 1.3 %collective-permute-start.9 = (f32[136,128]{1,0:T(8,128)S(1)}, f32[136,128]{1,0:T(8,128)S(1)}, u32[]{:S(2)}, u32[]{:S(2)}) collective-permute-start(f32[136,128]{1,0:T(8,128)S(1)} %get-tuple-element.25), channel_id=1, source_target_pairs={{0,8},{8,0},{1,9},{9,1},{2,10},{10,2},{3,11},{11,3},{4,12},{12,4},... | collective-permute-start | bytes 208904 | tf_op jit(solution)/shard_map/ppermute | solution.py:315
  72.7 4.3 %collective-permute-start.10 = (f32[1024,128]{1,0:T(8,128)S(1)}, f32[1024,128]{1,0:T(8,128)S(1)}, u32[]{:S(2)}, u32[]{:S(2)}) collective-permute-start(f32[1024,128]{1,0:T(8,128)S(1)} %get-tuple-element.28), channel_id=1, source_target_pairs={{0,8},{8,0},{1,9},{9,1},{2,10},{10,2},{3,11},{11,3},{4,12},{12,4},... | collective-permute-start | bytes 1572872 | tf_op jit(solution)/shard_map/ppermute | solution.py:315
  72.9 6.5 %collective-permute-start.13 = (f32[136,128]{1,0:T(8,128)S(1)}, f32[136,128]{1,0:T(8,128)S(1)}, u32[]{:S(2)}, u32[]{:S(2)}) collective-permute-start(f32[136,128]{1,0:T(8,128)S(1)} %add.19.refs_0_), channel_id=1, source_target_pairs={{0,6},{2,4},{4,2},{6,0},{1,7},{3,5},{5,3},{7,1},{8,14},{10,12},{12... | collective-permute-start | bytes 208904 | tf_op jit(solution)/shard_map/ppermute | solution.py:315
  76.0 6.4 %collective-permute-start.12 = (f32[136,128]{1,0:T(8,128)S(1)}, f32[136,128]{1,0:T(8,128)S(1)}, u32[]{:S(2)}, u32[]{:S(2)}) collective-permute-start(f32[136,128]{1,0:T(8,128)S(1)} %add.19.refs_0_), channel_id=1, source_target_pairs={{0,4},{2,6},{4,0},{6,2},{1,5},{3,7},{5,1},{7,3},{8,12},{10,14},{12... | collective-permute-start | bytes 208904 | tf_op jit(solution)/shard_map/ppermute | solution.py:315
  76.6 5.8 %collective-permute-start.11 = (f32[136,128]{1,0:T(8,128)S(1)}, f32[136,128]{1,0:T(8,128)S(1)}, u32[]{:S(2)}, u32[]{:S(2)}) collective-permute-start(f32[136,128]{1,0:T(8,128)S(1)} %add.19.refs_0_), channel_id=1, source_target_pairs={{0,2},{2,0},{4,6},{6,4},{1,3},{3,1},{5,7},{7,5},{8,10},{10,8},{12,... | collective-permute-start | bytes 208904 | tf_op jit(solution)/shard_map/ppermute | solution.py:315
  83.0 10.9 %all-to-all-start.2 = ((f32[16,4,128]{2,1,0:T(4,128)}), f32[16,4,128]{2,1,0:T(4,128)S(1)}, u32[]{:S(2)}, u32[]{:S(2)}) async-start(f32[16,4,128]{2,1,0:T(4,128)} %collect.1), calls=%async_computation.2 | async-start | bytes 65536 | tf_op jit(solution)/shard_map/all_to_all | solution.py:353

commit v8 on v7

--- a/solution.py
+++ b/solution.py
@@ -122,13 +122,13 @@
     return high, middle, (rest - middle.astype(F32)).astype(BF16)
 
 
-def contract_kernel(chunk, at_ref, x_hbm, a_hbm, c_hbm, p_hbm, b_ref, *scratch):
-    x_ref, w_ref, p_ref, a_ref, c_ref, sems = scratch
+def contract_kernel(chunk, at_ref, x_hbm, a_hbm, c_hbm, p_ref, b_ref, *scratch):
+    x_ref, w_ref, a_ref, c_ref, sems = scratch
     count, rows, rank = p_ref.shape
     span = 2 * count
     factors = [
-        pltpu.make_async_copy(a_hbm, a_ref, sems.at[2 * rows // chunk]),
-        pltpu.make_async_copy(c_hbm, c_ref, sems.at[2 * rows // chunk + 1]),
+        pltpu.make_async_copy(a_hbm, a_ref, sems.at[rows // chunk]),
+        pltpu.make_async_copy(c_hbm, c_ref, sems.at[rows // chunk + 1]),
     ]
     factors[0].start()
     factors[1].start()
@@ -166,15 +166,6 @@
                 term = value * c_ref[k : k + 1, :]
                 total = term if total is None else total + term
             b_ref[row : row + 128] = total
-        copy = pltpu.make_async_copy(
-            p_ref.at[:, pl.ds(at, chunk)],
-            p_hbm.at[:, pl.ds(at, chunk)],
-            sems.at[len(copies)],
-        )
-        copy.start()
-        copies.append(copy)
-    for copy in copies[rows // chunk :]:
-        copy.wait()
 
 
 def contract(at, x, factor_a, factor_c, rows):
@@ -183,18 +174,17 @@
     return pl.pallas_call(
         functools.partial(contract_kernel, chunk),
         out_shape=[
-            pltpu.HBM((count, rows, rank), F32),
+            jax.ShapeDtypeStruct((count, rows, rank), F32),
             jax.ShapeDtypeStruct((rows, rank), F32),
         ],
         in_specs=[SMEM, HBM, HBM, HBM],
-        out_specs=[HBM, VMEM],
+        out_specs=[VMEM, VMEM],
         scratch_shapes=[
             pltpu.VMEM((rows * 2 * count, depth // 2), F32),
             pltpu.VMEM((depth, 3 * rank), BF16),
-            pltpu.VMEM((count, rows, rank), F32),
             pltpu.VMEM((depth, rank), F32),
             pltpu.VMEM((count, rank), F32),
-            pltpu.SemaphoreType.DMA((2 * rows // chunk + 2,)),
+            pltpu.SemaphoreType.DMA((rows // chunk + 2,)),
         ],
         compiler_params=pltpu.CompilerParams(vmem_limit_bytes=12 << 20),
         cost_estimate=pl.CostEstimate(
@@ -207,25 +197,16 @@
 
 
 def parcels_kernel(x_ref, b_ref, b_far_ref, g_ref, g_far_ref, *outs):
-    depth, rows, _ = outs[0].shape
     block, slab = b_ref.shape[0] // 4, g_ref.shape[0] // 4
-    some, few = block // depth, slab // depth
     for n, out in enumerate(outs):
-        for z in range(depth):
-            at = n * block + z * some
-            out[z, :some] = b_ref[at : at + some] + b_far_ref[at : at + some]
-        for a in range(4):
-
-            @pl.when((x_ref[0] ^ n) == a)
-            def _():
-                for z in range(depth):
-                    at = a * slab + z * few
-                    out[z, some:] = 0.5 * (g_ref[at : at + few] + g_far_ref[at : at + few])
-
-
-def parcels(x, b, b_far, g, g_far, depth):
-    rank = b.shape[1]
-    shape = jax.ShapeDtypeStruct((depth, (b.shape[0] + g.shape[0]) // (4 * depth), rank), F32)
+        at = pl.ds(n * block, block)
+        out[:block] = b_ref[at] + b_far_ref[at]
+        at = pl.ds(pl.multiple_of((x_ref[0] ^ n) * slab, slab), slab)
+        out[block:] = 0.5 * (g_ref[at] + g_far_ref[at])
+
+
+def parcels(x, b, b_far, g, g_far):
+    shape = jax.ShapeDtypeStruct(((b.shape[0] + g.shape[0]) // 4, b.shape[1]), F32)
     return pl.pallas_call(
         parcels_kernel,
         out_shape=[shape] * 4,
@@ -236,6 +217,28 @@
     )(x, b, b_far, g, g_far)
 
 
+def column_kernel(slab, *refs):
+    out_ref = refs[-1]
+    depth = out_ref.shape[0]
+    block = refs[0].shape[0] - slab
+    some, few = block // depth, slab // depth
+    for z in range(depth):
+        out_ref[z, :some] = total(refs[:-1], pl.ds(z * some, some))
+        out_ref[z, some:] = total(refs[:-1], pl.ds(block + z * few, few))
+
+
+def column_sum(parts, depth, slab):
+    rows, rank = parts[0].shape
+    return pl.pallas_call(
+        functools.partial(column_kernel, slab),
+        out_shape=jax.ShapeDtypeStruct((depth, rows // depth, rank), F32),
+        in_specs=[VMEM] * 4,
+        out_specs=VMEM,
+        compiler_params=pltpu.CompilerParams(vmem_limit_bytes=2 << 20),
+        name="column_sum",
+    )(*parts)
+
+
 def spread_kernel(x_ref, out_ref):
     out_ref[...] = jnp.broadcast_to(jnp.sum(x_ref[...], axis=0)[None], out_ref.shape)
 
@@ -251,38 +254,45 @@
     )(x)
 
 
+def flatten_kernel(x_ref, out_ref, *, slab):
+    depth = x_ref.shape[0]
+    block = out_ref.shape[0] - slab
+    some, few = block // depth, slab // depth
+    for z in range(depth):
+        out_ref[z * some : (z + 1) * some] = x_ref[z, :some]
+        at = block + z * few
+        out_ref[at : at + few] = x_ref[z, some:]
+
+
+def flatten(x, slab):
+    depth, rows, rank = x.shape
+    return pl.pallas_call(
+        functools.partial(flatten_kernel, slab=slab),
+        out_shape=jax.ShapeDtypeStruct((depth * rows, rank), F32),
+        in_specs=[VMEM],
+        out_specs=VMEM,
+        compiler_params=pltpu.CompilerParams(vmem_limit_bytes=2 << 20),
+        name="flatten",
+    )(x)
+
+
 def solve_kernel(x_ref, *refs):
-    columns, (h_ref, p_hbm, q_hbm, g_ref, f_ref, out_ref, p_ref, q_ref, sems) = refs[:4], refs[4:]
-    depth, every, rank = columns[0].shape
-    few = rank // (4 * depth)
-    some = every - few
-    copies = [
-        pltpu.make_async_copy(p_hbm, p_ref, sems.at[0]),
-        pltpu.make_async_copy(q_hbm, q_ref, sems.at[1]),
-    ]
-    for copy in copies:
-        copy.start()
+    columns, (h_ref, p_ref, q_ref, g_ref, f_ref, out_ref) = refs[:4], refs[4:]
+    rank = g_ref.shape[0]
+    slab = rank // 4
+    block = columns[0].shape[0] - slab
     for n in range(4):
-        for a in range(4):
-
-            @pl.when((x_ref[0] ^ n) == a)
-            def _():
-                for z in range(depth):
-                    at = (a * depth + z) * few
-                    g_ref[at : at + few] = columns[n][z, some:]
-
+        at = pl.multiple_of((x_ref[0] ^ n) * slab, slab)
+        g_ref[pl.ds(at, slab)] = columns[n][block:]
     inverse = spd_inverse(g_ref[...] * h_ref[...], 16)
-    block = depth * some
     for n in range(4):
-        f = dot(columns[n][:, :some].reshape(block, rank), inverse)
+        f = dot(columns[n][:block], inverse)
         f_ref[n * block : (n + 1) * block] = f
     f = f_ref[...]
     out_ref[:rank] = lax.dot_general(
         f, f, (((0,), (0,)), ((), ())), precision=HIGH, preferred_element_type=F32
     )
     out_ref[rank:] = jnp.zeros((out_ref.shape[0] - rank, rank), F32)
-    for copy in copies:
-        copy.wait()
     for k in range(p_ref.shape[0]):
         both = (p_ref[k] + q_ref[k]) * f_ref[...]
         out_ref[rank + k : rank + k + 1] = jnp.sum(both, axis=0, keepdims=True)
@@ -298,13 +308,8 @@
             jax.ShapeDtypeStruct((rows, rank), F32),
             jax.ShapeDtypeStruct((rank + 8 * pl.cdiv(count, 8), rank), F32),
         ],
-        in_specs=[SMEM] + [VMEM] * 5 + [HBM] * 2,
+        in_specs=[SMEM] + [VMEM] * 7,
         out_specs=[VMEM] * 3,
-        scratch_shapes=[
-            pltpu.VMEM((count, rows, rank), F32),
-            pltpu.VMEM((count, rows, rank), F32),
-            pltpu.SemaphoreType.DMA((2,)),
-        ],
         compiler_params=pltpu.CompilerParams(vmem_limit_bytes=12 << 20),
         name="solve",
     )(x, *columns, gram_c, first, second)
@@ -333,11 +338,10 @@
     p_mine, b_mine = contract(jnp.stack([core, x]), flat, a_hbm, c_hbm, half)
     gram_part = dot(factor_a.T, factor_a)
     at = x.reshape(1)
-    sent = parcels(at, b_mine, swap(b_other, "c"), gram_part, swap(gram_part, "c"), depth)
+    sent = parcels(at, b_mine, swap(b_other, "c"), gram_part, swap(gram_part, "c"))
     got = [sent[0]] + [swap(sent[n], RING, n) for n in (1, 2, 3)]
-    column = (got[0] + got[1]) + (got[2] + got[3])
-    column = spread(lax.all_to_all(column, "z", 0, 0))
-    column = lax.all_to_all(column, "z", 0, 0)
+    column = spread(lax.all_to_all(column_sum(got, depth, rank // 4), "z", 0, 0))
+    column = flatten(lax.all_to_all(column, "z", 0, 0), rank // 4)
     columns = [column] + [swap(column, RING, n) for n in (1, 2, 3)]
     gram_a, f_mine, sums = solve(at, columns, gram_c, p_mine, swap(p_other, "c"))
 

time: 95 us -> 91.8 us (0.966)
  Pallas kernels: 23.6 us -> 21.3 us
    pallas_call x2 -> x4, Pallas kernels: 11.3 us -> 9.7 us  [the longest x2 9.65 us: contract(): pl.pallas_call(functools.partial(contract_kernel, chunk), out_shape=[jax....]
  transfers between devices with their start and end apart: 15 -> 15, of which waited for: 8 -> 8; matrix products, arithmetic and copies ran while one was open for 0% -> 0% of each run, Pallas kernels for 12% -> 11%
where the time goes in v8:
time: 91.8 us; the launch traced here: 91.6 us
  blocking collectives  30 us (33%)
  waiting for transfers between devices  21.8 us (24%)
  Pallas kernels  21.3 us (23%)
  starting transfers between devices  16.4 us (18%)
  matrix products  1.13 us (1%)
    ppermute x14, waiting for transfers between devices, swap(): return lax.ppermute(x, axis, [(i, i ^ bit) for i in range(n)])  18.3 us
    all_to_all x1, blocking collectives, body(): lax.all_to_all(column_sum(got, depth, rank // 4), 'z', 0, 0)  18.1 us
    ppermute x14, starting transfers between devices, swap(): return lax.ppermute(x, axis, [(i, i ^ bit) for i in range(n)])  13 us
    all_to_all x1, blocking collectives, body(): column = flatten(lax.all_to_all(column, 'z', 0, 0), rank // 4)  11.8 us
    pallas_call x2, Pallas kernels, contract(): pl.pallas_call(functools.partial(contract_kernel, chunk), out_shape=[jax....  9.65 us
    pallas_call x1, Pallas kernels, solve(): pl.pallas_call(solve_kernel, out_shape=[square, jax.ShapeDtypeStruct((row...  5.39 us
    pallas_call x1, Pallas kernels, inverse_of_product(): pl.pallas_call(inverse_kernel, out_shape=jax.ShapeDtypeStruct(first.shape...  3.93 us
    all_to_all x1, waiting for transfers between devices, body(): mttkrp_c = jnp.sum(lax.all_to_all(spread_c, plane, 0, 0), axis=0)  3.55 us
  transfers between devices with their start and end apart: 15, of which 8 were waited for; matrix products, arithmetic and copies ran while one was open for 0% of the time, Pallas kernels for 11%

profile of v8, /device:TPU:2, one launch (start us, length us, event | category | flops | bytes accessed | tf_op | source)
XLA Modules:
  0.0 91.6 jit_solution(9035655486269213137)
XLA Ops:
  0.6 0.1 pad_add_fusion
  0.7 0.0 copy-start.1
  0.7 4.8 %contract.3 = (f32[4,1024,128]{2,1,0:T(8,128)S(1)}, f32[1024,128]{1,0:T(8,128)S(1)}) custom-call(s32[2]{0:T(128)S(1)} %get-tuple-element.33.at_ref, f32[16384,128]{1,0:T(8,128)} %bitcast.17, f32[256,128]{1,0:T(8,128)} %a_hbm.3, f32[4,128]{1,0:T(4,128)} %c_hbm.3), custom_call_target="tpu_custom_call" | custom-call | flops 2147483648 | bytes 6291456 | tf_op jit(solution)/shard_map/contract/pallas_call | solution.py:174
  5.5 0.1 collective-permute-start.8
  5.6 0.5 collective-permute-start
  6.1 0.0 copy-done.1
  6.1 0.4 fusion.g_ref
  6.5 0.2 collective-permute-start.1
  6.7 4.8 %contract.2 = (f32[4,1024,128]{2,1,0:T(8,128)S(1)}, f32[1024,128]{1,0:T(8,128)S(1)}) custom-call(s32[2]{0:T(128)S(1)} %get-tuple-element.32.at_ref, f32[16384,128]{1,0:T(8,128)} %bitcast.18, f32[256,128]{1,0:T(8,128)} %a_hbm.3, f32[4,128]{1,0:T(4,128)} %c_hbm.3), custom_call_target="tpu_custom_call" | custom-call | flops 2147483648 | bytes 6291456 | tf_op jit(solution)/shard_map/contract/pallas_call | solution.py:174
  11.6 0.0 copy-start
  11.6 0.0 collective-permute-done.1.g_far_ref
  11.6 0.0 collective-permute-done.b_far_ref
  11.6 0.1 parcels.1
  11.7 2.2 %collective-permute-start.2 = (f32[288,128]{1,0:T(8,128)S(1)}, f32[288,128]{1,0:T(8,128)S(1)}, u32[]{:S(2)}, u32[]{:S(2)}) collective-permute-start(f32[288,128]{1,0:T(8,128)S(1)} %get-tuple-element.20), channel_id=1, source_target_pairs={{0,1},{1,0},{16,17},{17,16},{2,3},{3,2},{18,19},{19,18},{4,5},{5,4... | collective-permute-start | bytes 442376 | tf_op jit(solution)/shard_map/ppermute | solution.py:320
  13.9 1.4 %collective-permute-start.3 = (f32[288,128]{1,0:T(8,128)S(1)}, f32[288,128]{1,0:T(8,128)S(1)}, u32[]{:S(2)}, u32[]{:S(2)}) collective-permute-start(f32[288,128]{1,0:T(8,128)S(1)} %get-tuple-element.21), channel_id=1, source_target_pairs={{0,16},{1,17},{16,0},{17,1},{2,18},{3,19},{18,2},{19,3},{4,20},{5,... | collective-permute-start | bytes 442376 | tf_op jit(solution)/shard_map/ppermute | solution.py:320
  15.3 0.5 collective-permute-start.4
  15.8 4.1 %collective-permute-done.2.refs_1_ = f32[288,128]{1,0:T(8,128)S(1)} collective-permute-done((f32[288,128]{1,0:T(8,128)S(1)}, f32[288,128]{1,0:T(8,128)S(1)}, u32[]{:S(2)}, u32[]{:S(2)}) %collective-permute-start.2) | collective-permute-done | bytes 147488 | tf_op jit(solution)/shard_map/ppermute | solution.py:320
  19.9 2.8 %collective-permute-done.3.refs_2_ = f32[288,128]{1,0:T(8,128)S(1)} collective-permute-done((f32[288,128]{1,0:T(8,128)S(1)}, f32[288,128]{1,0:T(8,128)S(1)}, u32[]{:S(2)}, u32[]{:S(2)}) %collective-permute-start.3) | collective-permute-done | bytes 147488 | tf_op jit(solution)/shard_map/ppermute | solution.py:320
  22.7 0.0 collective-permute-done.4.refs_3_
  22.7 18.1 %all_to_all.15.x_ref = f32[8,36,128]{2,1,0:T(8,128)S(1)} all-to-all(f32[8,36,128]{2,1,0:T(8,128)S(1)} %column_sum.1), channel_id=1, replica_groups=mesh['z'=8,'xl'=2,'c'=2,'y'=4,'xh'=2] {'z'}, dimensions={0} | all-to-all | bytes 294912 | tf_op jit(solution)/shard_map/all_to_all | solution.py:343
  40.9 11.8 %all_to_all.16.x_ref = f32[8,36,128]{2,1,0:T(8,128)S(1)} all-to-all(f32[8,36,128]{2,1,0:T(8,128)S(1)} %spread.1), channel_id=1, replica_groups=mesh['z'=8,'xl'=2,'c'=2,'y'=4,'xh'=2] {'z'}, dimensions={0} | all-to-all | bytes 294912 | tf_op jit(solution)/shard_map/all_to_all | solution.py:344
  52.7 1.6 %collective-permute-start.7 = (f32[288,128]{1,0:T(8,128)S(1)}, f32[288,128]{1,0:T(8,128)S(1)}, u32[]{:S(2)}, u32[]{:S(2)}) collective-permute-start(f32[288,128]{1,0:T(8,128)S(1)} %flatten.1.refs_0_), channel_id=1, source_target_pairs={{0,17},{1,16},{16,1},{17,0},{2,19},{3,18},{18,3},{19,2},{4,21},{5,... | collective-permute-start | bytes 442376 | tf_op jit(solution)/shard_map/ppermute | solution.py:320
  54.3 1.8 %collective-permute-start.6 = (f32[288,128]{1,0:T(8,128)S(1)}, f32[288,128]{1,0:T(8,128)S(1)}, u32[]{:S(2)}, u32[]{:S(2)}) collective-permute-start(f32[288,128]{1,0:T(8,128)S(1)} %flatten.1.refs_0_), channel_id=1, source_target_pairs={{0,16},{1,17},{16,0},{17,1},{2,18},{3,19},{18,2},{19,3},{4,20},{5,... | collective-permute-start | bytes 442376 | tf_op jit(solution)/shard_map/ppermute | solution.py:320
  56.1 0.2 collective-permute-start.5
  56.3 3.2 %collective-permute-done.7.refs_3_ = f32[288,128]{1,0:T(8,128)S(1)} collective-permute-done((f32[288,128]{1,0:T(8,128)S(1)}, f32[288,128]{1,0:T(8,128)S(1)}, u32[]{:S(2)}, u32[]{:S(2)}) %collective-permute-start.7) | collective-permute-done | bytes 147488 | tf_op jit(solution)/shard_map/ppermute | solution.py:320
  59.5 0.0 collective-permute-done.6.refs_2_
  59.5 3.2 %collective-permute-done.5.refs_1_ = f32[288,128]{1,0:T(8,128)S(1)} collective-permute-done((f32[288,128]{1,0:T(8,128)S(1)}, f32[288,128]{1,0:T(8,128)S(1)}, u32[]{:S(2)}, u32[]{:S(2)}) %collective-permute-start.5) | collective-permute-done | bytes 147488 | tf_op jit(solution)/shard_map/ppermute | solution.py:320
  62.8 0.0 collective-permute-done.8.refs_6_
  62.8 0.0 copy-done
  62.8 5.4 %solve.1 = (f32[128,128]{1,0:T(8,128)S(1)}, f32[1024,128]{1,0:T(8,128)S(1)}, f32[136,128]{1,0:T(8,128)S(1)}) custom-call(s32[1]{0:T(128)} %bitcast.x_ref, f32[288,128]{1,0:T(8,128)S(1)} %flatten.1.refs_0_, f32[288,128]{1,0:T(8,128)S(1)} %collective-permute-done.5.refs_1_, f32[288,128]{1,0:T(8,128)S(1)} %collective-permute-done.6.refs_2_, ...), custom_call_target="tpu_custom_call" | custom-call | tf_op jit(solution)/shard_map/solve/pallas_call | solution.py:304
  68.2 0.1 collective-permute-start.9
  68.3 1.2 %collective-permute-done.9 = f32[136,128]{1,0:T(8,128)S(1)} collective-permute-done((f32[136,128]{1,0:T(8,128)S(1)}, f32[136,128]{1,0:T(8,128)S(1)}, u32[]{:S(2)}, u32[]{:S(2)}) %collective-permute-start.9) | collective-permute-done | bytes 69664 | tf_op jit(solution)/shard_map/ppermute | solution.py:320
  69.5 0.2 collective-permute-start.10
  69.8 3.0 %collective-permute-start.13 = (f32[136,128]{1,0:T(8,128)S(1)}, f32[136,128]{1,0:T(8,128)S(1)}, u32[]{:S(2)}, u32[]{:S(2)}) collective-permute-start(f32[136,128]{1,0:T(8,128)S(1)} %add.7.refs_0_), channel_id=1, source_target_pairs={{0,6},{2,4},{4,2},{6,0},{1,7},{3,5},{5,3},{7,1},{8,14},{10,12},{12... | collective-permute-start | bytes 208904 | tf_op jit(solution)/shard_map/ppermute | solution.py:320
  72.8 0.6 collective-permute-start.12
  73.4 0.4 collective-permute-start.11
  73.9 0.0 collective-permute-done.10
  73.9 1.6 %assemble.1 = f32[8,256,128]{2,1,0:T(8,128)} custom-call(s32[2]{0:T(128)S(1)} %get-tuple-element.32.at_ref, f32[4,256,128]{2,1,0:T(8,128)S(1)} %bitcast.15, f32[4,256,128]{2,1,0:T(8,128)S(1)} %bitcast.16), custom_call_target="tpu_custom_call" | custom-call | tf_op jit(solution)/shard_map/assemble/pallas_call | solution.py:108
  75.5 0.8 collective-permute-done.13.refs_3_
  76.3 2.9 %collective-permute-done.12.refs_2_ = f32[136,128]{1,0:T(8,128)S(1)} collective-permute-done((f32[136,128]{1,0:T(8,128)S(1)}, f32[136,128]{1,0:T(8,128)S(1)}, u32[]{:S(2)}, u32[]{:S(2)}) %collective-permute-start.12) | collective-permute-done | bytes 69664 | tf_op jit(solution)/shard_map/ppermute | solution.py:320
  79.2 0.0 collective-permute-done.11.refs_1_
  79.2 0.6 collect.1
  79.8 3.5 %all-to-all-start.2 = ((f32[16,4,128]{2,1,0:T(4,128)}), f32[16,4,128]{2,1,0:T(4,128)S(1)}, u32[]{:S(2)}, u32[]{:S(2)}) async-start(f32[16,4,128]{2,1,0:T(4,128)} %collect.1), calls=%async_computation.2 | async-start | bytes 65536 | tf_op jit(solution)/shard_map/all_to_all | solution.py:357
  83.3 3.9 %inverse_of_product.1 = f32[128,128]{1,0:T(8,128)S(1)} custom-call(f32[128,128]{1,0:T(8,128)S(1)} %get-tuple-element.31.first_ref, f32[136,128]{1,0:T(8,128)S(1)} %add.7.refs_0_, f32[136,128]{1,0:T(8,128)S(1)} %collective-permute-done.11.refs_1_, f32[136,128]{1,0:T(8,128)S(1)} %collective-permute-done.12.refs_2_, f32[136,128]{1,0:T(8,128)S(1)} %collective-permute-done.13.refs_3_), custom_call_target="tpu_custom_call" | custom-call | flops 3000000000 | bytes 524288 | tf_op jit(solution)/shard_map/inverse_of_product/pallas_call | solution.py:89
  87.2 3.5 %all-to-all-done.2 = f32[16,4,128]{2,1,0:T(4,128)S(1)} async-done(((f32[16,4,128]{2,1,0:T(4,128)}), f32[16,4,128]{2,1,0:T(4,128)S(1)}, u32[]{:S(2)}, u32[]{:S(2)}) %all-to-all-start.2) | async-done | bytes 32800 | tf_op jit(solution)/shard_map/all_to_all | solution.py:357
  90.8 0.7 fusion.1
  (5 shorter events, 0.1 us)
Async XLA Ops:
  0.7 5.4 %copy-start.1 = (f32[256,128]{1,0:T(8,128)S(1)}, f32[256,128]{1,0:T(8,128)}, u32[]{:S(2)}) copy-start(f32[256,128]{1,0:T(8,128)} %a_hbm.3) | copy-start | bytes 393220
  5.5 57.2 %collective-permute-start.8 = (f32[4,1024,128]{2,1,0:T(8,128)S(1)}, f32[4,1024,128]{2,1,0:T(8,128)S(1)}, u32[]{:S(2)}, u32[]{:S(2)}) collective-permute-start(f32[4,1024,128]{2,1,0:T(8,128)S(1)} %get-tuple-element.24), channel_id=1, source_target_pairs={{0,8},{8,0},{1,9},{9,1},{2,10},{10,2},{3,11},{11,3},{4,12},{12,4},... | collective-permute-start | bytes 6291464 | tf_op jit(solution)/shard_map/ppermute | solution.py:320
  5.6 5.9 %collective-permute-start = (f32[1024,128]{1,0:T(8,128)S(1)}, f32[1024,128]{1,0:T(8,128)S(1)}, u32[]{:S(2)}, u32[]{:S(2)}) collective-permute-start(f32[1024,128]{1,0:T(8,128)S(1)} %get-tuple-element.18), channel_id=1, source_target_pairs={{0,8},{8,0},{1,9},{9,1},{2,10},{10,2},{3,11},{11,3},{4,12},{12,4},... | collective-permute-start | bytes 1572872 | tf_op jit(solution)/shard_map/ppermute | solution.py:320
  6.5 5.0 %collective-permute-start.1 = (f32[128,128]{1,0:T(8,128)S(1)}, f32[128,128]{1,0:T(8,128)S(1)}, u32[]{:S(2)}, u32[]{:S(2)}) collective-permute-start(f32[128,128]{1,0:T(8,128)S(1)} %fusion.g_ref), channel_id=1, source_target_pairs={{0,8},{8,0},{1,9},{9,1},{2,10},{10,2},{3,11},{11,3},{4,12},{12,4},... | collective-permute-start | bytes 196616 | tf_op jit(solution)/shard_map/ppermute | solution.py:320
  11.6 51.2 %copy-start = (f32[128,128]{1,0:T(8,128)S(1)}, f32[128,128]{1,0:T(8,128)}, u32[]{:S(2)}) copy-start(f32[128,128]{1,0:T(8,128)} %refs_4_.1) | copy-start | bytes 196612
  11.7 8.2 %collective-permute-start.2 = (f32[288,128]{1,0:T(8,128)S(1)}, f32[288,128]{1,0:T(8,128)S(1)}, u32[]{:S(2)}, u32[]{:S(2)}) collective-permute-start(f32[288,128]{1,0:T(8,128)S(1)} %get-tuple-element.20), channel_id=1, source_target_pairs={{0,1},{1,0},{16,17},{17,16},{2,3},{3,2},{18,19},{19,18},{4,5},{5,4... | collective-permute-start | bytes 442376 | tf_op jit(solution)/shard_map/ppermute | solution.py:320
  13.9 8.8 %collective-permute-start.3 = (f32[288,128]{1,0:T(8,128)S(1)}, f32[288,128]{1,0:T(8,128)S(1)}, u32[]{:S(2)}, u32[]{:S(2)}) collective-permute-start(f32[288,128]{1,0:T(8,128)S(1)} %get-tuple-element.21), channel_id=1, source_target_pairs={{0,16},{1,17},{16,0},{17,1},{2,18},{3,19},{18,2},{19,3},{4,20},{5,... | collective-permute-start | bytes 442376 | tf_op jit(solution)/shard_map/ppermute | solution.py:320
  15.3 7.4 %collective-permute-start.4 = (f32[288,128]{1,0:T(8,128)S(1)}, f32[288,128]{1,0:T(8,128)S(1)}, u32[]{:S(2)}, u32[]{:S(2)}) collective-permute-start(f32[288,128]{1,0:T(8,128)S(1)} %get-tuple-element.22), channel_id=1, source_target_pairs={{0,17},{1,16},{16,1},{17,0},{2,19},{3,18},{18,3},{19,2},{4,21},{5,... | collective-permute-start | bytes 442376 | tf_op jit(solution)/shard_map/ppermute | solution.py:320
  52.7 6.8 %collective-permute-start.7 = (f32[288,128]{1,0:T(8,128)S(1)}, f32[288,128]{1,0:T(8,128)S(1)}, u32[]{:S(2)}, u32[]{:S(2)}) collective-permute-start(f32[288,128]{1,0:T(8,128)S(1)} %flatten.1.refs_0_), channel_id=1, source_target_pairs={{0,17},{1,16},{16,1},{17,0},{2,19},{3,18},{18,3},{19,2},{4,21},{5,... | collective-permute-start | bytes 442376 | tf_op jit(solution)/shard_map/ppermute | solution.py:320
  54.3 5.2 %collective-permute-start.6 = (f32[288,128]{1,0:T(8,128)S(1)}, f32[288,128]{1,0:T(8,128)S(1)}, u32[]{:S(2)}, u32[]{:S(2)}) collective-permute-start(f32[288,128]{1,0:T(8,128)S(1)} %flatten.1.refs_0_), channel_id=1, source_target_pairs={{0,16},{1,17},{16,0},{17,1},{2,18},{3,19},{18,2},{19,3},{4,20},{5,... | collective-permute-start | bytes 442376 | tf_op jit(solution)/shard_map/ppermute | solution.py:320
  56.1 6.6 %collective-permute-start.5 = (f32[288,128]{1,0:T(8,128)S(1)}, f32[288,128]{1,0:T(8,128)S(1)}, u32[]{:S(2)}, u32[]{:S(2)}) collective-permute-start(f32[288,128]{1,0:T(8,128)S(1)} %flatten.1.refs_0_), channel_id=1, source_target_pairs={{0,1},{1,0},{16,17},{17,16},{2,3},{3,2},{18,19},{19,18},{4,5},{5,4... | collective-permute-start | bytes 442376 | tf_op jit(solution)/shard_map/ppermute | solution.py:320
  68.2 1.3 %collective-permute-start.9 = (f32[136,128]{1,0:T(8,128)S(1)}, f32[136,128]{1,0:T(8,128)S(1)}, u32[]{:S(2)}, u32[]{:S(2)}) collective-permute-start(f32[136,128]{1,0:T(8,128)S(1)} %get-tuple-element.25), channel_id=1, source_target_pairs={{0,8},{8,0},{1,9},{9,1},{2,10},{10,2},{3,11},{11,3},{4,12},{12,4},... | collective-permute-start | bytes 208904 | tf_op jit(solution)/shard_map/ppermute | solution.py:320
  69.5 4.3 %collective-permute-start.10 = (f32[1024,128]{1,0:T(8,128)S(1)}, f32[1024,128]{1,0:T(8,128)S(1)}, u32[]{:S(2)}, u32[]{:S(2)}) collective-permute-start(f32[1024,128]{1,0:T(8,128)S(1)} %get-tuple-element.28), channel_id=1, source_target_pairs={{0,8},{8,0},{1,9},{9,1},{2,10},{10,2},{3,11},{11,3},{4,12},{12,4},... | collective-permute-start | bytes 1572872 | tf_op jit(solution)/shard_map/ppermute | solution.py:320
  69.8 6.5 %collective-permute-start.13 = (f32[136,128]{1,0:T(8,128)S(1)}, f32[136,128]{1,0:T(8,128)S(1)}, u32[]{:S(2)}, u32[]{:S(2)}) collective-permute-start(f32[136,128]{1,0:T(8,128)S(1)} %add.7.refs_0_), channel_id=1, source_target_pairs={{0,6},{2,4},{4,2},{6,0},{1,7},{3,5},{5,3},{7,1},{8,14},{10,12},{12... | collective-permute-start | bytes 208904 | tf_op jit(solution)/shard_map/ppermute | solution.py:320
  72.8 6.4 %collective-permute-start.12 = (f32[136,128]{1,0:T(8,128)S(1)}, f32[136,128]{1,0:T(8,128)S(1)}, u32[]{:S(2)}, u32[]{:S(2)}) collective-permute-start(f32[136,128]{1,0:T(8,128)S(1)} %add.7.refs_0_), channel_id=1, source_target_pairs={{0,4},{2,6},{4,0},{6,2},{1,5},{3,7},{5,1},{7,3},{8,12},{10,14},{12... | collective-permute-start | bytes 208904 | tf_op jit(solution)/shard_map/ppermute | solution.py:320
  73.4 5.8 %collective-permute-start.11 = (f32[136,128]{1,0:T(8,128)S(1)}, f32[136,128]{1,0:T(8,128)S(1)}, u32[]{:S(2)}, u32[]{:S(2)}) collective-permute-start(f32[136,128]{1,0:T(8,128)S(1)} %add.7.refs_0_), channel_id=1, source_target_pairs={{0,2},{2,0},{4,6},{6,4},{1,3},{3,1},{5,7},{7,5},{8,10},{10,8},{12,... | collective-permute-start | bytes 208904 | tf_op jit(solution)/shard_map/ppermute | solution.py:320
  79.8 11.0 %all-to-all-start.2 = ((f32[16,4,128]{2,1,0:T(4,128)}), f32[16,4,128]{2,1,0:T(4,128)S(1)}, u32[]{:S(2)}, u32[]{:S(2)}) async-start(f32[16,4,128]{2,1,0:T(4,128)} %collect.1), calls=%async_computation.2 | async-start | bytes 65536 | tf_op jit(solution)/shard_map/all_to_all | solution.py:357

commit v9 on v8

--- a/solution.py
+++ b/solution.py
@@ -56,6 +56,8 @@
 
 
 def total(refs, rows):
+    if len(refs) == 1:
+        return refs[0][rows]
     first, second, third, fourth = (ref[rows] for ref in refs)
     return (first + second) + (third + fourth)
 
@@ -89,7 +91,7 @@
     return pl.pallas_call(
         inverse_kernel,
         out_shape=jax.ShapeDtypeStruct(first.shape, F32),
-        in_specs=[VMEM] * 5,
+        in_specs=[VMEM] * (1 + len(parts)),
         out_specs=VMEM,
         compiler_params=pltpu.CompilerParams(vmem_limit_bytes=4 << 20),
         cost_estimate=pl.CostEstimate(flops=3 * 10**9, transcendentals=128, bytes_accessed=2**19),
@@ -196,47 +198,46 @@
     )(at, x, factor_a, factor_c)
 
 
-def parcels_kernel(x_ref, b_ref, b_far_ref, g_ref, g_far_ref, *outs):
-    block, slab = b_ref.shape[0] // 4, g_ref.shape[0] // 4
+def parcels_kernel(near_ref, far_ref, *outs):
+    block = near_ref.shape[0] // 4
     for n, out in enumerate(outs):
         at = pl.ds(n * block, block)
-        out[:block] = b_ref[at] + b_far_ref[at]
-        at = pl.ds(pl.multiple_of((x_ref[0] ^ n) * slab, slab), slab)
-        out[block:] = 0.5 * (g_ref[at] + g_far_ref[at])
-
-
-def parcels(x, b, b_far, g, g_far):
-    shape = jax.ShapeDtypeStruct(((b.shape[0] + g.shape[0]) // 4, b.shape[1]), F32)
+        out[...] = near_ref[at] + far_ref[at]
+
+
+def parcels(near, far):
+    shape = jax.ShapeDtypeStruct((near.shape[0] // 4, near.shape[1]), F32)
     return pl.pallas_call(
         parcels_kernel,
         out_shape=[shape] * 4,
-        in_specs=[SMEM] + [VMEM] * 4,
+        in_specs=[VMEM] * 2,
         out_specs=[VMEM] * 4,
         compiler_params=pltpu.CompilerParams(vmem_limit_bytes=6 << 20),
         name="parcels",
-    )(x, b, b_far, g, g_far)
-
-
-def column_kernel(slab, *refs):
+    )(near, far)
+
+
+def column_kernel(g_ref, g_far_ref, *refs):
     out_ref = refs[-1]
     depth = out_ref.shape[0]
-    block = refs[0].shape[0] - slab
-    some, few = block // depth, slab // depth
+    some, few = refs[0].shape[0] // depth, g_ref.shape[0] // depth
     for z in range(depth):
         out_ref[z, :some] = total(refs[:-1], pl.ds(z * some, some))
-        out_ref[z, some:] = total(refs[:-1], pl.ds(block + z * few, few))
-
-
-def column_sum(parts, depth, slab):
-    rows, rank = parts[0].shape
-    return pl.pallas_call(
-        functools.partial(column_kernel, slab),
+        at = pl.ds(z * few, few)
+        out_ref[z, some:] = g_ref[at] + g_far_ref[at]
+
+
+def column_sum(gram, gram_far, parts, depth):
+    rank = gram.shape[1]
+    rows = parts[0].shape[0] + gram.shape[0]
+    return pl.pallas_call(
+        column_kernel,
         out_shape=jax.ShapeDtypeStruct((depth, rows // depth, rank), F32),
-        in_specs=[VMEM] * 4,
+        in_specs=[VMEM] * 6,
         out_specs=VMEM,
         compiler_params=pltpu.CompilerParams(vmem_limit_bytes=2 << 20),
         name="column_sum",
-    )(*parts)
+    )(gram, gram_far, *parts)
 
 
 def spread_kernel(x_ref, out_ref):
@@ -254,39 +255,35 @@
     )(x)
 
 
-def flatten_kernel(x_ref, out_ref, *, slab):
+def flatten_kernel(x_ref, m_ref, g_ref):
     depth = x_ref.shape[0]
-    block = out_ref.shape[0] - slab
-    some, few = block // depth, slab // depth
+    some, few = m_ref.shape[0] // depth, g_ref.shape[0] // depth
     for z in range(depth):
-        out_ref[z * some : (z + 1) * some] = x_ref[z, :some]
-        at = block + z * few
-        out_ref[at : at + few] = x_ref[z, some:]
-
-
-def flatten(x, slab):
+        m_ref[z * some : (z + 1) * some] = x_ref[z, :some]
+        g_ref[z * few : (z + 1) * few] = x_ref[z, some:]
+
+
+def flatten(x):
     depth, rows, rank = x.shape
     return pl.pallas_call(
-        functools.partial(flatten_kernel, slab=slab),
-        out_shape=jax.ShapeDtypeStruct((depth * rows, rank), F32),
+        flatten_kernel,
+        out_shape=[
+            jax.ShapeDtypeStruct((depth * rows - rank, rank), F32),
+            jax.ShapeDtypeStruct((rank, rank), F32),
+        ],
         in_specs=[VMEM],
-        out_specs=VMEM,
+        out_specs=[VMEM] * 2,
         compiler_params=pltpu.CompilerParams(vmem_limit_bytes=2 << 20),
         name="flatten",
     )(x)
 
 
-def solve_kernel(x_ref, *refs):
-    columns, (h_ref, p_ref, q_ref, g_ref, f_ref, out_ref) = refs[:4], refs[4:]
-    rank = g_ref.shape[0]
-    slab = rank // 4
-    block = columns[0].shape[0] - slab
+def solve_kernel(*refs):
+    columns, (inv_ref, p_ref, q_ref, f_ref, out_ref) = refs[:4], refs[4:]
+    rank = inv_ref.shape[0]
+    block = columns[0].shape[0]
     for n in range(4):
-        at = pl.multiple_of((x_ref[0] ^ n) * slab, slab)
-        g_ref[pl.ds(at, slab)] = columns[n][block:]
-    inverse = spd_inverse(g_ref[...] * h_ref[...], 16)
-    for n in range(4):
-        f = dot(columns[n][:block], inverse)
+        f = dot(columns[n][...], inv_ref[...])
         f_ref[n * block : (n + 1) * block] = f
     f = f_ref[...]
     out_ref[:rank] = lax.dot_general(
@@ -298,21 +295,19 @@
         out_ref[rank + k : rank + k + 1] = jnp.sum(both, axis=0, keepdims=True)
 
 
-def solve(x, columns, gram_c, first, second):
+def solve(columns, inverse, first, second):
     count, rows, rank = first.shape
-    square = jax.ShapeDtypeStruct((rank, rank), F32)
     return pl.pallas_call(
         solve_kernel,
         out_shape=[
-            square,
             jax.ShapeDtypeStruct((rows, rank), F32),
             jax.ShapeDtypeStruct((rank + 8 * pl.cdiv(count, 8), rank), F32),
         ],
-        in_specs=[SMEM] + [VMEM] * 7,
-        out_specs=[VMEM] * 3,
+        in_specs=[VMEM] * 7,
+        out_specs=[VMEM] * 2,
         compiler_params=pltpu.CompilerParams(vmem_limit_bytes=12 << 20),
         name="solve",
-    )(x, *columns, gram_c, first, second)
+    )(*columns, inverse, first, second)
 
 
 def swap(x, axis, bit=1):
@@ -337,13 +332,15 @@
     p_other, b_other = contract(jnp.stack([1 - core, x]), flat, a_hbm, c_hbm, half)
     p_mine, b_mine = contract(jnp.stack([core, x]), flat, a_hbm, c_hbm, half)
     gram_part = dot(factor_a.T, factor_a)
-    at = x.reshape(1)
-    sent = parcels(at, b_mine, swap(b_other, "c"), gram_part, swap(gram_part, "c"))
+    gram_part = gram_part + swap(gram_part, "c")
+    sent = parcels(b_mine, swap(b_other, "c"))
     got = [sent[0]] + [swap(sent[n], RING, n) for n in (1, 2, 3)]
-    column = spread(lax.all_to_all(column_sum(got, depth, rank // 4), "z", 0, 0))
-    column = flatten(lax.all_to_all(column, "z", 0, 0), rank // 4)
+    column = column_sum(gram_part, swap(gram_part, "xl"), got, depth)
+    column = spread(lax.all_to_all(column, "z", 0, 0))
+    column, gram_a = flatten(lax.all_to_all(column, "z", 0, 0))
     columns = [column] + [swap(column, RING, n) for n in (1, 2, 3)]
-    gram_a, f_mine, sums = solve(at, columns, gram_c, p_mine, swap(p_other, "c"))
+    inverse = inverse_of_product(gram_a, [gram_c])
+    f_mine, sums = solve(columns, inverse, p_mine, swap(p_other, "c"))
 
     sums = sums + swap(sums, "c")
     sums, f_mine = lax.optimization_barrier((sums, f_mine))

time: 91.8 us -> 88.7 us (0.966)
  waiting for transfers between devices: 21.8 us -> 14.9 us
  starting transfers between devices: 16.4 us -> 19.5 us
    ppermute x14 -> x15, waiting for transfers between devices: 18.3 us -> 11.4 us  [swap(): return lax.ppermute(x, axis, [(i, i ^ bit) for i in range(n)])]
    pallas_call x4, Pallas kernels: 5.51 us -> 1.49 us  [the longest x1 1.37 us: solve(): pl.pallas_call(solve_kernel, out_shape=[jax.ShapeDtypeStruct((rows, rank)...]
    pallas_call x1 -> x2, Pallas kernels: 3.93 us -> 7.86 us  [inverse_of_product(): pl.pallas_call(inverse_kernel, out_shape=jax.ShapeDtypeStruct(first.shape...]
    ppermute x14 -> x15, starting transfers between devices: 13 us -> 15.3 us  [swap(): return lax.ppermute(x, axis, [(i, i ^ bit) for i in range(n)])]
  transfers between devices with their start and end apart: 15 -> 16, of which waited for: 8 -> 6; matrix products, arithmetic and copies ran while one was open for 0% -> 0% of each run, Pallas kernels for 11% -> 16%
where the time goes in v9:
time: 88.7 us; the launch traced here: 88.4 us
  blocking collectives  30.7 us (35%)
  Pallas kernels  21.2 us (24%)
  starting transfers between devices  19.5 us (22%)
  waiting for transfers between devices  14.9 us (17%)
  matrix products  1.13 us (1%)
    all_to_all x1, blocking collectives, body(): column = spread(lax.all_to_all(column, 'z', 0, 0))  18.5 us
    ppermute x15, starting transfers between devices, swap(): return lax.ppermute(x, axis, [(i, i ^ bit) for i in range(n)])  15.3 us
    all_to_all x1, blocking collectives, body(): column, gram_a = flatten(lax.all_to_all(column, 'z', 0, 0))  12.2 us
    ppermute x15, waiting for transfers between devices, swap(): return lax.ppermute(x, axis, [(i, i ^ bit) for i in range(n)])  11.4 us
    pallas_call x2, Pallas kernels, contract(): pl.pallas_call(functools.partial(contract_kernel, chunk), out_shape=[jax....  9.64 us
    pallas_call x2, Pallas kernels, inverse_of_product(): pl.pallas_call(inverse_kernel, out_shape=jax.ShapeDtypeStruct(first.shape...  7.86 us
    all_to_all x1, starting transfers between devices, body(): mttkrp_c = jnp.sum(lax.all_to_all(spread_c, plane, 0, 0), axis=0)  4.19 us
    all_to_all x1, waiting for transfers between devices, body(): mttkrp_c = jnp.sum(lax.all_to_all(spread_c, plane, 0, 0), axis=0)  3.55 us
  transfers between devices with their start and end apart: 16, of which 6 were waited for; matrix products, arithmetic and copies ran while one was open for 0% of the time, Pallas kernels for 16%

profile of v9, /device:TPU:2, one launch (start us, length us, event | category | flops | bytes accessed | tf_op | source)
XLA Modules:
  0.0 88.4 jit_solution(11431885223254494514)
XLA Ops:
  0.6 0.1 pad_add_fusion
  0.7 0.0 copy-start.1
  0.7 4.8 %contract.3 = (f32[4,1024,128]{2,1,0:T(8,128)S(1)}, f32[1024,128]{1,0:T(8,128)S(1)}) custom-call(s32[2]{0:T(128)S(1)} %get-tuple-element.35.at_ref, f32[16384,128]{1,0:T(8,128)} %bitcast.17, f32[256,128]{1,0:T(8,128)} %a_hbm.3, f32[4,128]{1,0:T(4,128)} %c_hbm.3), custom_call_target="tpu_custom_call" | custom-call | flops 2147483648 | bytes 6291456 | tf_op jit(solution)/shard_map/contract/pallas_call | solution.py:176
  5.6 0.1 collective-permute-start.9
  5.7 0.5 collective-permute-start.2
  6.2 0.0 copy-done.1
  6.2 0.4 fusion
  6.5 0.2 collective-permute-start
  6.7 4.8 %contract.2 = (f32[4,1024,128]{2,1,0:T(8,128)S(1)}, f32[1024,128]{1,0:T(8,128)S(1)}) custom-call(s32[2]{0:T(128)S(1)} %get-tuple-element.34.at_ref, f32[16384,128]{1,0:T(8,128)} %bitcast.18, f32[256,128]{1,0:T(8,128)} %a_hbm.3, f32[4,128]{1,0:T(4,128)} %c_hbm.3), custom_call_target="tpu_custom_call" | custom-call | flops 2147483648 | bytes 6291456 | tf_op jit(solution)/shard_map/contract/pallas_call | solution.py:176
  11.5 0.0 copy-start
  11.6 0.0 collective-permute-done.2.far_ref
  11.6 0.1 parcels.1
  11.6 2.2 %collective-permute-start.3 = (f32[256,128]{1,0:T(8,128)S(1)}, f32[256,128]{1,0:T(8,128)S(1)}, u32[]{:S(2)}, u32[]{:S(2)}) collective-permute-start(f32[256,128]{1,0:T(8,128)S(1)} %get-tuple-element.21), channel_id=1, source_target_pairs={{0,1},{1,0},{16,17},{17,16},{2,3},{3,2},{18,19},{19,18},{4,5},{5,4... | collective-permute-start | bytes 393224 | tf_op jit(solution)/shard_map/ppermute | solution.py:315
  13.9 1.4 %collective-permute-start.4 = (f32[256,128]{1,0:T(8,128)S(1)}, f32[256,128]{1,0:T(8,128)S(1)}, u32[]{:S(2)}, u32[]{:S(2)}) collective-permute-start(f32[256,128]{1,0:T(8,128)S(1)} %get-tuple-element.22), channel_id=1, source_target_pairs={{0,16},{1,17},{16,0},{17,1},{2,18},{3,19},{18,2},{19,3},{4,20},{5,... | collective-permute-start | bytes 393224 | tf_op jit(solution)/shard_map/ppermute | solution.py:315
  15.3 0.5 collective-permute-start.5
  15.8 0.0 collective-permute-done
  15.8 2.4 %collective-permute-start.1 = (f32[128,128]{1,0:T(8,128)S(1)}, f32[128,128]{1,0:T(8,128)S(1)}, u32[]{:S(2)}, u32[]{:S(2)}) collective-permute-start(f32[128,128]{1,0:T(8,128)S(1)} %add.9.g_ref), channel_id=1, source_target_pairs={{0,16},{16,0},{1,17},{17,1},{2,18},{18,2},{3,19},{19,3},{4,20},{20... | collective-permute-start | bytes 196616 | tf_op jit(solution)/shard_map/ppermute | solution.py:315
  18.2 5.1 %collective-permute-done.1.g_far_ref = f32[128,128]{1,0:T(8,128)S(1)} collective-permute-done((f32[128,128]{1,0:T(8,128)S(1)}, f32[128,128]{1,0:T(8,128)S(1)}, u32[]{:S(2)}, u32[]{:S(2)}) %collective-permute-start.1) | collective-permute-done | bytes 65568 | tf_op jit(solution)/shard_map/ppermute | solution.py:315
  23.3 0.0 collective-permute-done.3.refs_1_
  23.3 0.0 collective-permute-done.4.refs_2_
  23.3 0.0 collective-permute-done.5.refs_3_
  23.4 18.5 %all_to_all.15.x_ref = f32[8,48,128]{2,1,0:T(8,128)S(1)} all-to-all(f32[8,48,128]{2,1,0:T(8,128)S(1)} %column_sum.1), channel_id=1, replica_groups=mesh['z'=8,'xl'=2,'c'=2,'y'=4,'xh'=2] {'z'}, dimensions={0} | all-to-all | bytes 393216 | tf_op jit(solution)/shard_map/all_to_all | solution.py:339
  42.0 12.2 %all_to_all.16.x_ref = f32[8,48,128]{2,1,0:T(8,128)S(1)} all-to-all(f32[8,48,128]{2,1,0:T(8,128)S(1)} %spread.1), channel_id=1, replica_groups=mesh['z'=8,'xl'=2,'c'=2,'y'=4,'xh'=2] {'z'}, dimensions={0} | all-to-all | bytes 393216 | tf_op jit(solution)/shard_map/all_to_all | solution.py:340
  54.2 0.6 collective-permute-start.8
  54.7 1.7 %collective-permute-start.7 = (f32[256,128]{1,0:T(8,128)S(1)}, f32[256,128]{1,0:T(8,128)S(1)}, u32[]{:S(2)}, u32[]{:S(2)}) collective-permute-start(f32[256,128]{1,0:T(8,128)S(1)} %get-tuple-element.24.refs_0_), channel_id=1, source_target_pairs={{0,16},{1,17},{16,0},{17,1},{2,18},{3,19},{18,2},{19,3},{4,20},{5,... | collective-permute-start | bytes 393224 | tf_op jit(solution)/shard_map/ppermute | solution.py:315
  56.4 1.3 %collective-permute-start.6 = (f32[256,128]{1,0:T(8,128)S(1)}, f32[256,128]{1,0:T(8,128)S(1)}, u32[]{:S(2)}, u32[]{:S(2)}) collective-permute-start(f32[256,128]{1,0:T(8,128)S(1)} %get-tuple-element.24.refs_0_), channel_id=1, source_target_pairs={{0,1},{1,0},{16,17},{17,16},{2,3},{3,2},{18,19},{19,18},{4,5},{5,4... | collective-permute-start | bytes 393224 | tf_op jit(solution)/shard_map/ppermute | solution.py:315
  57.7 0.0 copy-done
  57.7 3.9 %inverse_of_product.2.refs_4_ = f32[128,128]{1,0:T(8,128)S(1)} custom-call(f32[128,128]{1,0:T(8,128)S(1)} %get-tuple-element.25.first_ref, f32[128,128]{1,0:T(8,128)S(1)} %copy-done), custom_call_target="tpu_custom_call" | custom-call | flops 3000000000 | bytes 524288 | tf_op jit(solution)/shard_map/inverse_of_product/pallas_call | solution.py:91
  61.7 0.0 collective-permute-done.8.refs_3_
  61.7 0.0 collective-permute-done.7.refs_2_
  61.7 1.2 %collective-permute-done.6.refs_1_ = f32[256,128]{1,0:T(8,128)S(1)} collective-permute-done((f32[256,128]{1,0:T(8,128)S(1)}, f32[256,128]{1,0:T(8,128)S(1)}, u32[]{:S(2)}, u32[]{:S(2)}) %collective-permute-start.6) | collective-permute-done | bytes 131104 | tf_op jit(solution)/shard_map/ppermute | solution.py:315
  62.9 0.0 collective-permute-done.9.refs_6_
  62.9 1.4 %solve.1 = (f32[1024,128]{1,0:T(8,128)S(1)}, f32[136,128]{1,0:T(8,128)S(1)}) custom-call(f32[256,128]{1,0:T(8,128)S(1)} %get-tuple-element.24.refs_0_, f32[256,128]{1,0:T(8,128)S(1)} %collective-permute-done.6.refs_1_, f32[256,128]{1,0:T(8,128)S(1)} %collective-permute-done.7.refs_2_, f32[256,128]{1,0:T(8,128)S(1)} %collective-permute-done.8.refs_3_, ...), custom_call_target="tpu_custom_call" | custom-call | tf_op jit(solution)/shard_map/solve/pallas_call | solution.py:300
  64.3 0.1 collective-permute-start.10
  64.4 1.2 %collective-permute-done.10 = f32[136,128]{1,0:T(8,128)S(1)} collective-permute-done((f32[136,128]{1,0:T(8,128)S(1)}, f32[136,128]{1,0:T(8,128)S(1)}, u32[]{:S(2)}, u32[]{:S(2)}) %collective-permute-start.10) | collective-permute-done | bytes 69664 | tf_op jit(solution)/shard_map/ppermute | solution.py:315
  65.7 0.2 collective-permute-start.11
  65.9 3.0 %collective-permute-start.14 = (f32[136,128]{1,0:T(8,128)S(1)}, f32[136,128]{1,0:T(8,128)S(1)}, u32[]{:S(2)}, u32[]{:S(2)}) collective-permute-start(f32[136,128]{1,0:T(8,128)S(1)} %add.11.refs_0_), channel_id=1, source_target_pairs={{0,6},{2,4},{4,2},{6,0},{1,7},{3,5},{5,3},{7,1},{8,14},{10,12},{12... | collective-permute-start | bytes 208904 | tf_op jit(solution)/shard_map/ppermute | solution.py:315
  68.9 0.6 collective-permute-start.13
  69.6 0.4 collective-permute-start.12
  70.0 0.0 collective-permute-done.11
  70.0 1.6 %assemble.1 = f32[8,256,128]{2,1,0:T(8,128)} custom-call(s32[2]{0:T(128)S(1)} %get-tuple-element.34.at_ref, f32[4,256,128]{2,1,0:T(8,128)S(1)} %bitcast.15, f32[4,256,128]{2,1,0:T(8,128)S(1)} %bitcast.16), custom_call_target="tpu_custom_call" | custom-call | tf_op jit(solution)/shard_map/assemble/pallas_call | solution.py:110
  71.6 0.8 collective-permute-done.14.refs_3_
  72.4 2.9 %collective-permute-done.13.refs_2_ = f32[136,128]{1,0:T(8,128)S(1)} collective-permute-done((f32[136,128]{1,0:T(8,128)S(1)}, f32[136,128]{1,0:T(8,128)S(1)}, u32[]{:S(2)}, u32[]{:S(2)}) %collective-permute-start.13) | collective-permute-done | bytes 69664 | tf_op jit(solution)/shard_map/ppermute | solution.py:315
  75.3 0.0 collective-permute-done.12.refs_1_
  75.3 0.6 collect.1
  75.9 4.2 %all-to-all-start.2 = ((f32[16,4,128]{2,1,0:T(4,128)}), f32[16,4,128]{2,1,0:T(4,128)S(1)}, u32[]{:S(2)}, u32[]{:S(2)}) async-start(f32[16,4,128]{2,1,0:T(4,128)} %collect.1), calls=%async_computation.2 | async-start | bytes 65536 | tf_op jit(solution)/shard_map/all_to_all | solution.py:354
  80.1 3.9 %inverse_of_product.3 = f32[128,128]{1,0:T(8,128)S(1)} custom-call(f32[128,128]{1,0:T(8,128)S(1)} %get-tuple-element.25.first_ref, f32[136,128]{1,0:T(8,128)S(1)} %add.11.refs_0_, f32[136,128]{1,0:T(8,128)S(1)} %collective-permute-done.12.refs_1_, f32[136,128]{1,0:T(8,128)S(1)} %collective-permute-done.13.refs_2_, f32[136,128]{1,0:T(8,128)S(1)} %collective-permute-done.14.refs_3_), custom_call_target="tpu_custom_call" | custom-call | flops 3000000000 | bytes 524288 | tf_op jit(solution)/shard_map/inverse_of_product/pallas_call | solution.py:91
  84.1 3.5 %all-to-all-done.2 = f32[16,4,128]{2,1,0:T(4,128)S(1)} async-done(((f32[16,4,128]{2,1,0:T(4,128)}), f32[16,4,128]{2,1,0:T(4,128)S(1)}, u32[]{:S(2)}, u32[]{:S(2)}) %all-to-all-start.2) | async-done | bytes 32800 | tf_op jit(solution)/shard_map/all_to_all | solution.py:354
  87.7 0.7 fusion.1
  (6 shorter events, 0.1 us)
Async XLA Ops:
  0.7 5.4 %copy-start.1 = (f32[256,128]{1,0:T(8,128)S(1)}, f32[256,128]{1,0:T(8,128)}, u32[]{:S(2)}) copy-start(f32[256,128]{1,0:T(8,128)} %a_hbm.3) | copy-start | bytes 393220
  5.6 57.4 %collective-permute-start.9 = (f32[4,1024,128]{2,1,0:T(8,128)S(1)}, f32[4,1024,128]{2,1,0:T(8,128)S(1)}, u32[]{:S(2)}, u32[]{:S(2)}) collective-permute-start(f32[4,1024,128]{2,1,0:T(8,128)S(1)} %get-tuple-element.27), channel_id=1, source_target_pairs={{0,8},{8,0},{1,9},{9,1},{2,10},{10,2},{3,11},{11,3},{4,12},{12,4},... | collective-permute-start | bytes 6291464 | tf_op jit(solution)/shard_map/ppermute | solution.py:315
  5.7 5.9 %collective-permute-start.2 = (f32[1024,128]{1,0:T(8,128)S(1)}, f32[1024,128]{1,0:T(8,128)S(1)}, u32[]{:S(2)}, u32[]{:S(2)}) collective-permute-start(f32[1024,128]{1,0:T(8,128)S(1)} %get-tuple-element.19), channel_id=1, source_target_pairs={{0,8},{8,0},{1,9},{9,1},{2,10},{10,2},{3,11},{11,3},{4,12},{12,4},... | collective-permute-start | bytes 1572872 | tf_op jit(solution)/shard_map/ppermute | solution.py:315
  6.5 9.3 %collective-permute-start = (f32[128,128]{1,0:T(8,128)S(1)}, f32[128,128]{1,0:T(8,128)S(1)}, u32[]{:S(2)}, u32[]{:S(2)}) collective-permute-start(f32[128,128]{1,0:T(8,128)S(1)} %fusion), channel_id=1, source_target_pairs={{0,8},{8,0},{1,9},{9,1},{2,10},{10,2},{3,11},{11,3},{4,12},{12,4},... | collective-permute-start | bytes 196616 | tf_op jit(solution)/shard_map/ppermute | solution.py:315
  11.5 46.2 %copy-start = (f32[128,128]{1,0:T(8,128)S(1)}, f32[128,128]{1,0:T(8,128)}, u32[]{:S(2)}) copy-start(f32[128,128]{1,0:T(8,128)} %refs_0_.1) | copy-start | bytes 196612
  11.6 11.7 %collective-permute-start.3 = (f32[256,128]{1,0:T(8,128)S(1)}, f32[256,128]{1,0:T(8,128)S(1)}, u32[]{:S(2)}, u32[]{:S(2)}) collective-permute-start(f32[256,128]{1,0:T(8,128)S(1)} %get-tuple-element.21), channel_id=1, source_target_pairs={{0,1},{1,0},{16,17},{17,16},{2,3},{3,2},{18,19},{19,18},{4,5},{5,4... | collective-permute-start | bytes 393224 | tf_op jit(solution)/shard_map/ppermute | solution.py:315
  13.9 9.5 %collective-permute-start.4 = (f32[256,128]{1,0:T(8,128)S(1)}, f32[256,128]{1,0:T(8,128)S(1)}, u32[]{:S(2)}, u32[]{:S(2)}) collective-permute-start(f32[256,128]{1,0:T(8,128)S(1)} %get-tuple-element.22), channel_id=1, source_target_pairs={{0,16},{1,17},{16,0},{17,1},{2,18},{3,19},{18,2},{19,3},{4,20},{5,... | collective-permute-start | bytes 393224 | tf_op jit(solution)/shard_map/ppermute | solution.py:315
  15.3 8.1 %collective-permute-start.5 = (f32[256,128]{1,0:T(8,128)S(1)}, f32[256,128]{1,0:T(8,128)S(1)}, u32[]{:S(2)}, u32[]{:S(2)}) collective-permute-start(f32[256,128]{1,0:T(8,128)S(1)} %get-tuple-element.23), channel_id=1, source_target_pairs={{0,17},{1,16},{16,1},{17,0},{2,19},{3,18},{18,3},{19,2},{4,21},{5,... | collective-permute-start | bytes 393224 | tf_op jit(solution)/shard_map/ppermute | solution.py:315
  15.8 7.5 %collective-permute-start.1 = (f32[128,128]{1,0:T(8,128)S(1)}, f32[128,128]{1,0:T(8,128)S(1)}, u32[]{:S(2)}, u32[]{:S(2)}) collective-permute-start(f32[128,128]{1,0:T(8,128)S(1)} %add.9.g_ref), channel_id=1, source_target_pairs={{0,16},{16,0},{1,17},{17,1},{2,18},{18,2},{3,19},{19,3},{4,20},{20... | collective-permute-start | bytes 196616 | tf_op jit(solution)/shard_map/ppermute | solution.py:315
  54.2 7.5 %collective-permute-start.8 = (f32[256,128]{1,0:T(8,128)S(1)}, f32[256,128]{1,0:T(8,128)S(1)}, u32[]{:S(2)}, u32[]{:S(2)}) collective-permute-start(f32[256,128]{1,0:T(8,128)S(1)} %get-tuple-element.24.refs_0_), channel_id=1, source_target_pairs={{0,17},{1,16},{16,1},{17,0},{2,19},{3,18},{18,3},{19,2},{4,21},{5,... | collective-permute-start | bytes 393224 | tf_op jit(solution)/shard_map/ppermute | solution.py:315
  54.7 6.9 %collective-permute-start.7 = (f32[256,128]{1,0:T(8,128)S(1)}, f32[256,128]{1,0:T(8,128)S(1)}, u32[]{:S(2)}, u32[]{:S(2)}) collective-permute-start(f32[256,128]{1,0:T(8,128)S(1)} %get-tuple-element.24.refs_0_), channel_id=1, source_target_pairs={{0,16},{1,17},{16,0},{17,1},{2,18},{3,19},{18,2},{19,3},{4,20},{5,... | collective-permute-start | bytes 393224 | tf_op jit(solution)/shard_map/ppermute | solution.py:315
  56.4 6.5 %collective-permute-start.6 = (f32[256,128]{1,0:T(8,128)S(1)}, f32[256,128]{1,0:T(8,128)S(1)}, u32[]{:S(2)}, u32[]{:S(2)}) collective-permute-start(f32[256,128]{1,0:T(8,128)S(1)} %get-tuple-element.24.refs_0_), channel_id=1, source_target_pairs={{0,1},{1,0},{16,17},{17,16},{2,3},{3,2},{18,19},{19,18},{4,5},{5,4... | collective-permute-start | bytes 393224 | tf_op jit(solution)/shard_map/ppermute | solution.py:315
  64.3 1.3 %collective-permute-start.10 = (f32[136,128]{1,0:T(8,128)S(1)}, f32[136,128]{1,0:T(8,128)S(1)}, u32[]{:S(2)}, u32[]{:S(2)}) collective-permute-start(f32[136,128]{1,0:T(8,128)S(1)} %get-tuple-element.28), channel_id=1, source_target_pairs={{0,8},{8,0},{1,9},{9,1},{2,10},{10,2},{3,11},{11,3},{4,12},{12,4},... | collective-permute-start | bytes 208904 | tf_op jit(solution)/shard_map/ppermute | solution.py:315
  65.7 4.3 %collective-permute-start.11 = (f32[1024,128]{1,0:T(8,128)S(1)}, f32[1024,128]{1,0:T(8,128)S(1)}, u32[]{:S(2)}, u32[]{:S(2)}) collective-permute-start(f32[1024,128]{1,0:T(8,128)S(1)} %get-tuple-element.31), channel_id=1, source_target_pairs={{0,8},{8,0},{1,9},{9,1},{2,10},{10,2},{3,11},{11,3},{4,12},{12,4},... | collective-permute-start | bytes 1572872 | tf_op jit(solution)/shard_map/ppermute | solution.py:315
  65.9 6.5 %collective-permute-start.14 = (f32[136,128]{1,0:T(8,128)S(1)}, f32[136,128]{1,0:T(8,128)S(1)}, u32[]{:S(2)}, u32[]{:S(2)}) collective-permute-start(f32[136,128]{1,0:T(8,128)S(1)} %add.11.refs_0_), channel_id=1, source_target_pairs={{0,6},{2,4},{4,2},{6,0},{1,7},{3,5},{5,3},{7,1},{8,14},{10,12},{12... | collective-permute-start | bytes 208904 | tf_op jit(solution)/shard_map/ppermute | solution.py:315
  68.9 6.4 %collective-permute-start.13 = (f32[136,128]{1,0:T(8,128)S(1)}, f32[136,128]{1,0:T(8,128)S(1)}, u32[]{:S(2)}, u32[]{:S(2)}) collective-permute-start(f32[136,128]{1,0:T(8,128)S(1)} %add.11.refs_0_), channel_id=1, source_target_pairs={{0,4},{2,6},{4,0},{6,2},{1,5},{3,7},{5,1},{7,3},{8,12},{10,14},{12... | collective-permute-start | bytes 208904 | tf_op jit(solution)/shard_map/ppermute | solution.py:315
  69.6 5.8 %collective-permute-start.12 = (f32[136,128]{1,0:T(8,128)S(1)}, f32[136,128]{1,0:T(8,128)S(1)}, u32[]{:S(2)}, u32[]{:S(2)}) collective-permute-start(f32[136,128]{1,0:T(8,128)S(1)} %add.11.refs_0_), channel_id=1, source_target_pairs={{0,2},{2,0},{4,6},{6,4},{1,3},{3,1},{5,7},{7,5},{8,10},{10,8},{12,... | collective-permute-start | bytes 208904 | tf_op jit(solution)/shard_map/ppermute | solution.py:315
  75.9 11.7 %all-to-all-start.2 = ((f32[16,4,128]{2,1,0:T(4,128)}), f32[16,4,128]{2,1,0:T(4,128)S(1)}, u32[]{:S(2)}, u32[]{:S(2)}) async-start(f32[16,4,128]{2,1,0:T(4,128)} %collect.1), calls=%async_computation.2 | async-start | bytes 65536 | tf_op jit(solution)/shard_map/all_to_all | solution.py:354

commit v10 on v9

--- a/solution.py
+++ b/solution.py
@@ -58,24 +58,30 @@
 def total(refs, rows):
     if len(refs) == 1:
         return refs[0][rows]
+    if len(refs) == 2:
+        return refs[0][rows] + refs[1][rows]
     first, second, third, fourth = (ref[rows] for ref in refs)
     return (first + second) + (third + fourth)
 
 
 def collect_kernel(*refs):
-    out_ref = refs[-1]
+    parts, (out_ref, g_ref) = refs[:4], refs[4:]
     count, rank = out_ref.shape[1:]
-    part = total(refs[:-1], pl.ds(rank, count))
+    part = total(parts, pl.ds(rank, count))
     out_ref[...] = jnp.broadcast_to(part[None], out_ref.shape)
+    g_ref[...] = total(parts, pl.ds(0, rank))
 
 
 def collect(parts, copies, count):
     rank = parts[0].shape[1]
     return pl.pallas_call(
         collect_kernel,
-        out_shape=jax.ShapeDtypeStruct((copies, count, rank), F32),
+        out_shape=[
+            jax.ShapeDtypeStruct((copies, count, rank), F32),
+            jax.ShapeDtypeStruct((rank, rank), F32),
+        ],
         in_specs=[VMEM] * 4,
-        out_specs=VMEM,
+        out_specs=[VMEM] * 2,
         compiler_params=pltpu.CompilerParams(vmem_limit_bytes=2 << 20),
         name="collect",
     )(*parts)
@@ -342,17 +348,16 @@
     inverse = inverse_of_product(gram_a, [gram_c])
     f_mine, sums = solve(columns, inverse, p_mine, swap(p_other, "c"))
 
-    sums = sums + swap(sums, "c")
-    sums, f_mine = lax.optimization_barrier((sums, f_mine))
     parts = [sums] + [swap(sums, "y", bit) for bit in (1, 2, 3)]
     shape = (4, half // 4, rank)
     f_other = swap(f_mine, "c").reshape(shape)
     factor_b = assemble(jnp.stack([core, x]), f_mine.reshape(shape), f_other)
     parts[0], factor_b = lax.optimization_barrier((parts[0], factor_b))
-    plane = ("z", "xl")
-    spread_c = collect(parts, lax.axis_size(plane), mode_three)
-    mttkrp_c = jnp.sum(lax.all_to_all(spread_c, plane, 0, 0), axis=0)
-    factor_c_new = dot(mttkrp_c, inverse_of_product(gram_a, parts))
+    split = ("z", "xl", "c")
+    spread_c, gram_b = collect(parts, lax.axis_size(split), mode_three)
+    gram_far = swap(gram_b, "c")
+    mttkrp_c = jnp.sum(lax.all_to_all(spread_c, split, 0, 0), axis=0)
+    factor_c_new = dot(mttkrp_c, inverse_of_product(gram_a, [gram_b, gram_far]))
     return (factor_b.reshape(mode_two, rank), factor_c_new)
 
 

time: 88.7 us -> 89.5 us (level); the launches traced: 88.4 us -> 87.9 us
    ppermute x15, waiting for transfers between devices: 11.4 us -> 10.2 us  [swap(): return lax.ppermute(x, axis, [(i, i ^ bit) for i in range(n)])]
  transfers between devices with their start and end apart: 16 -> 16, of which waited for: 6 -> 5; matrix products, arithmetic and copies ran while one was open for 0% -> 1% of each run, Pallas kernels for 16% -> 16%
where the time goes in v10:
time: 89.5 us; the launch traced here: 87.9 us
  blocking collectives  30.7 us (34%)
  Pallas kernels  21.2 us (24%)
  starting transfers between devices  19.6 us (22%)
  waiting for transfers between devices  14.2 us (16%)
  matrix products  1.13 us (1%)
    all_to_all x1, blocking collectives, body(): column = spread(lax.all_to_all(column, 'z', 0, 0))  18.5 us
    ppermute x15, starting transfers between devices, swap(): return lax.ppermute(x, axis, [(i, i ^ bit) for i in range(n)])  15.2 us
    all_to_all x1, blocking collectives, body(): column, gram_a = flatten(lax.all_to_all(column, 'z', 0, 0))  12.2 us
    ppermute x15, waiting for transfers between devices, swap(): return lax.ppermute(x, axis, [(i, i ^ bit) for i in range(n)])  10.2 us
    pallas_call x2, Pallas kernels, contract(): pl.pallas_call(functools.partial(contract_kernel, chunk), out_shape=[jax....  9.63 us
    pallas_call x2, Pallas kernels, inverse_of_product(): pl.pallas_call(inverse_kernel, out_shape=jax.ShapeDtypeStruct(first.shape...  7.85 us
    all_to_all x1, starting transfers between devices, body(): mttkrp_c = jnp.sum(lax.all_to_all(spread_c, split, 0, 0), axis=0)  4.42 us
    all_to_all x1, waiting for transfers between devices, body(): mttkrp_c = jnp.sum(lax.all_to_all(spread_c, split, 0, 0), axis=0)  4.01 us
  transfers between devices with their start and end apart: 16, of which 5 were waited for; matrix products, arithmetic and copies ran while one was open for 1% of the time, Pallas kernels for 16%

profile of v10, /device:TPU:2, one launch (start us, length us, event | category | flops | bytes accessed | tf_op | source)
XLA Modules:
  0.0 87.9 jit_solution(5200585872724988690)
XLA Ops:
  0.6 0.1 pad_add_fusion.1.at_ref
  0.7 0.0 copy-start.1
  0.7 4.8 %contract.3 = (f32[4,1024,128]{2,1,0:T(8,128)S(1)}, f32[1024,128]{1,0:T(8,128)S(1)}) custom-call(s32[2]{0:T(128)S(1)} %pad_add_fusion.1.at_ref, f32[16384,128]{1,0:T(8,128)} %bitcast.17, f32[256,128]{1,0:T(8,128)} %a_hbm.3, f32[4,128]{1,0:T(4,128)} %c_hbm.3), custom_call_target="tpu_custom_call" | custom-call | flops 2147483648 | bytes 6291456 | tf_op jit(solution)/shard_map/contract/pallas_call | solution.py:182
  5.5 0.1 collective-permute-start.9
  5.6 0.5 collective-permute-start.2
  6.1 0.0 copy-done.1
  6.1 0.4 fusion
  6.5 0.2 collective-permute-start
  6.7 0.1 pad_add_fusion.at_ref
  6.8 4.8 %contract.2 = (f32[4,1024,128]{2,1,0:T(8,128)S(1)}, f32[1024,128]{1,0:T(8,128)S(1)}) custom-call(s32[2]{0:T(128)S(1)} %pad_add_fusion.at_ref, f32[16384,128]{1,0:T(8,128)} %bitcast.18, f32[256,128]{1,0:T(8,128)} %a_hbm.3, f32[4,128]{1,0:T(4,128)} %c_hbm.3), custom_call_target="tpu_custom_call" | custom-call | flops 2147483648 | bytes 6291456 | tf_op jit(solution)/shard_map/contract/pallas_call | solution.py:182
  11.6 0.0 copy-start
  11.6 0.0 collective-permute-done.2.far_ref
  11.6 0.1 parcels.1
  11.7 2.2 %collective-permute-start.3 = (f32[256,128]{1,0:T(8,128)S(1)}, f32[256,128]{1,0:T(8,128)S(1)}, u32[]{:S(2)}, u32[]{:S(2)}) collective-permute-start(f32[256,128]{1,0:T(8,128)S(1)} %get-tuple-element.21), channel_id=1, source_target_pairs={{0,1},{1,0},{16,17},{17,16},{2,3},{3,2},{18,19},{19,18},{4,5},{5,4... | collective-permute-start | bytes 393224 | tf_op jit(solution)/shard_map/ppermute | solution.py:321
  13.9 1.4 %collective-permute-start.4 = (f32[256,128]{1,0:T(8,128)S(1)}, f32[256,128]{1,0:T(8,128)S(1)}, u32[]{:S(2)}, u32[]{:S(2)}) collective-permute-start(f32[256,128]{1,0:T(8,128)S(1)} %get-tuple-element.22), channel_id=1, source_target_pairs={{0,16},{1,17},{16,0},{17,1},{2,18},{3,19},{18,2},{19,3},{4,20},{5,... | collective-permute-start | bytes 393224 | tf_op jit(solution)/shard_map/ppermute | solution.py:321
  15.3 0.5 collective-permute-start.5
  15.9 0.0 collective-permute-done
  15.9 2.4 %collective-permute-start.1 = (f32[128,128]{1,0:T(8,128)S(1)}, f32[128,128]{1,0:T(8,128)S(1)}, u32[]{:S(2)}, u32[]{:S(2)}) collective-permute-start(f32[128,128]{1,0:T(8,128)S(1)} %add.6.g_ref), channel_id=1, source_target_pairs={{0,16},{16,0},{1,17},{17,1},{2,18},{18,2},{3,19},{19,3},{4,20},{20... | collective-permute-start | bytes 196616 | tf_op jit(solution)/shard_map/ppermute | solution.py:321
  18.3 5.1 %collective-permute-done.1.g_far_ref = f32[128,128]{1,0:T(8,128)S(1)} collective-permute-done((f32[128,128]{1,0:T(8,128)S(1)}, f32[128,128]{1,0:T(8,128)S(1)}, u32[]{:S(2)}, u32[]{:S(2)}) %collective-permute-start.1) | collective-permute-done | bytes 65568 | tf_op jit(solution)/shard_map/ppermute | solution.py:321
  23.4 0.0 collective-permute-done.3.refs_1_
  23.4 0.0 collective-permute-done.4.refs_2_
  23.4 0.0 collective-permute-done.5.refs_3_
  23.5 18.5 %all_to_all.15.x_ref = f32[8,48,128]{2,1,0:T(8,128)S(1)} all-to-all(f32[8,48,128]{2,1,0:T(8,128)S(1)} %column_sum.1), channel_id=1, replica_groups=mesh['z'=8,'xl'=2,'c'=2,'y'=4,'xh'=2] {'z'}, dimensions={0} | all-to-all | bytes 393216 | tf_op jit(solution)/shard_map/all_to_all | solution.py:345
  42.0 12.2 %all_to_all.16.x_ref = f32[8,48,128]{2,1,0:T(8,128)S(1)} all-to-all(f32[8,48,128]{2,1,0:T(8,128)S(1)} %spread.1), channel_id=1, replica_groups=mesh['z'=8,'xl'=2,'c'=2,'y'=4,'xh'=2] {'z'}, dimensions={0} | all-to-all | bytes 393216 | tf_op jit(solution)/shard_map/all_to_all | solution.py:346
  54.2 0.6 collective-permute-start.8
  54.8 1.7 %collective-permute-start.7 = (f32[256,128]{1,0:T(8,128)S(1)}, f32[256,128]{1,0:T(8,128)S(1)}, u32[]{:S(2)}, u32[]{:S(2)}) collective-permute-start(f32[256,128]{1,0:T(8,128)S(1)} %get-tuple-element.24.refs_0_), channel_id=1, source_target_pairs={{0,16},{1,17},{16,0},{17,1},{2,18},{3,19},{18,2},{19,3},{4,20},{5,... | collective-permute-start | bytes 393224 | tf_op jit(solution)/shard_map/ppermute | solution.py:321
  56.5 1.3 %collective-permute-start.6 = (f32[256,128]{1,0:T(8,128)S(1)}, f32[256,128]{1,0:T(8,128)S(1)}, u32[]{:S(2)}, u32[]{:S(2)}) collective-permute-start(f32[256,128]{1,0:T(8,128)S(1)} %get-tuple-element.24.refs_0_), channel_id=1, source_target_pairs={{0,1},{1,0},{16,17},{17,16},{2,3},{3,2},{18,19},{19,18},{4,5},{5,4... | collective-permute-start | bytes 393224 | tf_op jit(solution)/shard_map/ppermute | solution.py:321
  57.8 0.0 copy-done
  57.8 3.9 %inverse_of_product.2.refs_4_ = f32[128,128]{1,0:T(8,128)S(1)} custom-call(f32[128,128]{1,0:T(8,128)S(1)} %get-tuple-element.25.first_ref, f32[128,128]{1,0:T(8,128)S(1)} %copy-done), custom_call_target="tpu_custom_call" | custom-call | flops 3000000000 | bytes 524288 | tf_op jit(solution)/shard_map/inverse_of_product/pallas_call | solution.py:97
  61.7 0.0 collective-permute-done.8.refs_3_
  61.7 0.0 collective-permute-done.7.refs_2_
  61.8 1.2 %collective-permute-done.6.refs_1_ = f32[256,128]{1,0:T(8,128)S(1)} collective-permute-done((f32[256,128]{1,0:T(8,128)S(1)}, f32[256,128]{1,0:T(8,128)S(1)}, u32[]{:S(2)}, u32[]{:S(2)}) %collective-permute-start.6) | collective-permute-done | bytes 131104 | tf_op jit(solution)/shard_map/ppermute | solution.py:321
  63.0 0.0 collective-permute-done.9.refs_6_
  63.0 1.4 %solve.1 = (f32[1024,128]{1,0:T(8,128)S(1)}, f32[136,128]{1,0:T(8,128)S(1)}) custom-call(f32[256,128]{1,0:T(8,128)S(1)} %get-tuple-element.24.refs_0_, f32[256,128]{1,0:T(8,128)S(1)} %collective-permute-done.6.refs_1_, f32[256,128]{1,0:T(8,128)S(1)} %collective-permute-done.7.refs_2_, f32[256,128]{1,0:T(8,128)S(1)} %collective-permute-done.8.refs_3_, ...), custom_call_target="tpu_custom_call" | custom-call | tf_op jit(solution)/shard_map/solve/pallas_call | solution.py:306
  64.4 0.1 collective-permute-start.10
  64.5 3.1 %collective-permute-start.13 = (f32[136,128]{1,0:T(8,128)S(1)}, f32[136,128]{1,0:T(8,128)S(1)}, u32[]{:S(2)}, u32[]{:S(2)}) collective-permute-start(f32[136,128]{1,0:T(8,128)S(1)} %get-tuple-element.31.refs_0_), channel_id=1, source_target_pairs={{0,6},{2,4},{4,2},{6,0},{1,7},{3,5},{5,3},{7,1},{8,14},{10,12},{12... | collective-permute-start | bytes 208904 | tf_op jit(solution)/shard_map/ppermute | solution.py:321
  67.6 0.6 collective-permute-start.12
  68.2 0.4 collective-permute-start.11
  68.6 0.0 collective-permute-done.10
  68.7 1.6 %assemble.1 = f32[8,256,128]{2,1,0:T(8,128)} custom-call(s32[2]{0:T(128)S(1)} %pad_add_fusion.at_ref, f32[4,256,128]{2,1,0:T(8,128)S(1)} %bitcast.15, f32[4,256,128]{2,1,0:T(8,128)S(1)} %bitcast.16), custom_call_target="tpu_custom_call" | custom-call | tf_op jit(solution)/shard_map/assemble/pallas_call | solution.py:116
  70.2 0.9 %collective-permute-done.13.refs_3_ = f32[136,128]{1,0:T(8,128)S(1)} collective-permute-done((f32[136,128]{1,0:T(8,128)S(1)}, f32[136,128]{1,0:T(8,128)S(1)}, u32[]{:S(2)}, u32[]{:S(2)}) %collective-permute-start.13) | collective-permute-done | bytes 69664 | tf_op jit(solution)/shard_map/ppermute | solution.py:321
  71.1 2.9 %collective-permute-done.12.refs_2_ = f32[136,128]{1,0:T(8,128)S(1)} collective-permute-done((f32[136,128]{1,0:T(8,128)S(1)}, f32[136,128]{1,0:T(8,128)S(1)}, u32[]{:S(2)}, u32[]{:S(2)}) %collective-permute-start.12) | collective-permute-done | bytes 69664 | tf_op jit(solution)/shard_map/ppermute | solution.py:321
  74.1 0.0 collective-permute-done.11.refs_1_
  74.1 0.6 collect.1
  74.7 0.0 collective-permute-start.14
  74.7 4.4 %all-to-all-start.2 = ((f32[32,4,128]{2,1,0:T(4,128)}), f32[32,4,128]{2,1,0:T(4,128)S(1)}, u32[]{:S(2)}, u32[]{:S(2)}) async-start(f32[32,4,128]{2,1,0:T(4,128)} %get-tuple-element.32), calls=%async_computation.2 | async-start | bytes 131072 | tf_op jit(solution)/shard_map/all_to_all | solution.py:359
  79.1 0.0 collective-permute-done.14.refs_1_
  79.2 3.9 %inverse_of_product.3 = f32[128,128]{1,0:T(8,128)S(1)} custom-call(f32[128,128]{1,0:T(8,128)S(1)} %get-tuple-element.25.first_ref, f32[128,128]{1,0:T(8,128)S(1)} %get-tuple-element.33.refs_0_, f32[128,128]{1,0:T(8,128)S(1)} %collective-permute-done.14.refs_1_), custom_call_target="tpu_custom_call" | custom-call | flops 3000000000 | bytes 524288 | tf_op jit(solution)/shard_map/inverse_of_product/pallas_call | solution.py:97
  83.1 4.0 %all-to-all-done.2 = f32[32,4,128]{2,1,0:T(4,128)S(1)} async-done(((f32[32,4,128]{2,1,0:T(4,128)}), f32[32,4,128]{2,1,0:T(4,128)S(1)}, u32[]{:S(2)}, u32[]{:S(2)}) %all-to-all-start.2) | async-done | bytes 65568 | tf_op jit(solution)/shard_map/all_to_all | solution.py:359
  87.1 0.7 fusion.1
  (5 shorter events, 0.1 us)
Async XLA Ops:
  0.7 5.4 %copy-start.1 = (f32[256,128]{1,0:T(8,128)S(1)}, f32[256,128]{1,0:T(8,128)}, u32[]{:S(2)}) copy-start(f32[256,128]{1,0:T(8,128)} %a_hbm.3) | copy-start | bytes 393220
  5.5 57.4 %collective-permute-start.9 = (f32[4,1024,128]{2,1,0:T(8,128)S(1)}, f32[4,1024,128]{2,1,0:T(8,128)S(1)}, u32[]{:S(2)}, u32[]{:S(2)}) collective-permute-start(f32[4,1024,128]{2,1,0:T(8,128)S(1)} %get-tuple-element.27), channel_id=1, source_target_pairs={{0,8},{8,0},{1,9},{9,1},{2,10},{10,2},{3,11},{11,3},{4,12},{12,4},... | collective-permute-start | bytes 6291464 | tf_op jit(solution)/shard_map/ppermute | solution.py:321
  5.6 6.0 %collective-permute-start.2 = (f32[1024,128]{1,0:T(8,128)S(1)}, f32[1024,128]{1,0:T(8,128)S(1)}, u32[]{:S(2)}, u32[]{:S(2)}) collective-permute-start(f32[1024,128]{1,0:T(8,128)S(1)} %get-tuple-element.19), channel_id=1, source_target_pairs={{0,8},{8,0},{1,9},{9,1},{2,10},{10,2},{3,11},{11,3},{4,12},{12,4},... | collective-permute-start | bytes 1572872 | tf_op jit(solution)/shard_map/ppermute | solution.py:321
  6.5 9.4 %collective-permute-start = (f32[128,128]{1,0:T(8,128)S(1)}, f32[128,128]{1,0:T(8,128)S(1)}, u32[]{:S(2)}, u32[]{:S(2)}) collective-permute-start(f32[128,128]{1,0:T(8,128)S(1)} %fusion), channel_id=1, source_target_pairs={{0,8},{8,0},{1,9},{9,1},{2,10},{10,2},{3,11},{11,3},{4,12},{12,4},... | collective-permute-start | bytes 196616 | tf_op jit(solution)/shard_map/ppermute | solution.py:321
  11.6 46.2 %copy-start = (f32[128,128]{1,0:T(8,128)S(1)}, f32[128,128]{1,0:T(8,128)}, u32[]{:S(2)}) copy-start(f32[128,128]{1,0:T(8,128)} %refs_0_.1) | copy-start | bytes 196612
  11.7 11.7 %collective-permute-start.3 = (f32[256,128]{1,0:T(8,128)S(1)}, f32[256,128]{1,0:T(8,128)S(1)}, u32[]{:S(2)}, u32[]{:S(2)}) collective-permute-start(f32[256,128]{1,0:T(8,128)S(1)} %get-tuple-element.21), channel_id=1, source_target_pairs={{0,1},{1,0},{16,17},{17,16},{2,3},{3,2},{18,19},{19,18},{4,5},{5,4... | collective-permute-start | bytes 393224 | tf_op jit(solution)/shard_map/ppermute | solution.py:321
  13.9 9.5 %collective-permute-start.4 = (f32[256,128]{1,0:T(8,128)S(1)}, f32[256,128]{1,0:T(8,128)S(1)}, u32[]{:S(2)}, u32[]{:S(2)}) collective-permute-start(f32[256,128]{1,0:T(8,128)S(1)} %get-tuple-element.22), channel_id=1, source_target_pairs={{0,16},{1,17},{16,0},{17,1},{2,18},{3,19},{18,2},{19,3},{4,20},{5,... | collective-permute-start | bytes 393224 | tf_op jit(solution)/shard_map/ppermute | solution.py:321
  15.3 8.1 %collective-permute-start.5 = (f32[256,128]{1,0:T(8,128)S(1)}, f32[256,128]{1,0:T(8,128)S(1)}, u32[]{:S(2)}, u32[]{:S(2)}) collective-permute-start(f32[256,128]{1,0:T(8,128)S(1)} %get-tuple-element.23), channel_id=1, source_target_pairs={{0,17},{1,16},{16,1},{17,0},{2,19},{3,18},{18,3},{19,2},{4,21},{5,... | collective-permute-start | bytes 393224 | tf_op jit(solution)/shard_map/ppermute | solution.py:321
  15.9 7.5 %collective-permute-start.1 = (f32[128,128]{1,0:T(8,128)S(1)}, f32[128,128]{1,0:T(8,128)S(1)}, u32[]{:S(2)}, u32[]{:S(2)}) collective-permute-start(f32[128,128]{1,0:T(8,128)S(1)} %add.6.g_ref), channel_id=1, source_target_pairs={{0,16},{16,0},{1,17},{17,1},{2,18},{18,2},{3,19},{19,3},{4,20},{20... | collective-permute-start | bytes 196616 | tf_op jit(solution)/shard_map/ppermute | solution.py:321
  54.2 7.5 %collective-permute-start.8 = (f32[256,128]{1,0:T(8,128)S(1)}, f32[256,128]{1,0:T(8,128)S(1)}, u32[]{:S(2)}, u32[]{:S(2)}) collective-permute-start(f32[256,128]{1,0:T(8,128)S(1)} %get-tuple-element.24.refs_0_), channel_id=1, source_target_pairs={{0,17},{1,16},{16,1},{17,0},{2,19},{3,18},{18,3},{19,2},{4,21},{5,... | collective-permute-start | bytes 393224 | tf_op jit(solution)/shard_map/ppermute | solution.py:321
  54.8 6.9 %collective-permute-start.7 = (f32[256,128]{1,0:T(8,128)S(1)}, f32[256,128]{1,0:T(8,128)S(1)}, u32[]{:S(2)}, u32[]{:S(2)}) collective-permute-start(f32[256,128]{1,0:T(8,128)S(1)} %get-tuple-element.24.refs_0_), channel_id=1, source_target_pairs={{0,16},{1,17},{16,0},{17,1},{2,18},{3,19},{18,2},{19,3},{4,20},{5,... | collective-permute-start | bytes 393224 | tf_op jit(solution)/shard_map/ppermute | solution.py:321
  56.5 6.5 %collective-permute-start.6 = (f32[256,128]{1,0:T(8,128)S(1)}, f32[256,128]{1,0:T(8,128)S(1)}, u32[]{:S(2)}, u32[]{:S(2)}) collective-permute-start(f32[256,128]{1,0:T(8,128)S(1)} %get-tuple-element.24.refs_0_), channel_id=1, source_target_pairs={{0,1},{1,0},{16,17},{17,16},{2,3},{3,2},{18,19},{19,18},{4,5},{5,4... | collective-permute-start | bytes 393224 | tf_op jit(solution)/shard_map/ppermute | solution.py:321
  64.4 4.3 %collective-permute-start.10 = (f32[1024,128]{1,0:T(8,128)S(1)}, f32[1024,128]{1,0:T(8,128)S(1)}, u32[]{:S(2)}, u32[]{:S(2)}) collective-permute-start(f32[1024,128]{1,0:T(8,128)S(1)} %get-tuple-element.29), channel_id=1, source_target_pairs={{0,8},{8,0},{1,9},{9,1},{2,10},{10,2},{3,11},{11,3},{4,12},{12,4},... | collective-permute-start | bytes 1572872 | tf_op jit(solution)/shard_map/ppermute | solution.py:321
  64.5 6.7 %collective-permute-start.13 = (f32[136,128]{1,0:T(8,128)S(1)}, f32[136,128]{1,0:T(8,128)S(1)}, u32[]{:S(2)}, u32[]{:S(2)}) collective-permute-start(f32[136,128]{1,0:T(8,128)S(1)} %get-tuple-element.31.refs_0_), channel_id=1, source_target_pairs={{0,6},{2,4},{4,2},{6,0},{1,7},{3,5},{5,3},{7,1},{8,14},{10,12},{12... | collective-permute-start | bytes 208904 | tf_op jit(solution)/shard_map/ppermute | solution.py:321
  67.6 6.5 %collective-permute-start.12 = (f32[136,128]{1,0:T(8,128)S(1)}, f32[136,128]{1,0:T(8,128)S(1)}, u32[]{:S(2)}, u32[]{:S(2)}) collective-permute-start(f32[136,128]{1,0:T(8,128)S(1)} %get-tuple-element.31.refs_0_), channel_id=1, source_target_pairs={{0,4},{2,6},{4,0},{6,2},{1,5},{3,7},{5,1},{7,3},{8,12},{10,14},{12... | collective-permute-start | bytes 208904 | tf_op jit(solution)/shard_map/ppermute | solution.py:321
  68.2 5.9 %collective-permute-start.11 = (f32[136,128]{1,0:T(8,128)S(1)}, f32[136,128]{1,0:T(8,128)S(1)}, u32[]{:S(2)}, u32[]{:S(2)}) collective-permute-start(f32[136,128]{1,0:T(8,128)S(1)} %get-tuple-element.31.refs_0_), channel_id=1, source_target_pairs={{0,2},{2,0},{4,6},{6,4},{1,3},{3,1},{5,7},{7,5},{8,10},{10,8},{12,... | collective-permute-start | bytes 208904 | tf_op jit(solution)/shard_map/ppermute | solution.py:321
  74.7 4.4 %collective-permute-start.14 = (f32[128,128]{1,0:T(8,128)S(1)}, f32[128,128]{1,0:T(8,128)S(1)}, u32[]{:S(2)}, u32[]{:S(2)}) collective-permute-start(f32[128,128]{1,0:T(8,128)S(1)} %get-tuple-element.33.refs_0_), channel_id=1, source_target_pairs={{0,8},{8,0},{1,9},{9,1},{2,10},{10,2},{3,11},{11,3},{4,12},{12,4},... | collective-permute-start | bytes 196616 | tf_op jit(solution)/shard_map/ppermute | solution.py:321
  74.7 12.4 %all-to-all-start.2 = ((f32[32,4,128]{2,1,0:T(4,128)}), f32[32,4,128]{2,1,0:T(4,128)S(1)}, u32[]{:S(2)}, u32[]{:S(2)}) async-start(f32[32,4,128]{2,1,0:T(4,128)} %get-tuple-element.32), calls=%async_computation.2 | async-start | bytes 131072 | tf_op jit(solution)/shard_map/all_to_all | solution.py:359

commit v11 on v9

--- a/solution.py
+++ b/solution.py
@@ -99,6 +99,21 @@
     )(first, *parts)
 
 
+def product_kernel(x_ref, inv_ref, out_ref):
+    out_ref[...] = dot(jnp.sum(x_ref[...], axis=0), inv_ref[...])
+
+
+def product(x, inverse):
+    return pl.pallas_call(
+        product_kernel,
+        out_shape=jax.ShapeDtypeStruct(x.shape[1:], F32),
+        in_specs=[VMEM] * 2,
+        out_specs=VMEM,
+        compiler_params=pltpu.CompilerParams(vmem_limit_bytes=2 << 20),
+        name="product",
+    )(x, inverse)
+
+
 def assemble_kernel(at_ref, mine_ref, other_ref, out_ref):
     count = mine_ref.shape[0]
     for n in range(count):
@@ -124,16 +139,18 @@
     return high, middle, (rest - middle.astype(F32)).astype(BF16)
 
 
-def contract_kernel(chunk, at_ref, x_hbm, a_hbm, c_hbm, p_ref, b_ref, *scratch):
+def contract_kernel(chunk, resident, at_ref, x_hbm, a_in, c_in, p_ref, b_ref, *scratch):
     x_ref, w_ref, a_ref, c_ref, sems = scratch
+    if resident:
+        a_ref, c_ref = a_in, c_in
     count, rows, rank = p_ref.shape
     span = 2 * count
-    factors = [
-        pltpu.make_async_copy(a_hbm, a_ref, sems.at[rows // chunk]),
-        pltpu.make_async_copy(c_hbm, c_ref, sems.at[rows // chunk + 1]),
-    ]
-    factors[0].start()
-    factors[1].start()
+    factors = []
+    if not resident:
+        for n, (source, target) in enumerate(((a_in, a_ref), (c_in, c_ref))):
+            factors.append(pltpu.make_async_copy(source, target, sems.at[rows // chunk + n]))
+            factors[n].start()
+    part_rows = min(256, chunk)
     copies = []
     for n, at in enumerate(range(0, rows, chunk)):
         size = chunk * span
@@ -143,19 +160,19 @@
         )
         copy.start()
         copies.append(copy)
-    factors[0].wait()
-    factors[1].wait()
+    for copy in factors:
+        copy.wait()
     for n, part in enumerate(split3(a_ref[...])):
         w_ref[:, n * rank : (n + 1) * rank] = part
     for n, at in enumerate(range(0, rows, chunk)):
         copies[n].wait()
-        for row in range(at, at + chunk, 128):
+        for row in range(at, at + chunk, part_rows):
             total = None
             for k in range(count):
                 x = jnp.concatenate(
                     [
-                        x_ref[pl.ds(row * span + k, 128, stride=span), :],
-                        x_ref[pl.ds(row * span + count + k, 128, stride=span), :],
+                        x_ref[pl.ds(row * span + k, part_rows, stride=span), :],
+                        x_ref[pl.ds(row * span + count + k, part_rows, stride=span), :],
                     ],
                     axis=1,
                 )
@@ -164,22 +181,22 @@
                 y = mxu(high, wide) + mxu(middle, wide)
                 small = mxu(low, w_ref[:, :rank]) + mxu(high, w_ref[:, 2 * rank :])
                 value = y[:, :rank] + y[:, rank:] + small
-                p_ref[k, row : row + 128] = value
+                p_ref[k, row : row + part_rows] = value
                 term = value * c_ref[k : k + 1, :]
                 total = term if total is None else total + term
-            b_ref[row : row + 128] = total
-
-
-def contract(at, x, factor_a, factor_c, rows):
+            b_ref[row : row + part_rows] = total
+
+
+def contract(at, x, factor_a, factor_c, rows, resident):
     count, (depth, rank) = factor_c.shape[0], factor_a.shape
     chunk = rows // 4
     return pl.pallas_call(
-        functools.partial(contract_kernel, chunk),
+        functools.partial(contract_kernel, chunk, resident),
         out_shape=[
             jax.ShapeDtypeStruct((count, rows, rank), F32),
             jax.ShapeDtypeStruct((rows, rank), F32),
         ],
-        in_specs=[SMEM, HBM, HBM, HBM],
+        in_specs=[SMEM, HBM] + [VMEM if resident else HBM] * 2,
         out_specs=[VMEM, VMEM],
         scratch_shapes=[
             pltpu.VMEM((rows * 2 * count, depth // 2), F32),
@@ -329,8 +346,8 @@
         pltpu.with_memory_space_constraint(v, pltpu.HBM) for v in (flat, factor_a, factor_c)
     )
 
-    p_other, b_other = contract(jnp.stack([1 - core, x]), flat, a_hbm, c_hbm, half)
-    p_mine, b_mine = contract(jnp.stack([core, x]), flat, a_hbm, c_hbm, half)
+    p_other, b_other = contract(jnp.stack([1 - core, x]), flat, a_hbm, c_hbm, half, False)
+    p_mine, b_mine = contract(jnp.stack([core, x]), flat, factor_a, factor_c, half, True)
     gram_part = dot(factor_a.T, factor_a)
     gram_part = gram_part + swap(gram_part, "c")
     sent = parcels(b_mine, swap(b_other, "c"))
@@ -338,7 +355,8 @@
     column = column_sum(gram_part, swap(gram_part, "xl"), got, depth)
     column = spread(lax.all_to_all(column, "z", 0, 0))
     column, gram_a = flatten(lax.all_to_all(column, "z", 0, 0))
-    columns = [column] + [swap(column, RING, n) for n in (1, 2, 3)]
+    third, second, first = (swap(column, RING, n) for n in (3, 2, 1))
+    columns = [column, first, second, third]
     inverse = inverse_of_product(gram_a, [gram_c])
     f_mine, sums = solve(columns, inverse, p_mine, swap(p_other, "c"))
 
@@ -351,8 +369,8 @@
     parts[0], factor_b = lax.optimization_barrier((parts[0], factor_b))
     plane = ("z", "xl")
     spread_c = collect(parts, lax.axis_size(plane), mode_three)
-    mttkrp_c = jnp.sum(lax.all_to_all(spread_c, plane, 0, 0), axis=0)
-    factor_c_new = dot(mttkrp_c, inverse_of_product(gram_a, parts))
+    shares = lax.all_to_all(spread_c, plane, 0, 0)
+    factor_c_new = product(shares, inverse_of_product(gram_a, parts))
     return (factor_b.reshape(mode_two, rank), factor_c_new)
 
 

time: 88.7 us -> 88.6 us (level)
    pallas_call x2 -> x3, Pallas kernels: 9.64 us -> 10.4 us  [the longest x2 9.6 us: contract(): pl.pallas_call(functools.partial(contract_kernel, chunk, resident), out_s...]
where the time goes in v11:
time: 88.6 us; the launch traced here: 88.4 us
  blocking collectives  30.7 us (35%)
  Pallas kernels  21.9 us (25%)
  starting transfers between devices  19.5 us (22%)
  waiting for transfers between devices  14.9 us (17%)
    all_to_all x1, blocking collectives, body(): column = spread(lax.all_to_all(column, 'z', 0, 0))  18.5 us
    ppermute x15, starting transfers between devices, swap(): return lax.ppermute(x, axis, [(i, i ^ bit) for i in range(n)])  15.3 us
    all_to_all x1, blocking collectives, body(): column, gram_a = flatten(lax.all_to_all(column, 'z', 0, 0))  12.2 us
    ppermute x15, waiting for transfers between devices, swap(): return lax.ppermute(x, axis, [(i, i ^ bit) for i in range(n)])  11.4 us
    pallas_call x2, Pallas kernels, contract(): pl.pallas_call(functools.partial(contract_kernel, chunk, resident), out_s...  9.6 us
    pallas_call x2, Pallas kernels, inverse_of_product(): pl.pallas_call(inverse_kernel, out_shape=jax.ShapeDtypeStruct(first.shape...  7.85 us
    all_to_all x1, starting transfers between devices, body(): shares = lax.all_to_all(spread_c, plane, 0, 0)  4.21 us
    all_to_all x1, waiting for transfers between devices, body(): shares = lax.all_to_all(spread_c, plane, 0, 0)  3.55 us
  transfers between devices with their start and end apart: 16, of which 6 were waited for; matrix products, arithmetic and copies ran while one was open for 0% of the time, Pallas kernels for 16%

profile of v11, /device:TPU:2, one launch (start us, length us, event | category | flops | bytes accessed | tf_op | source)
XLA Modules:
  0.0 88.4 jit_solution(12139607409643813266)
XLA Ops:
  0.6 0.1 pad_add_fusion
  0.7 0.0 copy-start
  0.7 0.0 copy-start.1
  0.7 4.9 %contract.3 = (f32[4,1024,128]{2,1,0:T(8,128)S(1)}, f32[1024,128]{1,0:T(8,128)S(1)}) custom-call(s32[2]{0:T(128)S(1)} %get-tuple-element.35.at_ref, f32[16384,128]{1,0:T(8,128)} %bitcast.15, f32[256,128]{1,0:T(8,128)} %a_in.3, f32[4,128]{1,0:T(4,128)} %c_in.3), custom_call_target="tpu_custom_call" | custom-call | flops 2147483648 | bytes 6291456 | tf_op jit(solution)/shard_map/contract/pallas_call | solution.py:193
  5.6 0.1 collective-permute-start.9
  5.7 0.5 collective-permute-start.2
  6.2 0.0 copy-done
  6.2 0.4 fusion
  6.6 0.2 collective-permute-start
  6.8 0.0 copy-done.1
  6.8 4.7 %contract.2 = (f32[4,1024,128]{2,1,0:T(8,128)S(1)}, f32[1024,128]{1,0:T(8,128)S(1)}) custom-call(s32[2]{0:T(128)S(1)} %get-tuple-element.34.at_ref, f32[16384,128]{1,0:T(8,128)} %bitcast.16, f32[256,128]{1,0:T(8,128)S(1)} %copy-done, f32[4,128]{1,0:T(4,128)S(1)} %copy-done.1), custom_call_target="tpu_custom_call" | custom-call | flops 2147483648 | bytes 6291456 | tf_op jit(solution)/shard_map/contract/pallas_call | solution.py:193
  11.5 0.0 copy-start.2
  11.5 0.0 collective-permute-done.2.far_ref
  11.5 0.1 parcels.1
  11.6 2.2 %collective-permute-start.3 = (f32[256,128]{1,0:T(8,128)S(1)}, f32[256,128]{1,0:T(8,128)S(1)}, u32[]{:S(2)}, u32[]{:S(2)}) collective-permute-start(f32[256,128]{1,0:T(8,128)S(1)} %get-tuple-element.21), channel_id=1, source_target_pairs={{0,1},{1,0},{16,17},{17,16},{2,3},{3,2},{18,19},{19,18},{4,5},{5,4... | collective-permute-start | bytes 393224 | tf_op jit(solution)/shard_map/ppermute | solution.py:332
  13.8 1.4 %collective-permute-start.4 = (f32[256,128]{1,0:T(8,128)S(1)}, f32[256,128]{1,0:T(8,128)S(1)}, u32[]{:S(2)}, u32[]{:S(2)}) collective-permute-start(f32[256,128]{1,0:T(8,128)S(1)} %get-tuple-element.22), channel_id=1, source_target_pairs={{0,16},{1,17},{16,0},{17,1},{2,18},{3,19},{18,2},{19,3},{4,20},{5,... | collective-permute-start | bytes 393224 | tf_op jit(solution)/shard_map/ppermute | solution.py:332
  15.3 0.5 collective-permute-start.5
  15.8 0.0 collective-permute-done
  15.8 2.4 %collective-permute-start.1 = (f32[128,128]{1,0:T(8,128)S(1)}, f32[128,128]{1,0:T(8,128)S(1)}, u32[]{:S(2)}, u32[]{:S(2)}) collective-permute-start(f32[128,128]{1,0:T(8,128)S(1)} %add.9.g_ref), channel_id=1, source_target_pairs={{0,16},{16,0},{1,17},{17,1},{2,18},{18,2},{3,19},{19,3},{4,20},{20... | collective-permute-start | bytes 196616 | tf_op jit(solution)/shard_map/ppermute | solution.py:332
  18.2 5.1 %collective-permute-done.1.g_far_ref = f32[128,128]{1,0:T(8,128)S(1)} collective-permute-done((f32[128,128]{1,0:T(8,128)S(1)}, f32[128,128]{1,0:T(8,128)S(1)}, u32[]{:S(2)}, u32[]{:S(2)}) %collective-permute-start.1) | collective-permute-done | bytes 65568 | tf_op jit(solution)/shard_map/ppermute | solution.py:332
  23.3 0.0 collective-permute-done.3.refs_1_
  23.3 0.0 collective-permute-done.4.refs_2_
  23.3 0.0 collective-permute-done.5.refs_3_
  23.4 18.5 %all_to_all.15.x_ref = f32[8,48,128]{2,1,0:T(8,128)S(1)} all-to-all(f32[8,48,128]{2,1,0:T(8,128)S(1)} %column_sum.1), channel_id=1, replica_groups=mesh['z'=8,'xl'=2,'c'=2,'y'=4,'xh'=2] {'z'}, dimensions={0} | all-to-all | bytes 393216 | tf_op jit(solution)/shard_map/all_to_all | solution.py:356
  41.9 12.2 %all_to_all.16.x_ref = f32[8,48,128]{2,1,0:T(8,128)S(1)} all-to-all(f32[8,48,128]{2,1,0:T(8,128)S(1)} %spread.1), channel_id=1, replica_groups=mesh['z'=8,'xl'=2,'c'=2,'y'=4,'xh'=2] {'z'}, dimensions={0} | all-to-all | bytes 393216 | tf_op jit(solution)/shard_map/all_to_all | solution.py:357
  54.1 0.6 collective-permute-start.8
  54.7 1.7 %collective-permute-start.7 = (f32[256,128]{1,0:T(8,128)S(1)}, f32[256,128]{1,0:T(8,128)S(1)}, u32[]{:S(2)}, u32[]{:S(2)}) collective-permute-start(f32[256,128]{1,0:T(8,128)S(1)} %get-tuple-element.24.refs_0_), channel_id=1, source_target_pairs={{0,16},{1,17},{16,0},{17,1},{2,18},{3,19},{18,2},{19,3},{4,20},{5,... | collective-permute-start | bytes 393224 | tf_op jit(solution)/shard_map/ppermute | solution.py:332
  56.4 1.3 %collective-permute-start.6 = (f32[256,128]{1,0:T(8,128)S(1)}, f32[256,128]{1,0:T(8,128)S(1)}, u32[]{:S(2)}, u32[]{:S(2)}) collective-permute-start(f32[256,128]{1,0:T(8,128)S(1)} %get-tuple-element.24.refs_0_), channel_id=1, source_target_pairs={{0,1},{1,0},{16,17},{17,16},{2,3},{3,2},{18,19},{19,18},{4,5},{5,4... | collective-permute-start | bytes 393224 | tf_op jit(solution)/shard_map/ppermute | solution.py:332
  57.7 0.0 copy-done.2
  57.7 3.9 %inverse_of_product.2.refs_4_ = f32[128,128]{1,0:T(8,128)S(1)} custom-call(f32[128,128]{1,0:T(8,128)S(1)} %get-tuple-element.25.first_ref, f32[128,128]{1,0:T(8,128)S(1)} %copy-done.2), custom_call_target="tpu_custom_call" | custom-call | flops 3000000000 | bytes 524288 | tf_op jit(solution)/shard_map/inverse_of_product/pallas_call | solution.py:91
  61.6 0.0 collective-permute-done.8.refs_3_
  61.6 0.0 collective-permute-done.7.refs_2_
  61.7 1.2 %collective-permute-done.6.refs_1_ = f32[256,128]{1,0:T(8,128)S(1)} collective-permute-done((f32[256,128]{1,0:T(8,128)S(1)}, f32[256,128]{1,0:T(8,128)S(1)}, u32[]{:S(2)}, u32[]{:S(2)}) %collective-permute-start.6) | collective-permute-done | bytes 131104 | tf_op jit(solution)/shard_map/ppermute | solution.py:332
  62.9 0.0 collective-permute-done.9.refs_6_
  62.9 1.4 %solve.1 = (f32[1024,128]{1,0:T(8,128)S(1)}, f32[136,128]{1,0:T(8,128)S(1)}) custom-call(f32[256,128]{1,0:T(8,128)S(1)} %get-tuple-element.24.refs_0_, f32[256,128]{1,0:T(8,128)S(1)} %collective-permute-done.6.refs_1_, f32[256,128]{1,0:T(8,128)S(1)} %collective-permute-done.7.refs_2_, f32[256,128]{1,0:T(8,128)S(1)} %collective-permute-done.8.refs_3_, ...), custom_call_target="tpu_custom_call" | custom-call | tf_op jit(solution)/shard_map/solve/pallas_call | solution.py:317
  64.3 0.1 collective-permute-start.10
  64.4 1.2 %collective-permute-done.10 = f32[136,128]{1,0:T(8,128)S(1)} collective-permute-done((f32[136,128]{1,0:T(8,128)S(1)}, f32[136,128]{1,0:T(8,128)S(1)}, u32[]{:S(2)}, u32[]{:S(2)}) %collective-permute-start.10) | collective-permute-done | bytes 69664 | tf_op jit(solution)/shard_map/ppermute | solution.py:332
  65.6 0.2 collective-permute-start.11
  65.9 3.0 %collective-permute-start.14 = (f32[136,128]{1,0:T(8,128)S(1)}, f32[136,128]{1,0:T(8,128)S(1)}, u32[]{:S(2)}, u32[]{:S(2)}) collective-permute-start(f32[136,128]{1,0:T(8,128)S(1)} %add.11.refs_0_), channel_id=1, source_target_pairs={{0,6},{2,4},{4,2},{6,0},{1,7},{3,5},{5,3},{7,1},{8,14},{10,12},{12... | collective-permute-start | bytes 208904 | tf_op jit(solution)/shard_map/ppermute | solution.py:332
  68.9 0.6 collective-permute-start.13
  69.5 0.4 collective-permute-start.12
  70.0 0.0 collective-permute-done.11
  70.0 1.6 %assemble.1 = f32[8,256,128]{2,1,0:T(8,128)} custom-call(s32[2]{0:T(128)S(1)} %get-tuple-element.34.at_ref, f32[4,256,128]{2,1,0:T(8,128)S(1)} %bitcast.13, f32[4,256,128]{2,1,0:T(8,128)S(1)} %bitcast.14), custom_call_target="tpu_custom_call" | custom-call | tf_op jit(solution)/shard_map/assemble/pallas_call | solution.py:125
  71.6 0.8 collective-permute-done.14.refs_3_
  72.4 2.9 %collective-permute-done.13.refs_2_ = f32[136,128]{1,0:T(8,128)S(1)} collective-permute-done((f32[136,128]{1,0:T(8,128)S(1)}, f32[136,128]{1,0:T(8,128)S(1)}, u32[]{:S(2)}, u32[]{:S(2)}) %collective-permute-start.13) | collective-permute-done | bytes 69664 | tf_op jit(solution)/shard_map/ppermute | solution.py:332
  75.3 0.0 collective-permute-done.12.refs_1_
  75.3 0.6 collect.1
  75.9 4.2 %all-to-all-start.2 = ((f32[16,4,128]{2,1,0:T(4,128)}), f32[16,4,128]{2,1,0:T(4,128)S(1)}, u32[]{:S(2)}, u32[]{:S(2)}) async-start(f32[16,4,128]{2,1,0:T(4,128)} %collect.1), calls=%async_computation.2 | async-start | bytes 65536 | tf_op jit(solution)/shard_map/all_to_all | solution.py:372
  80.1 3.9 %inverse_of_product.3.inv_ref = f32[128,128]{1,0:T(8,128)S(1)} custom-call(f32[128,128]{1,0:T(8,128)S(1)} %get-tuple-element.25.first_ref, f32[136,128]{1,0:T(8,128)S(1)} %add.11.refs_0_, f32[136,128]{1,0:T(8,128)S(1)} %collective-permute-done.12.refs_1_, f32[136,128]{1,0:T(8,128)S(1)} %collective-permute-done.13.refs_2_, ...), custom_call_target="tpu_custom_call" | custom-call | flops 3000000000 | bytes 524288 | tf_op jit(solution)/shard_map/inverse_of_product/pallas_call | solution.py:91
  84.1 3.5 %all-to-all-done.2.x_ref = f32[16,4,128]{2,1,0:T(4,128)S(1)} async-done(((f32[16,4,128]{2,1,0:T(4,128)}), f32[16,4,128]{2,1,0:T(4,128)S(1)}, u32[]{:S(2)}, u32[]{:S(2)}) %all-to-all-start.2) | async-done | bytes 32800 | tf_op jit(solution)/shard_map/all_to_all | solution.py:372
  87.6 0.8 product.1
  (5 shorter events, 0.1 us)
Async XLA Ops:
  0.7 5.5 %copy-start = (f32[256,128]{1,0:T(8,128)S(1)}, f32[256,128]{1,0:T(8,128)}, u32[]{:S(2)}) copy-start(f32[256,128]{1,0:T(8,128)} %a_in.3) | copy-start | bytes 393220
  0.7 6.0 %copy-start.1 = (f32[4,128]{1,0:T(4,128)S(1)}, f32[4,128]{1,0:T(4,128)}, u32[]{:S(2)}) copy-start(f32[4,128]{1,0:T(4,128)} %c_in.3) | copy-start | bytes 6148
  5.6 57.3 %collective-permute-start.9 = (f32[4,1024,128]{2,1,0:T(8,128)S(1)}, f32[4,1024,128]{2,1,0:T(8,128)S(1)}, u32[]{:S(2)}, u32[]{:S(2)}) collective-permute-start(f32[4,1024,128]{2,1,0:T(8,128)S(1)} %get-tuple-element.27), channel_id=1, source_target_pairs={{0,8},{8,0},{1,9},{9,1},{2,10},{10,2},{3,11},{11,3},{4,12},{12,4},... | collective-permute-start | bytes 6291464 | tf_op jit(solution)/shard_map/ppermute | solution.py:332
  5.7 5.8 %collective-permute-start.2 = (f32[1024,128]{1,0:T(8,128)S(1)}, f32[1024,128]{1,0:T(8,128)S(1)}, u32[]{:S(2)}, u32[]{:S(2)}) collective-permute-start(f32[1024,128]{1,0:T(8,128)S(1)} %get-tuple-element.19), channel_id=1, source_target_pairs={{0,8},{8,0},{1,9},{9,1},{2,10},{10,2},{3,11},{11,3},{4,12},{12,4},... | collective-permute-start | bytes 1572872 | tf_op jit(solution)/shard_map/ppermute | solution.py:332
  6.6 9.2 %collective-permute-start = (f32[128,128]{1,0:T(8,128)S(1)}, f32[128,128]{1,0:T(8,128)S(1)}, u32[]{:S(2)}, u32[]{:S(2)}) collective-permute-start(f32[128,128]{1,0:T(8,128)S(1)} %fusion), channel_id=1, source_target_pairs={{0,8},{8,0},{1,9},{9,1},{2,10},{10,2},{3,11},{11,3},{4,12},{12,4},... | collective-permute-start | bytes 196616 | tf_op jit(solution)/shard_map/ppermute | solution.py:332
  11.5 46.2 %copy-start.2 = (f32[128,128]{1,0:T(8,128)S(1)}, f32[128,128]{1,0:T(8,128)}, u32[]{:S(2)}) copy-start(f32[128,128]{1,0:T(8,128)} %refs_0_.1) | copy-start | bytes 196612
  11.6 11.7 %collective-permute-start.3 = (f32[256,128]{1,0:T(8,128)S(1)}, f32[256,128]{1,0:T(8,128)S(1)}, u32[]{:S(2)}, u32[]{:S(2)}) collective-permute-start(f32[256,128]{1,0:T(8,128)S(1)} %get-tuple-element.21), channel_id=1, source_target_pairs={{0,1},{1,0},{16,17},{17,16},{2,3},{3,2},{18,19},{19,18},{4,5},{5,4... | collective-permute-start | bytes 393224 | tf_op jit(solution)/shard_map/ppermute | solution.py:332
  13.8 9.5 %collective-permute-start.4 = (f32[256,128]{1,0:T(8,128)S(1)}, f32[256,128]{1,0:T(8,128)S(1)}, u32[]{:S(2)}, u32[]{:S(2)}) collective-permute-start(f32[256,128]{1,0:T(8,128)S(1)} %get-tuple-element.22), channel_id=1, source_target_pairs={{0,16},{1,17},{16,0},{17,1},{2,18},{3,19},{18,2},{19,3},{4,20},{5,... | collective-permute-start | bytes 393224 | tf_op jit(solution)/shard_map/ppermute | solution.py:332
  15.3 8.1 %collective-permute-start.5 = (f32[256,128]{1,0:T(8,128)S(1)}, f32[256,128]{1,0:T(8,128)S(1)}, u32[]{:S(2)}, u32[]{:S(2)}) collective-permute-start(f32[256,128]{1,0:T(8,128)S(1)} %get-tuple-element.23), channel_id=1, source_target_pairs={{0,17},{1,16},{16,1},{17,0},{2,19},{3,18},{18,3},{19,2},{4,21},{5,... | collective-permute-start | bytes 393224 | tf_op jit(solution)/shard_map/ppermute | solution.py:332
  15.8 7.5 %collective-permute-start.1 = (f32[128,128]{1,0:T(8,128)S(1)}, f32[128,128]{1,0:T(8,128)S(1)}, u32[]{:S(2)}, u32[]{:S(2)}) collective-permute-start(f32[128,128]{1,0:T(8,128)S(1)} %add.9.g_ref), channel_id=1, source_target_pairs={{0,16},{16,0},{1,17},{17,1},{2,18},{18,2},{3,19},{19,3},{4,20},{20... | collective-permute-start | bytes 196616 | tf_op jit(solution)/shard_map/ppermute | solution.py:332
  54.1 7.5 %collective-permute-start.8 = (f32[256,128]{1,0:T(8,128)S(1)}, f32[256,128]{1,0:T(8,128)S(1)}, u32[]{:S(2)}, u32[]{:S(2)}) collective-permute-start(f32[256,128]{1,0:T(8,128)S(1)} %get-tuple-element.24.refs_0_), channel_id=1, source_target_pairs={{0,17},{1,16},{16,1},{17,0},{2,19},{3,18},{18,3},{19,2},{4,21},{5,... | collective-permute-start | bytes 393224 | tf_op jit(solution)/shard_map/ppermute | solution.py:332
  54.7 6.9 %collective-permute-start.7 = (f32[256,128]{1,0:T(8,128)S(1)}, f32[256,128]{1,0:T(8,128)S(1)}, u32[]{:S(2)}, u32[]{:S(2)}) collective-permute-start(f32[256,128]{1,0:T(8,128)S(1)} %get-tuple-element.24.refs_0_), channel_id=1, source_target_pairs={{0,16},{1,17},{16,0},{17,1},{2,18},{3,19},{18,2},{19,3},{4,20},{5,... | collective-permute-start | bytes 393224 | tf_op jit(solution)/shard_map/ppermute | solution.py:332
  56.4 6.5 %collective-permute-start.6 = (f32[256,128]{1,0:T(8,128)S(1)}, f32[256,128]{1,0:T(8,128)S(1)}, u32[]{:S(2)}, u32[]{:S(2)}) collective-permute-start(f32[256,128]{1,0:T(8,128)S(1)} %get-tuple-element.24.refs_0_), channel_id=1, source_target_pairs={{0,1},{1,0},{16,17},{17,16},{2,3},{3,2},{18,19},{19,18},{4,5},{5,4... | collective-permute-start | bytes 393224 | tf_op jit(solution)/shard_map/ppermute | solution.py:332
  64.3 1.3 %collective-permute-start.10 = (f32[136,128]{1,0:T(8,128)S(1)}, f32[136,128]{1,0:T(8,128)S(1)}, u32[]{:S(2)}, u32[]{:S(2)}) collective-permute-start(f32[136,128]{1,0:T(8,128)S(1)} %get-tuple-element.28), channel_id=1, source_target_pairs={{0,8},{8,0},{1,9},{9,1},{2,10},{10,2},{3,11},{11,3},{4,12},{12,4},... | collective-permute-start | bytes 208904 | tf_op jit(solution)/shard_map/ppermute | solution.py:332
  65.6 4.3 %collective-permute-start.11 = (f32[1024,128]{1,0:T(8,128)S(1)}, f32[1024,128]{1,0:T(8,128)S(1)}, u32[]{:S(2)}, u32[]{:S(2)}) collective-permute-start(f32[1024,128]{1,0:T(8,128)S(1)} %get-tuple-element.31), channel_id=1, source_target_pairs={{0,8},{8,0},{1,9},{9,1},{2,10},{10,2},{3,11},{11,3},{4,12},{12,4},... | collective-permute-start | bytes 1572872 | tf_op jit(solution)/shard_map/ppermute | solution.py:332
  65.9 6.5 %collective-permute-start.14 = (f32[136,128]{1,0:T(8,128)S(1)}, f32[136,128]{1,0:T(8,128)S(1)}, u32[]{:S(2)}, u32[]{:S(2)}) collective-permute-start(f32[136,128]{1,0:T(8,128)S(1)} %add.11.refs_0_), channel_id=1, source_target_pairs={{0,6},{2,4},{4,2},{6,0},{1,7},{3,5},{5,3},{7,1},{8,14},{10,12},{12... | collective-permute-start | bytes 208904 | tf_op jit(solution)/shard_map/ppermute | solution.py:332
  68.9 6.4 %collective-permute-start.13 = (f32[136,128]{1,0:T(8,128)S(1)}, f32[136,128]{1,0:T(8,128)S(1)}, u32[]{:S(2)}, u32[]{:S(2)}) collective-permute-start(f32[136,128]{1,0:T(8,128)S(1)} %add.11.refs_0_), channel_id=1, source_target_pairs={{0,4},{2,6},{4,0},{6,2},{1,5},{3,7},{5,1},{7,3},{8,12},{10,14},{12... | collective-permute-start | bytes 208904 | tf_op jit(solution)/shard_map/ppermute | solution.py:332
  69.5 5.8 %collective-permute-start.12 = (f32[136,128]{1,0:T(8,128)S(1)}, f32[136,128]{1,0:T(8,128)S(1)}, u32[]{:S(2)}, u32[]{:S(2)}) collective-permute-start(f32[136,128]{1,0:T(8,128)S(1)} %add.11.refs_0_), channel_id=1, source_target_pairs={{0,2},{2,0},{4,6},{6,4},{1,3},{3,1},{5,7},{7,5},{8,10},{10,8},{12,... | collective-permute-start | bytes 208904 | tf_op jit(solution)/shard_map/ppermute | solution.py:332
  75.9 11.7 %all-to-all-start.2 = ((f32[16,4,128]{2,1,0:T(4,128)}), f32[16,4,128]{2,1,0:T(4,128)S(1)}, u32[]{:S(2)}, u32[]{:S(2)}) async-start(f32[16,4,128]{2,1,0:T(4,128)} %collect.1), calls=%async_computation.2 | async-start | bytes 65536 | tf_op jit(solution)/shard_map/all_to_all | solution.py:372

commit v12 on v11

--- a/solution.py
+++ b/solution.py
@@ -97,6 +97,50 @@
         cost_estimate=pl.CostEstimate(flops=3 * 10**9, transcendentals=128, bytes_accessed=2**19),
         name="inverse_of_product",
     )(first, *parts)
+
+
+def gram_kernel(core_ref, a_ref, near_ref, far_ref, g_ref):
+    a = a_ref[...]
+    rows = near_ref.shape[0]
+    g_ref[...] = lax.dot_general(
+        a, a, (((0,), (0,)), ((), ())), precision=HIGH, preferred_element_type=F32
+    )
+    near_ref[...] = g_ref[pl.ds(pl.multiple_of(core_ref[0] * rows, rows), rows)]
+    far_ref[...] = g_ref[pl.ds(pl.multiple_of((1 - core_ref[0]) * rows, rows), rows)]
+
+
+def gram_halves(core, a):
+    rank = a.shape[1]
+    half = jax.ShapeDtypeStruct((rank // 2, rank), F32)
+    return pl.pallas_call(
+        gram_kernel,
+        out_shape=[half, half],
+        in_specs=[SMEM, VMEM],
+        out_specs=[VMEM] * 2,
+        scratch_shapes=[pltpu.VMEM((rank, rank), F32)],
+        compiler_params=pltpu.CompilerParams(vmem_limit_bytes=2 << 20),
+        name="gram_halves",
+    )(core, a)
+
+
+def first_inverse_kernel(core_ref, near_ref, far_ref, second_ref, g_ref, out_ref):
+    rows = near_ref.shape[0]
+    g_ref[pl.ds(pl.multiple_of(core_ref[0] * rows, rows), rows)] = near_ref[...]
+    g_ref[pl.ds(pl.multiple_of((1 - core_ref[0]) * rows, rows), rows)] = far_ref[...]
+    out_ref[...] = spd_inverse(g_ref[...] * second_ref[...], 16)
+
+
+def first_inverse(core, near, far, second):
+    square = jax.ShapeDtypeStruct(second.shape, F32)
+    return pl.pallas_call(
+        first_inverse_kernel,
+        out_shape=[square, square],
+        in_specs=[SMEM] + [VMEM] * 3,
+        out_specs=[VMEM] * 2,
+        compiler_params=pltpu.CompilerParams(vmem_limit_bytes=4 << 20),
+        cost_estimate=pl.CostEstimate(flops=3 * 10**9, transcendentals=128, bytes_accessed=2**19),
+        name="first_inverse",
+    )(core, near, far, second)
 
 
 def product_kernel(x_ref, inv_ref, out_ref):
@@ -280,13 +324,13 @@
         g_ref[z * few : (z + 1) * few] = x_ref[z, some:]
 
 
-def flatten(x):
+def flatten(x, count):
     depth, rows, rank = x.shape
     return pl.pallas_call(
         flatten_kernel,
         out_shape=[
-            jax.ShapeDtypeStruct((depth * rows - rank, rank), F32),
-            jax.ShapeDtypeStruct((rank, rank), F32),
+            jax.ShapeDtypeStruct((depth * rows - count, rank), F32),
+            jax.ShapeDtypeStruct((count, rank), F32),
         ],
         in_specs=[VMEM],
         out_specs=[VMEM] * 2,
@@ -347,17 +391,19 @@
     )
 
     p_other, b_other = contract(jnp.stack([1 - core, x]), flat, a_hbm, c_hbm, half, False)
-    p_mine, b_mine = contract(jnp.stack([core, x]), flat, factor_a, factor_c, half, True)
-    gram_part = dot(factor_a.T, factor_a)
-    gram_part = gram_part + swap(gram_part, "c")
+    near, far = gram_halves(core.reshape(1), factor_a)
+    here, near, far = lax.optimization_barrier((jnp.stack([core, x]), near, far))
+    p_mine, b_mine = contract(here, flat, factor_a, factor_c, half, True)
+    gram_part = near + swap(far, "c")
     sent = parcels(b_mine, swap(b_other, "c"))
     got = [sent[0]] + [swap(sent[n], RING, n) for n in (1, 2, 3)]
     column = column_sum(gram_part, swap(gram_part, "xl"), got, depth)
     column = spread(lax.all_to_all(column, "z", 0, 0))
-    column, gram_a = flatten(lax.all_to_all(column, "z", 0, 0))
+    column, near = flatten(lax.all_to_all(column, "z", 0, 0), rank // 2)
+    far = swap(near, "c")
     third, second, first = (swap(column, RING, n) for n in (3, 2, 1))
     columns = [column, first, second, third]
-    inverse = inverse_of_product(gram_a, [gram_c])
+    gram_a, inverse = first_inverse(core.reshape(1), near, far, gram_c)
     f_mine, sums = solve(columns, inverse, p_mine, swap(p_other, "c"))
 
     sums = sums + swap(sums, "c")
@@ -365,7 +411,7 @@
     parts = [sums] + [swap(sums, "y", bit) for bit in (1, 2, 3)]
     shape = (4, half // 4, rank)
     f_other = swap(f_mine, "c").reshape(shape)
-    factor_b = assemble(jnp.stack([core, x]), f_mine.reshape(shape), f_other)
+    factor_b = assemble(here, f_mine.reshape(shape), f_other)
     parts[0], factor_b = lax.optimization_barrier((parts[0], factor_b))
     plane = ("z", "xl")
     spread_c = collect(parts, lax.axis_size(plane), mode_three)

time: 88.6 us -> 88.2 us (level)
  blocking collectives: 30.7 us -> 29.5 us
    pallas_call x0 -> x2, Pallas kernels: none -> 4.25 us  [the longest x1 3.93 us: first_inverse(): pl.pallas_call(first_inverse_kernel, out_shape=[square, square], in_specs...]
    pallas_call x2 -> x1, Pallas kernels: 7.85 us -> 3.93 us  [inverse_of_product(): pl.pallas_call(inverse_kernel, out_shape=jax.ShapeDtypeStruct(first.shape...]
    ppermute x15 -> x16, waiting for transfers between devices: 11.4 us -> 11.6 us  [swap(): return lax.ppermute(x, axis, [(i, i ^ bit) for i in range(n)])]
    ppermute x15 -> x16, starting transfers between devices: 15.3 us -> 15.1 us  [swap(): return lax.ppermute(x, axis, [(i, i ^ bit) for i in range(n)])]
  transfers between devices with their start and end apart: 16 -> 17, of which waited for: 6 -> 8; matrix products, arithmetic and copies ran while one was open for 0% -> 0% of each run, Pallas kernels for 16% -> 17%
where the time goes in v12:
time: 88.2 us; the launch traced here: 88 us
  blocking collectives  29.5 us (33%)
  Pallas kernels  22.2 us (25%)
  starting transfers between devices  20.2 us (23%)
  waiting for transfers between devices  15.1 us (17%)
    all_to_all x1, blocking collectives, body(): column = spread(lax.all_to_all(column, 'z', 0, 0))  17.7 us
    ppermute x16, starting transfers between devices, swap(): return lax.ppermute(x, axis, [(i, i ^ bit) for i in range(n)])  15.1 us
    all_to_all x1, blocking collectives, body(): column, near = flatten(lax.all_to_all(column, 'z', 0, 0), rank // 2)  11.8 us
    ppermute x16, waiting for transfers between devices, swap(): return lax.ppermute(x, axis, [(i, i ^ bit) for i in range(n)])  11.6 us
    pallas_call x2, Pallas kernels, contract(): pl.pallas_call(functools.partial(contract_kernel, chunk, resident), out_s...  9.61 us
    all_to_all x1, starting transfers between devices, body(): shares = lax.all_to_all(spread_c, plane, 0, 0)  5.07 us
    pallas_call x1, Pallas kernels, first_inverse(): pl.pallas_call(first_inverse_kernel, out_shape=[square, square], in_specs...  3.93 us
    pallas_call x1, Pallas kernels, inverse_of_product(): pl.pallas_call(inverse_kernel, out_shape=jax.ShapeDtypeStruct(first.shape...  3.93 us
  transfers between devices with their start and end apart: 17, of which 8 were waited for; matrix products, arithmetic and copies ran while one was open for 0% of the time, Pallas kernels for 17%

profile of v12, /device:TPU:2, one launch (start us, length us, event | category | flops | bytes accessed | tf_op | source)
XLA Modules:
  0.0 88.0 jit_solution(2438300520485852384)
XLA Ops:
  0.6 0.1 pad_add_fusion
  0.7 0.0 copy-start
  0.7 0.0 copy-start.1
  0.7 4.9 %contract.3 = (f32[4,1024,128]{2,1,0:T(8,128)S(1)}, f32[1024,128]{1,0:T(8,128)S(1)}) custom-call(s32[2]{0:T(128)S(1)} %get-tuple-element.49.at_ref, f32[16384,128]{1,0:T(8,128)} %bitcast.13, f32[256,128]{1,0:T(8,128)} %a_in.3, f32[4,128]{1,0:T(4,128)} %c_in.3), custom_call_target="tpu_custom_call" | custom-call | flops 2147483648 | bytes 6291456 | tf_op jit(solution)/shard_map/contract/pallas_call | solution.py:237
  5.6 0.1 collective-permute-start.10
  5.7 0.5 collective-permute-start.2
  6.2 0.0 copy-done
  6.2 0.3 gram_halves.1
  6.5 0.0 copy-done.1
  6.5 4.7 %contract.2 = (f32[4,1024,128]{2,1,0:T(8,128)S(1)}, f32[1024,128]{1,0:T(8,128)S(1)}) custom-call(s32[2]{0:T(128)S(1)} %get-tuple-element.29.at_ref, f32[16384,128]{1,0:T(8,128)} %bitcast.14, f32[256,128]{1,0:T(8,128)S(1)} %copy-done, f32[4,128]{1,0:T(4,128)S(1)} %copy-done.1), custom_call_target="tpu_custom_call" | custom-call | flops 2147483648 | bytes 6291456 | tf_op jit(solution)/shard_map/contract/pallas_call | solution.py:237
  11.3 0.0 copy-start.2
  11.3 0.0 collective-permute-done.2.far_ref
  11.3 0.1 parcels.1
  11.4 2.2 %collective-permute-start.3 = (f32[256,128]{1,0:T(8,128)S(1)}, f32[256,128]{1,0:T(8,128)S(1)}, u32[]{:S(2)}, u32[]{:S(2)}) collective-permute-start(f32[256,128]{1,0:T(8,128)S(1)} %get-tuple-element.33), channel_id=1, source_target_pairs={{0,1},{1,0},{16,17},{17,16},{2,3},{3,2},{18,19},{19,18},{4,5},{5,4... | collective-permute-start | bytes 393224 | tf_op jit(solution)/shard_map/ppermute | solution.py:376
  13.6 1.4 %collective-permute-start.4 = (f32[256,128]{1,0:T(8,128)S(1)}, f32[256,128]{1,0:T(8,128)S(1)}, u32[]{:S(2)}, u32[]{:S(2)}) collective-permute-start(f32[256,128]{1,0:T(8,128)S(1)} %get-tuple-element.34), channel_id=1, source_target_pairs={{0,16},{1,17},{16,0},{17,1},{2,18},{3,19},{18,2},{19,3},{4,20},{5,... | collective-permute-start | bytes 393224 | tf_op jit(solution)/shard_map/ppermute | solution.py:376
  15.0 0.5 collective-permute-start.5
  15.5 0.0 collective-permute-start
  15.5 1.2 %collective-permute-done = f32[64,128]{1,0:T(8,128)S(1)} collective-permute-done((f32[64,128]{1,0:T(8,128)S(1)}, f32[64,128]{1,0:T(8,128)S(1)}, u32[]{:S(2)}, u32[]{:S(2)}) %collective-permute-start) | collective-permute-done | bytes 32800 | tf_op jit(solution)/shard_map/ppermute | solution.py:376
  16.8 2.3 %collective-permute-start.1 = (f32[64,128]{1,0:T(8,128)S(1)}, f32[64,128]{1,0:T(8,128)S(1)}, u32[]{:S(2)}, u32[]{:S(2)}) collective-permute-start(f32[64,128]{1,0:T(8,128)S(1)} %add.10.g_ref), channel_id=1, source_target_pairs={{0,16},{16,0},{1,17},{17,1},{2,18},{18,2},{3,19},{19,3},{4,20},{20... | collective-permute-start | bytes 98312 | tf_op jit(solution)/shard_map/ppermute | solution.py:376
  19.0 3.0 %collective-permute-done.1.g_far_ref = f32[64,128]{1,0:T(8,128)S(1)} collective-permute-done((f32[64,128]{1,0:T(8,128)S(1)}, f32[64,128]{1,0:T(8,128)S(1)}, u32[]{:S(2)}, u32[]{:S(2)}) %collective-permute-start.1) | collective-permute-done | bytes 32800 | tf_op jit(solution)/shard_map/ppermute | solution.py:376
  22.0 0.0 collective-permute-done.3.refs_1_
  22.0 0.0 collective-permute-done.4.refs_2_
  22.0 0.0 collective-permute-done.5.refs_3_
  22.0 17.7 %all_to_all.15.x_ref = f32[8,40,128]{2,1,0:T(8,128)S(1)} all-to-all(f32[8,40,128]{2,1,0:T(8,128)S(1)} %column_sum.1), channel_id=1, replica_groups=mesh['z'=8,'xl'=2,'c'=2,'y'=4,'xh'=2] {'z'}, dimensions={0} | all-to-all | bytes 327680 | tf_op jit(solution)/shard_map/all_to_all | solution.py:401
  39.8 11.8 %all_to_all.16.x_ref = f32[8,40,128]{2,1,0:T(8,128)S(1)} all-to-all(f32[8,40,128]{2,1,0:T(8,128)S(1)} %spread.1), channel_id=1, replica_groups=mesh['z'=8,'xl'=2,'c'=2,'y'=4,'xh'=2] {'z'}, dimensions={0} | all-to-all | bytes 327680 | tf_op jit(solution)/shard_map/all_to_all | solution.py:402
  51.6 0.1 collective-permute-start.9
  51.7 1.3 %collective-permute-start.8 = (f32[256,128]{1,0:T(8,128)S(1)}, f32[256,128]{1,0:T(8,128)S(1)}, u32[]{:S(2)}, u32[]{:S(2)}) collective-permute-start(f32[256,128]{1,0:T(8,128)S(1)} %get-tuple-element.36.refs_0_), channel_id=1, source_target_pairs={{0,17},{1,16},{16,1},{17,0},{2,19},{3,18},{18,3},{19,2},{4,21},{5,... | collective-permute-start | bytes 393224 | tf_op jit(solution)/shard_map/ppermute | solution.py:376
  53.0 1.8 %collective-permute-start.7 = (f32[256,128]{1,0:T(8,128)S(1)}, f32[256,128]{1,0:T(8,128)S(1)}, u32[]{:S(2)}, u32[]{:S(2)}) collective-permute-start(f32[256,128]{1,0:T(8,128)S(1)} %get-tuple-element.36.refs_0_), channel_id=1, source_target_pairs={{0,16},{1,17},{16,0},{17,1},{2,18},{3,19},{18,2},{19,3},{4,20},{5,... | collective-permute-start | bytes 393224 | tf_op jit(solution)/shard_map/ppermute | solution.py:376
  54.8 0.4 collective-permute-start.6
  55.3 0.0 collective-permute-done.9.far_ref
  55.3 0.0 copy-done.2
  55.3 3.9 %first_inverse.1 = (f32[128,128]{1,0:T(8,128)S(1)}, f32[128,128]{1,0:T(8,128)S(1)}) custom-call(s32[1]{0:T(128)} %bitcast.core_ref, f32[64,128]{1,0:T(8,128)S(1)} %get-tuple-element.37.near_ref, f32[64,128]{1,0:T(8,128)S(1)} %collective-permute-done.9.far_ref, f32[128,128]{1,0:T(8,128)S(1)} %copy-done.2), custom_call_target="tpu_custom_call" | custom-call | flops 3000000000 | bytes 524288 | tf_op jit(solution)/shard_map/first_inverse/pallas_call | solution.py:135
  59.2 0.0 collective-permute-done.8.refs_3_
  59.2 0.2 collective-permute-done.7.refs_2_
  59.4 2.2 %collective-permute-done.6.refs_1_ = f32[256,128]{1,0:T(8,128)S(1)} collective-permute-done((f32[256,128]{1,0:T(8,128)S(1)}, f32[256,128]{1,0:T(8,128)S(1)}, u32[]{:S(2)}, u32[]{:S(2)}) %collective-permute-start.6) | collective-permute-done | bytes 131104 | tf_op jit(solution)/shard_map/ppermute | solution.py:376
  61.6 0.0 collective-permute-done.10.refs_6_
  61.6 1.4 %solve.1 = (f32[1024,128]{1,0:T(8,128)S(1)}, f32[136,128]{1,0:T(8,128)S(1)}) custom-call(f32[256,128]{1,0:T(8,128)S(1)} %get-tuple-element.36.refs_0_, f32[256,128]{1,0:T(8,128)S(1)} %collective-permute-done.6.refs_1_, f32[256,128]{1,0:T(8,128)S(1)} %collective-permute-done.7.refs_2_, f32[256,128]{1,0:T(8,128)S(1)} %collective-permute-done.8.refs_3_, ...), custom_call_target="tpu_custom_call" | custom-call | tf_op jit(solution)/shard_map/solve/pallas_call | solution.py:361
  63.0 0.1 collective-permute-start.11
  63.1 1.2 %collective-permute-done.11 = f32[136,128]{1,0:T(8,128)S(1)} collective-permute-done((f32[136,128]{1,0:T(8,128)S(1)}, f32[136,128]{1,0:T(8,128)S(1)}, u32[]{:S(2)}, u32[]{:S(2)}) %collective-permute-start.11) | collective-permute-done | bytes 69664 | tf_op jit(solution)/shard_map/ppermute | solution.py:376
  64.4 0.2 collective-permute-start.12
  64.6 3.0 %collective-permute-start.15 = (f32[136,128]{1,0:T(8,128)S(1)}, f32[136,128]{1,0:T(8,128)S(1)}, u32[]{:S(2)}, u32[]{:S(2)}) collective-permute-start(f32[136,128]{1,0:T(8,128)S(1)} %add.11.refs_0_), channel_id=1, source_target_pairs={{0,6},{2,4},{4,2},{6,0},{1,7},{3,5},{5,3},{7,1},{8,14},{10,12},{12... | collective-permute-start | bytes 208904 | tf_op jit(solution)/shard_map/ppermute | solution.py:376
  67.6 0.6 collective-permute-start.14
  68.3 0.5 collective-permute-start.13
  68.7 0.0 collective-permute-done.12
  68.7 1.6 %assemble.1 = f32[8,256,128]{2,1,0:T(8,128)} custom-call(s32[2]{0:T(128)S(1)} %get-tuple-element.29.at_ref, f32[4,256,128]{2,1,0:T(8,128)S(1)} %bitcast.11, f32[4,256,128]{2,1,0:T(8,128)S(1)} %bitcast.12), custom_call_target="tpu_custom_call" | custom-call | tf_op jit(solution)/shard_map/assemble/pallas_call | solution.py:169
  70.3 0.8 collective-permute-done.15.refs_3_
  71.1 2.9 %collective-permute-done.14.refs_2_ = f32[136,128]{1,0:T(8,128)S(1)} collective-permute-done((f32[136,128]{1,0:T(8,128)S(1)}, f32[136,128]{1,0:T(8,128)S(1)}, u32[]{:S(2)}, u32[]{:S(2)}) %collective-permute-start.14) | collective-permute-done | bytes 69664 | tf_op jit(solution)/shard_map/ppermute | solution.py:376
  74.0 0.0 collective-permute-done.13.refs_1_
  74.0 0.6 collect.1
  74.7 5.1 %all-to-all-start.2 = ((f32[16,4,128]{2,1,0:T(4,128)}), f32[16,4,128]{2,1,0:T(4,128)S(1)}, u32[]{:S(2)}, u32[]{:S(2)}) async-start(f32[16,4,128]{2,1,0:T(4,128)} %collect.1), calls=%async_computation.2 | async-start | bytes 65536 | tf_op jit(solution)/shard_map/all_to_all | solution.py:418
  79.7 3.9 %inverse_of_product.1.inv_ref = f32[128,128]{1,0:T(8,128)S(1)} custom-call(f32[128,128]{1,0:T(8,128)S(1)} %get-tuple-element.47.first_ref, f32[136,128]{1,0:T(8,128)S(1)} %add.11.refs_0_, f32[136,128]{1,0:T(8,128)S(1)} %collective-permute-done.13.refs_1_, f32[136,128]{1,0:T(8,128)S(1)} %collective-permute-done.14.refs_2_, ...), custom_call_target="tpu_custom_call" | custom-call | flops 3000000000 | bytes 524288 | tf_op jit(solution)/shard_map/inverse_of_product/pallas_call | solution.py:91
  83.7 3.5 %all-to-all-done.2.x_ref = f32[16,4,128]{2,1,0:T(4,128)S(1)} async-done(((f32[16,4,128]{2,1,0:T(4,128)}), f32[16,4,128]{2,1,0:T(4,128)S(1)}, u32[]{:S(2)}, u32[]{:S(2)}) %all-to-all-start.2) | async-done | bytes 32800 | tf_op jit(solution)/shard_map/all_to_all | solution.py:418
  87.2 0.8 product.1
  (5 shorter events, 0.1 us)
Async XLA Ops:
  0.7 5.5 %copy-start = (f32[256,128]{1,0:T(8,128)S(1)}, f32[256,128]{1,0:T(8,128)}, u32[]{:S(2)}) copy-start(f32[256,128]{1,0:T(8,128)} %a_in.3) | copy-start | bytes 393220
  0.7 5.8 %copy-start.1 = (f32[4,128]{1,0:T(4,128)S(1)}, f32[4,128]{1,0:T(4,128)}, u32[]{:S(2)}) copy-start(f32[4,128]{1,0:T(4,128)} %c_in.3) | copy-start | bytes 6148
  5.6 56.0 %collective-permute-start.10 = (f32[4,1024,128]{2,1,0:T(8,128)S(1)}, f32[4,1024,128]{2,1,0:T(8,128)S(1)}, u32[]{:S(2)}, u32[]{:S(2)}) collective-permute-start(f32[4,1024,128]{2,1,0:T(8,128)S(1)} %get-tuple-element.40), channel_id=1, source_target_pairs={{0,8},{8,0},{1,9},{9,1},{2,10},{10,2},{3,11},{11,3},{4,12},{12,4},... | collective-permute-start | bytes 6291464 | tf_op jit(solution)/shard_map/ppermute | solution.py:376
  5.7 5.6 %collective-permute-start.2 = (f32[1024,128]{1,0:T(8,128)S(1)}, f32[1024,128]{1,0:T(8,128)S(1)}, u32[]{:S(2)}, u32[]{:S(2)}) collective-permute-start(f32[1024,128]{1,0:T(8,128)S(1)} %get-tuple-element.31), channel_id=1, source_target_pairs={{0,8},{8,0},{1,9},{9,1},{2,10},{10,2},{3,11},{11,3},{4,12},{12,4},... | collective-permute-start | bytes 1572872 | tf_op jit(solution)/shard_map/ppermute | solution.py:376
  11.3 44.0 %copy-start.2 = (f32[128,128]{1,0:T(8,128)S(1)}, f32[128,128]{1,0:T(8,128)}, u32[]{:S(2)}) copy-start(f32[128,128]{1,0:T(8,128)} %second_ref.1) | copy-start | bytes 196612
  11.4 10.6 %collective-permute-start.3 = (f32[256,128]{1,0:T(8,128)S(1)}, f32[256,128]{1,0:T(8,128)S(1)}, u32[]{:S(2)}, u32[]{:S(2)}) collective-permute-start(f32[256,128]{1,0:T(8,128)S(1)} %get-tuple-element.33), channel_id=1, source_target_pairs={{0,1},{1,0},{16,17},{17,16},{2,3},{3,2},{18,19},{19,18},{4,5},{5,4... | collective-permute-start | bytes 393224 | tf_op jit(solution)/shard_map/ppermute | solution.py:376
  13.6 8.4 %collective-permute-start.4 = (f32[256,128]{1,0:T(8,128)S(1)}, f32[256,128]{1,0:T(8,128)S(1)}, u32[]{:S(2)}, u32[]{:S(2)}) collective-permute-start(f32[256,128]{1,0:T(8,128)S(1)} %get-tuple-element.34), channel_id=1, source_target_pairs={{0,16},{1,17},{16,0},{17,1},{2,18},{3,19},{18,2},{19,3},{4,20},{5,... | collective-permute-start | bytes 393224 | tf_op jit(solution)/shard_map/ppermute | solution.py:376
  15.0 7.0 %collective-permute-start.5 = (f32[256,128]{1,0:T(8,128)S(1)}, f32[256,128]{1,0:T(8,128)S(1)}, u32[]{:S(2)}, u32[]{:S(2)}) collective-permute-start(f32[256,128]{1,0:T(8,128)S(1)} %get-tuple-element.35), channel_id=1, source_target_pairs={{0,17},{1,16},{16,1},{17,0},{2,19},{3,18},{18,3},{19,2},{4,21},{5,... | collective-permute-start | bytes 393224 | tf_op jit(solution)/shard_map/ppermute | solution.py:376
  15.5 1.2 %collective-permute-start = (f32[64,128]{1,0:T(8,128)S(1)}, f32[64,128]{1,0:T(8,128)S(1)}, u32[]{:S(2)}, u32[]{:S(2)}) collective-permute-start(f32[64,128]{1,0:T(8,128)S(1)} %get-tuple-element.28), channel_id=1, source_target_pairs={{0,8},{8,0},{1,9},{9,1},{2,10},{10,2},{3,11},{11,3},{4,12},{12,4},... | collective-permute-start | bytes 98312 | tf_op jit(solution)/shard_map/ppermute | solution.py:376
  16.8 5.2 %collective-permute-start.1 = (f32[64,128]{1,0:T(8,128)S(1)}, f32[64,128]{1,0:T(8,128)S(1)}, u32[]{:S(2)}, u32[]{:S(2)}) collective-permute-start(f32[64,128]{1,0:T(8,128)S(1)} %add.10.g_ref), channel_id=1, source_target_pairs={{0,16},{16,0},{1,17},{17,1},{2,18},{18,2},{3,19},{19,3},{4,20},{20... | collective-permute-start | bytes 98312 | tf_op jit(solution)/shard_map/ppermute | solution.py:376
  51.6 3.7 %collective-permute-start.9 = (f32[64,128]{1,0:T(8,128)S(1)}, f32[64,128]{1,0:T(8,128)S(1)}, u32[]{:S(2)}, u32[]{:S(2)}) collective-permute-start(f32[64,128]{1,0:T(8,128)S(1)} %get-tuple-element.37.near_ref), channel_id=1, source_target_pairs={{0,8},{8,0},{1,9},{9,1},{2,10},{10,2},{3,11},{11,3},{4,12},{12,4},... | collective-permute-start | bytes 98312 | tf_op jit(solution)/shard_map/ppermute | solution.py:376
  51.7 7.5 %collective-permute-start.8 = (f32[256,128]{1,0:T(8,128)S(1)}, f32[256,128]{1,0:T(8,128)S(1)}, u32[]{:S(2)}, u32[]{:S(2)}) collective-permute-start(f32[256,128]{1,0:T(8,128)S(1)} %get-tuple-element.36.refs_0_), channel_id=1, source_target_pairs={{0,17},{1,16},{16,1},{17,0},{2,19},{3,18},{18,3},{19,2},{4,21},{5,... | collective-permute-start | bytes 393224 | tf_op jit(solution)/shard_map/ppermute | solution.py:376
  53.0 6.3 %collective-permute-start.7 = (f32[256,128]{1,0:T(8,128)S(1)}, f32[256,128]{1,0:T(8,128)S(1)}, u32[]{:S(2)}, u32[]{:S(2)}) collective-permute-start(f32[256,128]{1,0:T(8,128)S(1)} %get-tuple-element.36.refs_0_), channel_id=1, source_target_pairs={{0,16},{1,17},{16,0},{17,1},{2,18},{3,19},{18,2},{19,3},{4,20},{5,... | collective-permute-start | bytes 393224 | tf_op jit(solution)/shard_map/ppermute | solution.py:376
  54.8 6.8 %collective-permute-start.6 = (f32[256,128]{1,0:T(8,128)S(1)}, f32[256,128]{1,0:T(8,128)S(1)}, u32[]{:S(2)}, u32[]{:S(2)}) collective-permute-start(f32[256,128]{1,0:T(8,128)S(1)} %get-tuple-element.36.refs_0_), channel_id=1, source_target_pairs={{0,1},{1,0},{16,17},{17,16},{2,3},{3,2},{18,19},{19,18},{4,5},{5,4... | collective-permute-start | bytes 393224 | tf_op jit(solution)/shard_map/ppermute | solution.py:376
  63.0 1.3 %collective-permute-start.11 = (f32[136,128]{1,0:T(8,128)S(1)}, f32[136,128]{1,0:T(8,128)S(1)}, u32[]{:S(2)}, u32[]{:S(2)}) collective-permute-start(f32[136,128]{1,0:T(8,128)S(1)} %get-tuple-element.41), channel_id=1, source_target_pairs={{0,8},{8,0},{1,9},{9,1},{2,10},{10,2},{3,11},{11,3},{4,12},{12,4},... | collective-permute-start | bytes 208904 | tf_op jit(solution)/shard_map/ppermute | solution.py:376
  64.4 4.3 %collective-permute-start.12 = (f32[1024,128]{1,0:T(8,128)S(1)}, f32[1024,128]{1,0:T(8,128)S(1)}, u32[]{:S(2)}, u32[]{:S(2)}) collective-permute-start(f32[1024,128]{1,0:T(8,128)S(1)} %get-tuple-element.44), channel_id=1, source_target_pairs={{0,8},{8,0},{1,9},{9,1},{2,10},{10,2},{3,11},{11,3},{4,12},{12,4},... | collective-permute-start | bytes 1572872 | tf_op jit(solution)/shard_map/ppermute | solution.py:376
  64.6 6.5 %collective-permute-start.15 = (f32[136,128]{1,0:T(8,128)S(1)}, f32[136,128]{1,0:T(8,128)S(1)}, u32[]{:S(2)}, u32[]{:S(2)}) collective-permute-start(f32[136,128]{1,0:T(8,128)S(1)} %add.11.refs_0_), channel_id=1, source_target_pairs={{0,6},{2,4},{4,2},{6,0},{1,7},{3,5},{5,3},{7,1},{8,14},{10,12},{12... | collective-permute-start | bytes 208904 | tf_op jit(solution)/shard_map/ppermute | solution.py:376
  67.6 6.4 %collective-permute-start.14 = (f32[136,128]{1,0:T(8,128)S(1)}, f32[136,128]{1,0:T(8,128)S(1)}, u32[]{:S(2)}, u32[]{:S(2)}) collective-permute-start(f32[136,128]{1,0:T(8,128)S(1)} %add.11.refs_0_), channel_id=1, source_target_pairs={{0,4},{2,6},{4,0},{6,2},{1,5},{3,7},{5,1},{7,3},{8,12},{10,14},{12... | collective-permute-start | bytes 208904 | tf_op jit(solution)/shard_map/ppermute | solution.py:376
  68.3 5.8 %collective-permute-start.13 = (f32[136,128]{1,0:T(8,128)S(1)}, f32[136,128]{1,0:T(8,128)S(1)}, u32[]{:S(2)}, u32[]{:S(2)}) collective-permute-start(f32[136,128]{1,0:T(8,128)S(1)} %add.11.refs_0_), channel_id=1, source_target_pairs={{0,2},{2,0},{4,6},{6,4},{1,3},{3,1},{5,7},{7,5},{8,10},{10,8},{12,... | collective-permute-start | bytes 208904 | tf_op jit(solution)/shard_map/ppermute | solution.py:376
  74.7 12.6 %all-to-all-start.2 = ((f32[16,4,128]{2,1,0:T(4,128)}), f32[16,4,128]{2,1,0:T(4,128)S(1)}, u32[]{:S(2)}, u32[]{:S(2)}) async-start(f32[16,4,128]{2,1,0:T(4,128)} %collect.1), calls=%async_computation.2 | async-start | bytes 65536 | tf_op jit(solution)/shard_map/all_to_all | solution.py:418

commit v13 on v12

--- a/solution.py
+++ b/solution.py
@@ -340,7 +340,8 @@
 
 
 def solve_kernel(*refs):
-    columns, (inv_ref, p_ref, q_ref, f_ref, out_ref) = refs[:4], refs[4:]
+    own, third, second, first, inv_ref, p_ref, q_ref, f_ref, out_ref = refs
+    columns = own, first, second, third
     rank = inv_ref.shape[0]
     block = columns[0].shape[0]
     for n in range(4):
@@ -368,7 +369,7 @@
         out_specs=[VMEM] * 2,
         compiler_params=pltpu.CompilerParams(vmem_limit_bytes=12 << 20),
         name="solve",
-    )(*columns, inverse, first, second)
+    )(columns[0], *columns[:0:-1], inverse, first, second)
 
 
 def swap(x, axis, bit=1):

time: 88.2 us -> 87.9 us (level)
    all_to_all x1, starting transfers between devices: 5.07 us -> 3.94 us  [body(): shares = lax.all_to_all(spread_c, plane, 0, 0)]
where the time goes in v13:
time: 87.9 us; the launch traced here: 87.2 us
  blocking collectives  29.5 us (34%)
  Pallas kernels  22.2 us (25%)
  starting transfers between devices  19.7 us (22%)
  waiting for transfers between devices  14.8 us (17%)
    all_to_all x1, blocking collectives, body(): column = spread(lax.all_to_all(column, 'z', 0, 0))  17.7 us
    ppermute x16, starting transfers between devices, swap(): return lax.ppermute(x, axis, [(i, i ^ bit) for i in range(n)])  15.8 us
    all_to_all x1, blocking collectives, body(): column, near = flatten(lax.all_to_all(column, 'z', 0, 0), rank // 2)  11.8 us
    ppermute x16, waiting for transfers between devices, swap(): return lax.ppermute(x, axis, [(i, i ^ bit) for i in range(n)])  11.3 us
    pallas_call x2, Pallas kernels, contract(): pl.pallas_call(functools.partial(contract_kernel, chunk, resident), out_s...  9.61 us
    all_to_all x1, starting transfers between devices, body(): shares = lax.all_to_all(spread_c, plane, 0, 0)  3.94 us
    pallas_call x1, Pallas kernels, first_inverse(): pl.pallas_call(first_inverse_kernel, out_shape=[square, square], in_specs...  3.93 us
    pallas_call x1, Pallas kernels, inverse_of_product(): pl.pallas_call(inverse_kernel, out_shape=jax.ShapeDtypeStruct(first.shape...  3.93 us
  transfers between devices with their start and end apart: 17, of which 8 were waited for; matrix products, arithmetic and copies ran while one was open for 0% of the time, Pallas kernels for 17%

profile of v13, /device:TPU:2, one launch (start us, length us, event | category | flops | bytes accessed | tf_op | source)
XLA Modules:
  0.0 87.2 jit_solution(706216929410556196)
XLA Ops:
  0.6 0.1 pad_add_fusion
  0.7 0.0 copy-start
  0.7 0.0 copy-start.1
  0.7 4.9 %contract.3 = (f32[4,1024,128]{2,1,0:T(8,128)S(1)}, f32[1024,128]{1,0:T(8,128)S(1)}) custom-call(s32[2]{0:T(128)S(1)} %get-tuple-element.49.at_ref, f32[16384,128]{1,0:T(8,128)} %bitcast.13, f32[256,128]{1,0:T(8,128)} %a_in.3, f32[4,128]{1,0:T(4,128)} %c_in.3), custom_call_target="tpu_custom_call" | custom-call | flops 2147483648 | bytes 6291456 | tf_op jit(solution)/shard_map/contract/pallas_call | solution.py:237
  5.6 0.1 collective-permute-start.10
  5.7 0.5 collective-permute-start.2
  6.2 0.0 copy-done
  6.2 0.3 gram_halves.1
  6.5 0.0 copy-done.1
  6.5 4.7 %contract.2 = (f32[4,1024,128]{2,1,0:T(8,128)S(1)}, f32[1024,128]{1,0:T(8,128)S(1)}) custom-call(s32[2]{0:T(128)S(1)} %get-tuple-element.29.at_ref, f32[16384,128]{1,0:T(8,128)} %bitcast.14, f32[256,128]{1,0:T(8,128)S(1)} %copy-done, f32[4,128]{1,0:T(4,128)S(1)} %copy-done.1), custom_call_target="tpu_custom_call" | custom-call | flops 2147483648 | bytes 6291456 | tf_op jit(solution)/shard_map/contract/pallas_call | solution.py:237
  11.3 0.0 copy-start.2
  11.3 0.0 collective-permute-done.2.far_ref
  11.3 0.1 parcels.1
  11.4 2.2 %collective-permute-start.3 = (f32[256,128]{1,0:T(8,128)S(1)}, f32[256,128]{1,0:T(8,128)S(1)}, u32[]{:S(2)}, u32[]{:S(2)}) collective-permute-start(f32[256,128]{1,0:T(8,128)S(1)} %get-tuple-element.33), channel_id=1, source_target_pairs={{0,1},{1,0},{16,17},{17,16},{2,3},{3,2},{18,19},{19,18},{4,5},{5,4... | collective-permute-start | bytes 393224 | tf_op jit(solution)/shard_map/ppermute | solution.py:377
  13.6 1.4 %collective-permute-start.4 = (f32[256,128]{1,0:T(8,128)S(1)}, f32[256,128]{1,0:T(8,128)S(1)}, u32[]{:S(2)}, u32[]{:S(2)}) collective-permute-start(f32[256,128]{1,0:T(8,128)S(1)} %get-tuple-element.34), channel_id=1, source_target_pairs={{0,16},{1,17},{16,0},{17,1},{2,18},{3,19},{18,2},{19,3},{4,20},{5,... | collective-permute-start | bytes 393224 | tf_op jit(solution)/shard_map/ppermute | solution.py:377
  15.0 0.5 collective-permute-start.5
  15.5 0.0 collective-permute-start
  15.5 1.2 %collective-permute-done = f32[64,128]{1,0:T(8,128)S(1)} collective-permute-done((f32[64,128]{1,0:T(8,128)S(1)}, f32[64,128]{1,0:T(8,128)S(1)}, u32[]{:S(2)}, u32[]{:S(2)}) %collective-permute-start) | collective-permute-done | bytes 32800 | tf_op jit(solution)/shard_map/ppermute | solution.py:377
  16.8 2.3 %collective-permute-start.1 = (f32[64,128]{1,0:T(8,128)S(1)}, f32[64,128]{1,0:T(8,128)S(1)}, u32[]{:S(2)}, u32[]{:S(2)}) collective-permute-start(f32[64,128]{1,0:T(8,128)S(1)} %add.10.g_ref), channel_id=1, source_target_pairs={{0,16},{16,0},{1,17},{17,1},{2,18},{18,2},{3,19},{19,3},{4,20},{20... | collective-permute-start | bytes 98312 | tf_op jit(solution)/shard_map/ppermute | solution.py:377
  19.0 3.0 %collective-permute-done.1.g_far_ref = f32[64,128]{1,0:T(8,128)S(1)} collective-permute-done((f32[64,128]{1,0:T(8,128)S(1)}, f32[64,128]{1,0:T(8,128)S(1)}, u32[]{:S(2)}, u32[]{:S(2)}) %collective-permute-start.1) | collective-permute-done | bytes 32800 | tf_op jit(solution)/shard_map/ppermute | solution.py:377
  22.0 0.0 collective-permute-done.3.refs_1_
  22.0 0.0 collective-permute-done.4.refs_2_
  22.0 0.0 collective-permute-done.5.refs_3_
  22.0 17.7 %all_to_all.15.x_ref = f32[8,40,128]{2,1,0:T(8,128)S(1)} all-to-all(f32[8,40,128]{2,1,0:T(8,128)S(1)} %column_sum.1), channel_id=1, replica_groups=mesh['z'=8,'xl'=2,'c'=2,'y'=4,'xh'=2] {'z'}, dimensions={0} | all-to-all | bytes 327680 | tf_op jit(solution)/shard_map/all_to_all | solution.py:402
  39.8 11.8 %all_to_all.16.x_ref = f32[8,40,128]{2,1,0:T(8,128)S(1)} all-to-all(f32[8,40,128]{2,1,0:T(8,128)S(1)} %spread.1), channel_id=1, replica_groups=mesh['z'=8,'xl'=2,'c'=2,'y'=4,'xh'=2] {'z'}, dimensions={0} | all-to-all | bytes 327680 | tf_op jit(solution)/shard_map/all_to_all | solution.py:403
  51.6 0.1 collective-permute-start.9
  51.7 2.0 %collective-permute-start.8 = (f32[256,128]{1,0:T(8,128)S(1)}, f32[256,128]{1,0:T(8,128)S(1)}, u32[]{:S(2)}, u32[]{:S(2)}) collective-permute-start(f32[256,128]{1,0:T(8,128)S(1)} %get-tuple-element.36.refs_0_), channel_id=1, source_target_pairs={{0,1},{1,0},{16,17},{17,16},{2,3},{3,2},{18,19},{19,18},{4,5},{5,4... | collective-permute-start | bytes 393224 | tf_op jit(solution)/shard_map/ppermute | solution.py:377
  53.7 1.4 %collective-permute-start.7 = (f32[256,128]{1,0:T(8,128)S(1)}, f32[256,128]{1,0:T(8,128)S(1)}, u32[]{:S(2)}, u32[]{:S(2)}) collective-permute-start(f32[256,128]{1,0:T(8,128)S(1)} %get-tuple-element.36.refs_0_), channel_id=1, source_target_pairs={{0,16},{1,17},{16,0},{17,1},{2,18},{3,19},{18,2},{19,3},{4,20},{5,... | collective-permute-start | bytes 393224 | tf_op jit(solution)/shard_map/ppermute | solution.py:377
  55.1 0.8 collective-permute-start.6
  55.9 0.0 collective-permute-done.9.far_ref
  55.9 0.0 copy-done.2
  55.9 3.9 %first_inverse.1 = (f32[128,128]{1,0:T(8,128)S(1)}, f32[128,128]{1,0:T(8,128)S(1)}) custom-call(s32[1]{0:T(128)} %bitcast.core_ref, f32[64,128]{1,0:T(8,128)S(1)} %get-tuple-element.37.near_ref, f32[64,128]{1,0:T(8,128)S(1)} %collective-permute-done.9.far_ref, f32[128,128]{1,0:T(8,128)S(1)} %copy-done.2), custom_call_target="tpu_custom_call" | custom-call | flops 3000000000 | bytes 524288 | tf_op jit(solution)/shard_map/first_inverse/pallas_call | solution.py:135
  59.8 0.0 collective-permute-done.8.refs_3_
  59.8 1.9 %collective-permute-done.7.refs_2_ = f32[256,128]{1,0:T(8,128)S(1)} collective-permute-done((f32[256,128]{1,0:T(8,128)S(1)}, f32[256,128]{1,0:T(8,128)S(1)}, u32[]{:S(2)}, u32[]{:S(2)}) %collective-permute-start.7) | collective-permute-done | bytes 131104 | tf_op jit(solution)/shard_map/ppermute | solution.py:377
  61.7 0.2 collective-permute-done.6.refs_1_
  61.9 0.0 collective-permute-done.10.refs_6_
  61.9 1.4 %solve.1 = (f32[1024,128]{1,0:T(8,128)S(1)}, f32[136,128]{1,0:T(8,128)S(1)}) custom-call(f32[256,128]{1,0:T(8,128)S(1)} %get-tuple-element.36.refs_0_, f32[256,128]{1,0:T(8,128)S(1)} %collective-permute-done.6.refs_1_, f32[256,128]{1,0:T(8,128)S(1)} %collective-permute-done.7.refs_2_, f32[256,128]{1,0:T(8,128)S(1)} %collective-permute-done.8.refs_3_, ...), custom_call_target="tpu_custom_call" | custom-call | tf_op jit(solution)/shard_map/solve/pallas_call | solution.py:362
  63.3 0.1 collective-permute-start.11
  63.4 1.2 %collective-permute-done.11 = f32[136,128]{1,0:T(8,128)S(1)} collective-permute-done((f32[136,128]{1,0:T(8,128)S(1)}, f32[136,128]{1,0:T(8,128)S(1)}, u32[]{:S(2)}, u32[]{:S(2)}) %collective-permute-start.11) | collective-permute-done | bytes 69664 | tf_op jit(solution)/shard_map/ppermute | solution.py:377
  64.7 0.2 collective-permute-start.12
  64.9 3.0 %collective-permute-start.15 = (f32[136,128]{1,0:T(8,128)S(1)}, f32[136,128]{1,0:T(8,128)S(1)}, u32[]{:S(2)}, u32[]{:S(2)}) collective-permute-start(f32[136,128]{1,0:T(8,128)S(1)} %add.11.refs_0_), channel_id=1, source_target_pairs={{0,6},{2,4},{4,2},{6,0},{1,7},{3,5},{5,3},{7,1},{8,14},{10,12},{12... | collective-permute-start | bytes 208904 | tf_op jit(solution)/shard_map/ppermute | solution.py:377
  67.9 0.6 collective-permute-start.14
  68.6 0.4 collective-permute-start.13
  69.0 0.0 collective-permute-done.12
  69.0 1.6 %assemble.1 = f32[8,256,128]{2,1,0:T(8,128)} custom-call(s32[2]{0:T(128)S(1)} %get-tuple-element.29.at_ref, f32[4,256,128]{2,1,0:T(8,128)S(1)} %bitcast.11, f32[4,256,128]{2,1,0:T(8,128)S(1)} %bitcast.12), custom_call_target="tpu_custom_call" | custom-call | tf_op jit(solution)/shard_map/assemble/pallas_call | solution.py:169
  70.6 0.8 collective-permute-done.15.refs_3_
  71.4 2.9 %collective-permute-done.14.refs_2_ = f32[136,128]{1,0:T(8,128)S(1)} collective-permute-done((f32[136,128]{1,0:T(8,128)S(1)}, f32[136,128]{1,0:T(8,128)S(1)}, u32[]{:S(2)}, u32[]{:S(2)}) %collective-permute-start.14) | collective-permute-done | bytes 69664 | tf_op jit(solution)/shard_map/ppermute | solution.py:377
  74.4 0.0 collective-permute-done.13.refs_1_
  74.4 0.6 collect.1
  75.0 3.9 %all-to-all-start.2 = ((f32[16,4,128]{2,1,0:T(4,128)}), f32[16,4,128]{2,1,0:T(4,128)S(1)}, u32[]{:S(2)}, u32[]{:S(2)}) async-start(f32[16,4,128]{2,1,0:T(4,128)} %collect.1), calls=%async_computation.2 | async-start | bytes 65536 | tf_op jit(solution)/shard_map/all_to_all | solution.py:419
  78.9 3.9 %inverse_of_product.1.inv_ref = f32[128,128]{1,0:T(8,128)S(1)} custom-call(f32[128,128]{1,0:T(8,128)S(1)} %get-tuple-element.47.first_ref, f32[136,128]{1,0:T(8,128)S(1)} %add.11.refs_0_, f32[136,128]{1,0:T(8,128)S(1)} %collective-permute-done.13.refs_1_, f32[136,128]{1,0:T(8,128)S(1)} %collective-permute-done.14.refs_2_, ...), custom_call_target="tpu_custom_call" | custom-call | flops 3000000000 | bytes 524288 | tf_op jit(solution)/shard_map/inverse_of_product/pallas_call | solution.py:91
  82.9 3.5 %all-to-all-done.2.x_ref = f32[16,4,128]{2,1,0:T(4,128)S(1)} async-done(((f32[16,4,128]{2,1,0:T(4,128)}), f32[16,4,128]{2,1,0:T(4,128)S(1)}, u32[]{:S(2)}, u32[]{:S(2)}) %all-to-all-start.2) | async-done | bytes 32800 | tf_op jit(solution)/shard_map/all_to_all | solution.py:419
  86.4 0.8 product.1
  (5 shorter events, 0.1 us)
Async XLA Ops:
  0.7 5.5 %copy-start = (f32[256,128]{1,0:T(8,128)S(1)}, f32[256,128]{1,0:T(8,128)}, u32[]{:S(2)}) copy-start(f32[256,128]{1,0:T(8,128)} %a_in.3) | copy-start | bytes 393220
  0.7 5.8 %copy-start.1 = (f32[4,128]{1,0:T(4,128)S(1)}, f32[4,128]{1,0:T(4,128)}, u32[]{:S(2)}) copy-start(f32[4,128]{1,0:T(4,128)} %c_in.3) | copy-start | bytes 6148
  5.6 56.4 %collective-permute-start.10 = (f32[4,1024,128]{2,1,0:T(8,128)S(1)}, f32[4,1024,128]{2,1,0:T(8,128)S(1)}, u32[]{:S(2)}, u32[]{:S(2)}) collective-permute-start(f32[4,1024,128]{2,1,0:T(8,128)S(1)} %get-tuple-element.40), channel_id=1, source_target_pairs={{0,8},{8,0},{1,9},{9,1},{2,10},{10,2},{3,11},{11,3},{4,12},{12,4},... | collective-permute-start | bytes 6291464 | tf_op jit(solution)/shard_map/ppermute | solution.py:377
  5.7 5.6 %collective-permute-start.2 = (f32[1024,128]{1,0:T(8,128)S(1)}, f32[1024,128]{1,0:T(8,128)S(1)}, u32[]{:S(2)}, u32[]{:S(2)}) collective-permute-start(f32[1024,128]{1,0:T(8,128)S(1)} %get-tuple-element.31), channel_id=1, source_target_pairs={{0,8},{8,0},{1,9},{9,1},{2,10},{10,2},{3,11},{11,3},{4,12},{12,4},... | collective-permute-start | bytes 1572872 | tf_op jit(solution)/shard_map/ppermute | solution.py:377
  11.3 44.6 %copy-start.2 = (f32[128,128]{1,0:T(8,128)S(1)}, f32[128,128]{1,0:T(8,128)}, u32[]{:S(2)}) copy-start(f32[128,128]{1,0:T(8,128)} %second_ref.1) | copy-start | bytes 196612
  11.4 10.6 %collective-permute-start.3 = (f32[256,128]{1,0:T(8,128)S(1)}, f32[256,128]{1,0:T(8,128)S(1)}, u32[]{:S(2)}, u32[]{:S(2)}) collective-permute-start(f32[256,128]{1,0:T(8,128)S(1)} %get-tuple-element.33), channel_id=1, source_target_pairs={{0,1},{1,0},{16,17},{17,16},{2,3},{3,2},{18,19},{19,18},{4,5},{5,4... | collective-permute-start | bytes 393224 | tf_op jit(solution)/shard_map/ppermute | solution.py:377
  13.6 8.4 %collective-permute-start.4 = (f32[256,128]{1,0:T(8,128)S(1)}, f32[256,128]{1,0:T(8,128)S(1)}, u32[]{:S(2)}, u32[]{:S(2)}) collective-permute-start(f32[256,128]{1,0:T(8,128)S(1)} %get-tuple-element.34), channel_id=1, source_target_pairs={{0,16},{1,17},{16,0},{17,1},{2,18},{3,19},{18,2},{19,3},{4,20},{5,... | collective-permute-start | bytes 393224 | tf_op jit(solution)/shard_map/ppermute | solution.py:377
  15.0 7.0 %collective-permute-start.5 = (f32[256,128]{1,0:T(8,128)S(1)}, f32[256,128]{1,0:T(8,128)S(1)}, u32[]{:S(2)}, u32[]{:S(2)}) collective-permute-start(f32[256,128]{1,0:T(8,128)S(1)} %get-tuple-element.35), channel_id=1, source_target_pairs={{0,17},{1,16},{16,1},{17,0},{2,19},{3,18},{18,3},{19,2},{4,21},{5,... | collective-permute-start | bytes 393224 | tf_op jit(solution)/shard_map/ppermute | solution.py:377
  15.5 1.2 %collective-permute-start = (f32[64,128]{1,0:T(8,128)S(1)}, f32[64,128]{1,0:T(8,128)S(1)}, u32[]{:S(2)}, u32[]{:S(2)}) collective-permute-start(f32[64,128]{1,0:T(8,128)S(1)} %get-tuple-element.28), channel_id=1, source_target_pairs={{0,8},{8,0},{1,9},{9,1},{2,10},{10,2},{3,11},{11,3},{4,12},{12,4},... | collective-permute-start | bytes 98312 | tf_op jit(solution)/shard_map/ppermute | solution.py:377
  16.8 5.2 %collective-permute-start.1 = (f32[64,128]{1,0:T(8,128)S(1)}, f32[64,128]{1,0:T(8,128)S(1)}, u32[]{:S(2)}, u32[]{:S(2)}) collective-permute-start(f32[64,128]{1,0:T(8,128)S(1)} %add.10.g_ref), channel_id=1, source_target_pairs={{0,16},{16,0},{1,17},{17,1},{2,18},{18,2},{3,19},{19,3},{4,20},{20... | collective-permute-start | bytes 98312 | tf_op jit(solution)/shard_map/ppermute | solution.py:377
  51.6 4.3 %collective-permute-start.9 = (f32[64,128]{1,0:T(8,128)S(1)}, f32[64,128]{1,0:T(8,128)S(1)}, u32[]{:S(2)}, u32[]{:S(2)}) collective-permute-start(f32[64,128]{1,0:T(8,128)S(1)} %get-tuple-element.37.near_ref), channel_id=1, source_target_pairs={{0,8},{8,0},{1,9},{9,1},{2,10},{10,2},{3,11},{11,3},{4,12},{12,4},... | collective-permute-start | bytes 98312 | tf_op jit(solution)/shard_map/ppermute | solution.py:377
  51.7 8.1 %collective-permute-start.8 = (f32[256,128]{1,0:T(8,128)S(1)}, f32[256,128]{1,0:T(8,128)S(1)}, u32[]{:S(2)}, u32[]{:S(2)}) collective-permute-start(f32[256,128]{1,0:T(8,128)S(1)} %get-tuple-element.36.refs_0_), channel_id=1, source_target_pairs={{0,1},{1,0},{16,17},{17,16},{2,3},{3,2},{18,19},{19,18},{4,5},{5,4... | collective-permute-start | bytes 393224 | tf_op jit(solution)/shard_map/ppermute | solution.py:377
  53.7 8.1 %collective-permute-start.7 = (f32[256,128]{1,0:T(8,128)S(1)}, f32[256,128]{1,0:T(8,128)S(1)}, u32[]{:S(2)}, u32[]{:S(2)}) collective-permute-start(f32[256,128]{1,0:T(8,128)S(1)} %get-tuple-element.36.refs_0_), channel_id=1, source_target_pairs={{0,16},{1,17},{16,0},{17,1},{2,18},{3,19},{18,2},{19,3},{4,20},{5,... | collective-permute-start | bytes 393224 | tf_op jit(solution)/shard_map/ppermute | solution.py:377
  55.1 6.8 %collective-permute-start.6 = (f32[256,128]{1,0:T(8,128)S(1)}, f32[256,128]{1,0:T(8,128)S(1)}, u32[]{:S(2)}, u32[]{:S(2)}) collective-permute-start(f32[256,128]{1,0:T(8,128)S(1)} %get-tuple-element.36.refs_0_), channel_id=1, source_target_pairs={{0,17},{1,16},{16,1},{17,0},{2,19},{3,18},{18,3},{19,2},{4,21},{5,... | collective-permute-start | bytes 393224 | tf_op jit(solution)/shard_map/ppermute | solution.py:377
  63.3 1.3 %collective-permute-start.11 = (f32[136,128]{1,0:T(8,128)S(1)}, f32[136,128]{1,0:T(8,128)S(1)}, u32[]{:S(2)}, u32[]{:S(2)}) collective-permute-start(f32[136,128]{1,0:T(8,128)S(1)} %get-tuple-element.41), channel_id=1, source_target_pairs={{0,8},{8,0},{1,9},{9,1},{2,10},{10,2},{3,11},{11,3},{4,12},{12,4},... | collective-permute-start | bytes 208904 | tf_op jit(solution)/shard_map/ppermute | solution.py:377
  64.7 4.3 %collective-permute-start.12 = (f32[1024,128]{1,0:T(8,128)S(1)}, f32[1024,128]{1,0:T(8,128)S(1)}, u32[]{:S(2)}, u32[]{:S(2)}) collective-permute-start(f32[1024,128]{1,0:T(8,128)S(1)} %get-tuple-element.44), channel_id=1, source_target_pairs={{0,8},{8,0},{1,9},{9,1},{2,10},{10,2},{3,11},{11,3},{4,12},{12,4},... | collective-permute-start | bytes 1572872 | tf_op jit(solution)/shard_map/ppermute | solution.py:377
  64.9 6.5 %collective-permute-start.15 = (f32[136,128]{1,0:T(8,128)S(1)}, f32[136,128]{1,0:T(8,128)S(1)}, u32[]{:S(2)}, u32[]{:S(2)}) collective-permute-start(f32[136,128]{1,0:T(8,128)S(1)} %add.11.refs_0_), channel_id=1, source_target_pairs={{0,6},{2,4},{4,2},{6,0},{1,7},{3,5},{5,3},{7,1},{8,14},{10,12},{12... | collective-permute-start | bytes 208904 | tf_op jit(solution)/shard_map/ppermute | solution.py:377
  67.9 6.4 %collective-permute-start.14 = (f32[136,128]{1,0:T(8,128)S(1)}, f32[136,128]{1,0:T(8,128)S(1)}, u32[]{:S(2)}, u32[]{:S(2)}) collective-permute-start(f32[136,128]{1,0:T(8,128)S(1)} %add.11.refs_0_), channel_id=1, source_target_pairs={{0,4},{2,6},{4,0},{6,2},{1,5},{3,7},{5,1},{7,3},{8,12},{10,14},{12... | collective-permute-start | bytes 208904 | tf_op jit(solution)/shard_map/ppermute | solution.py:377
  68.6 5.8 %collective-permute-start.13 = (f32[136,128]{1,0:T(8,128)S(1)}, f32[136,128]{1,0:T(8,128)S(1)}, u32[]{:S(2)}, u32[]{:S(2)}) collective-permute-start(f32[136,128]{1,0:T(8,128)S(1)} %add.11.refs_0_), channel_id=1, source_target_pairs={{0,2},{2,0},{4,6},{6,4},{1,3},{3,1},{5,7},{7,5},{8,10},{10,8},{12,... | collective-permute-start | bytes 208904 | tf_op jit(solution)/shard_map/ppermute | solution.py:377
  75.0 11.4 %all-to-all-start.2 = ((f32[16,4,128]{2,1,0:T(4,128)}), f32[16,4,128]{2,1,0:T(4,128)S(1)}, u32[]{:S(2)}, u32[]{:S(2)}) async-start(f32[16,4,128]{2,1,0:T(4,128)} %collect.1), calls=%async_computation.2 | async-start | bytes 65536 | tf_op jit(solution)/shard_map/all_to_all | solution.py:419

commit v14 on v13

--- a/solution.py
+++ b/solution.py
@@ -409,7 +409,7 @@
 
     sums = sums + swap(sums, "c")
     sums, f_mine = lax.optimization_barrier((sums, f_mine))
-    parts = [sums] + [swap(sums, "y", bit) for bit in (1, 2, 3)]
+    parts = [sums] + [swap(sums, "y", bit) for bit in (1, 3, 2)]
     shape = (4, half // 4, rank)
     f_other = swap(f_mine, "c").reshape(shape)
     factor_b = assemble(here, f_mine.reshape(shape), f_other)

time: 87.9 us -> 87.2 us (level)
  waiting for transfers between devices: 14.8 us -> 13.9 us
where the time goes in v14:
time: 87.2 us; the launch traced here: 86.4 us
  blocking collectives  29.5 us (34%)
  Pallas kernels  22.2 us (25%)
  starting transfers between devices  19.9 us (23%)
  waiting for transfers between devices  13.9 us (16%)
    all_to_all x1, blocking collectives, body(): column = spread(lax.all_to_all(column, 'z', 0, 0))  17.7 us
    ppermute x16, starting transfers between devices, swap(): return lax.ppermute(x, axis, [(i, i ^ bit) for i in range(n)])  15.9 us
    all_to_all x1, blocking collectives, body(): column, near = flatten(lax.all_to_all(column, 'z', 0, 0), rank // 2)  11.8 us
    ppermute x16, waiting for transfers between devices, swap(): return lax.ppermute(x, axis, [(i, i ^ bit) for i in range(n)])  10.4 us
    pallas_call x2, Pallas kernels, contract(): pl.pallas_call(functools.partial(contract_kernel, chunk, resident), out_s...  9.61 us
    all_to_all x1, starting transfers between devices, body(): shares = lax.all_to_all(spread_c, plane, 0, 0)  3.94 us
    pallas_call x1, Pallas kernels, first_inverse(): pl.pallas_call(first_inverse_kernel, out_shape=[square, square], in_specs...  3.93 us
    pallas_call x1, Pallas kernels, inverse_of_product(): pl.pallas_call(inverse_kernel, out_shape=jax.ShapeDtypeStruct(first.shape...  3.93 us
  transfers between devices with their start and end apart: 17, of which 8 were waited for; matrix products, arithmetic and copies ran while one was open for 0% of the time, Pallas kernels for 17%

profile of v14, /device:TPU:2, one launch (start us, length us, event | category | flops | bytes accessed | tf_op | source)
XLA Modules:
  0.0 86.4 jit_solution(7100296357757384630)
XLA Ops:
  0.6 0.1 pad_add_fusion
  0.7 0.0 copy-start
  0.7 0.0 copy-start.1
  0.7 4.9 %contract.3 = (f32[4,1024,128]{2,1,0:T(8,128)S(1)}, f32[1024,128]{1,0:T(8,128)S(1)}) custom-call(s32[2]{0:T(128)S(1)} %get-tuple-element.49.at_ref, f32[16384,128]{1,0:T(8,128)} %bitcast.13, f32[256,128]{1,0:T(8,128)} %a_in.3, f32[4,128]{1,0:T(4,128)} %c_in.3), custom_call_target="tpu_custom_call" | custom-call | flops 2147483648 | bytes 6291456 | tf_op jit(solution)/shard_map/contract/pallas_call | solution.py:237
  5.6 0.1 collective-permute-start.10
  5.7 0.5 collective-permute-start.2
  6.2 0.0 copy-done
  6.2 0.3 gram_halves.1
  6.5 0.0 copy-done.1
  6.5 4.7 %contract.2 = (f32[4,1024,128]{2,1,0:T(8,128)S(1)}, f32[1024,128]{1,0:T(8,128)S(1)}) custom-call(s32[2]{0:T(128)S(1)} %get-tuple-element.29.at_ref, f32[16384,128]{1,0:T(8,128)} %bitcast.14, f32[256,128]{1,0:T(8,128)S(1)} %copy-done, f32[4,128]{1,0:T(4,128)S(1)} %copy-done.1), custom_call_target="tpu_custom_call" | custom-call | flops 2147483648 | bytes 6291456 | tf_op jit(solution)/shard_map/contract/pallas_call | solution.py:237
  11.3 0.0 copy-start.2
  11.3 0.0 collective-permute-done.2.far_ref
  11.3 0.1 parcels.1
  11.4 2.2 %collective-permute-start.3 = (f32[256,128]{1,0:T(8,128)S(1)}, f32[256,128]{1,0:T(8,128)S(1)}, u32[]{:S(2)}, u32[]{:S(2)}) collective-permute-start(f32[256,128]{1,0:T(8,128)S(1)} %get-tuple-element.33), channel_id=1, source_target_pairs={{0,1},{1,0},{16,17},{17,16},{2,3},{3,2},{18,19},{19,18},{4,5},{5,4... | collective-permute-start | bytes 393224 | tf_op jit(solution)/shard_map/ppermute | solution.py:377
  13.6 1.4 %collective-permute-start.4 = (f32[256,128]{1,0:T(8,128)S(1)}, f32[256,128]{1,0:T(8,128)S(1)}, u32[]{:S(2)}, u32[]{:S(2)}) collective-permute-start(f32[256,128]{1,0:T(8,128)S(1)} %get-tuple-element.34), channel_id=1, source_target_pairs={{0,16},{1,17},{16,0},{17,1},{2,18},{3,19},{18,2},{19,3},{4,20},{5,... | collective-permute-start | bytes 393224 | tf_op jit(solution)/shard_map/ppermute | solution.py:377
  15.0 0.5 collective-permute-start.5
  15.5 0.0 collective-permute-start
  15.5 1.2 %collective-permute-done = f32[64,128]{1,0:T(8,128)S(1)} collective-permute-done((f32[64,128]{1,0:T(8,128)S(1)}, f32[64,128]{1,0:T(8,128)S(1)}, u32[]{:S(2)}, u32[]{:S(2)}) %collective-permute-start) | collective-permute-done | bytes 32800 | tf_op jit(solution)/shard_map/ppermute | solution.py:377
  16.8 2.3 %collective-permute-start.1 = (f32[64,128]{1,0:T(8,128)S(1)}, f32[64,128]{1,0:T(8,128)S(1)}, u32[]{:S(2)}, u32[]{:S(2)}) collective-permute-start(f32[64,128]{1,0:T(8,128)S(1)} %add.10.g_ref), channel_id=1, source_target_pairs={{0,16},{16,0},{1,17},{17,1},{2,18},{18,2},{3,19},{19,3},{4,20},{20... | collective-permute-start | bytes 98312 | tf_op jit(solution)/shard_map/ppermute | solution.py:377
  19.0 3.0 %collective-permute-done.1.g_far_ref = f32[64,128]{1,0:T(8,128)S(1)} collective-permute-done((f32[64,128]{1,0:T(8,128)S(1)}, f32[64,128]{1,0:T(8,128)S(1)}, u32[]{:S(2)}, u32[]{:S(2)}) %collective-permute-start.1) | collective-permute-done | bytes 32800 | tf_op jit(solution)/shard_map/ppermute | solution.py:377
  22.0 0.0 collective-permute-done.3.refs_1_
  22.0 0.0 collective-permute-done.4.refs_2_
  22.0 0.0 collective-permute-done.5.refs_3_
  22.0 17.7 %all_to_all.15.x_ref = f32[8,40,128]{2,1,0:T(8,128)S(1)} all-to-all(f32[8,40,128]{2,1,0:T(8,128)S(1)} %column_sum.1), channel_id=1, replica_groups=mesh['z'=8,'xl'=2,'c'=2,'y'=4,'xh'=2] {'z'}, dimensions={0} | all-to-all | bytes 327680 | tf_op jit(solution)/shard_map/all_to_all | solution.py:402
  39.8 11.8 %all_to_all.16.x_ref = f32[8,40,128]{2,1,0:T(8,128)S(1)} all-to-all(f32[8,40,128]{2,1,0:T(8,128)S(1)} %spread.1), channel_id=1, replica_groups=mesh['z'=8,'xl'=2,'c'=2,'y'=4,'xh'=2] {'z'}, dimensions={0} | all-to-all | bytes 327680 | tf_op jit(solution)/shard_map/all_to_all | solution.py:403
  51.6 0.1 collective-permute-start.9
  51.7 2.0 %collective-permute-start.8 = (f32[256,128]{1,0:T(8,128)S(1)}, f32[256,128]{1,0:T(8,128)S(1)}, u32[]{:S(2)}, u32[]{:S(2)}) collective-permute-start(f32[256,128]{1,0:T(8,128)S(1)} %get-tuple-element.36.refs_0_), channel_id=1, source_target_pairs={{0,1},{1,0},{16,17},{17,16},{2,3},{3,2},{18,19},{19,18},{4,5},{5,4... | collective-permute-start | bytes 393224 | tf_op jit(solution)/shard_map/ppermute | solution.py:377
  53.7 1.4 %collective-permute-start.7 = (f32[256,128]{1,0:T(8,128)S(1)}, f32[256,128]{1,0:T(8,128)S(1)}, u32[]{:S(2)}, u32[]{:S(2)}) collective-permute-start(f32[256,128]{1,0:T(8,128)S(1)} %get-tuple-element.36.refs_0_), channel_id=1, source_target_pairs={{0,16},{1,17},{16,0},{17,1},{2,18},{3,19},{18,2},{19,3},{4,20},{5,... | collective-permute-start | bytes 393224 | tf_op jit(solution)/shard_map/ppermute | solution.py:377
  55.1 0.8 collective-permute-start.6
  55.9 0.0 collective-permute-done.9.far_ref
  55.9 0.0 copy-done.2
  55.9 3.9 %first_inverse.1 = (f32[128,128]{1,0:T(8,128)S(1)}, f32[128,128]{1,0:T(8,128)S(1)}) custom-call(s32[1]{0:T(128)} %bitcast.core_ref, f32[64,128]{1,0:T(8,128)S(1)} %get-tuple-element.37.near_ref, f32[64,128]{1,0:T(8,128)S(1)} %collective-permute-done.9.far_ref, f32[128,128]{1,0:T(8,128)S(1)} %copy-done.2), custom_call_target="tpu_custom_call" | custom-call | flops 3000000000 | bytes 524288 | tf_op jit(solution)/shard_map/first_inverse/pallas_call | solution.py:135
  59.8 0.0 collective-permute-done.8.refs_3_
  59.8 1.9 %collective-permute-done.7.refs_2_ = f32[256,128]{1,0:T(8,128)S(1)} collective-permute-done((f32[256,128]{1,0:T(8,128)S(1)}, f32[256,128]{1,0:T(8,128)S(1)}, u32[]{:S(2)}, u32[]{:S(2)}) %collective-permute-start.7) | collective-permute-done | bytes 131104 | tf_op jit(solution)/shard_map/ppermute | solution.py:377
  61.7 0.2 collective-permute-done.6.refs_1_
  61.9 0.0 collective-permute-done.10.refs_6_
  61.9 1.4 %solve.1 = (f32[1024,128]{1,0:T(8,128)S(1)}, f32[136,128]{1,0:T(8,128)S(1)}) custom-call(f32[256,128]{1,0:T(8,128)S(1)} %get-tuple-element.36.refs_0_, f32[256,128]{1,0:T(8,128)S(1)} %collective-permute-done.6.refs_1_, f32[256,128]{1,0:T(8,128)S(1)} %collective-permute-done.7.refs_2_, f32[256,128]{1,0:T(8,128)S(1)} %collective-permute-done.8.refs_3_, ...), custom_call_target="tpu_custom_call" | custom-call | tf_op jit(solution)/shard_map/solve/pallas_call | solution.py:362
  63.3 0.1 collective-permute-start.11
  63.4 1.2 %collective-permute-done.11 = f32[136,128]{1,0:T(8,128)S(1)} collective-permute-done((f32[136,128]{1,0:T(8,128)S(1)}, f32[136,128]{1,0:T(8,128)S(1)}, u32[]{:S(2)}, u32[]{:S(2)}) %collective-permute-start.11) | collective-permute-done | bytes 69664 | tf_op jit(solution)/shard_map/ppermute | solution.py:377
  64.7 0.2 collective-permute-start.12
  64.9 3.2 %collective-permute-start.15 = (f32[136,128]{1,0:T(8,128)S(1)}, f32[136,128]{1,0:T(8,128)S(1)}, u32[]{:S(2)}, u32[]{:S(2)}) collective-permute-start(f32[136,128]{1,0:T(8,128)S(1)} %add.11.refs_0_), channel_id=1, source_target_pairs={{0,4},{2,6},{4,0},{6,2},{1,5},{3,7},{5,1},{7,3},{8,12},{10,14},{12... | collective-permute-start | bytes 208904 | tf_op jit(solution)/shard_map/ppermute | solution.py:377
  68.1 1.1 %collective-permute-start.14 = (f32[136,128]{1,0:T(8,128)S(1)}, f32[136,128]{1,0:T(8,128)S(1)}, u32[]{:S(2)}, u32[]{:S(2)}) collective-permute-start(f32[136,128]{1,0:T(8,128)S(1)} %add.11.refs_0_), channel_id=1, source_target_pairs={{0,6},{2,4},{4,2},{6,0},{1,7},{3,5},{5,3},{7,1},{8,14},{10,12},{12... | collective-permute-start | bytes 208904 | tf_op jit(solution)/shard_map/ppermute | solution.py:377
  69.2 0.0 collective-permute-start.13
  69.2 0.0 collective-permute-done.12
  69.2 1.6 %assemble.1 = f32[8,256,128]{2,1,0:T(8,128)} custom-call(s32[2]{0:T(128)S(1)} %get-tuple-element.29.at_ref, f32[4,256,128]{2,1,0:T(8,128)S(1)} %bitcast.11, f32[4,256,128]{2,1,0:T(8,128)S(1)} %bitcast.12), custom_call_target="tpu_custom_call" | custom-call | tf_op jit(solution)/shard_map/assemble/pallas_call | solution.py:169
  70.8 0.1 collective-permute-done.15.refs_3_
  70.9 2.8 %collective-permute-done.14.refs_2_ = f32[136,128]{1,0:T(8,128)S(1)} collective-permute-done((f32[136,128]{1,0:T(8,128)S(1)}, f32[136,128]{1,0:T(8,128)S(1)}, u32[]{:S(2)}, u32[]{:S(2)}) %collective-permute-start.14) | collective-permute-done | bytes 69664 | tf_op jit(solution)/shard_map/ppermute | solution.py:377
  73.6 0.0 collective-permute-done.13.refs_1_
  73.6 0.6 collect.1
  74.3 3.9 %all-to-all-start.2 = ((f32[16,4,128]{2,1,0:T(4,128)}), f32[16,4,128]{2,1,0:T(4,128)S(1)}, u32[]{:S(2)}, u32[]{:S(2)}) async-start(f32[16,4,128]{2,1,0:T(4,128)} %collect.1), calls=%async_computation.2 | async-start | bytes 65536 | tf_op jit(solution)/shard_map/all_to_all | solution.py:419
  78.2 3.9 %inverse_of_product.1.inv_ref = f32[128,128]{1,0:T(8,128)S(1)} custom-call(f32[128,128]{1,0:T(8,128)S(1)} %get-tuple-element.47.first_ref, f32[136,128]{1,0:T(8,128)S(1)} %add.11.refs_0_, f32[136,128]{1,0:T(8,128)S(1)} %collective-permute-done.13.refs_1_, f32[136,128]{1,0:T(8,128)S(1)} %collective-permute-done.14.refs_2_, ...), custom_call_target="tpu_custom_call" | custom-call | flops 3000000000 | bytes 524288 | tf_op jit(solution)/shard_map/inverse_of_product/pallas_call | solution.py:91
  82.1 3.5 %all-to-all-done.2.x_ref = f32[16,4,128]{2,1,0:T(4,128)S(1)} async-done(((f32[16,4,128]{2,1,0:T(4,128)}), f32[16,4,128]{2,1,0:T(4,128)S(1)}, u32[]{:S(2)}, u32[]{:S(2)}) %all-to-all-start.2) | async-done | bytes 32800 | tf_op jit(solution)/shard_map/all_to_all | solution.py:419
  85.7 0.8 product.1
  (5 shorter events, 0.1 us)
Async XLA Ops:
  0.7 5.5 %copy-start = (f32[256,128]{1,0:T(8,128)S(1)}, f32[256,128]{1,0:T(8,128)}, u32[]{:S(2)}) copy-start(f32[256,128]{1,0:T(8,128)} %a_in.3) | copy-start | bytes 393220
  0.7 5.8 %copy-start.1 = (f32[4,128]{1,0:T(4,128)S(1)}, f32[4,128]{1,0:T(4,128)}, u32[]{:S(2)}) copy-start(f32[4,128]{1,0:T(4,128)} %c_in.3) | copy-start | bytes 6148
  5.6 56.4 %collective-permute-start.10 = (f32[4,1024,128]{2,1,0:T(8,128)S(1)}, f32[4,1024,128]{2,1,0:T(8,128)S(1)}, u32[]{:S(2)}, u32[]{:S(2)}) collective-permute-start(f32[4,1024,128]{2,1,0:T(8,128)S(1)} %get-tuple-element.40), channel_id=1, source_target_pairs={{0,8},{8,0},{1,9},{9,1},{2,10},{10,2},{3,11},{11,3},{4,12},{12,4},... | collective-permute-start | bytes 6291464 | tf_op jit(solution)/shard_map/ppermute | solution.py:377
  5.7 5.6 %collective-permute-start.2 = (f32[1024,128]{1,0:T(8,128)S(1)}, f32[1024,128]{1,0:T(8,128)S(1)}, u32[]{:S(2)}, u32[]{:S(2)}) collective-permute-start(f32[1024,128]{1,0:T(8,128)S(1)} %get-tuple-element.31), channel_id=1, source_target_pairs={{0,8},{8,0},{1,9},{9,1},{2,10},{10,2},{3,11},{11,3},{4,12},{12,4},... | collective-permute-start | bytes 1572872 | tf_op jit(solution)/shard_map/ppermute | solution.py:377
  11.3 44.6 %copy-start.2 = (f32[128,128]{1,0:T(8,128)S(1)}, f32[128,128]{1,0:T(8,128)}, u32[]{:S(2)}) copy-start(f32[128,128]{1,0:T(8,128)} %second_ref.1) | copy-start | bytes 196612
  11.4 10.6 %collective-permute-start.3 = (f32[256,128]{1,0:T(8,128)S(1)}, f32[256,128]{1,0:T(8,128)S(1)}, u32[]{:S(2)}, u32[]{:S(2)}) collective-permute-start(f32[256,128]{1,0:T(8,128)S(1)} %get-tuple-element.33), channel_id=1, source_target_pairs={{0,1},{1,0},{16,17},{17,16},{2,3},{3,2},{18,19},{19,18},{4,5},{5,4... | collective-permute-start | bytes 393224 | tf_op jit(solution)/shard_map/ppermute | solution.py:377
  13.6 8.4 %collective-permute-start.4 = (f32[256,128]{1,0:T(8,128)S(1)}, f32[256,128]{1,0:T(8,128)S(1)}, u32[]{:S(2)}, u32[]{:S(2)}) collective-permute-start(f32[256,128]{1,0:T(8,128)S(1)} %get-tuple-element.34), channel_id=1, source_target_pairs={{0,16},{1,17},{16,0},{17,1},{2,18},{3,19},{18,2},{19,3},{4,20},{5,... | collective-permute-start | bytes 393224 | tf_op jit(solution)/shard_map/ppermute | solution.py:377
  15.0 7.0 %collective-permute-start.5 = (f32[256,128]{1,0:T(8,128)S(1)}, f32[256,128]{1,0:T(8,128)S(1)}, u32[]{:S(2)}, u32[]{:S(2)}) collective-permute-start(f32[256,128]{1,0:T(8,128)S(1)} %get-tuple-element.35), channel_id=1, source_target_pairs={{0,17},{1,16},{16,1},{17,0},{2,19},{3,18},{18,3},{19,2},{4,21},{5,... | collective-permute-start | bytes 393224 | tf_op jit(solution)/shard_map/ppermute | solution.py:377
  15.5 1.2 %collective-permute-start = (f32[64,128]{1,0:T(8,128)S(1)}, f32[64,128]{1,0:T(8,128)S(1)}, u32[]{:S(2)}, u32[]{:S(2)}) collective-permute-start(f32[64,128]{1,0:T(8,128)S(1)} %get-tuple-element.28), channel_id=1, source_target_pairs={{0,8},{8,0},{1,9},{9,1},{2,10},{10,2},{3,11},{11,3},{4,12},{12,4},... | collective-permute-start | bytes 98312 | tf_op jit(solution)/shard_map/ppermute | solution.py:377
  16.8 5.2 %collective-permute-start.1 = (f32[64,128]{1,0:T(8,128)S(1)}, f32[64,128]{1,0:T(8,128)S(1)}, u32[]{:S(2)}, u32[]{:S(2)}) collective-permute-start(f32[64,128]{1,0:T(8,128)S(1)} %add.10.g_ref), channel_id=1, source_target_pairs={{0,16},{16,0},{1,17},{17,1},{2,18},{18,2},{3,19},{19,3},{4,20},{20... | collective-permute-start | bytes 98312 | tf_op jit(solution)/shard_map/ppermute | solution.py:377
  51.6 4.3 %collective-permute-start.9 = (f32[64,128]{1,0:T(8,128)S(1)}, f32[64,128]{1,0:T(8,128)S(1)}, u32[]{:S(2)}, u32[]{:S(2)}) collective-permute-start(f32[64,128]{1,0:T(8,128)S(1)} %get-tuple-element.37.near_ref), channel_id=1, source_target_pairs={{0,8},{8,0},{1,9},{9,1},{2,10},{10,2},{3,11},{11,3},{4,12},{12,4},... | collective-permute-start | bytes 98312 | tf_op jit(solution)/shard_map/ppermute | solution.py:377
  51.7 8.1 %collective-permute-start.8 = (f32[256,128]{1,0:T(8,128)S(1)}, f32[256,128]{1,0:T(8,128)S(1)}, u32[]{:S(2)}, u32[]{:S(2)}) collective-permute-start(f32[256,128]{1,0:T(8,128)S(1)} %get-tuple-element.36.refs_0_), channel_id=1, source_target_pairs={{0,1},{1,0},{16,17},{17,16},{2,3},{3,2},{18,19},{19,18},{4,5},{5,4... | collective-permute-start | bytes 393224 | tf_op jit(solution)/shard_map/ppermute | solution.py:377
  53.7 8.1 %collective-permute-start.7 = (f32[256,128]{1,0:T(8,128)S(1)}, f32[256,128]{1,0:T(8,128)S(1)}, u32[]{:S(2)}, u32[]{:S(2)}) collective-permute-start(f32[256,128]{1,0:T(8,128)S(1)} %get-tuple-element.36.refs_0_), channel_id=1, source_target_pairs={{0,16},{1,17},{16,0},{17,1},{2,18},{3,19},{18,2},{19,3},{4,20},{5,... | collective-permute-start | bytes 393224 | tf_op jit(solution)/shard_map/ppermute | solution.py:377
  55.1 6.8 %collective-permute-start.6 = (f32[256,128]{1,0:T(8,128)S(1)}, f32[256,128]{1,0:T(8,128)S(1)}, u32[]{:S(2)}, u32[]{:S(2)}) collective-permute-start(f32[256,128]{1,0:T(8,128)S(1)} %get-tuple-element.36.refs_0_), channel_id=1, source_target_pairs={{0,17},{1,16},{16,1},{17,0},{2,19},{3,18},{18,3},{19,2},{4,21},{5,... | collective-permute-start | bytes 393224 | tf_op jit(solution)/shard_map/ppermute | solution.py:377
  63.3 1.3 %collective-permute-start.11 = (f32[136,128]{1,0:T(8,128)S(1)}, f32[136,128]{1,0:T(8,128)S(1)}, u32[]{:S(2)}, u32[]{:S(2)}) collective-permute-start(f32[136,128]{1,0:T(8,128)S(1)} %get-tuple-element.41), channel_id=1, source_target_pairs={{0,8},{8,0},{1,9},{9,1},{2,10},{10,2},{3,11},{11,3},{4,12},{12,4},... | collective-permute-start | bytes 208904 | tf_op jit(solution)/shard_map/ppermute | solution.py:377
  64.7 4.5 %collective-permute-start.12 = (f32[1024,128]{1,0:T(8,128)S(1)}, f32[1024,128]{1,0:T(8,128)S(1)}, u32[]{:S(2)}, u32[]{:S(2)}) collective-permute-start(f32[1024,128]{1,0:T(8,128)S(1)} %get-tuple-element.44), channel_id=1, source_target_pairs={{0,8},{8,0},{1,9},{9,1},{2,10},{10,2},{3,11},{11,3},{4,12},{12,4},... | collective-permute-start | bytes 1572872 | tf_op jit(solution)/shard_map/ppermute | solution.py:377
  64.9 5.9 %collective-permute-start.15 = (f32[136,128]{1,0:T(8,128)S(1)}, f32[136,128]{1,0:T(8,128)S(1)}, u32[]{:S(2)}, u32[]{:S(2)}) collective-permute-start(f32[136,128]{1,0:T(8,128)S(1)} %add.11.refs_0_), channel_id=1, source_target_pairs={{0,4},{2,6},{4,0},{6,2},{1,5},{3,7},{5,1},{7,3},{8,12},{10,14},{12... | collective-permute-start | bytes 208904 | tf_op jit(solution)/shard_map/ppermute | solution.py:377
  68.1 5.5 %collective-permute-start.14 = (f32[136,128]{1,0:T(8,128)S(1)}, f32[136,128]{1,0:T(8,128)S(1)}, u32[]{:S(2)}, u32[]{:S(2)}) collective-permute-start(f32[136,128]{1,0:T(8,128)S(1)} %add.11.refs_0_), channel_id=1, source_target_pairs={{0,6},{2,4},{4,2},{6,0},{1,7},{3,5},{5,3},{7,1},{8,14},{10,12},{12... | collective-permute-start | bytes 208904 | tf_op jit(solution)/shard_map/ppermute | solution.py:377
  69.2 4.5 %collective-permute-start.13 = (f32[136,128]{1,0:T(8,128)S(1)}, f32[136,128]{1,0:T(8,128)S(1)}, u32[]{:S(2)}, u32[]{:S(2)}) collective-permute-start(f32[136,128]{1,0:T(8,128)S(1)} %add.11.refs_0_), channel_id=1, source_target_pairs={{0,2},{2,0},{4,6},{6,4},{1,3},{3,1},{5,7},{7,5},{8,10},{10,8},{12,... | collective-permute-start | bytes 208904 | tf_op jit(solution)/shard_map/ppermute | solution.py:377
  74.3 11.4 %all-to-all-start.2 = ((f32[16,4,128]{2,1,0:T(4,128)}), f32[16,4,128]{2,1,0:T(4,128)S(1)}, u32[]{:S(2)}, u32[]{:S(2)}) async-start(f32[16,4,128]{2,1,0:T(4,128)} %collect.1), calls=%async_computation.2 | async-start | bytes 65536 | tf_op jit(solution)/shard_map/all_to_all | solution.py:419
